TPU v7x, 32 devices: a whole 2x2x4 slice. The times are simulated.
32 devices in a mesh: section: 4 (over y, x), dp: 8 (over z, core).
Axes of the slice: x: 2, y: 2, z: 4, core: 2. Of those that a mesh axis runs over, the one named last changes fastest.
Arguments:
- acts: bfloat16 [4, 2048, 2560], P('section', 'dp'), may hold values from -6 to 6
- gates: bfloat16 [4, 2048, 1280], P('section', 'dp'), may hold values from -6 to 6
- w_value: bfloat16 [4, 2560, 1280], P('section', 'dp'), may hold values from -0.125 to 0.125
- w_out: bfloat16 [4, 2560, 1280], P('section', 'dp'), may hold values from -0.125 to 0.125
- residual_error: bfloat16 [4, 20480, 1280], P('section', 'dp'), may hold values from -48 to 48
- grad_top: bfloat16 [2048, 2560], P('dp'), may hold values from -6 to 6
- warm_factor: float32 [4, 4, 1280], P('section'), may hold values from -6 to 6
Outputs:
- grad_in: bfloat16 [4, 2048, 2560], P('section', 'dp')
- basis_out: float32 [4, 4, 2560], P('section')
- right_out: float32 [4, 4, 1280], P('section')
All inputs are finite; a program needn't handle non-finite values.
Results may differ from a plain program's by a relative error of at most 0.009.
Values may be sent and summed in bfloat16 or wider, within the bound.
No kernel may reach another device: no remote copies, remote signals or barrier semaphores. Data moves between devices by JAX's collectives and lax.ppermute only.
A program may use at most 128 MiB of HBM per device.

v0:
```python
import math

import jax
import jax.numpy as jnp
from jax import lax
from jax.experimental import pallas as pl
from jax.experimental.pallas import tpu as pltpu
from jax.sharding import PartitionSpec as P


MICRO = 4
CORES = 2
HIGHEST = lax.Precision.HIGHEST
VMEM = pl.BlockSpec(memory_space=pltpu.VMEM)
ANY = pl.BlockSpec(memory_space=pl.ANY)


def put(whole, pieces, shape, dtype):
    arrays = list({id(piece): piece for _, piece, _, _ in pieces}.values())
    rows = arrays[0].shape[0]
    if rows % 16:
        whole = jnp.zeros(shape, dtype) if whole is None else whole
        rank = lax.axis_index("dp")
        for kind, piece, source, valid in pieces:
            at = jnp.clip(source(rank), 0, shape[1] // rows - 1) * rows
            held = lax.dynamic_slice(whole, (kind, at, 0), (1,) + piece.shape)
            piece = jnp.where(valid(rank), piece[None], held)
            whole = lax.dynamic_update_slice(whole, piece, (kind, at, 0))
        return whole

    def body(*refs):
        out, done = refs[-2:]
        rank = lax.axis_index("dp")
        for phase in ("start", "wait"):
            for sem, (kind, piece, source, valid) in enumerate(pieces):
                ref = refs[[array is piece for array in arrays].index(True)]

                @pl.when(valid(rank))
                def _():
                    at = pl.ds(pl.multiple_of(source(rank) * rows, 16), rows)
                    copy = pltpu.make_async_copy(ref, out.at[kind, at], done.at[sem])
                    getattr(copy, phase)()

    held = [] if whole is None else [whole]
    return pl.pallas_call(
        body,
        in_specs=[ANY] * len(arrays) + [VMEM] * len(held),
        out_specs=VMEM,
        out_shape=jax.ShapeDtypeStruct(shape, dtype),
        input_output_aliases={len(arrays): 0} if held else {},
        scratch_shapes=[pltpu.SemaphoreType.DMA((len(pieces),))],
        compiler_params=pltpu.CompilerParams(vmem_limit_bytes=4 << 20),
        name="put",
    )(*arrays, *held)


def gather_weights(matrices):
    sections = lax.axis_size("section")
    replicas = lax.axis_size("dp")
    chips = replicas // CORES
    top = sections - 1
    relayed = top > 0 and chips > 3
    rows, channels = matrices[0].shape
    shape, dtype = (len(matrices), replicas * rows, channels), matrices[0].dtype

    def permute(value, moves):
        pairs = [
            ((s * chips + c) * CORES + k, (t * chips + d) * CORES + k)
            for s, c, t, d in moves
            for k in range(CORES)
        ]
        return lax.ppermute(value, ("section", "dp"), pairs)

    def line(value, moves, skip=()):
        moves = [(s, c, s, d) for s in range(sections) for c, d in moves]
        return permute(value, [move for move in moves if move not in skip])

    def swap(value, first=0, last=chips):
        pairs = [(i, i ^ 1) for i in range(first * CORES, last * CORES)]
        return lax.ppermute(value, "dp", pairs)

    def shards(piece, other, by, first=0, last=chips, at_top=None):
        def source(rank):
            return rank + by * CORES

        def beside(rank):
            return rank + by * CORES + 1 - 2 * (rank % CORES)

        def valid(rank):
            inside = (rank >= first * CORES) & (rank < last * CORES)
            if at_top is not None:
                inside &= (lax.axis_index("section") == top) == at_top
            return inside

        return [(piece, source, valid), (other, beside, valid)]

    inner, outer = (1, chips - 2), (0, chips - 1)
    dropped = [(top, c, top, d) for c, d in zip(inner, outer)] if relayed else []
    up, down = list(matrices), list(matrices)
    relay = None
    groups = [[], [], []]
    for step in range(1, chips):
        for kind in range(len(matrices)):
            skip = dropped if step == 1 and kind == 1 else ()
            if step < chips - 1:
                moves = [(c - 1, c) for c in range(step, chips)]
                up[kind] = line(up[kind], moves, skip)
                moves = [(c + 1, c) for c in range(chips - step)]
                down[kind] = line(down[kind], moves, skip)
            else:
                low = lax.axis_index("dp") < replicas // 2
                last = jnp.where(low, down[kind], up[kind])
                moves = [(1, 0), (chips - 2, chips - 1)]
                up[kind] = line(last, moves)
        if step == 1:
            if relayed:
                relay = permute(matrices[1], [(top, c, 0, c) for c in inner])
                relay = permute(relay, [(0, c, 0, d) for c, d in zip(inner, outer)])
                relay = permute(relay, [(0, c, top, c) for c in outer])
            for kind, matrix in enumerate(matrices):
                own = shards(matrix, swap(matrix), 0)
                groups[0] += [(kind,) + piece for piece in own]
        for kind in range(len(matrices)):
            if step < chips - 1:
                from_below = swap(up[kind], step, chips)
                from_above = swap(down[kind], 0, chips - step)
                low, high = (1, chips - 1) if step == 1 and kind == 1 and relayed else (0, chips)
                pieces = shards(up[kind], from_below, -step, step, high)
                pieces += shards(down[kind], from_above, step, low, chips - step)
                if low:
                    pieces += shards(up[kind], from_below, -step, high, chips, False)
                    pieces += shards(down[kind], from_above, step, 0, low, False)
            else:
                other = swap(up[kind])
                pieces = shards(up[kind], other, step, 0, 1)
                pieces += shards(up[kind], other, -step, step, chips)
            behind = 2 * (chips - 1 - step) + len(matrices) - 1 - kind
            groups[0 if behind > 3 else 1 if behind else 2] += [
                (kind,) + piece for piece in pieces
            ]
        if relayed and step == chips - 2:
            other = swap(relay)
            pieces = shards(relay, other, 1, 0, 1, True)
            pieces += shards(relay, other, -1, chips - 1, chips, True)
            groups[1] += [(1,) + piece for piece in pieces]
    whole = None
    for group in groups:
        whole = put(whole, group, shape, dtype)
    return whole


def stage(whole, arriving, gates, held, early, *, section, part, block):
    width = arriving.shape[1]
    row_count, channels = gates.shape
    lanes, deep = math.gcd(channels, 256), math.gcd(width, 512)
    at = pl.ds(part * block, block)
    read = at if arriving.shape[0] == row_count else pl.ds(0, block)

    def body(w, arr, gate, *refs):
        vg_ref, passed_ref, send = refs[-3:]

        @pl.when(lax.axis_index("section") == section)
        def _():
            def forward(step, carry):
                cols = pl.ds(pl.multiple_of(step * lanes, lanes), lanes)
                hidden = jnp.dot(
                    arr[read], w[0, :width, cols], preferred_element_type=jnp.float32
                )
                hidden = hidden * gate[at, cols].astype(jnp.float32)
                vg_ref[at, cols] = hidden.astype(jnp.bfloat16)
                return carry

            lax.fori_loop(0, channels // lanes, forward, 0)

            def backward(step, carry):
                cols = pl.ds(pl.multiple_of(step * deep, deep), deep)
                back = lax.dot_general(
                    vg_ref[at], w[1, cols], (((1,), (1,)), ((), ())),
                    preferred_element_type=jnp.float32,
                )
                passed = (arr[read, cols].astype(jnp.float32) + back).astype(jnp.bfloat16)
                passed_ref[at, cols] = passed
                send[:, cols] = passed
                return carry

            lax.fori_loop(0, width // deep, backward, 0)

    return pl.pallas_call(
        body,
        in_specs=[VMEM] * 3 + [ANY] + [VMEM] * len(held),
        out_specs=[VMEM] * 3,
        out_shape=[
            jax.ShapeDtypeStruct((row_count, channels), jnp.bfloat16),
            jax.ShapeDtypeStruct((row_count, width), jnp.bfloat16),
            jax.ShapeDtypeStruct((block, width), jnp.bfloat16),
        ],
        input_output_aliases={4 + k: k for k in range(len(held))},
        compiler_params=pltpu.CompilerParams(vmem_limit_bytes=8 << 20),
        cost_estimate=pl.CostEstimate(
            flops=4 * block * width * channels,
            bytes_accessed=4 * width * channels,
            transcendentals=0,
        ),
    )(whole, arriving, gates, early, *held)


def split3(value):
    high = value.astype(jnp.bfloat16)
    rest = value - high.astype(jnp.float32)
    middle = rest.astype(jnp.bfloat16)
    low = (rest - middle.astype(jnp.float32)).astype(jnp.bfloat16)
    return jnp.concatenate([high, middle, low], 0)


def join3(value):
    count = value.shape[0] // 3
    return value[:count] + (value[count : 2 * count] + value[2 * count :])


def orthonormal(vectors):
    result = []
    for column in range(vectors.shape[0]):
        current = vectors[column : column + 1]
        for previous in result:
            current = current - jnp.mean(current * previous, axis=1, keepdims=True) * previous
        mean = jnp.mean(current * current, axis=1, keepdims=True)
        result.append(current / jnp.sqrt(mean + 1e-06))
    return jnp.concatenate(result, 0)


def second_half(left, right, inputs, value_grads, error, passed_rows):
    def body(left, right, acts, vg, err, passed, basis_ref, second_ref, out_ref, done):
        copy = pltpu.make_async_copy(passed, out_ref, done)
        copy.start()
        basis = orthonormal(left[...] + right[...])
        basis_ref[...] = basis
        parts = split3(basis)
        mapped = lax.dot_general(
            parts, acts[...], (((1,), (1,)), ((), ())), preferred_element_type=jnp.float32
        )
        second = jnp.dot(parts, err[...], preferred_element_type=jnp.float32)
        second = second + jnp.dot(
            split3(join3(mapped)), vg[...], preferred_element_type=jnp.float32
        )
        second_ref[...] = join3(second)
        copy.wait()

    rank, width = left.shape
    channels = value_grads.shape[1]
    return pl.pallas_call(
        body,
        in_specs=[VMEM] * 6,
        out_specs=[VMEM, VMEM, ANY],
        out_shape=[
            jax.ShapeDtypeStruct((rank, width), jnp.float32),
            jax.ShapeDtypeStruct((rank, channels), jnp.float32),
            jax.ShapeDtypeStruct(passed_rows.shape, passed_rows.dtype),
        ],
        scratch_shapes=[pltpu.SemaphoreType.DMA],
        compiler_params=pltpu.CompilerParams(vmem_limit_bytes=8 << 20),
        name="second_half",
    )(left, right, inputs, value_grads, error, passed_rows)


def exchange(value, by):
    replicas = lax.axis_size("dp")
    return lax.ppermute(value, "dp", [(i, i ^ by) for i in range(replicas)])


def sum_but_last(value):
    by = 1
    while by * 2 < lax.axis_size("dp"):
        value = value + exchange(value, by)
        by *= 2
    return value, exchange(value, by)


def local(acts, gates, w_value, w_out, residual_error, grad_top, warm_factor):
    sections = lax.axis_size("section")
    replicas = lax.axis_size("dp")
    inputs, gate_rows, error, warm = acts[0], gates[0], residual_error[0], warm_factor[0]
    row_count, width = inputs.shape
    error_part = lax.dot_general(
        warm, error.astype(jnp.float32), (((1,), (1,)), ((), ())), precision=HIGHEST
    )
    whole = gather_weights((w_out[0], w_value[0]))
    arriving = [grad_top] * MICRO
    held = []
    for section in reversed(range(sections)):
        for k in range(MICRO):
            *held, send = stage(
                whole, arriving[k], gate_rows, held, error_part,
                section=section, part=k, block=row_count // MICRO,
            )
            if section:
                arriving[k] = lax.ppermute(send, "section", [(section, section - 1)])
    value_grads, passed_rows = held
    projected = jnp.dot(value_grads.astype(jnp.float32), warm.T, precision=HIGHEST)
    factor = lax.dot_general(
        projected, inputs.astype(jnp.float32), (((0,), (0,)), ((), ())), precision=HIGHEST
    )
    left, right = sum_but_last(factor + error_part)
    basis, second, grad_in = second_half(left, right, inputs, value_grads, error, passed_rows)
    left, right = sum_but_last(second)
    right_out = (left + right) / math.sqrt(row_count * replicas * width)
    return grad_in[None], basis[None], right_out[None]


def solution(mesh):
    return jax.shard_map(
        local,
        mesh=mesh,
        in_specs=(
            P("section", "dp", None),
            P("section", "dp", None),
            P("section", "dp", None),
            P("section", "dp", None),
            P("section", "dp", None),
            P("dp", None),
            P("section", None, None),
        ),
        out_specs=(P("section", "dp", None), P("section", None, None), P("section", None, None)),
        check_vma=False,
    )
```

profile of v0, /device:TPU:0, one launch (start us, length us, event | category | flops | bytes accessed | tf_op | source)
XLA Modules:
  0.0 240.8 jit_solution(12608991317902761449)
XLA Ops:
  0.6 5.9 %collective-permute-start.2 = (bf16[320,1280]{1,0:T(8,128)(2,1)}, bf16[320,1280]{1,0:T(8,128)(2,1)}, u32[]{:S(2)}, u32[]{:S(2)}) collective-permute-start(bf16[320,1280]{1,0:T(8,128)(2,1)} %bitcast.40), channel_id=1, source_target_pairs={{0,2},{1,3},{2,4},{3,5},{4,6},{5,7},{8,10},{9,11},{10,12},{11,13},... | collective-permute-start | bytes 2457608 | tf_op jit(solution)/shard_map/ppermute | solution.py:72
  6.5 1.3 collective-permute-start
  7.8 1.3 collective-permute-start.9
  9.1 6.1 %collective-permute-start.6 = (bf16[320,1280]{1,0:T(8,128)(2,1)}, bf16[320,1280]{1,0:T(8,128)(2,1)}, u32[]{:S(2)}, u32[]{:S(2)}) collective-permute-start(bf16[320,1280]{1,0:T(8,128)(2,1)} %bitcast.46), channel_id=1, source_target_pairs={{0,2},{1,3},{2,4},{3,5},{4,6},{5,7},{8,10},{9,11},{10,12},{11,13},... | collective-permute-start | bytes 2457608 | tf_op jit(solution)/shard_map/ppermute | solution.py:72
  15.2 9.3 %collective-permute-done.2.refs_8_ = bf16[320,1280]{1,0:T(8,128)(2,1)} collective-permute-done((bf16[320,1280]{1,0:T(8,128)(2,1)}, bf16[320,1280]{1,0:T(8,128)(2,1)}, u32[]{:S(2)}, u32[]{:S(2)}) %collective-permute-start.2) | collective-permute-done | bytes 819232 | tf_op jit(solution)/shard_map/ppermute | solution.py:72
  24.5 5.3 %collective-permute-done.refs_10_ = bf16[320,1280]{1,0:T(8,128)(2,1)} collective-permute-done((bf16[320,1280]{1,0:T(8,128)(2,1)}, bf16[320,1280]{1,0:T(8,128)(2,1)}, u32[]{:S(2)}, u32[]{:S(2)}) %collective-permute-start) | collective-permute-done | bytes 819232 | tf_op jit(solution)/shard_map/ppermute | solution.py:72
  29.8 1.6 collective-permute-start.14
  31.4 14.6 %collective-permute-done.9.refs_6_ = bf16[320,1280]{1,0:T(8,128)(2,1)} collective-permute-done((bf16[320,1280]{1,0:T(8,128)(2,1)}, bf16[320,1280]{1,0:T(8,128)(2,1)}, u32[]{:S(2)}, u32[]{:S(2)}) %collective-permute-start.9) | collective-permute-done | bytes 819232 | tf_op jit(solution)/shard_map/ppermute | solution.py:72
  46.0 1.3 collective-permute-start.10
  47.3 0.7 collective-permute-start.7
  48.0 0.9 copy-done.6
  48.9 0.7 collective-permute-start.3
  49.7 0.9 copy-done.8
  50.5 1.3 collective-permute-start.1
  51.9 0.7 collective-permute-start.24
  52.6 16.6 %collective-permute-done.10.refs_2_ = bf16[320,1280]{1,0:T(8,128)(2,1)S(1)} collective-permute-done((bf16[320,1280]{1,0:T(8,128)(2,1)}, bf16[320,1280]{1,0:T(8,128)(2,1)S(1)}, u32[]{:S(2)}, u32[]{:S(2)}) %collective-permute-start.10) | collective-permute-done | bytes 819232 | tf_op jit(solution)/shard_map/ppermute | solution.py:72
  69.2 1.9 collective-permute-start.25
  71.1 0.7 collective-permute-start.22
  71.8 2.4 collective-permute-start.23
  74.3 10.2 %collective-permute-done.1.refs_6_ = bf16[320,1280]{1,0:T(8,128)(2,1)S(1)} collective-permute-done((bf16[320,1280]{1,0:T(8,128)(2,1)}, bf16[320,1280]{1,0:T(8,128)(2,1)S(1)}, u32[]{:S(2)}, u32[]{:S(2)}) %collective-permute-start.1) | collective-permute-done | bytes 819232 | tf_op jit(solution)/shard_map/ppermute | solution.py:72
  84.5 1.3 collective-permute-start.15
  86.0 1.6 collective-permute-start.18
  87.6 0.7 collective-permute-start.12
  88.3 1.9 collective-permute-start.13
  90.2 18.8 %collective-permute-done.15 = bf16[320,1280]{1,0:T(8,128)(2,1)S(1)} collective-permute-done((bf16[320,1280]{1,0:T(8,128)(2,1)}, bf16[320,1280]{1,0:T(8,128)(2,1)S(1)}, u32[]{:S(2)}, u32[]{:S(2)}) %collective-permute-start.15) | collective-permute-done | bytes 819232 | tf_op jit(solution)/shard_map/ppermute | solution.py:72
  109.0 1.3 collective-permute-start.16
  110.4 1.3 collective-permute-start.4
  111.7 14.9 %collective-permute-done.18.refs_10_ = bf16[320,1280]{1,0:T(8,128)(2,1)S(1)} collective-permute-done((bf16[320,1280]{1,0:T(8,128)(2,1)S(1)}, bf16[320,1280]{1,0:T(8,128)(2,1)S(1)}, u32[]{:S(2)}, u32[]{:S(2)}) %collective-permute-start.18) | collective-permute-done | bytes 819232 | tf_op jit(solution)/shard_map/ppermute | solution.py:72
  126.6 1.9 collective-permute-start.11
  128.5 0.7 collective-permute-start.8
  129.2 3.6 %collective-permute-start.19 = (bf16[320,1280]{1,0:T(8,128)(2,1)S(1)}, bf16[320,1280]{1,0:T(8,128)(2,1)S(1)}, u32[]{:S(2)}, u32[]{:S(2)}) collective-permute-start(bf16[320,1280]{1,0:T(8,128)(2,1)S(1)} %collective-permute-done.18.refs_10_), channel_id=1, source_target_pairs={{0,1},{1,0},{2,3},{3,2},{4,5},{5,4},{6,7},{7,6},{8,9},{9,8},{10,11... | collective-permute-start | bytes 2457608 | tf_op jit(solution)/shard_map/ppermute | solution.py:80
  133.2 10.7 %collective-permute-done.4.refs_0_ = bf16[320,1280]{1,0:T(8,128)(2,1)S(1)} collective-permute-done((bf16[320,1280]{1,0:T(8,128)(2,1)S(1)}, bf16[320,1280]{1,0:T(8,128)(2,1)S(1)}, u32[]{:S(2)}, u32[]{:S(2)}) %collective-permute-start.4) | collective-permute-done | bytes 819232 | tf_op jit(solution)/shard_map/ppermute | solution.py:72
  143.9 8.0 %fusion.2.refs_0_ = f32[4,2560]{1,0:T(4,128)S(1)} fusion(f32[1,4,1280]{2,1,0:T(4,128)S(1)} %copy-done, bf16[1,2560,1280]{2,1,0:T(8,128)(2,1)} %param.11), kind=kOutput, calls=%fused_computation.5 | convolution fusion | flops 157286400 | bytes 6615040 | tf_op jit(solution)/shard_map/dot_general | solution.py:283
  152.0 2.0 put.3.refs_12_
  154.0 0.8 put.4.refs_2_
  155.2 0.8 copy-done.1
  157.1 0.7 collective-permute-start.28
  157.8 0.7 collective-permute-start.27
  158.5 0.7 collective-permute-start.26
  159.2 0.7 collective-permute-start.33
  160.0 0.7 collective-permute-start.32
  162.1 1.3 collective-permute-start.37
  163.5 1.3 collective-permute-start.36
  165.0 1.3 collective-permute-start.35
  166.3 1.3 collective-permute-start.34
  167.6 21.5 %collective-permute-done.37.arr = bf16[64,2560]{1,0:T(8,128)(2,1)S(1)} collective-permute-done((bf16[64,2560]{1,0:T(8,128)(2,1)S(1)}, bf16[64,2560]{1,0:T(8,128)(2,1)S(1)}, u32[]{:S(2)}, u32[]{:S(2)}) %collective-permute-start.37) | collective-permute-done | bytes 327712 | tf_op jit(solution)/shard_map/ppermute | solution.py:296
  189.1 5.1 %shard_map.106 = (bf16[256,1280]{1,0:T(8,128)(2,1)S(1)}, bf16[256,2560]{1,0:T(8,128)(2,1)S(1)}, bf16[64,2560]{1,0:T(8,128)(2,1)}) custom-call(bf16[2,2560,1280]{2,1,0:T(8,128)(2,1)S(1)} %put.5.w, bf16[64,2560]{1,0:T(8,128)(2,1)S(1)} %collective-permute-done.37.arr, bf16[256,1280]{1,0:T(8,128)(2,1)S(1)} %bitcast.32, ...), custom_call_target="tpu_custom_call", output_to_operand_aliasing={{0}: (4, {}), {1}: (5, {})} | custom-call | flops 838860800 | bytes 13107200 | tf_op jit(solution)/shard_map/pallas_call | solution.py:188
  194.2 1.9 collective-permute-done.36.arr
  196.1 5.1 %shard_map.107 = (bf16[256,1280]{1,0:T(8,128)(2,1)S(1)}, bf16[256,2560]{1,0:T(8,128)(2,1)S(1)}, bf16[64,2560]{1,0:T(8,128)(2,1)}) custom-call(bf16[2,2560,1280]{2,1,0:T(8,128)(2,1)S(1)} %put.5.w, bf16[64,2560]{1,0:T(8,128)(2,1)S(1)} %collective-permute-done.36.arr, bf16[256,1280]{1,0:T(8,128)(2,1)S(1)} %bitcast.33, ...), custom_call_target="tpu_custom_call", output_to_operand_aliasing={{0}: (4, {}), {1}: (5, {})} | custom-call | flops 838860800 | bytes 13107200 | tf_op jit(solution)/shard_map/pallas_call | solution.py:188
  201.2 1.9 collective-permute-done.35.arr
  203.1 5.1 %shard_map.108 = (bf16[256,1280]{1,0:T(8,128)(2,1)S(1)}, bf16[256,2560]{1,0:T(8,128)(2,1)S(1)}, bf16[64,2560]{1,0:T(8,128)(2,1)}) custom-call(bf16[2,2560,1280]{2,1,0:T(8,128)(2,1)S(1)} %put.5.w, bf16[64,2560]{1,0:T(8,128)(2,1)S(1)} %collective-permute-done.35.arr, bf16[256,1280]{1,0:T(8,128)(2,1)S(1)} %bitcast.34, ...), custom_call_target="tpu_custom_call", output_to_operand_aliasing={{0}: (4, {}), {1}: (5, {})} | custom-call | flops 838860800 | bytes 13107200 | tf_op jit(solution)/shard_map/pallas_call | solution.py:188
  208.3 2.5 %collective-permute-done.34.arr = bf16[64,2560]{1,0:T(8,128)(2,1)S(1)} collective-permute-done((bf16[64,2560]{1,0:T(8,128)(2,1)S(1)}, bf16[64,2560]{1,0:T(8,128)(2,1)S(1)}, u32[]{:S(2)}, u32[]{:S(2)}) %collective-permute-start.34) | collective-permute-done | bytes 327712 | tf_op jit(solution)/shard_map/ppermute | solution.py:296
  210.8 5.1 %shard_map.109 = (bf16[256,1280]{1,0:T(8,128)(2,1)S(1)}, bf16[256,2560]{1,0:T(8,128)(2,1)S(1)}, bf16[64,2560]{1,0:T(8,128)(2,1)}) custom-call(bf16[2,2560,1280]{2,1,0:T(8,128)(2,1)S(1)} %put.5.w, bf16[64,2560]{1,0:T(8,128)(2,1)S(1)} %collective-permute-done.34.arr, bf16[256,1280]{1,0:T(8,128)(2,1)S(1)} %bitcast.35, ...), custom_call_target="tpu_custom_call", output_to_operand_aliasing={{0}: (4, {}), {1}: (5, {})} | custom-call | flops 838860800 | bytes 13107200 | tf_op jit(solution)/shard_map/pallas_call | solution.py:188
  217.2 1.2 collective-permute-done.38
  218.5 2.0 collective-permute-start.39
  220.4 2.1 collective-permute-done.39
  222.5 2.9 %collective-permute-start.40 = (f32[4,2560]{1,0:T(4,128)S(1)}, f32[4,2560]{1,0:T(4,128)S(1)}, u32[]{:S(2)}, u32[]{:S(2)}) collective-permute-start(f32[4,2560]{1,0:T(4,128)S(1)} %add.20.left), channel_id=1, source_target_pairs={{0,4},{1,5},{2,6},{3,7},{4,0},{5,1},{6,2},{7,3},{8,12},{9,13},{10,... | collective-permute-start | bytes 122888 | tf_op jit(solution)/shard_map/ppermute | solution.py:267
  225.4 2.1 collective-permute-done.40.right
  227.5 2.8 %second_half.1 = (f32[4,2560]{1,0:T(4,128)}, f32[4,1280]{1,0:T(4,128)S(1)}, bf16[256,2560]{1,0:T(8,128)(2,1)}) custom-call(f32[4,2560]{1,0:T(4,128)S(1)} %add.20.left, f32[4,2560]{1,0:T(4,128)S(1)} %collective-permute-done.40.right, bf16[256,2560]{1,0:T(8,128)(2,1)S(1)} %bitcast.39, bf16[256,1280]{1,0:T(8,128)(2,1)S(1)} %get-tuple-element.92.vg, ...), custom_call_target="tpu_custom_call" | custom-call | tf_op jit(solution)/shard_map/second_half/pallas_call | solution.py:250
  230.4 1.2 collective-permute-done.41
  231.6 2.0 collective-permute-start.42
  233.6 1.9 collective-permute-done.42
  235.4 3.0 %collective-permute-start.43 = (f32[4,1280]{1,0:T(4,128)S(1)}, f32[4,1280]{1,0:T(4,128)S(1)}, u32[]{:S(2)}, u32[]{:S(2)}) collective-permute-start(f32[4,1280]{1,0:T(4,128)S(1)} %add.22), channel_id=1, source_target_pairs={{0,4},{1,5},{2,6},{3,7},{4,0},{5,1},{6,2},{7,3},{8,12},{9,13},{10,... | collective-permute-start | bytes 61448 | tf_op jit(solution)/shard_map/ppermute | solution.py:267
  238.4 1.8 collective-permute-done.43
  (79 shorter events, 5.9 us)
Async XLA Ops:
  0.6 143.3 %copy-start = (f32[1,4,1280]{2,1,0:T(4,128)S(1)}, f32[1,4,1280]{2,1,0:T(4,128)}, u32[]{:S(2)}) copy-start(f32[1,4,1280]{2,1,0:T(4,128)} %param.13) | copy-start | bytes 61444
  0.6 23.9 %collective-permute-start.2 = (bf16[320,1280]{1,0:T(8,128)(2,1)}, bf16[320,1280]{1,0:T(8,128)(2,1)}, u32[]{:S(2)}, u32[]{:S(2)}) collective-permute-start(bf16[320,1280]{1,0:T(8,128)(2,1)} %bitcast.40), channel_id=1, source_target_pairs={{0,2},{1,3},{2,4},{3,5},{4,6},{5,7},{8,10},{9,11},{10,12},{11,13},... | collective-permute-start | bytes 2457608 | tf_op jit(solution)/shard_map/ppermute | solution.py:72
  6.5 23.3 %collective-permute-start = (bf16[320,1280]{1,0:T(8,128)(2,1)}, bf16[320,1280]{1,0:T(8,128)(2,1)}, u32[]{:S(2)}, u32[]{:S(2)}) collective-permute-start(bf16[320,1280]{1,0:T(8,128)(2,1)} %bitcast.41), channel_id=1, source_target_pairs={{2,0},{3,1},{4,2},{5,3},{6,4},{7,5},{10,8},{11,9},{12,10},{13,11},... | collective-permute-start | bytes 2457608 | tf_op jit(solution)/shard_map/ppermute | solution.py:72
  7.8 38.2 %collective-permute-start.9 = (bf16[320,1280]{1,0:T(8,128)(2,1)}, bf16[320,1280]{1,0:T(8,128)(2,1)}, u32[]{:S(2)}, u32[]{:S(2)}) collective-permute-start(bf16[320,1280]{1,0:T(8,128)(2,1)} %bitcast.45), channel_id=1, source_target_pairs={{2,0},{3,1},{4,2},{5,3},{6,4},{7,5},{10,8},{11,9},{12,10},{13,11},... | collective-permute-start | bytes 2457608 | tf_op jit(solution)/shard_map/ppermute | solution.py:72
  9.1 38.2 %collective-permute-start.6 = (bf16[320,1280]{1,0:T(8,128)(2,1)}, bf16[320,1280]{1,0:T(8,128)(2,1)}, u32[]{:S(2)}, u32[]{:S(2)}) collective-permute-start(bf16[320,1280]{1,0:T(8,128)(2,1)} %bitcast.46), channel_id=1, source_target_pairs={{0,2},{1,3},{2,4},{3,5},{4,6},{5,7},{8,10},{9,11},{10,12},{11,13},... | collective-permute-start | bytes 2457608 | tf_op jit(solution)/shard_map/ppermute | solution.py:72
  15.2 32.8 %collective-permute-start.21 = (bf16[320,1280]{1,0:T(8,128)(2,1)}, bf16[320,1280]{1,0:T(8,128)(2,1)S(1)}, u32[]{:S(2)}, u32[]{:S(2)}) collective-permute-start(bf16[320,1280]{1,0:T(8,128)(2,1)} %bitcast.42), channel_id=1, source_target_pairs={{0,1},{1,0},{2,3},{3,2},{4,5},{5,4},{6,7},{7,6},{8,9},{9,8},{10,11... | collective-permute-start | bytes 2457608 | tf_op jit(solution)/shard_map/ppermute | solution.py:80
  24.5 25.1 %collective-permute-start.20 = (bf16[320,1280]{1,0:T(8,128)(2,1)}, bf16[320,1280]{1,0:T(8,128)(2,1)S(1)}, u32[]{:S(2)}, u32[]{:S(2)}) collective-permute-start(bf16[320,1280]{1,0:T(8,128)(2,1)} %bitcast.47), channel_id=1, source_target_pairs={{0,1},{1,0},{2,3},{3,2},{4,5},{5,4},{6,7},{7,6},{8,9},{9,8},{10,11... | collective-permute-start | bytes 2457608 | tf_op jit(solution)/shard_map/ppermute | solution.py:80
  29.8 22.0 %collective-permute-start.14 = (bf16[320,1280]{1,0:T(8,128)(2,1)}, bf16[320,1280]{1,0:T(8,128)(2,1)}, u32[]{:S(2)}, u32[]{:S(2)}) collective-permute-start(bf16[320,1280]{1,0:T(8,128)(2,1)} %bitcast.43), channel_id=1, source_target_pairs={{26,2},{27,3},{28,4},{29,5}} | collective-permute-start | bytes 2457608 | tf_op jit(solution)/shard_map/ppermute | solution.py:72
  46.0 23.2 %collective-permute-start.10 = (bf16[320,1280]{1,0:T(8,128)(2,1)}, bf16[320,1280]{1,0:T(8,128)(2,1)S(1)}, u32[]{:S(2)}, u32[]{:S(2)}) collective-permute-start(bf16[320,1280]{1,0:T(8,128)(2,1)} %collective-permute-done.9.refs_6_), channel_id=1, source_target_pairs={{2,0},{3,1},{4,2},{5,3},{10,8},{11,9},{12,10},{13,11},{18,16},{19,... | collective-permute-start | bytes 2457608 | tf_op jit(solution)/shard_map/ppermute | solution.py:72
  47.3 23.8 %collective-permute-start.7 = (bf16[320,1280]{1,0:T(8,128)(2,1)}, bf16[320,1280]{1,0:T(8,128)(2,1)S(1)}, u32[]{:S(2)}, u32[]{:S(2)}) collective-permute-start(bf16[320,1280]{1,0:T(8,128)(2,1)} %collective-permute-done.6.refs_4_), channel_id=1, source_target_pairs={{2,4},{3,5},{4,6},{5,7},{10,12},{11,13},{12,14},{13,15},{18,20},{1... | collective-permute-start | bytes 2457608 | tf_op jit(solution)/shard_map/ppermute | solution.py:72
  48.0 0.9 copy-start.6
  48.9 22.9 %collective-permute-start.3 = (bf16[320,1280]{1,0:T(8,128)(2,1)}, bf16[320,1280]{1,0:T(8,128)(2,1)S(1)}, u32[]{:S(2)}, u32[]{:S(2)}) collective-permute-start(bf16[320,1280]{1,0:T(8,128)(2,1)} %collective-permute-done.2.refs_8_), channel_id=1, source_target_pairs={{2,4},{3,5},{4,6},{5,7},{10,12},{11,13},{12,14},{13,15},{18,20},{1... | collective-permute-start | bytes 2457608 | tf_op jit(solution)/shard_map/ppermute | solution.py:72
  49.7 0.9 copy-start.8
  50.5 33.9 %collective-permute-start.1 = (bf16[320,1280]{1,0:T(8,128)(2,1)}, bf16[320,1280]{1,0:T(8,128)(2,1)S(1)}, u32[]{:S(2)}, u32[]{:S(2)}) collective-permute-start(bf16[320,1280]{1,0:T(8,128)(2,1)} %collective-permute-done.refs_10_), channel_id=1, source_target_pairs={{2,0},{3,1},{4,2},{5,3},{10,8},{11,9},{12,10},{13,11},{18,16},{19,... | collective-permute-start | bytes 2457608 | tf_op jit(solution)/shard_map/ppermute | solution.py:72
  51.9 34.2 %collective-permute-start.24 = (bf16[320,1280]{1,0:T(8,128)(2,1)}, bf16[320,1280]{1,0:T(8,128)(2,1)S(1)}, u32[]{:S(2)}, u32[]{:S(2)}) collective-permute-start(bf16[320,1280]{1,0:T(8,128)(2,1)} %collective-permute-done.2.refs_8_), channel_id=1, source_target_pairs={{2,3},{3,2},{4,5},{5,4},{6,7},{7,6},{10,11},{11,10},{12,13},{13,12... | collective-permute-start | bytes 2457608 | tf_op jit(solution)/shard_map/ppermute | solution.py:80
  69.2 18.4 %collective-permute-start.25 = (bf16[320,1280]{1,0:T(8,128)(2,1)}, bf16[320,1280]{1,0:T(8,128)(2,1)S(1)}, u32[]{:S(2)}, u32[]{:S(2)}) collective-permute-start(bf16[320,1280]{1,0:T(8,128)(2,1)} %collective-permute-done.refs_10_), channel_id=1, source_target_pairs={{0,1},{1,0},{2,3},{3,2},{4,5},{5,4},{8,9},{9,8},{10,11},{11,10},{1... | collective-permute-start | bytes 2457608 | tf_op jit(solution)/shard_map/ppermute | solution.py:80
  71.1 17.2 %collective-permute-start.22 = (bf16[320,1280]{1,0:T(8,128)(2,1)}, bf16[320,1280]{1,0:T(8,128)(2,1)S(1)}, u32[]{:S(2)}, u32[]{:S(2)}) collective-permute-start(bf16[320,1280]{1,0:T(8,128)(2,1)} %collective-permute-done.6.refs_4_), channel_id=1, source_target_pairs={{2,3},{3,2},{4,5},{5,4},{6,7},{7,6},{10,11},{11,10},{12,13},{13,12... | collective-permute-start | bytes 2457608 | tf_op jit(solution)/shard_map/ppermute | solution.py:80
  71.8 38.5 %collective-permute-start.23 = (bf16[320,1280]{1,0:T(8,128)(2,1)}, bf16[320,1280]{1,0:T(8,128)(2,1)S(1)}, u32[]{:S(2)}, u32[]{:S(2)}) collective-permute-start(bf16[320,1280]{1,0:T(8,128)(2,1)} %collective-permute-done.9.refs_6_), channel_id=1, source_target_pairs={{0,1},{1,0},{2,3},{3,2},{4,5},{5,4},{8,9},{9,8},{10,11},{11,10},{1... | collective-permute-start | bytes 2457608 | tf_op jit(solution)/shard_map/ppermute | solution.py:80
  84.5 24.5 %collective-permute-start.15 = (bf16[320,1280]{1,0:T(8,128)(2,1)}, bf16[320,1280]{1,0:T(8,128)(2,1)S(1)}, u32[]{:S(2)}, u32[]{:S(2)}) collective-permute-start(bf16[320,1280]{1,0:T(8,128)(2,1)} %collective-permute-done.14), channel_id=1, source_target_pairs={{2,0},{3,1},{4,6},{5,7}} | collective-permute-start | bytes 2457608 | tf_op jit(solution)/shard_map/ppermute | solution.py:72
  86.0 66.0 %copy-start.4 = (bf16[1,320,1280]{2,1,0:T(8,128)(2,1)S(1)}, bf16[1,320,1280]{2,1,0:T(8,128)(2,1)}, u32[]{:S(2)}) copy-start(bf16[1,320,1280]{2,1,0:T(8,128)(2,1)} %param.9) | copy-start | bytes 2457604
  86.0 66.0 %copy-start.5 = (bf16[1,320,1280]{2,1,0:T(8,128)(2,1)S(1)}, bf16[1,320,1280]{2,1,0:T(8,128)(2,1)}, u32[]{:S(2)}) copy-start(bf16[1,320,1280]{2,1,0:T(8,128)(2,1)} %param.10) | copy-start | bytes 2457604
  86.0 66.0 %copy-start.7 = (bf16[320,1280]{1,0:T(8,128)(2,1)S(1)}, bf16[320,1280]{1,0:T(8,128)(2,1)}, u32[]{:S(2)}) copy-start(bf16[320,1280]{1,0:T(8,128)(2,1)} %copy-done.6) | copy-start | bytes 2457604
  86.0 66.0 %copy-start.9 = (bf16[320,1280]{1,0:T(8,128)(2,1)S(1)}, bf16[320,1280]{1,0:T(8,128)(2,1)}, u32[]{:S(2)}) copy-start(bf16[320,1280]{1,0:T(8,128)(2,1)} %copy-done.8) | copy-start | bytes 2457604
  86.0 40.6 %collective-permute-start.18 = (bf16[320,1280]{1,0:T(8,128)(2,1)S(1)}, bf16[320,1280]{1,0:T(8,128)(2,1)S(1)}, u32[]{:S(2)}, u32[]{:S(2)}) collective-permute-start(bf16[320,1280]{1,0:T(8,128)(2,1)S(1)} %broadcast_select_fusion), channel_id=1, source_target_pairs={{2,0},{3,1},{4,6},{5,7},{10,8},{11,9},{12,14},{13,15},{18,16},{19,... | collective-permute-start | bytes 2457608 | tf_op jit(solution)/shard_map/ppermute | solution.py:72
  87.6 40.9 %collective-permute-start.12 = (bf16[320,1280]{1,0:T(8,128)(2,1)S(1)}, bf16[320,1280]{1,0:T(8,128)(2,1)S(1)}, u32[]{:S(2)}, u32[]{:S(2)}) collective-permute-start(bf16[320,1280]{1,0:T(8,128)(2,1)S(1)} %collective-permute-done.3.refs_4_), channel_id=1, source_target_pairs={{4,5},{5,4},{6,7},{7,6},{12,13},{13,12},{14,15},{15,14},{20,21},{2... | collective-permute-start | bytes 2457608 | tf_op jit(solution)/shard_map/ppermute | solution.py:80
  88.3 40.9 %collective-permute-start.13 = (bf16[320,1280]{1,0:T(8,128)(2,1)S(1)}, bf16[320,1280]{1,0:T(8,128)(2,1)S(1)}, u32[]{:S(2)}, u32[]{:S(2)}) collective-permute-start(bf16[320,1280]{1,0:T(8,128)(2,1)S(1)} %collective-permute-done.1.refs_6_), channel_id=1, source_target_pairs={{0,1},{1,0},{2,3},{3,2},{8,9},{9,8},{10,11},{11,10},{16,17},{17,16... | collective-permute-start | bytes 2457608 | tf_op jit(solution)/shard_map/ppermute | solution.py:80
  109.0 23.8 %collective-permute-start.16 = (bf16[320,1280]{1,0:T(8,128)(2,1)S(1)}, bf16[320,1280]{1,0:T(8,128)(2,1)S(1)}, u32[]{:S(2)}, u32[]{:S(2)}) collective-permute-start(bf16[320,1280]{1,0:T(8,128)(2,1)S(1)} %collective-permute-done.15), channel_id=1, source_target_pairs={{0,24},{1,25},{6,30},{7,31}} | collective-permute-start | bytes 2457608 | tf_op jit(solution)/shard_map/ppermute | solution.py:72
  110.4 33.6 %collective-permute-start.4 = (bf16[320,1280]{1,0:T(8,128)(2,1)S(1)}, bf16[320,1280]{1,0:T(8,128)(2,1)S(1)}, u32[]{:S(2)}, u32[]{:S(2)}) collective-permute-start(bf16[320,1280]{1,0:T(8,128)(2,1)S(1)} %broadcast_select_fusion.1), channel_id=1, source_target_pairs={{2,0},{3,1},{4,6},{5,7},{10,8},{11,9},{12,14},{13,15},{18,16},{19,... | collective-permute-start | bytes 2457608 | tf_op jit(solution)/shard_map/ppermute | solution.py:72
  126.6 27.4 %collective-permute-start.11 = (bf16[320,1280]{1,0:T(8,128)(2,1)S(1)}, bf16[320,1280]{1,0:T(8,128)(2,1)S(1)}, u32[]{:S(2)}, u32[]{:S(2)}) collective-permute-start(bf16[320,1280]{1,0:T(8,128)(2,1)S(1)} %collective-permute-done.10.refs_2_), channel_id=1, source_target_pairs={{0,1},{1,0},{2,3},{3,2},{8,9},{9,8},{10,11},{11,10},{16,17},{17,16... | collective-permute-start | bytes 2457608 | tf_op jit(solution)/shard_map/ppermute | solution.py:80
  128.5 25.5 %collective-permute-start.8 = (bf16[320,1280]{1,0:T(8,128)(2,1)S(1)}, bf16[320,1280]{1,0:T(8,128)(2,1)S(1)}, u32[]{:S(2)}, u32[]{:S(2)}) collective-permute-start(bf16[320,1280]{1,0:T(8,128)(2,1)S(1)} %collective-permute-done.7.refs_0_), channel_id=1, source_target_pairs={{4,5},{5,4},{6,7},{7,6},{12,13},{13,12},{14,15},{15,14},{20,21},{2... | collective-permute-start | bytes 2457608 | tf_op jit(solution)/shard_map/ppermute | solution.py:80
  129.2 24.8 %collective-permute-start.19 = (bf16[320,1280]{1,0:T(8,128)(2,1)S(1)}, bf16[320,1280]{1,0:T(8,128)(2,1)S(1)}, u32[]{:S(2)}, u32[]{:S(2)}) collective-permute-start(bf16[320,1280]{1,0:T(8,128)(2,1)S(1)} %collective-permute-done.18.refs_10_), channel_id=1, source_target_pairs={{0,1},{1,0},{2,3},{3,2},{4,5},{5,4},{6,7},{7,6},{8,9},{9,8},{10,11... | collective-permute-start | bytes 2457608 | tf_op jit(solution)/shard_map/ppermute | solution.py:80
  132.8 21.2 %collective-permute-start.17 = (bf16[320,1280]{1,0:T(8,128)(2,1)S(1)}, bf16[320,1280]{1,0:T(8,128)(2,1)S(1)}, u32[]{:S(2)}, u32[]{:S(2)}) collective-permute-start(bf16[320,1280]{1,0:T(8,128)(2,1)S(1)} %collective-permute-done.16.refs_8_), channel_id=1, source_target_pairs={{0,1},{1,0},{2,3},{3,2},{4,5},{5,4},{6,7},{7,6},{8,9},{9,8},{10,11... | collective-permute-start | bytes 2457608 | tf_op jit(solution)/shard_map/ppermute | solution.py:80
  143.9 10.9 %collective-permute-start.5 = (bf16[320,1280]{1,0:T(8,128)(2,1)S(1)}, bf16[320,1280]{1,0:T(8,128)(2,1)S(1)}, u32[]{:S(2)}, u32[]{:S(2)}) collective-permute-start(bf16[320,1280]{1,0:T(8,128)(2,1)S(1)} %collective-permute-done.4.refs_0_), channel_id=1, source_target_pairs={{0,1},{1,0},{2,3},{3,2},{4,5},{5,4},{6,7},{7,6},{8,9},{9,8},{10,11... | collective-permute-start | bytes 2457608 | tf_op jit(solution)/shard_map/ppermute | solution.py:80
  154.9 1.1 copy-start.1
  154.9 1.5 copy-start.2
  156.4 2.8 %collective-permute-start.29 = (bf16[64,2560]{1,0:T(8,128)(2,1)S(1)}, bf16[64,2560]{1,0:T(8,128)(2,1)S(1)}, u32[]{:S(2)}, u32[]{:S(2)}) collective-permute-start(bf16[64,2560]{1,0:T(8,128)(2,1)S(1)} %get-tuple-element.59), channel_id=1, source_target_pairs={{24,16},{25,17},{26,18},{27,19},{28,20},{29,21},{30,22},{31,23}} | collective-permute-start | bytes 983048 | tf_op jit(solution)/shard_map/ppermute | solution.py:296
  157.1 2.9 %collective-permute-start.28 = (bf16[64,2560]{1,0:T(8,128)(2,1)S(1)}, bf16[64,2560]{1,0:T(8,128)(2,1)S(1)}, u32[]{:S(2)}, u32[]{:S(2)}) collective-permute-start(bf16[64,2560]{1,0:T(8,128)(2,1)S(1)} %get-tuple-element.58), channel_id=1, source_target_pairs={{24,16},{25,17},{26,18},{27,19},{28,20},{29,21},{30,22},{31,23}} | collective-permute-start | bytes 983048 | tf_op jit(solution)/shard_map/ppermute | solution.py:296
  157.8 2.9 %collective-permute-start.27 = (bf16[64,2560]{1,0:T(8,128)(2,1)S(1)}, bf16[64,2560]{1,0:T(8,128)(2,1)S(1)}, u32[]{:S(2)}, u32[]{:S(2)}) collective-permute-start(bf16[64,2560]{1,0:T(8,128)(2,1)S(1)} %get-tuple-element.57), channel_id=1, source_target_pairs={{24,16},{25,17},{26,18},{27,19},{28,20},{29,21},{30,22},{31,23}} | collective-permute-start | bytes 983048 | tf_op jit(solution)/shard_map/ppermute | solution.py:296
  158.5 2.9 %collective-permute-start.26 = (bf16[64,2560]{1,0:T(8,128)(2,1)S(1)}, bf16[64,2560]{1,0:T(8,128)(2,1)S(1)}, u32[]{:S(2)}, u32[]{:S(2)}) collective-permute-start(bf16[64,2560]{1,0:T(8,128)(2,1)S(1)} %get-tuple-element.56), channel_id=1, source_target_pairs={{24,16},{25,17},{26,18},{27,19},{28,20},{29,21},{30,22},{31,23}} | collective-permute-start | bytes 983048 | tf_op jit(solution)/shard_map/ppermute | solution.py:296
  159.2 2.9 %collective-permute-start.33 = (bf16[64,2560]{1,0:T(8,128)(2,1)S(1)}, bf16[64,2560]{1,0:T(8,128)(2,1)S(1)}, u32[]{:S(2)}, u32[]{:S(2)}) collective-permute-start(bf16[64,2560]{1,0:T(8,128)(2,1)S(1)} %get-tuple-element.71), channel_id=1, source_target_pairs={{16,8},{17,9},{18,10},{19,11},{20,12},{21,13},{22,14},{23,15}} | collective-permute-start | bytes 983048 | tf_op jit(solution)/shard_map/ppermute | solution.py:296
  160.0 3.5 %collective-permute-start.32 = (bf16[64,2560]{1,0:T(8,128)(2,1)S(1)}, bf16[64,2560]{1,0:T(8,128)(2,1)S(1)}, u32[]{:S(2)}, u32[]{:S(2)}) collective-permute-start(bf16[64,2560]{1,0:T(8,128)(2,1)S(1)} %get-tuple-element.70), channel_id=1, source_target_pairs={{16,8},{17,9},{18,10},{19,11},{20,12},{21,13},{22,14},{23,15}} | collective-permute-start | bytes 983048 | tf_op jit(solution)/shard_map/ppermute | solution.py:296
  160.7 4.1 %collective-permute-start.31 = (bf16[64,2560]{1,0:T(8,128)(2,1)S(1)}, bf16[64,2560]{1,0:T(8,128)(2,1)S(1)}, u32[]{:S(2)}, u32[]{:S(2)}) collective-permute-start(bf16[64,2560]{1,0:T(8,128)(2,1)S(1)} %get-tuple-element.69), channel_id=1, source_target_pairs={{16,8},{17,9},{18,10},{19,11},{20,12},{21,13},{22,14},{23,15}} | collective-permute-start | bytes 983048 | tf_op jit(solution)/shard_map/ppermute | solution.py:296
  161.4 4.9 %collective-permute-start.30 = (bf16[64,2560]{1,0:T(8,128)(2,1)S(1)}, bf16[64,2560]{1,0:T(8,128)(2,1)S(1)}, u32[]{:S(2)}, u32[]{:S(2)}) collective-permute-start(bf16[64,2560]{1,0:T(8,128)(2,1)S(1)} %get-tuple-element.68), channel_id=1, source_target_pairs={{16,8},{17,9},{18,10},{19,11},{20,12},{21,13},{22,14},{23,15}} | collective-permute-start | bytes 983048 | tf_op jit(solution)/shard_map/ppermute | solution.py:296
  162.1 27.0 %collective-permute-start.37 = (bf16[64,2560]{1,0:T(8,128)(2,1)S(1)}, bf16[64,2560]{1,0:T(8,128)(2,1)S(1)}, u32[]{:S(2)}, u32[]{:S(2)}) collective-permute-start(bf16[64,2560]{1,0:T(8,128)(2,1)S(1)} %get-tuple-element.83), channel_id=1, source_target_pairs={{8,0},{9,1},{10,2},{11,3},{12,4},{13,5},{14,6},{15,7}} | collective-permute-start | bytes 983048 | tf_op jit(solution)/shard_map/ppermute | solution.py:296
  163.5 32.6 %collective-permute-start.36 = (bf16[64,2560]{1,0:T(8,128)(2,1)S(1)}, bf16[64,2560]{1,0:T(8,128)(2,1)S(1)}, u32[]{:S(2)}, u32[]{:S(2)}) collective-permute-start(bf16[64,2560]{1,0:T(8,128)(2,1)S(1)} %get-tuple-element.82), channel_id=1, source_target_pairs={{8,0},{9,1},{10,2},{11,3},{12,4},{13,5},{14,6},{15,7}} | collective-permute-start | bytes 983048 | tf_op jit(solution)/shard_map/ppermute | solution.py:296
  165.0 38.1 %collective-permute-start.35 = (bf16[64,2560]{1,0:T(8,128)(2,1)S(1)}, bf16[64,2560]{1,0:T(8,128)(2,1)S(1)}, u32[]{:S(2)}, u32[]{:S(2)}) collective-permute-start(bf16[64,2560]{1,0:T(8,128)(2,1)S(1)} %get-tuple-element.81), channel_id=1, source_target_pairs={{8,0},{9,1},{10,2},{11,3},{12,4},{13,5},{14,6},{15,7}} | collective-permute-start | bytes 983048 | tf_op jit(solution)/shard_map/ppermute | solution.py:296
  166.3 44.4 %collective-permute-start.34 = (bf16[64,2560]{1,0:T(8,128)(2,1)S(1)}, bf16[64,2560]{1,0:T(8,128)(2,1)S(1)}, u32[]{:S(2)}, u32[]{:S(2)}) collective-permute-start(bf16[64,2560]{1,0:T(8,128)(2,1)S(1)} %get-tuple-element.80), channel_id=1, source_target_pairs={{8,0},{9,1},{10,2},{11,3},{12,4},{13,5},{14,6},{15,7}} | collective-permute-start | bytes 983048 | tf_op jit(solution)/shard_map/ppermute | solution.py:296
  210.8 16.8 %slice-start = ((s8[6553600]{0:T(1024)(128)(4,1)}), s8[4194304]{0:T(1024)(128)(4,1)S(1)}, s32[]{:S(2)}) async-start(s8[6553600]{0:T(1024)(128)(4,1)} %bitcast.36), calls=%async_computation | async-start | bytes 8388608
  210.8 5.8 %copy-start.3 = (bf16[1,256,2560]{2,1,0:T(8,128)(2,1)S(1)}, bf16[1,256,2560]{2,1,0:T(8,128)(2,1)}, u32[]{:S(2)}) copy-start(bf16[1,256,2560]{2,1,0:T(8,128)(2,1)} %param.7) | copy-start | bytes 3932164
  210.8 16.8 %slice-start.1 = ((s8[6553600]{0:T(1024)(128)(4,1)}), s8[2359296]{0:T(1024)(128)(4,1)S(1)}, s32[]{:S(2)}) async-start(s8[6553600]{0:T(1024)(128)(4,1)} %bitcast.36), calls=%async_computation.1 | async-start | bytes 4718592
  217.2 1.2 collective-permute-start.38
  218.5 4.1 %collective-permute-start.39 = (f32[4,2560]{1,0:T(4,128)S(1)}, f32[4,2560]{1,0:T(4,128)S(1)}, u32[]{:S(2)}, u32[]{:S(2)}) collective-permute-start(f32[4,2560]{1,0:T(4,128)S(1)} %add.19), channel_id=1, source_target_pairs={{0,2},{1,3},{2,0},{3,1},{4,6},{5,7},{6,4},{7,5},{8,10},{9,11},{10,... | collective-permute-start | bytes 122888 | tf_op jit(solution)/shard_map/ppermute | solution.py:267
  222.5 5.0 %collective-permute-start.40 = (f32[4,2560]{1,0:T(4,128)S(1)}, f32[4,2560]{1,0:T(4,128)S(1)}, u32[]{:S(2)}, u32[]{:S(2)}) collective-permute-start(f32[4,2560]{1,0:T(4,128)S(1)} %add.20.left), channel_id=1, source_target_pairs={{0,4},{1,5},{2,6},{3,7},{4,0},{5,1},{6,2},{7,3},{8,12},{9,13},{10,... | collective-permute-start | bytes 122888 | tf_op jit(solution)/shard_map/ppermute | solution.py:267
  230.3 1.3 collective-permute-start.41
  231.6 3.8 %collective-permute-start.42 = (f32[4,1280]{1,0:T(4,128)S(1)}, f32[4,1280]{1,0:T(4,128)S(1)}, u32[]{:S(2)}, u32[]{:S(2)}) collective-permute-start(f32[4,1280]{1,0:T(4,128)S(1)} %add.21), channel_id=1, source_target_pairs={{0,2},{1,3},{2,0},{3,1},{4,6},{5,7},{6,4},{7,5},{8,10},{9,11},{10,... | collective-permute-start | bytes 61448 | tf_op jit(solution)/shard_map/ppermute | solution.py:267
  235.4 4.8 %collective-permute-start.43 = (f32[4,1280]{1,0:T(4,128)S(1)}, f32[4,1280]{1,0:T(4,128)S(1)}, u32[]{:S(2)}, u32[]{:S(2)}) collective-permute-start(f32[4,1280]{1,0:T(4,128)S(1)} %add.22), channel_id=1, source_target_pairs={{0,4},{1,5},{2,6},{3,7},{4,0},{5,1},{6,2},{7,3},{8,12},{9,13},{10,... | collective-permute-start | bytes 61448 | tf_op jit(solution)/shard_map/ppermute | solution.py:267
where the time goes:
time: 242 us; the launch traced here: 241 us
  waiting for transfers between devices  138 us (57%)
  starting transfers between devices  61 us (25%)
  Pallas kernels  26.7 us (11%)
  matrix products  9.33 us (4%)
  local copies, waits for them, and re-layouts  3.09 us (1%)
    ppermute x13, waiting for transfers between devices, permute(): return lax.ppermute(value, ('section', 'dp'), pairs)  100 us
    ppermute x12, waiting for transfers between devices, local(): arriving[k] = lax.ppermute(send, 'section', [(section, section - 1)])  27.8 us
    ppermute x13, starting transfers between devices, permute(): return lax.ppermute(value, ('section', 'dp'), pairs)  25.5 us
    pallas_call x16, Pallas kernels, stage(): pl.pallas_call(body, in_specs=[VMEM] * 3 + [ANY] + [VMEM] * len(held), ou...  20.8 us
    ppermute x13, starting transfers between devices, swap(): return lax.ppermute(value, 'dp', pairs)  14.9 us
    ppermute x12, starting transfers between devices, local(): arriving[k] = lax.ppermute(send, 'section', [(section, section - 1)])  10.6 us
    ppermute x6, waiting for transfers between devices, exchange(): return lax.ppermute(value, 'dp', [(i, i ^ by) for i in range(replicas)])  10.2 us
    ppermute x6, starting transfers between devices, exchange(): return lax.ppermute(value, 'dp', [(i, i ^ by) for i in range(replicas)])  9.94 us
  transfers between devices with their start and end apart: 44, of which 18 were waited for; matrix products, arithmetic and copies ran while one was open for 3% of the time, Pallas kernels for 8%

commit v1 on v0

--- a/solution.py
+++ b/solution.py
@@ -8,14 +8,14 @@
 from jax.sharding import PartitionSpec as P
 
 
-MICRO = 4
+SIXTEENTHS = (3, 3, 3, 3, 4)
 CORES = 2
 HIGHEST = lax.Precision.HIGHEST
 VMEM = pl.BlockSpec(memory_space=pltpu.VMEM)
 ANY = pl.BlockSpec(memory_space=pl.ANY)
 
 
-def put(whole, pieces, shape, dtype):
+def put(whole, pieces, shape, dtype, after=()):
     arrays = list({id(piece): piece for _, piece, _, _ in pieces}.values())
     rows = arrays[0].shape[0]
     if rows % 16:
@@ -44,14 +44,14 @@
     held = [] if whole is None else [whole]
     return pl.pallas_call(
         body,
-        in_specs=[ANY] * len(arrays) + [VMEM] * len(held),
+        in_specs=[ANY] * (len(arrays) + len(after)) + [VMEM] * len(held),
         out_specs=VMEM,
         out_shape=jax.ShapeDtypeStruct(shape, dtype),
-        input_output_aliases={len(arrays): 0} if held else {},
+        input_output_aliases={len(arrays) + len(after): 0} if held else {},
         scratch_shapes=[pltpu.SemaphoreType.DMA((len(pieces),))],
         compiler_params=pltpu.CompilerParams(vmem_limit_bytes=4 << 20),
         name="put",
-    )(*arrays, *held)
+    )(*arrays, *after, *held)
 
 
 def gather_weights(matrices):
@@ -111,7 +111,11 @@
                 low = lax.axis_index("dp") < replicas // 2
                 last = jnp.where(low, down[kind], up[kind])
                 moves = [(1, 0), (chips - 2, chips - 1)]
-                up[kind] = line(last, moves)
+                split = kind == 1 and top > 0
+                skip = [(s, c, s, d) for s in range(top) for c, d in moves] if split else ()
+                up[kind] = line(last, moves, skip)
+                if split:
+                    late = permute(last, skip)
         if step == 1:
             if relayed:
                 relay = permute(matrices[1], [(top, c, 0, c) for c in inner])
@@ -132,8 +136,9 @@
                     pieces += shards(down[kind], from_above, step, 0, low, False)
             else:
                 other = swap(up[kind])
-                pieces = shards(up[kind], other, step, 0, 1)
-                pieces += shards(up[kind], other, -step, step, chips)
+                whose = True if kind == 1 and top else None
+                pieces = shards(up[kind], other, step, 0, 1, whose)
+                pieces += shards(up[kind], other, -step, step, chips, whose)
             behind = 2 * (chips - 1 - step) + len(matrices) - 1 - kind
             groups[0 if behind > 3 else 1 if behind else 2] += [
                 (kind,) + piece for piece in pieces
@@ -146,14 +151,23 @@
     whole = None
     for group in groups:
         whole = put(whole, group, shape, dtype)
-    return whole
-
-
-def stage(whole, arriving, gates, held, early, *, section, part, block):
+
+    def finish(whole, after):
+        if not top:
+            return whole
+        other = swap(late)
+        pieces = shards(late, other, chips - 1, 0, 1, False)
+        pieces += shards(late, other, 1 - chips, chips - 1, chips, False)
+        return put(whole, [(1,) + piece for piece in pieces], shape, dtype, after)
+
+    return whole, finish
+
+
+def stage(whole, arriving, gates, held, early, *, section, first, block):
     width = arriving.shape[1]
     row_count, channels = gates.shape
     lanes, deep = math.gcd(channels, 256), math.gcd(width, 512)
-    at = pl.ds(part * block, block)
+    at = pl.ds(first, block)
     read = at if arriving.shape[0] == row_count else pl.ds(0, block)
 
     def body(w, arr, gate, *refs):
@@ -283,17 +297,21 @@
     error_part = lax.dot_general(
         warm, error.astype(jnp.float32), (((1,), (1,)), ((), ())), precision=HIGHEST
     )
-    whole = gather_weights((w_out[0], w_value[0]))
-    arriving = [grad_top] * MICRO
+    whole, finish = gather_weights((w_out[0], w_value[0]))
+    blocks = [count * row_count // 16 for count in SIXTEENTHS]
+    firsts = [sum(blocks[:k]) for k in range(len(blocks))]
+    arriving = [grad_top] * len(blocks)
     held = []
     for section in reversed(range(sections)):
-        for k in range(MICRO):
+        for k, (first, block) in enumerate(zip(firsts, blocks)):
             *held, send = stage(
                 whole, arriving[k], gate_rows, held, error_part,
-                section=section, part=k, block=row_count // MICRO,
+                section=section, first=first, block=block,
             )
             if section:
                 arriving[k] = lax.ppermute(send, "section", [(section, section - 1)])
+        if section == sections - 1:
+            whole = finish(whole, held[:1])
     value_grads, passed_rows = held
     projected = jnp.dot(value_grads.astype(jnp.float32), warm.T, precision=HIGHEST)
     factor = lax.dot_general(

time: 242 us -> 275 us (1.14)
  starting transfers between devices: 61 us -> 85.4 us
  waiting for transfers between devices: 138 us -> 143 us
  Pallas kernels: 26.7 us -> 31.2 us
    ppermute x12 -> x15, waiting for transfers between devices: 27.8 us -> 50.6 us  [local(): arriving[k] = lax.ppermute(send, 'section', [(section, section - 1)])]
    ppermute x13 -> x14, starting transfers between devices: 14.9 us -> 33.4 us  [swap(): return lax.ppermute(value, 'dp', pairs)]
    ppermute x13 -> x14, waiting for transfers between devices: 100 us -> 82.3 us  [permute(): return lax.ppermute(value, ('section', 'dp'), pairs)]
    pallas_call x16 -> x20, Pallas kernels: 20.8 us -> 25.1 us  [stage(): pl.pallas_call(body, in_specs=[VMEM] * 3 + [ANY] + [VMEM] * len(held), ou...]
    ppermute x12 -> x15, starting transfers between devices: 10.6 us -> 13.4 us  [local(): arriving[k] = lax.ppermute(send, 'section', [(section, section - 1)])]
    ppermute x13 -> x14, starting transfers between devices: 25.5 us -> 27.5 us  [permute(): return lax.ppermute(value, ('section', 'dp'), pairs)]
  transfers between devices with their start and end apart: 44 -> 49, of which waited for: 18 -> 19; matrix products, arithmetic and copies ran while one was open for 3% -> 3% of each run, Pallas kernels for 8% -> 8%
where the time goes in v1:
time: 275 us; the launch traced here: 274 us
  waiting for transfers between devices  143 us (52%)
  starting transfers between devices  85.4 us (31%)
  Pallas kernels  31.2 us (11%)
  matrix products  9.33 us (3%)
  local copies, waits for them, and re-layouts  3.33 us (1%)
    ppermute x14, waiting for transfers between devices, permute(): return lax.ppermute(value, ('section', 'dp'), pairs)  82.3 us
    ppermute x15, waiting for transfers between devices, local(): arriving[k] = lax.ppermute(send, 'section', [(section, section - 1)])  50.6 us
    ppermute x14, starting transfers between devices, swap(): return lax.ppermute(value, 'dp', pairs)  33.4 us
    ppermute x14, starting transfers between devices, permute(): return lax.ppermute(value, ('section', 'dp'), pairs)  27.5 us
    pallas_call x20, Pallas kernels, stage(): pl.pallas_call(body, in_specs=[VMEM] * 3 + [ANY] + [VMEM] * len(held), ou...  25.1 us
    ppermute x15, starting transfers between devices, local(): arriving[k] = lax.ppermute(send, 'section', [(section, section - 1)])  13.4 us
    ppermute x6, starting transfers between devices, exchange(): return lax.ppermute(value, 'dp', [(i, i ^ by) for i in range(replicas)])  11.1 us
    ppermute x6, waiting for transfers between devices, exchange(): return lax.ppermute(value, 'dp', [(i, i ^ by) for i in range(replicas)])  9.93 us
  transfers between devices with their start and end apart: 49, of which 19 were waited for; matrix products, arithmetic and copies ran while one was open for 3% of the time, Pallas kernels for 8%

profile of v1, /device:TPU:0, one launch (start us, length us, event | category | flops | bytes accessed | tf_op | source)
XLA Modules:
  0.0 274.5 jit_solution(14399140614816647167)
XLA Ops:
  0.6 5.0 %collective-permute-start.2 = (bf16[320,1280]{1,0:T(8,128)(2,1)}, bf16[320,1280]{1,0:T(8,128)(2,1)S(1)}, u32[]{:S(2)}, u32[]{:S(2)}) collective-permute-start(bf16[320,1280]{1,0:T(8,128)(2,1)} %bitcast.44), channel_id=1, source_target_pairs={{0,2},{1,3},{2,4},{3,5},{4,6},{5,7},{8,10},{9,11},{10,12},{11,13},... | collective-permute-start | bytes 2457608 | tf_op jit(solution)/shard_map/ppermute | solution.py:72
  5.7 4.3 %collective-permute-start.11 = (bf16[320,1280]{1,0:T(8,128)(2,1)}, bf16[320,1280]{1,0:T(8,128)(2,1)S(1)}, u32[]{:S(2)}, u32[]{:S(2)}) collective-permute-start(bf16[320,1280]{1,0:T(8,128)(2,1)} %bitcast.49), channel_id=1, source_target_pairs={{2,0},{3,1},{4,2},{5,3},{6,4},{7,5},{10,8},{11,9},{12,10},{13,11},... | collective-permute-start | bytes 2457608 | tf_op jit(solution)/shard_map/ppermute | solution.py:72
  10.0 5.3 %collective-permute-start.8 = (bf16[320,1280]{1,0:T(8,128)(2,1)}, bf16[320,1280]{1,0:T(8,128)(2,1)}, u32[]{:S(2)}, u32[]{:S(2)}) collective-permute-start(bf16[320,1280]{1,0:T(8,128)(2,1)} %bitcast.50), channel_id=1, source_target_pairs={{0,2},{1,3},{2,4},{3,5},{4,6},{5,7},{8,10},{9,11},{10,12},{11,13},... | collective-permute-start | bytes 2457608 | tf_op jit(solution)/shard_map/ppermute | solution.py:72
  15.3 1.3 collective-permute-start
  16.7 7.9 %collective-permute-done.2.refs_8_ = bf16[320,1280]{1,0:T(8,128)(2,1)S(1)} collective-permute-done((bf16[320,1280]{1,0:T(8,128)(2,1)}, bf16[320,1280]{1,0:T(8,128)(2,1)S(1)}, u32[]{:S(2)}, u32[]{:S(2)}) %collective-permute-start.2) | collective-permute-done | bytes 819232 | tf_op jit(solution)/shard_map/ppermute | solution.py:72
  24.5 7.2 %collective-permute-done.11.refs_6_ = bf16[320,1280]{1,0:T(8,128)(2,1)S(1)} collective-permute-done((bf16[320,1280]{1,0:T(8,128)(2,1)}, bf16[320,1280]{1,0:T(8,128)(2,1)S(1)}, u32[]{:S(2)}, u32[]{:S(2)}) %collective-permute-start.11) | collective-permute-done | bytes 819232 | tf_op jit(solution)/shard_map/ppermute | solution.py:72
  31.8 1.3 collective-permute-start.12
  33.0 7.9 %collective-permute-done.8.refs_4_ = bf16[320,1280]{1,0:T(8,128)(2,1)} collective-permute-done((bf16[320,1280]{1,0:T(8,128)(2,1)}, bf16[320,1280]{1,0:T(8,128)(2,1)}, u32[]{:S(2)}, u32[]{:S(2)}) %collective-permute-start.8) | collective-permute-done | bytes 819232 | tf_op jit(solution)/shard_map/ppermute | solution.py:72
  41.0 0.7 collective-permute-start.9
  41.7 7.7 %collective-permute-done.refs_10_ = bf16[320,1280]{1,0:T(8,128)(2,1)} collective-permute-done((bf16[320,1280]{1,0:T(8,128)(2,1)}, bf16[320,1280]{1,0:T(8,128)(2,1)}, u32[]{:S(2)}, u32[]{:S(2)}) %collective-permute-start) | collective-permute-done | bytes 819232 | tf_op jit(solution)/shard_map/ppermute | solution.py:72
  49.4 1.6 collective-permute-start.16
  51.0 0.9 copy-done.8
  51.9 7.1 %collective-permute-start.26 = (bf16[320,1280]{1,0:T(8,128)(2,1)S(1)}, bf16[320,1280]{1,0:T(8,128)(2,1)}, u32[]{:S(2)}, u32[]{:S(2)}) collective-permute-start(bf16[320,1280]{1,0:T(8,128)(2,1)S(1)} %collective-permute-done.2.refs_8_), channel_id=1, source_target_pairs={{2,3},{3,2},{4,5},{5,4},{6,7},{7,6},{10,11},{11,10},{12,13},{13,12... | collective-permute-start | bytes 2457608 | tf_op jit(solution)/shard_map/ppermute | solution.py:80
  59.1 0.9 copy-done.10
  60.0 2.3 collective-permute-start.27
  62.3 4.0 %collective-permute-done.12.refs_2_ = bf16[320,1280]{1,0:T(8,128)(2,1)S(1)} collective-permute-done((bf16[320,1280]{1,0:T(8,128)(2,1)S(1)}, bf16[320,1280]{1,0:T(8,128)(2,1)S(1)}, u32[]{:S(2)}, u32[]{:S(2)}) %collective-permute-start.12) | collective-permute-done | bytes 819232 | tf_op jit(solution)/shard_map/ppermute | solution.py:72
  66.3 0.7 collective-permute-start.3
  67.0 1.4 collective-permute-start.1
  68.6 7.0 %collective-permute-start.24 = (bf16[320,1280]{1,0:T(8,128)(2,1)}, bf16[320,1280]{1,0:T(8,128)(2,1)S(1)}, u32[]{:S(2)}, u32[]{:S(2)}) collective-permute-start(bf16[320,1280]{1,0:T(8,128)(2,1)} %collective-permute-done.8.refs_4_), channel_id=1, source_target_pairs={{2,3},{3,2},{4,5},{5,4},{6,7},{7,6},{10,11},{11,10},{12,13},{13,12... | collective-permute-start | bytes 2457608 | tf_op jit(solution)/shard_map/ppermute | solution.py:80
  75.6 2.3 collective-permute-start.25
  77.9 1.3 collective-permute-start.17
  79.3 1.3 collective-permute-start.20
  80.6 10.1 %collective-permute-done.1.refs_6_ = bf16[320,1280]{1,0:T(8,128)(2,1)S(1)} collective-permute-done((bf16[320,1280]{1,0:T(8,128)(2,1)}, bf16[320,1280]{1,0:T(8,128)(2,1)S(1)}, u32[]{:S(2)}, u32[]{:S(2)}) %collective-permute-start.1) | collective-permute-done | bytes 819232 | tf_op jit(solution)/shard_map/ppermute | solution.py:72
  90.6 0.7 collective-permute-start.14
  91.5 2.2 collective-permute-start.15
  93.7 0.7 collective-permute-start.10
  94.4 13.8 %collective-permute-done.17 = bf16[320,1280]{1,0:T(8,128)(2,1)S(1)} collective-permute-done((bf16[320,1280]{1,0:T(8,128)(2,1)}, bf16[320,1280]{1,0:T(8,128)(2,1)S(1)}, u32[]{:S(2)}, u32[]{:S(2)}) %collective-permute-start.17) | collective-permute-done | bytes 819232 | tf_op jit(solution)/shard_map/ppermute | solution.py:72
  108.2 1.3 collective-permute-start.18
  109.5 15.0 %collective-permute-done.20.refs_10_ = bf16[320,1280]{1,0:T(8,128)(2,1)S(1)} collective-permute-done((bf16[320,1280]{1,0:T(8,128)(2,1)S(1)}, bf16[320,1280]{1,0:T(8,128)(2,1)S(1)}, u32[]{:S(2)}, u32[]{:S(2)}) %collective-permute-start.20) | collective-permute-done | bytes 819232 | tf_op jit(solution)/shard_map/ppermute | solution.py:72
  124.5 0.7 collective-permute-start.6
  125.3 1.3 collective-permute-start.4
  126.6 1.9 collective-permute-start.13
  128.5 3.0 %collective-permute-start.21 = (bf16[320,1280]{1,0:T(8,128)(2,1)S(1)}, bf16[320,1280]{1,0:T(8,128)(2,1)S(1)}, u32[]{:S(2)}, u32[]{:S(2)}) collective-permute-start(bf16[320,1280]{1,0:T(8,128)(2,1)S(1)} %collective-permute-done.20.refs_10_), channel_id=1, source_target_pairs={{0,1},{1,0},{2,3},{3,2},{4,5},{5,4},{6,7},{7,6},{8,9},{9,8},{10,11... | collective-permute-start | bytes 2457608 | tf_op jit(solution)/shard_map/ppermute | solution.py:80
  131.5 5.7 %collective-permute-start.19 = (bf16[320,1280]{1,0:T(8,128)(2,1)S(1)}, bf16[320,1280]{1,0:T(8,128)(2,1)S(1)}, u32[]{:S(2)}, u32[]{:S(2)}) collective-permute-start(bf16[320,1280]{1,0:T(8,128)(2,1)S(1)} %collective-permute-done.18.refs_8_), channel_id=1, source_target_pairs={{0,1},{1,0},{2,3},{3,2},{4,5},{5,4},{6,7},{7,6},{8,9},{9,8},{10,11... | collective-permute-start | bytes 2457608 | tf_op jit(solution)/shard_map/ppermute | solution.py:80
  137.6 8.6 %collective-permute-done.4.refs_0_ = bf16[320,1280]{1,0:T(8,128)(2,1)S(1)} collective-permute-done((bf16[320,1280]{1,0:T(8,128)(2,1)S(1)}, bf16[320,1280]{1,0:T(8,128)(2,1)S(1)}, u32[]{:S(2)}, u32[]{:S(2)}) %collective-permute-start.4) | collective-permute-done | bytes 819232 | tf_op jit(solution)/shard_map/ppermute | solution.py:72
  146.2 8.0 %fusion.2.refs_0_ = f32[4,2560]{1,0:T(4,128)S(1)} fusion(f32[1,4,1280]{2,1,0:T(4,128)S(1)} %copy-done, bf16[1,2560,1280]{2,1,0:T(8,128)(2,1)} %param.11), kind=kOutput, calls=%fused_computation.5 | convolution fusion | flops 157286400 | bytes 6615040 | tf_op jit(solution)/shard_map/dot_general | solution.py:297
  154.3 2.2 put.4.refs_12_
  156.5 0.8 put.5.refs_2_
  157.4 1.0 copy-done.1
  161.0 0.7 collective-permute-start.28
  165.6 0.9 collective-permute-start.34
  166.5 1.3 collective-permute-start.42
  167.8 1.3 collective-permute-start.41
  169.1 1.3 collective-permute-start.40
  170.5 1.3 collective-permute-start.38
  171.8 1.3 collective-permute-start.39
  173.1 14.4 %collective-permute-done.42.arr = bf16[48,2560]{1,0:T(8,128)(2,1)S(1)} collective-permute-done((bf16[48,2560]{1,0:T(8,128)(2,1)S(1)}, bf16[48,2560]{1,0:T(8,128)(2,1)S(1)}, u32[]{:S(2)}, u32[]{:S(2)}) %collective-permute-start.42) | collective-permute-done | bytes 245792 | tf_op jit(solution)/shard_map/ppermute | solution.py:312
  187.5 4.9 %shard_map.109 = (bf16[256,1280]{1,0:T(8,128)(2,1)S(1)}, bf16[256,2560]{1,0:T(8,128)(2,1)S(1)}, bf16[48,2560]{1,0:T(8,128)(2,1)}) custom-call(bf16[2,2560,1280]{2,1,0:T(8,128)(2,1)S(1)} %put.7.w, bf16[48,2560]{1,0:T(8,128)(2,1)S(1)} %collective-permute-done.42.arr, bf16[256,1280]{1,0:T(8,128)(2,1)S(1)} %bitcast.35, ...), custom_call_target="tpu_custom_call", output_to_operand_aliasing={{0}: (4, {}), {1}: (5, {})} | custom-call | flops 629145600 | bytes 13107200 | tf_op jit(solution)/shard_map/pallas_call | solution.py:202
  193.1 4.9 %shard_map.110 = (bf16[256,1280]{1,0:T(8,128)(2,1)S(1)}, bf16[256,2560]{1,0:T(8,128)(2,1)S(1)}, bf16[48,2560]{1,0:T(8,128)(2,1)}) custom-call(bf16[2,2560,1280]{2,1,0:T(8,128)(2,1)S(1)} %put.7.w, bf16[48,2560]{1,0:T(8,128)(2,1)S(1)} %collective-permute-done.41.arr, bf16[256,1280]{1,0:T(8,128)(2,1)S(1)} %bitcast.36, ...), custom_call_target="tpu_custom_call", output_to_operand_aliasing={{0}: (4, {}), {1}: (5, {})} | custom-call | flops 629145600 | bytes 13107200 | tf_op jit(solution)/shard_map/pallas_call | solution.py:202
  198.7 4.9 %shard_map.111 = (bf16[256,1280]{1,0:T(8,128)(2,1)S(1)}, bf16[256,2560]{1,0:T(8,128)(2,1)S(1)}, bf16[48,2560]{1,0:T(8,128)(2,1)}) custom-call(bf16[2,2560,1280]{2,1,0:T(8,128)(2,1)S(1)} %put.7.w, bf16[48,2560]{1,0:T(8,128)(2,1)S(1)} %collective-permute-done.40.arr, bf16[256,1280]{1,0:T(8,128)(2,1)S(1)} %bitcast.37, ...), custom_call_target="tpu_custom_call", output_to_operand_aliasing={{0}: (4, {}), {1}: (5, {})} | custom-call | flops 629145600 | bytes 13107200 | tf_op jit(solution)/shard_map/pallas_call | solution.py:202
  203.6 34.9 %collective-permute-done.39.arr = bf16[48,2560]{1,0:T(8,128)(2,1)S(1)} collective-permute-done((bf16[48,2560]{1,0:T(8,128)(2,1)S(1)}, bf16[48,2560]{1,0:T(8,128)(2,1)S(1)}, u32[]{:S(2)}, u32[]{:S(2)}) %collective-permute-start.39) | collective-permute-done | bytes 245792 | tf_op jit(solution)/shard_map/ppermute | solution.py:312
  238.5 4.9 %shard_map.112 = (bf16[256,1280]{1,0:T(8,128)(2,1)S(1)}, bf16[256,2560]{1,0:T(8,128)(2,1)S(1)}, bf16[48,2560]{1,0:T(8,128)(2,1)}) custom-call(bf16[2,2560,1280]{2,1,0:T(8,128)(2,1)S(1)} %put.7.w, bf16[48,2560]{1,0:T(8,128)(2,1)S(1)} %collective-permute-done.39.arr, bf16[256,1280]{1,0:T(8,128)(2,1)S(1)} %bitcast.38, ...), custom_call_target="tpu_custom_call", output_to_operand_aliasing={{0}: (4, {}), {1}: (5, {})} | custom-call | flops 629145600 | bytes 13107200 | tf_op jit(solution)/shard_map/pallas_call | solution.py:202
  243.5 5.1 %shard_map.113 = (bf16[256,1280]{1,0:T(8,128)(2,1)S(1)}, bf16[256,2560]{1,0:T(8,128)(2,1)S(1)}, bf16[64,2560]{1,0:T(8,128)(2,1)}) custom-call(bf16[2,2560,1280]{2,1,0:T(8,128)(2,1)S(1)} %put.7.w, bf16[64,2560]{1,0:T(8,128)(2,1)S(1)} %collective-permute-done.38.arr, bf16[256,1280]{1,0:T(8,128)(2,1)S(1)} %bitcast.39, ...), custom_call_target="tpu_custom_call", output_to_operand_aliasing={{0}: (4, {}), {1}: (5, {})} | custom-call | flops 838860800 | bytes 13107200 | tf_op jit(solution)/shard_map/pallas_call | solution.py:202
  250.0 1.2 collective-permute-done.43
  251.2 3.0 %collective-permute-start.44 = (f32[4,2560]{1,0:T(4,128)S(1)}, f32[4,2560]{1,0:T(4,128)S(1)}, u32[]{:S(2)}, u32[]{:S(2)}) collective-permute-start(f32[4,2560]{1,0:T(4,128)S(1)} %add.19), channel_id=1, source_target_pairs={{0,2},{1,3},{2,0},{3,1},{4,6},{5,7},{6,4},{7,5},{8,10},{9,11},{10,... | collective-permute-start | bytes 122888 | tf_op jit(solution)/shard_map/ppermute | solution.py:281
  254.2 2.0 collective-permute-done.44
  256.2 3.0 %collective-permute-start.45 = (f32[4,2560]{1,0:T(4,128)S(1)}, f32[4,2560]{1,0:T(4,128)S(1)}, u32[]{:S(2)}, u32[]{:S(2)}) collective-permute-start(f32[4,2560]{1,0:T(4,128)S(1)} %add.20.left), channel_id=1, source_target_pairs={{0,4},{1,5},{2,6},{3,7},{4,0},{5,1},{6,2},{7,3},{8,12},{9,13},{10,... | collective-permute-start | bytes 122888 | tf_op jit(solution)/shard_map/ppermute | solution.py:281
  259.2 2.0 collective-permute-done.45.right
  261.2 2.8 %second_half.1 = (f32[4,2560]{1,0:T(4,128)}, f32[4,1280]{1,0:T(4,128)S(1)}, bf16[256,2560]{1,0:T(8,128)(2,1)}) custom-call(f32[4,2560]{1,0:T(4,128)S(1)} %add.20.left, f32[4,2560]{1,0:T(4,128)S(1)} %collective-permute-done.45.right, bf16[256,2560]{1,0:T(8,128)(2,1)S(1)} %bitcast.43, bf16[256,1280]{1,0:T(8,128)(2,1)S(1)} %get-tuple-element.114.vg, ...), custom_call_target="tpu_custom_call" | custom-call | tf_op jit(solution)/shard_map/second_half/pallas_call | solution.py:264
  264.1 1.2 collective-permute-done.46
  265.3 2.0 collective-permute-start.47
  267.3 1.8 collective-permute-done.47
  269.1 3.0 %collective-permute-start.48 = (f32[4,1280]{1,0:T(4,128)S(1)}, f32[4,1280]{1,0:T(4,128)S(1)}, u32[]{:S(2)}, u32[]{:S(2)}) collective-permute-start(f32[4,1280]{1,0:T(4,128)S(1)} %add.22), channel_id=1, source_target_pairs={{0,4},{1,5},{2,6},{3,7},{4,0},{5,1},{6,2},{7,3},{8,12},{9,13},{10,... | collective-permute-start | bytes 61448 | tf_op jit(solution)/shard_map/ppermute | solution.py:281
  272.1 1.8 collective-permute-done.48
  (98 shorter events, 10.6 us)
Async XLA Ops:
  0.6 145.6 %copy-start = (f32[1,4,1280]{2,1,0:T(4,128)S(1)}, f32[1,4,1280]{2,1,0:T(4,128)}, u32[]{:S(2)}) copy-start(f32[1,4,1280]{2,1,0:T(4,128)} %param.13) | copy-start | bytes 61444
  0.6 23.9 %collective-permute-start.2 = (bf16[320,1280]{1,0:T(8,128)(2,1)}, bf16[320,1280]{1,0:T(8,128)(2,1)S(1)}, u32[]{:S(2)}, u32[]{:S(2)}) collective-permute-start(bf16[320,1280]{1,0:T(8,128)(2,1)} %bitcast.44), channel_id=1, source_target_pairs={{0,2},{1,3},{2,4},{3,5},{4,6},{5,7},{8,10},{9,11},{10,12},{11,13},... | collective-permute-start | bytes 2457608 | tf_op jit(solution)/shard_map/ppermute | solution.py:72
  5.7 26.1 %collective-permute-start.11 = (bf16[320,1280]{1,0:T(8,128)(2,1)}, bf16[320,1280]{1,0:T(8,128)(2,1)S(1)}, u32[]{:S(2)}, u32[]{:S(2)}) collective-permute-start(bf16[320,1280]{1,0:T(8,128)(2,1)} %bitcast.49), channel_id=1, source_target_pairs={{2,0},{3,1},{4,2},{5,3},{6,4},{7,5},{10,8},{11,9},{12,10},{13,11},... | collective-permute-start | bytes 2457608 | tf_op jit(solution)/shard_map/ppermute | solution.py:72
  10.0 31.0 %collective-permute-start.8 = (bf16[320,1280]{1,0:T(8,128)(2,1)}, bf16[320,1280]{1,0:T(8,128)(2,1)}, u32[]{:S(2)}, u32[]{:S(2)}) collective-permute-start(bf16[320,1280]{1,0:T(8,128)(2,1)} %bitcast.50), channel_id=1, source_target_pairs={{0,2},{1,3},{2,4},{3,5},{4,6},{5,7},{8,10},{9,11},{10,12},{11,13},... | collective-permute-start | bytes 2457608 | tf_op jit(solution)/shard_map/ppermute | solution.py:72
  15.3 34.1 %collective-permute-start = (bf16[320,1280]{1,0:T(8,128)(2,1)}, bf16[320,1280]{1,0:T(8,128)(2,1)}, u32[]{:S(2)}, u32[]{:S(2)}) collective-permute-start(bf16[320,1280]{1,0:T(8,128)(2,1)} %bitcast.45), channel_id=1, source_target_pairs={{2,0},{3,1},{4,2},{5,3},{6,4},{7,5},{10,8},{11,9},{12,10},{13,11},... | collective-permute-start | bytes 2457608 | tf_op jit(solution)/shard_map/ppermute | solution.py:72
  16.6 34.4 %collective-permute-start.23 = (bf16[320,1280]{1,0:T(8,128)(2,1)}, bf16[320,1280]{1,0:T(8,128)(2,1)S(1)}, u32[]{:S(2)}, u32[]{:S(2)}) collective-permute-start(bf16[320,1280]{1,0:T(8,128)(2,1)} %bitcast.46), channel_id=1, source_target_pairs={{0,1},{1,0},{2,3},{3,2},{4,5},{5,4},{6,7},{7,6},{8,9},{9,8},{10,11... | collective-permute-start | bytes 2457608 | tf_op jit(solution)/shard_map/ppermute | solution.py:80
  24.5 34.5 %collective-permute-start.22 = (bf16[320,1280]{1,0:T(8,128)(2,1)}, bf16[320,1280]{1,0:T(8,128)(2,1)S(1)}, u32[]{:S(2)}, u32[]{:S(2)}) collective-permute-start(bf16[320,1280]{1,0:T(8,128)(2,1)} %bitcast.51), channel_id=1, source_target_pairs={{0,1},{1,0},{2,3},{3,2},{4,5},{5,4},{6,7},{7,6},{8,9},{9,8},{10,11... | collective-permute-start | bytes 2457608 | tf_op jit(solution)/shard_map/ppermute | solution.py:80
  31.8 30.5 %copy-start.6 = (bf16[320,1280]{1,0:T(8,128)(2,1)}, bf16[320,1280]{1,0:T(8,128)(2,1)S(1)}, u32[]{:S(2)}) copy-start(bf16[320,1280]{1,0:T(8,128)(2,1)S(1)} %collective-permute-done.11.refs_6_) | copy-start | bytes 2457604
  31.8 34.5 %collective-permute-start.12 = (bf16[320,1280]{1,0:T(8,128)(2,1)S(1)}, bf16[320,1280]{1,0:T(8,128)(2,1)S(1)}, u32[]{:S(2)}, u32[]{:S(2)}) collective-permute-start(bf16[320,1280]{1,0:T(8,128)(2,1)S(1)} %collective-permute-done.11.refs_6_), channel_id=1, source_target_pairs={{2,0},{3,1},{4,2},{5,3},{10,8},{11,9},{12,10},{13,11},{18,16},{19,... | collective-permute-start | bytes 2457608 | tf_op jit(solution)/shard_map/ppermute | solution.py:72
  41.0 26.1 %collective-permute-start.9 = (bf16[320,1280]{1,0:T(8,128)(2,1)}, bf16[320,1280]{1,0:T(8,128)(2,1)S(1)}, u32[]{:S(2)}, u32[]{:S(2)}) collective-permute-start(bf16[320,1280]{1,0:T(8,128)(2,1)} %collective-permute-done.8.refs_4_), channel_id=1, source_target_pairs={{2,4},{3,5},{4,6},{5,7},{10,12},{11,13},{12,14},{13,15},{18,20},{1... | collective-permute-start | bytes 2457608 | tf_op jit(solution)/shard_map/ppermute | solution.py:72
  49.4 19.1 %collective-permute-start.16 = (bf16[320,1280]{1,0:T(8,128)(2,1)}, bf16[320,1280]{1,0:T(8,128)(2,1)}, u32[]{:S(2)}, u32[]{:S(2)}) collective-permute-start(bf16[320,1280]{1,0:T(8,128)(2,1)} %bitcast.47), channel_id=1, source_target_pairs={{26,2},{27,3},{28,4},{29,5}} | collective-permute-start | bytes 2457608 | tf_op jit(solution)/shard_map/ppermute | solution.py:72
  51.0 0.9 copy-start.8
  51.9 23.7 %collective-permute-start.26 = (bf16[320,1280]{1,0:T(8,128)(2,1)S(1)}, bf16[320,1280]{1,0:T(8,128)(2,1)}, u32[]{:S(2)}, u32[]{:S(2)}) collective-permute-start(bf16[320,1280]{1,0:T(8,128)(2,1)S(1)} %collective-permute-done.2.refs_8_), channel_id=1, source_target_pairs={{2,3},{3,2},{4,5},{5,4},{6,7},{7,6},{10,11},{11,10},{12,13},{13,12... | collective-permute-start | bytes 2457608 | tf_op jit(solution)/shard_map/ppermute | solution.py:80
  59.1 0.9 copy-start.10
  60.0 18.0 %collective-permute-start.27 = (bf16[320,1280]{1,0:T(8,128)(2,1)}, bf16[320,1280]{1,0:T(8,128)(2,1)}, u32[]{:S(2)}, u32[]{:S(2)}) collective-permute-start(bf16[320,1280]{1,0:T(8,128)(2,1)} %collective-permute-done.refs_10_), channel_id=1, source_target_pairs={{0,1},{1,0},{2,3},{3,2},{4,5},{5,4},{8,9},{9,8},{10,11},{11,10},{1... | collective-permute-start | bytes 2457608 | tf_op jit(solution)/shard_map/ppermute | solution.py:80
  66.3 12.9 %collective-permute-start.3 = (bf16[320,1280]{1,0:T(8,128)(2,1)S(1)}, bf16[320,1280]{1,0:T(8,128)(2,1)S(1)}, u32[]{:S(2)}, u32[]{:S(2)}) collective-permute-start(bf16[320,1280]{1,0:T(8,128)(2,1)S(1)} %collective-permute-done.2.refs_8_), channel_id=1, source_target_pairs={{2,4},{3,5},{4,6},{5,7},{10,12},{11,13},{12,14},{13,15},{18,20},{1... | collective-permute-start | bytes 2457608 | tf_op jit(solution)/shard_map/ppermute | solution.py:72
  67.0 8.6 %copy-start.7 = (bf16[320,1280]{1,0:T(8,128)(2,1)S(1)}, bf16[320,1280]{1,0:T(8,128)(2,1)}, u32[]{:S(2)}) copy-start(bf16[320,1280]{1,0:T(8,128)(2,1)} %copy-done.6) | copy-start | bytes 2457604
  67.0 23.6 %collective-permute-start.1 = (bf16[320,1280]{1,0:T(8,128)(2,1)}, bf16[320,1280]{1,0:T(8,128)(2,1)S(1)}, u32[]{:S(2)}, u32[]{:S(2)}) collective-permute-start(bf16[320,1280]{1,0:T(8,128)(2,1)} %collective-permute-done.refs_10_), channel_id=1, source_target_pairs={{2,0},{3,1},{4,2},{5,3},{10,8},{11,9},{12,10},{13,11},{18,16},{19,... | collective-permute-start | bytes 2457608 | tf_op jit(solution)/shard_map/ppermute | solution.py:72
  68.6 22.9 %collective-permute-start.24 = (bf16[320,1280]{1,0:T(8,128)(2,1)}, bf16[320,1280]{1,0:T(8,128)(2,1)S(1)}, u32[]{:S(2)}, u32[]{:S(2)}) collective-permute-start(bf16[320,1280]{1,0:T(8,128)(2,1)} %collective-permute-done.8.refs_4_), channel_id=1, source_target_pairs={{2,3},{3,2},{4,5},{5,4},{6,7},{7,6},{10,11},{11,10},{12,13},{13,12... | collective-permute-start | bytes 2457608 | tf_op jit(solution)/shard_map/ppermute | solution.py:80
  75.6 18.1 %collective-permute-start.25 = (bf16[320,1280]{1,0:T(8,128)(2,1)S(1)}, bf16[320,1280]{1,0:T(8,128)(2,1)S(1)}, u32[]{:S(2)}, u32[]{:S(2)}) collective-permute-start(bf16[320,1280]{1,0:T(8,128)(2,1)S(1)} %copy-done.7), channel_id=1, source_target_pairs={{0,1},{1,0},{2,3},{3,2},{4,5},{5,4},{8,9},{9,8},{10,11},{11,10},{1... | collective-permute-start | bytes 2457608 | tf_op jit(solution)/shard_map/ppermute | solution.py:80
  77.9 30.2 %collective-permute-start.17 = (bf16[320,1280]{1,0:T(8,128)(2,1)}, bf16[320,1280]{1,0:T(8,128)(2,1)S(1)}, u32[]{:S(2)}, u32[]{:S(2)}) collective-permute-start(bf16[320,1280]{1,0:T(8,128)(2,1)} %collective-permute-done.16), channel_id=1, source_target_pairs={{2,0},{3,1},{4,6},{5,7}} | collective-permute-start | bytes 2457608 | tf_op jit(solution)/shard_map/ppermute | solution.py:72
  79.3 45.3 %collective-permute-start.20 = (bf16[320,1280]{1,0:T(8,128)(2,1)S(1)}, bf16[320,1280]{1,0:T(8,128)(2,1)S(1)}, u32[]{:S(2)}, u32[]{:S(2)}) collective-permute-start(bf16[320,1280]{1,0:T(8,128)(2,1)S(1)} %broadcast_select_fusion), channel_id=1, source_target_pairs={{2,0},{3,1},{4,6},{5,7},{10,8},{11,9},{12,14},{13,15},{18,16},{19,... | collective-permute-start | bytes 2457608 | tf_op jit(solution)/shard_map/ppermute | solution.py:72
  90.6 34.6 %collective-permute-start.14 = (bf16[320,1280]{1,0:T(8,128)(2,1)S(1)}, bf16[320,1280]{1,0:T(8,128)(2,1)S(1)}, u32[]{:S(2)}, u32[]{:S(2)}) collective-permute-start(bf16[320,1280]{1,0:T(8,128)(2,1)S(1)} %collective-permute-done.3.refs_4_), channel_id=1, source_target_pairs={{4,5},{5,4},{6,7},{7,6},{12,13},{13,12},{14,15},{15,14},{20,21},{2... | collective-permute-start | bytes 2457608 | tf_op jit(solution)/shard_map/ppermute | solution.py:80
  91.5 62.8 %copy-start.4 = (bf16[1,320,1280]{2,1,0:T(8,128)(2,1)S(1)}, bf16[1,320,1280]{2,1,0:T(8,128)(2,1)}, u32[]{:S(2)}) copy-start(bf16[1,320,1280]{2,1,0:T(8,128)(2,1)} %param.9) | copy-start | bytes 2457604
  91.5 62.8 %copy-start.5 = (bf16[1,320,1280]{2,1,0:T(8,128)(2,1)S(1)}, bf16[1,320,1280]{2,1,0:T(8,128)(2,1)}, u32[]{:S(2)}) copy-start(bf16[1,320,1280]{2,1,0:T(8,128)(2,1)} %param.10) | copy-start | bytes 2457604
  91.5 62.8 %copy-start.9 = (bf16[320,1280]{1,0:T(8,128)(2,1)S(1)}, bf16[320,1280]{1,0:T(8,128)(2,1)}, u32[]{:S(2)}) copy-start(bf16[320,1280]{1,0:T(8,128)(2,1)} %copy-done.8) | copy-start | bytes 2457604
  91.5 62.8 %copy-start.11 = (bf16[320,1280]{1,0:T(8,128)(2,1)S(1)}, bf16[320,1280]{1,0:T(8,128)(2,1)}, u32[]{:S(2)}) copy-start(bf16[320,1280]{1,0:T(8,128)(2,1)} %copy-done.10) | copy-start | bytes 2457604
  91.5 35.1 %collective-permute-start.15 = (bf16[320,1280]{1,0:T(8,128)(2,1)S(1)}, bf16[320,1280]{1,0:T(8,128)(2,1)S(1)}, u32[]{:S(2)}, u32[]{:S(2)}) collective-permute-start(bf16[320,1280]{1,0:T(8,128)(2,1)S(1)} %collective-permute-done.1.refs_6_), channel_id=1, source_target_pairs={{0,1},{1,0},{2,3},{3,2},{8,9},{9,8},{10,11},{11,10},{16,17},{17,16... | collective-permute-start | bytes 2457608 | tf_op jit(solution)/shard_map/ppermute | solution.py:80
  93.7 34.8 %collective-permute-start.10 = (bf16[320,1280]{1,0:T(8,128)(2,1)S(1)}, bf16[320,1280]{1,0:T(8,128)(2,1)S(1)}, u32[]{:S(2)}, u32[]{:S(2)}) collective-permute-start(bf16[320,1280]{1,0:T(8,128)(2,1)S(1)} %collective-permute-done.9.refs_0_), channel_id=1, source_target_pairs={{4,5},{5,4},{6,7},{7,6},{12,13},{13,12},{14,15},{15,14},{20,21},{2... | collective-permute-start | bytes 2457608 | tf_op jit(solution)/shard_map/ppermute | solution.py:80
  108.2 23.3 %collective-permute-start.18 = (bf16[320,1280]{1,0:T(8,128)(2,1)S(1)}, bf16[320,1280]{1,0:T(8,128)(2,1)S(1)}, u32[]{:S(2)}, u32[]{:S(2)}) collective-permute-start(bf16[320,1280]{1,0:T(8,128)(2,1)S(1)} %collective-permute-done.17), channel_id=1, source_target_pairs={{0,24},{1,25},{6,30},{7,31}} | collective-permute-start | bytes 2457608 | tf_op jit(solution)/shard_map/ppermute | solution.py:72
  124.5 12.7 %collective-permute-start.6 = (bf16[320,1280]{1,0:T(8,128)(2,1)S(1)}, bf16[320,1280]{1,0:T(8,128)(2,1)S(1)}, u32[]{:S(2)}, u32[]{:S(2)}) collective-permute-start(bf16[320,1280]{1,0:T(8,128)(2,1)S(1)} %broadcast_select_fusion.1), channel_id=1, source_target_pairs={{26,24},{27,25},{28,30},{29,31}} | collective-permute-start | bytes 2457608 | tf_op jit(solution)/shard_map/ppermute | solution.py:72
  125.3 21.0 %collective-permute-start.4 = (bf16[320,1280]{1,0:T(8,128)(2,1)S(1)}, bf16[320,1280]{1,0:T(8,128)(2,1)S(1)}, u32[]{:S(2)}, u32[]{:S(2)}) collective-permute-start(bf16[320,1280]{1,0:T(8,128)(2,1)S(1)} %broadcast_select_fusion.1), channel_id=1, source_target_pairs={{2,0},{3,1},{4,6},{5,7},{10,8},{11,9},{12,14},{13,15},{18,16},{19,... | collective-permute-start | bytes 2457608 | tf_op jit(solution)/shard_map/ppermute | solution.py:72
  126.6 29.9 %collective-permute-start.13 = (bf16[320,1280]{1,0:T(8,128)(2,1)S(1)}, bf16[320,1280]{1,0:T(8,128)(2,1)S(1)}, u32[]{:S(2)}, u32[]{:S(2)}) collective-permute-start(bf16[320,1280]{1,0:T(8,128)(2,1)S(1)} %collective-permute-done.12.refs_2_), channel_id=1, source_target_pairs={{0,1},{1,0},{2,3},{3,2},{8,9},{9,8},{10,11},{11,10},{16,17},{17,16... | collective-permute-start | bytes 2457608 | tf_op jit(solution)/shard_map/ppermute | solution.py:80
  128.5 28.0 %collective-permute-start.21 = (bf16[320,1280]{1,0:T(8,128)(2,1)S(1)}, bf16[320,1280]{1,0:T(8,128)(2,1)S(1)}, u32[]{:S(2)}, u32[]{:S(2)}) collective-permute-start(bf16[320,1280]{1,0:T(8,128)(2,1)S(1)} %collective-permute-done.20.refs_10_), channel_id=1, source_target_pairs={{0,1},{1,0},{2,3},{3,2},{4,5},{5,4},{6,7},{7,6},{8,9},{9,8},{10,11... | collective-permute-start | bytes 2457608 | tf_op jit(solution)/shard_map/ppermute | solution.py:80
  131.5 25.0 %collective-permute-start.19 = (bf16[320,1280]{1,0:T(8,128)(2,1)S(1)}, bf16[320,1280]{1,0:T(8,128)(2,1)S(1)}, u32[]{:S(2)}, u32[]{:S(2)}) collective-permute-start(bf16[320,1280]{1,0:T(8,128)(2,1)S(1)} %collective-permute-done.18.refs_8_), channel_id=1, source_target_pairs={{0,1},{1,0},{2,3},{3,2},{4,5},{5,4},{6,7},{7,6},{8,9},{9,8},{10,11... | collective-permute-start | bytes 2457608 | tf_op jit(solution)/shard_map/ppermute | solution.py:80
  137.2 20.1 %collective-permute-start.7 = (bf16[320,1280]{1,0:T(8,128)(2,1)S(1)}, bf16[320,1280]{1,0:T(8,128)(2,1)S(1)}, u32[]{:S(2)}, u32[]{:S(2)}) collective-permute-start(bf16[320,1280]{1,0:T(8,128)(2,1)S(1)} %collective-permute-done.6.refs_0_), channel_id=1, source_target_pairs={{0,1},{1,0},{2,3},{3,2},{4,5},{5,4},{6,7},{7,6},{8,9},{9,8},{10,11... | collective-permute-start | bytes 2457608 | tf_op jit(solution)/shard_map/ppermute | solution.py:80
  146.2 15.5 %collective-permute-start.5 = (bf16[320,1280]{1,0:T(8,128)(2,1)S(1)}, bf16[320,1280]{1,0:T(8,128)(2,1)S(1)}, u32[]{:S(2)}, u32[]{:S(2)}) collective-permute-start(bf16[320,1280]{1,0:T(8,128)(2,1)S(1)} %collective-permute-done.4.refs_0_), channel_id=1, source_target_pairs={{0,1},{1,0},{2,3},{3,2},{4,5},{5,4},{6,7},{7,6},{8,9},{9,8},{10,11... | collective-permute-start | bytes 2457608 | tf_op jit(solution)/shard_map/ppermute | solution.py:80
  157.3 1.1 copy-start.1
  157.3 1.5 copy-start.2
  158.8 3.8 %collective-permute-start.32 = (bf16[48,2560]{1,0:T(8,128)(2,1)S(1)}, bf16[48,2560]{1,0:T(8,128)(2,1)S(1)}, u32[]{:S(2)}, u32[]{:S(2)}) collective-permute-start(bf16[48,2560]{1,0:T(8,128)(2,1)S(1)} %get-tuple-element.74), channel_id=1, source_target_pairs={{24,16},{25,17},{26,18},{27,19},{28,20},{29,21},{30,22},{31,23}} | collective-permute-start | bytes 737288 | tf_op jit(solution)/shard_map/ppermute | solution.py:312
  159.5 3.8 %collective-permute-start.31 = (bf16[48,2560]{1,0:T(8,128)(2,1)S(1)}, bf16[48,2560]{1,0:T(8,128)(2,1)S(1)}, u32[]{:S(2)}, u32[]{:S(2)}) collective-permute-start(bf16[48,2560]{1,0:T(8,128)(2,1)S(1)} %get-tuple-element.73), channel_id=1, source_target_pairs={{24,16},{25,17},{26,18},{27,19},{28,20},{29,21},{30,22},{31,23}} | collective-permute-start | bytes 737288 | tf_op jit(solution)/shard_map/ppermute | solution.py:312
  160.2 3.8 %collective-permute-start.30 = (bf16[48,2560]{1,0:T(8,128)(2,1)S(1)}, bf16[48,2560]{1,0:T(8,128)(2,1)S(1)}, u32[]{:S(2)}, u32[]{:S(2)}) collective-permute-start(bf16[48,2560]{1,0:T(8,128)(2,1)S(1)} %get-tuple-element.72), channel_id=1, source_target_pairs={{24,16},{25,17},{26,18},{27,19},{28,20},{29,21},{30,22},{31,23}} | collective-permute-start | bytes 737288 | tf_op jit(solution)/shard_map/ppermute | solution.py:312
  161.0 3.9 %collective-permute-start.28 = (bf16[64,2560]{1,0:T(8,128)(2,1)S(1)}, bf16[64,2560]{1,0:T(8,128)(2,1)S(1)}, u32[]{:S(2)}, u32[]{:S(2)}) collective-permute-start(bf16[64,2560]{1,0:T(8,128)(2,1)S(1)} %get-tuple-element.70), channel_id=1, source_target_pairs={{24,16},{25,17},{26,18},{27,19},{28,20},{29,21},{30,22},{31,23}} | collective-permute-start | bytes 983048 | tf_op jit(solution)/shard_map/ppermute | solution.py:312
  161.7 3.1 %collective-permute-start.29 = (bf16[48,2560]{1,0:T(8,128)(2,1)S(1)}, bf16[48,2560]{1,0:T(8,128)(2,1)S(1)}, u32[]{:S(2)}, u32[]{:S(2)}) collective-permute-start(bf16[48,2560]{1,0:T(8,128)(2,1)S(1)} %get-tuple-element.71), channel_id=1, source_target_pairs={{24,16},{25,17},{26,18},{27,19},{28,20},{29,21},{30,22},{31,23}} | collective-permute-start | bytes 737288 | tf_op jit(solution)/shard_map/ppermute | solution.py:312
  162.7 3.8 %collective-permute-start.37 = (bf16[48,2560]{1,0:T(8,128)(2,1)S(1)}, bf16[48,2560]{1,0:T(8,128)(2,1)S(1)}, u32[]{:S(2)}, u32[]{:S(2)}) collective-permute-start(bf16[48,2560]{1,0:T(8,128)(2,1)S(1)} %get-tuple-element.88), channel_id=1, source_target_pairs={{16,8},{17,9},{18,10},{19,11},{20,12},{21,13},{22,14},{23,15}} | collective-permute-start | bytes 737288 | tf_op jit(solution)/shard_map/ppermute | solution.py:312
  163.4 4.4 %collective-permute-start.36 = (bf16[48,2560]{1,0:T(8,128)(2,1)S(1)}, bf16[48,2560]{1,0:T(8,128)(2,1)S(1)}, u32[]{:S(2)}, u32[]{:S(2)}) collective-permute-start(bf16[48,2560]{1,0:T(8,128)(2,1)S(1)} %get-tuple-element.87), channel_id=1, source_target_pairs={{16,8},{17,9},{18,10},{19,11},{20,12},{21,13},{22,14},{23,15}} | collective-permute-start | bytes 737288 | tf_op jit(solution)/shard_map/ppermute | solution.py:312
  164.1 5.0 %collective-permute-start.35 = (bf16[48,2560]{1,0:T(8,128)(2,1)S(1)}, bf16[48,2560]{1,0:T(8,128)(2,1)S(1)}, u32[]{:S(2)}, u32[]{:S(2)}) collective-permute-start(bf16[48,2560]{1,0:T(8,128)(2,1)S(1)} %get-tuple-element.86), channel_id=1, source_target_pairs={{16,8},{17,9},{18,10},{19,11},{20,12},{21,13},{22,14},{23,15}} | collective-permute-start | bytes 737288 | tf_op jit(solution)/shard_map/ppermute | solution.py:312
  164.9 5.6 %collective-permute-start.33 = (bf16[64,2560]{1,0:T(8,128)(2,1)S(1)}, bf16[64,2560]{1,0:T(8,128)(2,1)S(1)}, u32[]{:S(2)}, u32[]{:S(2)}) collective-permute-start(bf16[64,2560]{1,0:T(8,128)(2,1)S(1)} %get-tuple-element.84), channel_id=1, source_target_pairs={{16,8},{17,9},{18,10},{19,11},{20,12},{21,13},{22,14},{23,15}} | collective-permute-start | bytes 983048 | tf_op jit(solution)/shard_map/ppermute | solution.py:312
  165.6 4.9 %collective-permute-start.34 = (bf16[48,2560]{1,0:T(8,128)(2,1)S(1)}, bf16[48,2560]{1,0:T(8,128)(2,1)S(1)}, u32[]{:S(2)}, u32[]{:S(2)}) collective-permute-start(bf16[48,2560]{1,0:T(8,128)(2,1)S(1)} %get-tuple-element.85), channel_id=1, source_target_pairs={{16,8},{17,9},{18,10},{19,11},{20,12},{21,13},{22,14},{23,15}} | collective-permute-start | bytes 737288 | tf_op jit(solution)/shard_map/ppermute | solution.py:312
  166.5 21.1 %collective-permute-start.42 = (bf16[48,2560]{1,0:T(8,128)(2,1)S(1)}, bf16[48,2560]{1,0:T(8,128)(2,1)S(1)}, u32[]{:S(2)}, u32[]{:S(2)}) collective-permute-start(bf16[48,2560]{1,0:T(8,128)(2,1)S(1)} %get-tuple-element.103), channel_id=1, source_target_pairs={{8,0},{9,1},{10,2},{11,3},{12,4},{13,5},{14,6},{15,7}} | collective-permute-start | bytes 737288 | tf_op jit(solution)/shard_map/ppermute | solution.py:312
  167.8 25.3 %collective-permute-start.41 = (bf16[48,2560]{1,0:T(8,128)(2,1)S(1)}, bf16[48,2560]{1,0:T(8,128)(2,1)S(1)}, u32[]{:S(2)}, u32[]{:S(2)}) collective-permute-start(bf16[48,2560]{1,0:T(8,128)(2,1)S(1)} %get-tuple-element.102), channel_id=1, source_target_pairs={{8,0},{9,1},{10,2},{11,3},{12,4},{13,5},{14,6},{15,7}} | collective-permute-start | bytes 737288 | tf_op jit(solution)/shard_map/ppermute | solution.py:312
  169.1 29.6 %collective-permute-start.40 = (bf16[48,2560]{1,0:T(8,128)(2,1)S(1)}, bf16[48,2560]{1,0:T(8,128)(2,1)S(1)}, u32[]{:S(2)}, u32[]{:S(2)}) collective-permute-start(bf16[48,2560]{1,0:T(8,128)(2,1)S(1)} %get-tuple-element.101), channel_id=1, source_target_pairs={{8,0},{9,1},{10,2},{11,3},{12,4},{13,5},{14,6},{15,7}} | collective-permute-start | bytes 737288 | tf_op jit(solution)/shard_map/ppermute | solution.py:312
  170.5 72.9 %collective-permute-start.38 = (bf16[64,2560]{1,0:T(8,128)(2,1)S(1)}, bf16[64,2560]{1,0:T(8,128)(2,1)S(1)}, u32[]{:S(2)}, u32[]{:S(2)}) collective-permute-start(bf16[64,2560]{1,0:T(8,128)(2,1)S(1)} %get-tuple-element.99), channel_id=1, source_target_pairs={{8,0},{9,1},{10,2},{11,3},{12,4},{13,5},{14,6},{15,7}} | collective-permute-start | bytes 983048 | tf_op jit(solution)/shard_map/ppermute | solution.py:312
  171.8 66.7 %collective-permute-start.39 = (bf16[48,2560]{1,0:T(8,128)(2,1)S(1)}, bf16[48,2560]{1,0:T(8,128)(2,1)S(1)}, u32[]{:S(2)}, u32[]{:S(2)}) collective-permute-start(bf16[48,2560]{1,0:T(8,128)(2,1)S(1)} %get-tuple-element.100), channel_id=1, source_target_pairs={{8,0},{9,1},{10,2},{11,3},{12,4},{13,5},{14,6},{15,7}} | collective-permute-start | bytes 737288 | tf_op jit(solution)/shard_map/ppermute | solution.py:312
  243.4 17.7 %slice-start = ((s8[6553600]{0:T(1024)(128)(4,1)}), s8[4194304]{0:T(1024)(128)(4,1)S(1)}, s32[]{:S(2)}) async-start(s8[6553600]{0:T(1024)(128)(4,1)} %bitcast.40), calls=%async_computation | async-start | bytes 8388608
  243.5 5.8 %copy-start.3 = (bf16[1,256,2560]{2,1,0:T(8,128)(2,1)S(1)}, bf16[1,256,2560]{2,1,0:T(8,128)(2,1)}, u32[]{:S(2)}) copy-start(bf16[1,256,2560]{2,1,0:T(8,128)(2,1)} %param.7) | copy-start | bytes 3932164
  243.5 17.7 %slice-start.1 = ((s8[6553600]{0:T(1024)(128)(4,1)}), s8[2359296]{0:T(1024)(128)(4,1)S(1)}, s32[]{:S(2)}) async-start(s8[6553600]{0:T(1024)(128)(4,1)} %bitcast.40), calls=%async_computation.1 | async-start | bytes 4718592
  249.9 1.2 collective-permute-start.43
  251.2 5.0 %collective-permute-start.44 = (f32[4,2560]{1,0:T(4,128)S(1)}, f32[4,2560]{1,0:T(4,128)S(1)}, u32[]{:S(2)}, u32[]{:S(2)}) collective-permute-start(f32[4,2560]{1,0:T(4,128)S(1)} %add.19), channel_id=1, source_target_pairs={{0,2},{1,3},{2,0},{3,1},{4,6},{5,7},{6,4},{7,5},{8,10},{9,11},{10,... | collective-permute-start | bytes 122888 | tf_op jit(solution)/shard_map/ppermute | solution.py:281
  256.2 5.0 %collective-permute-start.45 = (f32[4,2560]{1,0:T(4,128)S(1)}, f32[4,2560]{1,0:T(4,128)S(1)}, u32[]{:S(2)}, u32[]{:S(2)}) collective-permute-start(f32[4,2560]{1,0:T(4,128)S(1)} %add.20.left), channel_id=1, source_target_pairs={{0,4},{1,5},{2,6},{3,7},{4,0},{5,1},{6,2},{7,3},{8,12},{9,13},{10,... | collective-permute-start | bytes 122888 | tf_op jit(solution)/shard_map/ppermute | solution.py:281
  264.0 1.3 collective-permute-start.46
  265.3 3.8 %collective-permute-start.47 = (f32[4,1280]{1,0:T(4,128)S(1)}, f32[4,1280]{1,0:T(4,128)S(1)}, u32[]{:S(2)}, u32[]{:S(2)}) collective-permute-start(f32[4,1280]{1,0:T(4,128)S(1)} %add.21), channel_id=1, source_target_pairs={{0,2},{1,3},{2,0},{3,1},{4,6},{5,7},{6,4},{7,5},{8,10},{9,11},{10,... | collective-permute-start | bytes 61448 | tf_op jit(solution)/shard_map/ppermute | solution.py:281
  269.1 4.7 %collective-permute-start.48 = (f32[4,1280]{1,0:T(4,128)S(1)}, f32[4,1280]{1,0:T(4,128)S(1)}, u32[]{:S(2)}, u32[]{:S(2)}) collective-permute-start(f32[4,1280]{1,0:T(4,128)S(1)} %add.22), channel_id=1, source_target_pairs={{0,4},{1,5},{2,6},{3,7},{4,0},{5,1},{6,2},{7,3},{8,12},{9,13},{10,... | collective-permute-start | bytes 61448 | tf_op jit(solution)/shard_map/ppermute | solution.py:281

commit v2 on v1

--- a/solution.py
+++ b/solution.py
@@ -17,11 +17,12 @@
 
 def put(whole, pieces, shape, dtype, after=()):
     arrays = list({id(piece): piece for _, piece, _, _ in pieces}.values())
-    rows = arrays[0].shape[0]
+    rows = arrays[0].shape[-2]
     if rows % 16:
         whole = jnp.zeros(shape, dtype) if whole is None else whole
         rank = lax.axis_index("dp")
         for kind, piece, source, valid in pieces:
+            piece = piece[kind] if piece.ndim == 3 else piece
             at = jnp.clip(source(rank), 0, shape[1] // rows - 1) * rows
             held = lax.dynamic_slice(whole, (kind, at, 0), (1,) + piece.shape)
             piece = jnp.where(valid(rank), piece[None], held)
@@ -38,7 +39,8 @@
                 @pl.when(valid(rank))
                 def _():
                     at = pl.ds(pl.multiple_of(source(rank) * rows, 16), rows)
-                    copy = pltpu.make_async_copy(ref, out.at[kind, at], done.at[sem])
+                    part = ref.at[kind] if len(ref.shape) == 3 else ref
+                    copy = pltpu.make_async_copy(part, out.at[kind, at], done.at[sem])
                     getattr(copy, phase)()
 
     held = [] if whole is None else [whole]
@@ -75,8 +77,8 @@
         moves = [(s, c, s, d) for s in range(sections) for c, d in moves]
         return permute(value, [move for move in moves if move not in skip])
 
-    def swap(value, first=0, last=chips):
-        pairs = [(i, i ^ 1) for i in range(first * CORES, last * CORES)]
+    def swap(value):
+        pairs = [(i, i ^ 1) for i in range(replicas)]
         return lax.ppermute(value, "dp", pairs)
 
     def shards(piece, other, by, first=0, last=chips, at_top=None):
@@ -121,13 +123,13 @@
                 relay = permute(matrices[1], [(top, c, 0, c) for c in inner])
                 relay = permute(relay, [(0, c, 0, d) for c, d in zip(inner, outer)])
                 relay = permute(relay, [(0, c, top, c) for c in outer])
+            both = swap(jnp.stack(matrices))
             for kind, matrix in enumerate(matrices):
-                own = shards(matrix, swap(matrix), 0)
-                groups[0] += [(kind,) + piece for piece in own]
+                groups[0] += [(kind,) + piece for piece in shards(matrix, both, 0)]
         for kind in range(len(matrices)):
             if step < chips - 1:
-                from_below = swap(up[kind], step, chips)
-                from_above = swap(down[kind], 0, chips - step)
+                from_below = swap(up[kind])
+                from_above = swap(down[kind])
                 low, high = (1, chips - 1) if step == 1 and kind == 1 and relayed else (0, chips)
                 pieces = shards(up[kind], from_below, -step, step, high)
                 pieces += shards(down[kind], from_above, step, low, chips - step)
@@ -140,7 +142,7 @@
                 pieces = shards(up[kind], other, step, 0, 1, whose)
                 pieces += shards(up[kind], other, -step, step, chips, whose)
             behind = 2 * (chips - 1 - step) + len(matrices) - 1 - kind
-            groups[0 if behind > 3 else 1 if behind else 2] += [
+            groups[0 if behind > 3 else 1 if behind > 1 else 2] += [
                 (kind,) + piece for piece in pieces
             ]
         if relayed and step == chips - 2:

time: 275 us -> 265 us (0.964)
  starting transfers between devices: 85.4 us -> 40.2 us
  waiting for transfers between devices: 143 us -> 174 us
    ppermute x14 -> x13, starting transfers between devices: 33.4 us -> 1.81 us  [swap(): return lax.ppermute(value, 'dp', pairs)]
    ppermute x14, waiting for transfers between devices: 82.3 us -> 111 us  [permute(): return lax.ppermute(value, ('section', 'dp'), pairs)]
    ppermute x6, starting transfers between devices: 11.1 us -> 0.64 us  [exchange(): return lax.ppermute(value, 'dp', [(i, i ^ by) for i in range(replicas)])]
    ppermute x6, waiting for transfers between devices: 9.93 us -> 19.5 us  [exchange(): return lax.ppermute(value, 'dp', [(i, i ^ by) for i in range(replicas)])]
    ppermute x15, waiting for transfers between devices: 50.6 us -> 43.5 us  [local(): arriving[k] = lax.ppermute(send, 'section', [(section, section - 1)])]
    ppermute x14, starting transfers between devices: 27.5 us -> 24.5 us  [permute(): return lax.ppermute(value, ('section', 'dp'), pairs)]
  transfers between devices with their start and end apart: 49 -> 48, of which waited for: 19 -> 20; matrix products, arithmetic and copies ran while one was open for 3% -> 4% of each run, Pallas kernels for 8% -> 9%
where the time goes in v2:
time: 265 us; the launch traced here: 264 us
  waiting for transfers between devices  174 us (66%)
  starting transfers between devices  40.2 us (15%)
  Pallas kernels  31.4 us (12%)
  matrix products  9.31 us (4%)
  local copies, waits for them, and re-layouts  4.09 us (2%)
  other arithmetic  3.54 us (1%)
    ppermute x14, waiting for transfers between devices, permute(): return lax.ppermute(value, ('section', 'dp'), pairs)  111 us
    ppermute x15, waiting for transfers between devices, local(): arriving[k] = lax.ppermute(send, 'section', [(section, section - 1)])  43.5 us
    pallas_call x20, Pallas kernels, stage(): pl.pallas_call(body, in_specs=[VMEM] * 3 + [ANY] + [VMEM] * len(held), ou...  25.3 us
    ppermute x14, starting transfers between devices, permute(): return lax.ppermute(value, ('section', 'dp'), pairs)  24.5 us
    ppermute x6, waiting for transfers between devices, exchange(): return lax.ppermute(value, 'dp', [(i, i ^ by) for i in range(replicas)])  19.5 us
    ppermute x15, starting transfers between devices, local(): arriving[k] = lax.ppermute(send, 'section', [(section, section - 1)])  13.2 us
    dot_general x1, matrix products, local(): lax.dot_general(warm, error.astype(jnp.float32), (((1,), (1,)), ((), ()))...  8.01 us
  transfers between devices with their start and end apart: 48, of which 20 were waited for; matrix products, arithmetic and copies ran while one was open for 4% of the time, Pallas kernels for 9%

profile of v2, /device:TPU:0, one launch (start us, length us, event | category | flops | bytes accessed | tf_op | source)
XLA Modules:
  0.0 263.8 jit_solution(12638418750481332369)
XLA Ops:
  0.6 5.9 %collective-permute-start.2 = (bf16[320,1280]{1,0:T(8,128)(2,1)}, bf16[320,1280]{1,0:T(8,128)(2,1)}, u32[]{:S(2)}, u32[]{:S(2)}) collective-permute-start(bf16[320,1280]{1,0:T(8,128)(2,1)} %bitcast.44), channel_id=1, source_target_pairs={{0,2},{1,3},{2,4},{3,5},{4,6},{5,7},{8,10},{9,11},{10,12},{11,13},... | collective-permute-start | bytes 2457608 | tf_op jit(solution)/shard_map/ppermute | solution.py:74
  6.6 1.3 collective-permute-start
  7.8 5.4 %collective-permute-start.8 = (bf16[320,1280]{1,0:T(8,128)(2,1)}, bf16[320,1280]{1,0:T(8,128)(2,1)}, u32[]{:S(2)}, u32[]{:S(2)}) collective-permute-start(bf16[320,1280]{1,0:T(8,128)(2,1)} %bitcast.48), channel_id=1, source_target_pairs={{0,2},{1,3},{2,4},{3,5},{4,6},{5,7},{8,10},{9,11},{10,12},{11,13},... | collective-permute-start | bytes 2457608 | tf_op jit(solution)/shard_map/ppermute | solution.py:74
  13.3 1.3 collective-permute-start.6
  14.6 0.7 collective-permute-start.18
  15.3 9.3 %collective-permute-done.2.refs_7_ = bf16[320,1280]{1,0:T(8,128)(2,1)} collective-permute-done((bf16[320,1280]{1,0:T(8,128)(2,1)}, bf16[320,1280]{1,0:T(8,128)(2,1)}, u32[]{:S(2)}, u32[]{:S(2)}) %collective-permute-start.2) | collective-permute-done | bytes 819232 | tf_op jit(solution)/shard_map/ppermute | solution.py:74
  24.5 5.3 %collective-permute-done.refs_9_ = bf16[320,1280]{1,0:T(8,128)(2,1)} collective-permute-done((bf16[320,1280]{1,0:T(8,128)(2,1)}, bf16[320,1280]{1,0:T(8,128)(2,1)}, u32[]{:S(2)}, u32[]{:S(2)}) %collective-permute-start) | collective-permute-done | bytes 819232 | tf_op jit(solution)/shard_map/ppermute | solution.py:74
  29.9 11.1 %collective-permute-done.8.refs_3_ = bf16[320,1280]{1,0:T(8,128)(2,1)} collective-permute-done((bf16[320,1280]{1,0:T(8,128)(2,1)}, bf16[320,1280]{1,0:T(8,128)(2,1)}, u32[]{:S(2)}, u32[]{:S(2)}) %collective-permute-start.8) | collective-permute-done | bytes 819232 | tf_op jit(solution)/shard_map/ppermute | solution.py:74
  41.0 5.0 %collective-permute-done.6.refs_5_ = bf16[320,1280]{1,0:T(8,128)(2,1)} collective-permute-done((bf16[320,1280]{1,0:T(8,128)(2,1)}, bf16[320,1280]{1,0:T(8,128)(2,1)}, u32[]{:S(2)}, u32[]{:S(2)}) %collective-permute-start.6) | collective-permute-done | bytes 819232 | tf_op jit(solution)/shard_map/ppermute | solution.py:74
  46.0 0.7 collective-permute-start.3
  46.7 1.3 collective-permute-start.1
  48.1 1.0 copy-done.6
  49.1 0.7 collective-permute-start.9
  49.8 2.7 %pad_maximum_fusion = bf16[2,320,1280]{2,1,0:T(8,128)(2,1)} fusion(bf16[1,320,1280]{2,1,0:T(8,128)(2,1)} %param.9, bf16[1,320,1280]{2,1,0:T(8,128)(2,1)} %param.10), kind=kLoop, calls=%fused_computation.1 | loop fusion | flops 819200 | bytes 3276800 | tf_op jit(solution)/shard_map/stack | solution.py:126
  52.5 1.0 copy-done.8
  53.5 0.9 copy-done.10
  54.4 1.3 collective-permute-start.7
  56.2 15.2 %collective-permute-done.1.refs_6_ = bf16[320,1280]{1,0:T(8,128)(2,1)S(1)} collective-permute-done((bf16[320,1280]{1,0:T(8,128)(2,1)}, bf16[320,1280]{1,0:T(8,128)(2,1)S(1)}, u32[]{:S(2)}, u32[]{:S(2)}) %collective-permute-start.1) | collective-permute-done | bytes 819232 | tf_op jit(solution)/shard_map/ppermute | solution.py:74
  71.4 1.3 collective-permute-start.19
  72.9 16.1 %collective-permute-done.7.refs_2_ = bf16[320,1280]{1,0:T(8,128)(2,1)S(1)} collective-permute-done((bf16[320,1280]{1,0:T(8,128)(2,1)}, bf16[320,1280]{1,0:T(8,128)(2,1)S(1)}, u32[]{:S(2)}, u32[]{:S(2)}) %collective-permute-start.7) | collective-permute-done | bytes 819232 | tf_op jit(solution)/shard_map/ppermute | solution.py:74
  89.7 14.6 %collective-permute-done.19 = bf16[320,1280]{1,0:T(8,128)(2,1)S(1)} collective-permute-done((bf16[320,1280]{1,0:T(8,128)(2,1)}, bf16[320,1280]{1,0:T(8,128)(2,1)S(1)}, u32[]{:S(2)}, u32[]{:S(2)}) %collective-permute-start.19) | collective-permute-done | bytes 819232 | tf_op jit(solution)/shard_map/ppermute | solution.py:74
  104.3 1.3 collective-permute-start.20
  105.6 0.7 collective-permute-start.12
  106.3 1.3 collective-permute-start.10
  107.7 1.3 collective-permute-start.4
  109.0 12.3 %collective-permute-done.20.refs_8_ = bf16[320,1280]{1,0:T(8,128)(2,1)S(1)} collective-permute-done((bf16[320,1280]{1,0:T(8,128)(2,1)S(1)}, bf16[320,1280]{1,0:T(8,128)(2,1)S(1)}, u32[]{:S(2)}, u32[]{:S(2)}) %collective-permute-start.20) | collective-permute-done | bytes 819232 | tf_op jit(solution)/shard_map/ppermute | solution.py:74
  121.8 7.5 %collective-permute-done.10.refs_0_ = bf16[320,1280]{1,0:T(8,128)(2,1)S(1)} collective-permute-done((bf16[320,1280]{1,0:T(8,128)(2,1)S(1)}, bf16[320,1280]{1,0:T(8,128)(2,1)S(1)}, u32[]{:S(2)}, u32[]{:S(2)}) %collective-permute-start.10) | collective-permute-done | bytes 819232 | tf_op jit(solution)/shard_map/ppermute | solution.py:74
  129.4 14.4 %collective-permute-done.4.refs_0_ = bf16[320,1280]{1,0:T(8,128)(2,1)S(1)} collective-permute-done((bf16[320,1280]{1,0:T(8,128)(2,1)S(1)}, bf16[320,1280]{1,0:T(8,128)(2,1)S(1)}, u32[]{:S(2)}, u32[]{:S(2)}) %collective-permute-start.4) | collective-permute-done | bytes 819232 | tf_op jit(solution)/shard_map/ppermute | solution.py:74
  143.8 8.0 %fusion.2.refs_0_ = f32[4,2560]{1,0:T(4,128)S(1)} fusion(f32[1,4,1280]{2,1,0:T(4,128)S(1)} %copy-done, bf16[1,2560,1280]{2,1,0:T(8,128)(2,1)} %param.11), kind=kOutput, calls=%fused_computation.6 | convolution fusion | flops 157286400 | bytes 6615040 | tf_op jit(solution)/shard_map/dot_general | solution.py:299
  151.9 2.2 put.4.refs_10_
  155.0 0.7 copy-done.1
  156.2 0.7 collective-permute-start.31
  156.9 0.7 collective-permute-start.30
  157.6 0.7 collective-permute-start.29
  158.3 0.7 collective-permute-start.27
  159.0 0.7 collective-permute-start.28
  160.0 0.7 collective-permute-start.36
  160.7 0.7 collective-permute-start.35
  161.5 0.7 collective-permute-start.34
  162.2 0.7 collective-permute-start.32
  162.9 0.7 collective-permute-start.33
  163.6 1.3 collective-permute-start.41
  165.2 1.3 collective-permute-start.40
  166.5 1.3 collective-permute-start.39
  167.9 1.3 collective-permute-start.37
  169.2 1.3 collective-permute-start.38
  170.5 7.3 %collective-permute-done.41.arr = bf16[48,2560]{1,0:T(8,128)(2,1)S(1)} collective-permute-done((bf16[48,2560]{1,0:T(8,128)(2,1)S(1)}, bf16[48,2560]{1,0:T(8,128)(2,1)S(1)}, u32[]{:S(2)}, u32[]{:S(2)}) %collective-permute-start.41) | collective-permute-done | bytes 245792 | tf_op jit(solution)/shard_map/ppermute | solution.py:314
  177.7 4.9 %shard_map.109 = (bf16[256,1280]{1,0:T(8,128)(2,1)S(1)}, bf16[256,2560]{1,0:T(8,128)(2,1)S(1)}, bf16[48,2560]{1,0:T(8,128)(2,1)}) custom-call(bf16[2,2560,1280]{2,1,0:T(8,128)(2,1)S(1)} %put.7.w, bf16[48,2560]{1,0:T(8,128)(2,1)S(1)} %collective-permute-done.41.arr, bf16[256,1280]{1,0:T(8,128)(2,1)S(1)} %bitcast.35, ...), custom_call_target="tpu_custom_call", output_to_operand_aliasing={{0}: (4, {}), {1}: (5, {})} | custom-call | flops 629145600 | bytes 13107200 | tf_op jit(solution)/shard_map/pallas_call | solution.py:204
  182.7 0.8 collective-permute-done.40.arr
  183.5 4.9 %shard_map.110 = (bf16[256,1280]{1,0:T(8,128)(2,1)S(1)}, bf16[256,2560]{1,0:T(8,128)(2,1)S(1)}, bf16[48,2560]{1,0:T(8,128)(2,1)}) custom-call(bf16[2,2560,1280]{2,1,0:T(8,128)(2,1)S(1)} %put.7.w, bf16[48,2560]{1,0:T(8,128)(2,1)S(1)} %collective-permute-done.40.arr, bf16[256,1280]{1,0:T(8,128)(2,1)S(1)} %bitcast.36, ...), custom_call_target="tpu_custom_call", output_to_operand_aliasing={{0}: (4, {}), {1}: (5, {})} | custom-call | flops 629145600 | bytes 13107200 | tf_op jit(solution)/shard_map/pallas_call | solution.py:204
  188.4 0.6 collective-permute-done.39.arr
  189.1 4.9 %shard_map.111 = (bf16[256,1280]{1,0:T(8,128)(2,1)S(1)}, bf16[256,2560]{1,0:T(8,128)(2,1)S(1)}, bf16[48,2560]{1,0:T(8,128)(2,1)}) custom-call(bf16[2,2560,1280]{2,1,0:T(8,128)(2,1)S(1)} %put.7.w, bf16[48,2560]{1,0:T(8,128)(2,1)S(1)} %collective-permute-done.39.arr, bf16[256,1280]{1,0:T(8,128)(2,1)S(1)} %bitcast.37, ...), custom_call_target="tpu_custom_call", output_to_operand_aliasing={{0}: (4, {}), {1}: (5, {})} | custom-call | flops 629145600 | bytes 13107200 | tf_op jit(solution)/shard_map/pallas_call | solution.py:204
  194.0 34.7 %collective-permute-done.38.arr = bf16[48,2560]{1,0:T(8,128)(2,1)S(1)} collective-permute-done((bf16[48,2560]{1,0:T(8,128)(2,1)S(1)}, bf16[48,2560]{1,0:T(8,128)(2,1)S(1)}, u32[]{:S(2)}, u32[]{:S(2)}) %collective-permute-start.38) | collective-permute-done | bytes 245792 | tf_op jit(solution)/shard_map/ppermute | solution.py:314
  228.7 4.9 %shard_map.112 = (bf16[256,1280]{1,0:T(8,128)(2,1)S(1)}, bf16[256,2560]{1,0:T(8,128)(2,1)S(1)}, bf16[48,2560]{1,0:T(8,128)(2,1)}) custom-call(bf16[2,2560,1280]{2,1,0:T(8,128)(2,1)S(1)} %put.7.w, bf16[48,2560]{1,0:T(8,128)(2,1)S(1)} %collective-permute-done.38.arr, bf16[256,1280]{1,0:T(8,128)(2,1)S(1)} %bitcast.38, ...), custom_call_target="tpu_custom_call", output_to_operand_aliasing={{0}: (4, {}), {1}: (5, {})} | custom-call | flops 629145600 | bytes 13107200 | tf_op jit(solution)/shard_map/pallas_call | solution.py:204
  233.7 5.1 %shard_map.113 = (bf16[256,1280]{1,0:T(8,128)(2,1)S(1)}, bf16[256,2560]{1,0:T(8,128)(2,1)S(1)}, bf16[64,2560]{1,0:T(8,128)(2,1)}) custom-call(bf16[2,2560,1280]{2,1,0:T(8,128)(2,1)S(1)} %put.7.w, bf16[64,2560]{1,0:T(8,128)(2,1)S(1)} %collective-permute-done.37.arr, bf16[256,1280]{1,0:T(8,128)(2,1)S(1)} %bitcast.39, ...), custom_call_target="tpu_custom_call", output_to_operand_aliasing={{0}: (4, {}), {1}: (5, {})} | custom-call | flops 838860800 | bytes 13107200 | tf_op jit(solution)/shard_map/pallas_call | solution.py:204
  238.8 0.6 fusion
  239.5 0.7 convolution_add_fusion
  240.2 1.2 collective-permute-done.42
  241.6 3.8 %collective-permute-done.43 = f32[4,2560]{1,0:T(4,128)S(1)} collective-permute-done((f32[4,2560]{1,0:T(4,128)S(1)}, f32[4,2560]{1,0:T(4,128)S(1)}, u32[]{:S(2)}, u32[]{:S(2)}) %collective-permute-start.43) | collective-permute-done | bytes 40992 | tf_op jit(solution)/shard_map/ppermute | solution.py:283
  245.6 4.9 %collective-permute-done.44.right = f32[4,2560]{1,0:T(4,128)S(1)} collective-permute-done((f32[4,2560]{1,0:T(4,128)S(1)}, f32[4,2560]{1,0:T(4,128)S(1)}, u32[]{:S(2)}, u32[]{:S(2)}) %collective-permute-start.44) | collective-permute-done | bytes 40992 | tf_op jit(solution)/shard_map/ppermute | solution.py:283
  250.5 2.8 %second_half.1 = (f32[4,2560]{1,0:T(4,128)}, f32[4,1280]{1,0:T(4,128)S(1)}, bf16[256,2560]{1,0:T(8,128)(2,1)}) custom-call(f32[4,2560]{1,0:T(4,128)S(1)} %add.20.left, f32[4,2560]{1,0:T(4,128)S(1)} %collective-permute-done.44.right, bf16[256,2560]{1,0:T(8,128)(2,1)S(1)} %bitcast.43, bf16[256,1280]{1,0:T(8,128)(2,1)S(1)} %get-tuple-element.114.vg, ...), custom_call_target="tpu_custom_call" | custom-call | tf_op jit(solution)/shard_map/second_half/pallas_call | solution.py:266
  253.4 1.2 collective-permute-done.45
  254.8 3.7 %collective-permute-done.46 = f32[4,1280]{1,0:T(4,128)S(1)} collective-permute-done((f32[4,1280]{1,0:T(4,128)S(1)}, f32[4,1280]{1,0:T(4,128)S(1)}, u32[]{:S(2)}, u32[]{:S(2)}) %collective-permute-start.46) | collective-permute-done | bytes 20512 | tf_op jit(solution)/shard_map/ppermute | solution.py:283
  258.5 4.7 %collective-permute-done.47 = f32[4,1280]{1,0:T(4,128)S(1)} collective-permute-done((f32[4,1280]{1,0:T(4,128)S(1)}, f32[4,1280]{1,0:T(4,128)S(1)}, u32[]{:S(2)}, u32[]{:S(2)}) %collective-permute-start.47) | collective-permute-done | bytes 20512 | tf_op jit(solution)/shard_map/ppermute | solution.py:283
  (99 shorter events, 5.5 us)
Async XLA Ops:
  0.6 143.2 %copy-start = (f32[1,4,1280]{2,1,0:T(4,128)S(1)}, f32[1,4,1280]{2,1,0:T(4,128)}, u32[]{:S(2)}) copy-start(f32[1,4,1280]{2,1,0:T(4,128)} %param.13) | copy-start | bytes 61444
  0.6 23.9 %collective-permute-start.2 = (bf16[320,1280]{1,0:T(8,128)(2,1)}, bf16[320,1280]{1,0:T(8,128)(2,1)}, u32[]{:S(2)}, u32[]{:S(2)}) collective-permute-start(bf16[320,1280]{1,0:T(8,128)(2,1)} %bitcast.44), channel_id=1, source_target_pairs={{0,2},{1,3},{2,4},{3,5},{4,6},{5,7},{8,10},{9,11},{10,12},{11,13},... | collective-permute-start | bytes 2457608 | tf_op jit(solution)/shard_map/ppermute | solution.py:74
  6.6 23.3 %collective-permute-start = (bf16[320,1280]{1,0:T(8,128)(2,1)}, bf16[320,1280]{1,0:T(8,128)(2,1)}, u32[]{:S(2)}, u32[]{:S(2)}) collective-permute-start(bf16[320,1280]{1,0:T(8,128)(2,1)} %bitcast.45), channel_id=1, source_target_pairs={{2,0},{3,1},{4,2},{5,3},{6,4},{7,5},{10,8},{11,9},{12,10},{13,11},... | collective-permute-start | bytes 2457608 | tf_op jit(solution)/shard_map/ppermute | solution.py:74
  7.8 33.1 %collective-permute-start.8 = (bf16[320,1280]{1,0:T(8,128)(2,1)}, bf16[320,1280]{1,0:T(8,128)(2,1)}, u32[]{:S(2)}, u32[]{:S(2)}) collective-permute-start(bf16[320,1280]{1,0:T(8,128)(2,1)} %bitcast.48), channel_id=1, source_target_pairs={{0,2},{1,3},{2,4},{3,5},{4,6},{5,7},{8,10},{9,11},{10,12},{11,13},... | collective-permute-start | bytes 2457608 | tf_op jit(solution)/shard_map/ppermute | solution.py:74
  13.3 32.7 %collective-permute-start.6 = (bf16[320,1280]{1,0:T(8,128)(2,1)}, bf16[320,1280]{1,0:T(8,128)(2,1)}, u32[]{:S(2)}, u32[]{:S(2)}) collective-permute-start(bf16[320,1280]{1,0:T(8,128)(2,1)} %bitcast.49), channel_id=1, source_target_pairs={{2,0},{3,1},{4,2},{5,3},{6,4},{7,5},{10,8},{11,9},{12,10},{13,11},... | collective-permute-start | bytes 2457608 | tf_op jit(solution)/shard_map/ppermute | solution.py:74
  14.6 32.2 %collective-permute-start.18 = (bf16[320,1280]{1,0:T(8,128)(2,1)}, bf16[320,1280]{1,0:T(8,128)(2,1)S(1)}, u32[]{:S(2)}, u32[]{:S(2)}) collective-permute-start(bf16[320,1280]{1,0:T(8,128)(2,1)} %bitcast.46), channel_id=1, source_target_pairs={{26,2},{27,3},{28,4},{29,5}} | collective-permute-start | bytes 2457608 | tf_op jit(solution)/shard_map/ppermute | solution.py:74
  24.5 23.5 %collective-permute-start.25 = (bf16[320,1280]{1,0:T(8,128)(2,1)}, bf16[320,1280]{1,0:T(8,128)(2,1)S(1)}, u32[]{:S(2)}, u32[]{:S(2)}) collective-permute-start(bf16[320,1280]{1,0:T(8,128)(2,1)} %collective-permute-done.2.refs_7_), channel_id=1, source_target_pairs={{0,1},{1,0},{2,3},{3,2},{4,5},{5,4},{6,7},{7,6},{8,9},{9,8},{10,11... | collective-permute-start | bytes 2457608 | tf_op jit(solution)/shard_map/ppermute | solution.py:82
  29.9 22.6 %collective-permute-start.26 = (bf16[320,1280]{1,0:T(8,128)(2,1)}, bf16[320,1280]{1,0:T(8,128)(2,1)S(1)}, u32[]{:S(2)}, u32[]{:S(2)}) collective-permute-start(bf16[320,1280]{1,0:T(8,128)(2,1)} %collective-permute-done.refs_9_), channel_id=1, source_target_pairs={{0,1},{1,0},{2,3},{3,2},{4,5},{5,4},{6,7},{7,6},{8,9},{9,8},{10,11... | collective-permute-start | bytes 2457608 | tf_op jit(solution)/shard_map/ppermute | solution.py:82
  41.0 12.5 %collective-permute-start.23 = (bf16[320,1280]{1,0:T(8,128)(2,1)}, bf16[320,1280]{1,0:T(8,128)(2,1)S(1)}, u32[]{:S(2)}, u32[]{:S(2)}) collective-permute-start(bf16[320,1280]{1,0:T(8,128)(2,1)} %collective-permute-done.8.refs_3_), channel_id=1, source_target_pairs={{0,1},{1,0},{2,3},{3,2},{4,5},{5,4},{6,7},{7,6},{8,9},{9,8},{10,11... | collective-permute-start | bytes 2457608 | tf_op jit(solution)/shard_map/ppermute | solution.py:82
  46.0 9.6 %collective-permute-start.3 = (bf16[320,1280]{1,0:T(8,128)(2,1)}, bf16[320,1280]{1,0:T(8,128)(2,1)S(1)}, u32[]{:S(2)}, u32[]{:S(2)}) collective-permute-start(bf16[320,1280]{1,0:T(8,128)(2,1)} %collective-permute-done.2.refs_7_), channel_id=1, source_target_pairs={{2,4},{3,5},{4,6},{5,7},{10,12},{11,13},{12,14},{13,15},{18,20},{1... | collective-permute-start | bytes 2457608 | tf_op jit(solution)/shard_map/ppermute | solution.py:74
  46.7 1.3 copy-start.12
  46.7 24.7 %collective-permute-start.1 = (bf16[320,1280]{1,0:T(8,128)(2,1)}, bf16[320,1280]{1,0:T(8,128)(2,1)S(1)}, u32[]{:S(2)}, u32[]{:S(2)}) collective-permute-start(bf16[320,1280]{1,0:T(8,128)(2,1)} %collective-permute-done.refs_9_), channel_id=1, source_target_pairs={{2,0},{3,1},{4,2},{5,3},{10,8},{11,9},{12,10},{13,11},{18,16},{19,... | collective-permute-start | bytes 2457608 | tf_op jit(solution)/shard_map/ppermute | solution.py:74
  48.1 1.0 copy-start.6
  49.1 23.7 %collective-permute-start.9 = (bf16[320,1280]{1,0:T(8,128)(2,1)}, bf16[320,1280]{1,0:T(8,128)(2,1)S(1)}, u32[]{:S(2)}, u32[]{:S(2)}) collective-permute-start(bf16[320,1280]{1,0:T(8,128)(2,1)} %collective-permute-done.8.refs_3_), channel_id=1, source_target_pairs={{2,4},{3,5},{4,6},{5,7},{10,12},{11,13},{12,14},{13,15},{18,20},{1... | collective-permute-start | bytes 2457608 | tf_op jit(solution)/shard_map/ppermute | solution.py:74
  52.5 1.0 copy-start.8
  53.5 52.1 %collective-permute-start.22 = (bf16[2,320,1280]{2,1,0:T(8,128)(2,1)}, bf16[2,320,1280]{2,1,0:T(8,128)(2,1)}, u32[]{:S(2)}, u32[]{:S(2)}) collective-permute-start(bf16[2,320,1280]{2,1,0:T(8,128)(2,1)} %pad_maximum_fusion), channel_id=1, source_target_pairs={{0,1},{1,0},{2,3},{3,2},{4,5},{5,4},{6,7},{7,6},{8,9},{9,8},{10,11... | collective-permute-start | bytes 4915208 | tf_op jit(solution)/shard_map/ppermute | solution.py:82
  53.5 0.9 copy-start.10
  54.4 34.6 %collective-permute-start.7 = (bf16[320,1280]{1,0:T(8,128)(2,1)}, bf16[320,1280]{1,0:T(8,128)(2,1)S(1)}, u32[]{:S(2)}, u32[]{:S(2)}) collective-permute-start(bf16[320,1280]{1,0:T(8,128)(2,1)} %collective-permute-done.6.refs_5_), channel_id=1, source_target_pairs={{2,0},{3,1},{4,2},{5,3},{10,8},{11,9},{12,10},{13,11},{18,16},{19,... | collective-permute-start | bytes 2457608 | tf_op jit(solution)/shard_map/ppermute | solution.py:74
  55.7 33.5 %collective-permute-start.24 = (bf16[320,1280]{1,0:T(8,128)(2,1)}, bf16[320,1280]{1,0:T(8,128)(2,1)S(1)}, u32[]{:S(2)}, u32[]{:S(2)}) collective-permute-start(bf16[320,1280]{1,0:T(8,128)(2,1)} %collective-permute-done.6.refs_5_), channel_id=1, source_target_pairs={{0,1},{1,0},{2,3},{3,2},{4,5},{5,4},{6,7},{7,6},{8,9},{9,8},{10,11... | collective-permute-start | bytes 2457608 | tf_op jit(solution)/shard_map/ppermute | solution.py:82
  71.4 32.8 %collective-permute-start.19 = (bf16[320,1280]{1,0:T(8,128)(2,1)}, bf16[320,1280]{1,0:T(8,128)(2,1)S(1)}, u32[]{:S(2)}, u32[]{:S(2)}) collective-permute-start(bf16[320,1280]{1,0:T(8,128)(2,1)} %copy-done.12), channel_id=1, source_target_pairs={{2,0},{3,1},{4,6},{5,7}} | collective-permute-start | bytes 2457608 | tf_op jit(solution)/shard_map/ppermute | solution.py:74
  72.7 33.6 %collective-permute-start.16 = (bf16[320,1280]{1,0:T(8,128)(2,1)S(1)}, bf16[320,1280]{1,0:T(8,128)(2,1)S(1)}, u32[]{:S(2)}, u32[]{:S(2)}) collective-permute-start(bf16[320,1280]{1,0:T(8,128)(2,1)S(1)} %collective-permute-done.3.refs_4_), channel_id=1, source_target_pairs={{0,1},{1,0},{2,3},{3,2},{4,5},{5,4},{6,7},{7,6},{8,9},{9,8},{10,11... | collective-permute-start | bytes 2457608 | tf_op jit(solution)/shard_map/ppermute | solution.py:82
  89.0 18.7 %collective-permute-start.17 = (bf16[320,1280]{1,0:T(8,128)(2,1)S(1)}, bf16[320,1280]{1,0:T(8,128)(2,1)S(1)}, u32[]{:S(2)}, u32[]{:S(2)}) collective-permute-start(bf16[320,1280]{1,0:T(8,128)(2,1)S(1)} %collective-permute-done.1.refs_6_), channel_id=1, source_target_pairs={{0,1},{1,0},{2,3},{3,2},{4,5},{5,4},{6,7},{7,6},{8,9},{9,8},{10,11... | collective-permute-start | bytes 2457608 | tf_op jit(solution)/shard_map/ppermute | solution.py:82
  89.1 62.7 %copy-start.4 = (bf16[1,320,1280]{2,1,0:T(8,128)(2,1)S(1)}, bf16[1,320,1280]{2,1,0:T(8,128)(2,1)}, u32[]{:S(2)}) copy-start(bf16[1,320,1280]{2,1,0:T(8,128)(2,1)} %param.9) | copy-start | bytes 2457604
  89.1 62.7 %copy-start.5 = (bf16[1,320,1280]{2,1,0:T(8,128)(2,1)S(1)}, bf16[1,320,1280]{2,1,0:T(8,128)(2,1)}, u32[]{:S(2)}) copy-start(bf16[1,320,1280]{2,1,0:T(8,128)(2,1)} %param.10) | copy-start | bytes 2457604
  89.1 62.7 %copy-start.7 = (bf16[320,1280]{1,0:T(8,128)(2,1)S(1)}, bf16[320,1280]{1,0:T(8,128)(2,1)}, u32[]{:S(2)}) copy-start(bf16[320,1280]{1,0:T(8,128)(2,1)} %copy-done.6) | copy-start | bytes 2457604
  89.1 62.7 %copy-start.9 = (bf16[320,1280]{1,0:T(8,128)(2,1)S(1)}, bf16[320,1280]{1,0:T(8,128)(2,1)}, u32[]{:S(2)}) copy-start(bf16[320,1280]{1,0:T(8,128)(2,1)} %copy-done.8) | copy-start | bytes 2457604
  89.1 62.7 %copy-start.11 = (bf16[320,1280]{1,0:T(8,128)(2,1)S(1)}, bf16[320,1280]{1,0:T(8,128)(2,1)}, u32[]{:S(2)}) copy-start(bf16[320,1280]{1,0:T(8,128)(2,1)} %copy-done.10) | copy-start | bytes 2457604
  89.1 19.8 %collective-permute-start.14 = (bf16[320,1280]{1,0:T(8,128)(2,1)S(1)}, bf16[320,1280]{1,0:T(8,128)(2,1)S(1)}, u32[]{:S(2)}, u32[]{:S(2)}) collective-permute-start(bf16[320,1280]{1,0:T(8,128)(2,1)S(1)} %collective-permute-done.9.refs_0_), channel_id=1, source_target_pairs={{0,1},{1,0},{2,3},{3,2},{4,5},{5,4},{6,7},{7,6},{8,9},{9,8},{10,11... | collective-permute-start | bytes 2457608 | tf_op jit(solution)/shard_map/ppermute | solution.py:82
  104.3 17.1 %collective-permute-start.20 = (bf16[320,1280]{1,0:T(8,128)(2,1)S(1)}, bf16[320,1280]{1,0:T(8,128)(2,1)S(1)}, u32[]{:S(2)}, u32[]{:S(2)}) collective-permute-start(bf16[320,1280]{1,0:T(8,128)(2,1)S(1)} %collective-permute-done.19), channel_id=1, source_target_pairs={{0,24},{1,25},{6,30},{7,31}} | collective-permute-start | bytes 2457608 | tf_op jit(solution)/shard_map/ppermute | solution.py:74
  105.6 15.7 %collective-permute-start.12 = (bf16[320,1280]{1,0:T(8,128)(2,1)S(1)}, bf16[320,1280]{1,0:T(8,128)(2,1)S(1)}, u32[]{:S(2)}, u32[]{:S(2)}) collective-permute-start(bf16[320,1280]{1,0:T(8,128)(2,1)S(1)} %broadcast_select_fusion.1), channel_id=1, source_target_pairs={{26,24},{27,25},{28,30},{29,31}} | collective-permute-start | bytes 2457608 | tf_op jit(solution)/shard_map/ppermute | solution.py:74
  106.3 23.0 %collective-permute-start.10 = (bf16[320,1280]{1,0:T(8,128)(2,1)S(1)}, bf16[320,1280]{1,0:T(8,128)(2,1)S(1)}, u32[]{:S(2)}, u32[]{:S(2)}) collective-permute-start(bf16[320,1280]{1,0:T(8,128)(2,1)S(1)} %broadcast_select_fusion), channel_id=1, source_target_pairs={{2,0},{3,1},{4,6},{5,7},{10,8},{11,9},{12,14},{13,15},{18,16},{19,... | collective-permute-start | bytes 2457608 | tf_op jit(solution)/shard_map/ppermute | solution.py:74
  107.7 36.1 %collective-permute-start.4 = (bf16[320,1280]{1,0:T(8,128)(2,1)S(1)}, bf16[320,1280]{1,0:T(8,128)(2,1)S(1)}, u32[]{:S(2)}, u32[]{:S(2)}) collective-permute-start(bf16[320,1280]{1,0:T(8,128)(2,1)S(1)} %broadcast_select_fusion.1), channel_id=1, source_target_pairs={{2,0},{3,1},{4,6},{5,7},{10,8},{11,9},{12,14},{13,15},{18,16},{19,... | collective-permute-start | bytes 2457608 | tf_op jit(solution)/shard_map/ppermute | solution.py:74
  109.0 45.1 %collective-permute-start.15 = (bf16[320,1280]{1,0:T(8,128)(2,1)S(1)}, bf16[320,1280]{1,0:T(8,128)(2,1)S(1)}, u32[]{:S(2)}, u32[]{:S(2)}) collective-permute-start(bf16[320,1280]{1,0:T(8,128)(2,1)S(1)} %collective-permute-done.7.refs_2_), channel_id=1, source_target_pairs={{0,1},{1,0},{2,3},{3,2},{4,5},{5,4},{6,7},{7,6},{8,9},{9,8},{10,11... | collective-permute-start | bytes 2457608 | tf_op jit(solution)/shard_map/ppermute | solution.py:82
  121.3 32.8 %collective-permute-start.21 = (bf16[320,1280]{1,0:T(8,128)(2,1)S(1)}, bf16[320,1280]{1,0:T(8,128)(2,1)S(1)}, u32[]{:S(2)}, u32[]{:S(2)}) collective-permute-start(bf16[320,1280]{1,0:T(8,128)(2,1)S(1)} %collective-permute-done.20.refs_8_), channel_id=1, source_target_pairs={{0,1},{1,0},{2,3},{3,2},{4,5},{5,4},{6,7},{7,6},{8,9},{9,8},{10,11... | collective-permute-start | bytes 2457608 | tf_op jit(solution)/shard_map/ppermute | solution.py:82
  121.3 33.4 %collective-permute-start.13 = (bf16[320,1280]{1,0:T(8,128)(2,1)S(1)}, bf16[320,1280]{1,0:T(8,128)(2,1)S(1)}, u32[]{:S(2)}, u32[]{:S(2)}) collective-permute-start(bf16[320,1280]{1,0:T(8,128)(2,1)S(1)} %collective-permute-done.12.refs_2_), channel_id=1, source_target_pairs={{0,1},{1,0},{2,3},{3,2},{4,5},{5,4},{6,7},{7,6},{8,9},{9,8},{10,11... | collective-permute-start | bytes 2457608 | tf_op jit(solution)/shard_map/ppermute | solution.py:82
  129.4 25.3 %collective-permute-start.11 = (bf16[320,1280]{1,0:T(8,128)(2,1)S(1)}, bf16[320,1280]{1,0:T(8,128)(2,1)S(1)}, u32[]{:S(2)}, u32[]{:S(2)}) collective-permute-start(bf16[320,1280]{1,0:T(8,128)(2,1)S(1)} %collective-permute-done.10.refs_0_), channel_id=1, source_target_pairs={{0,1},{1,0},{2,3},{3,2},{4,5},{5,4},{6,7},{7,6},{8,9},{9,8},{10,11... | collective-permute-start | bytes 2457608 | tf_op jit(solution)/shard_map/ppermute | solution.py:82
  143.8 15.2 %collective-permute-start.5 = (bf16[320,1280]{1,0:T(8,128)(2,1)S(1)}, bf16[320,1280]{1,0:T(8,128)(2,1)S(1)}, u32[]{:S(2)}, u32[]{:S(2)}) collective-permute-start(bf16[320,1280]{1,0:T(8,128)(2,1)S(1)} %collective-permute-done.4.refs_0_), channel_id=1, source_target_pairs={{0,1},{1,0},{2,3},{3,2},{4,5},{5,4},{6,7},{7,6},{8,9},{9,8},{10,11... | collective-permute-start | bytes 2457608 | tf_op jit(solution)/shard_map/ppermute | solution.py:82
  154.7 1.1 copy-start.1
  154.7 1.5 copy-start.2
  156.2 3.8 %collective-permute-start.31 = (bf16[48,2560]{1,0:T(8,128)(2,1)S(1)}, bf16[48,2560]{1,0:T(8,128)(2,1)S(1)}, u32[]{:S(2)}, u32[]{:S(2)}) collective-permute-start(bf16[48,2560]{1,0:T(8,128)(2,1)S(1)} %get-tuple-element.74), channel_id=1, source_target_pairs={{24,16},{25,17},{26,18},{27,19},{28,20},{29,21},{30,22},{31,23}} | collective-permute-start | bytes 737288 | tf_op jit(solution)/shard_map/ppermute | solution.py:314
  156.9 3.8 %collective-permute-start.30 = (bf16[48,2560]{1,0:T(8,128)(2,1)S(1)}, bf16[48,2560]{1,0:T(8,128)(2,1)S(1)}, u32[]{:S(2)}, u32[]{:S(2)}) collective-permute-start(bf16[48,2560]{1,0:T(8,128)(2,1)S(1)} %get-tuple-element.73), channel_id=1, source_target_pairs={{24,16},{25,17},{26,18},{27,19},{28,20},{29,21},{30,22},{31,23}} | collective-permute-start | bytes 737288 | tf_op jit(solution)/shard_map/ppermute | solution.py:314
  157.6 3.8 %collective-permute-start.29 = (bf16[48,2560]{1,0:T(8,128)(2,1)S(1)}, bf16[48,2560]{1,0:T(8,128)(2,1)S(1)}, u32[]{:S(2)}, u32[]{:S(2)}) collective-permute-start(bf16[48,2560]{1,0:T(8,128)(2,1)S(1)} %get-tuple-element.72), channel_id=1, source_target_pairs={{24,16},{25,17},{26,18},{27,19},{28,20},{29,21},{30,22},{31,23}} | collective-permute-start | bytes 737288 | tf_op jit(solution)/shard_map/ppermute | solution.py:314
  158.3 3.9 %collective-permute-start.27 = (bf16[64,2560]{1,0:T(8,128)(2,1)S(1)}, bf16[64,2560]{1,0:T(8,128)(2,1)S(1)}, u32[]{:S(2)}, u32[]{:S(2)}) collective-permute-start(bf16[64,2560]{1,0:T(8,128)(2,1)S(1)} %get-tuple-element.70), channel_id=1, source_target_pairs={{24,16},{25,17},{26,18},{27,19},{28,20},{29,21},{30,22},{31,23}} | collective-permute-start | bytes 983048 | tf_op jit(solution)/shard_map/ppermute | solution.py:314
  159.0 3.1 %collective-permute-start.28 = (bf16[48,2560]{1,0:T(8,128)(2,1)S(1)}, bf16[48,2560]{1,0:T(8,128)(2,1)S(1)}, u32[]{:S(2)}, u32[]{:S(2)}) collective-permute-start(bf16[48,2560]{1,0:T(8,128)(2,1)S(1)} %get-tuple-element.71), channel_id=1, source_target_pairs={{24,16},{25,17},{26,18},{27,19},{28,20},{29,21},{30,22},{31,23}} | collective-permute-start | bytes 737288 | tf_op jit(solution)/shard_map/ppermute | solution.py:314
  160.0 3.6 %collective-permute-start.36 = (bf16[48,2560]{1,0:T(8,128)(2,1)S(1)}, bf16[48,2560]{1,0:T(8,128)(2,1)S(1)}, u32[]{:S(2)}, u32[]{:S(2)}) collective-permute-start(bf16[48,2560]{1,0:T(8,128)(2,1)S(1)} %get-tuple-element.88), channel_id=1, source_target_pairs={{16,8},{17,9},{18,10},{19,11},{20,12},{21,13},{22,14},{23,15}} | collective-permute-start | bytes 737288 | tf_op jit(solution)/shard_map/ppermute | solution.py:314
  160.7 4.2 %collective-permute-start.35 = (bf16[48,2560]{1,0:T(8,128)(2,1)S(1)}, bf16[48,2560]{1,0:T(8,128)(2,1)S(1)}, u32[]{:S(2)}, u32[]{:S(2)}) collective-permute-start(bf16[48,2560]{1,0:T(8,128)(2,1)S(1)} %get-tuple-element.87), channel_id=1, source_target_pairs={{16,8},{17,9},{18,10},{19,11},{20,12},{21,13},{22,14},{23,15}} | collective-permute-start | bytes 737288 | tf_op jit(solution)/shard_map/ppermute | solution.py:314
  161.5 5.0 %collective-permute-start.34 = (bf16[48,2560]{1,0:T(8,128)(2,1)S(1)}, bf16[48,2560]{1,0:T(8,128)(2,1)S(1)}, u32[]{:S(2)}, u32[]{:S(2)}) collective-permute-start(bf16[48,2560]{1,0:T(8,128)(2,1)S(1)} %get-tuple-element.86), channel_id=1, source_target_pairs={{16,8},{17,9},{18,10},{19,11},{20,12},{21,13},{22,14},{23,15}} | collective-permute-start | bytes 737288 | tf_op jit(solution)/shard_map/ppermute | solution.py:314
  162.2 5.6 %collective-permute-start.32 = (bf16[64,2560]{1,0:T(8,128)(2,1)S(1)}, bf16[64,2560]{1,0:T(8,128)(2,1)S(1)}, u32[]{:S(2)}, u32[]{:S(2)}) collective-permute-start(bf16[64,2560]{1,0:T(8,128)(2,1)S(1)} %get-tuple-element.84), channel_id=1, source_target_pairs={{16,8},{17,9},{18,10},{19,11},{20,12},{21,13},{22,14},{23,15}} | collective-permute-start | bytes 983048 | tf_op jit(solution)/shard_map/ppermute | solution.py:314
  162.9 4.9 %collective-permute-start.33 = (bf16[48,2560]{1,0:T(8,128)(2,1)S(1)}, bf16[48,2560]{1,0:T(8,128)(2,1)S(1)}, u32[]{:S(2)}, u32[]{:S(2)}) collective-permute-start(bf16[48,2560]{1,0:T(8,128)(2,1)S(1)} %get-tuple-element.85), channel_id=1, source_target_pairs={{16,8},{17,9},{18,10},{19,11},{20,12},{21,13},{22,14},{23,15}} | collective-permute-start | bytes 737288 | tf_op jit(solution)/shard_map/ppermute | solution.py:314
  163.6 14.1 %collective-permute-start.41 = (bf16[48,2560]{1,0:T(8,128)(2,1)S(1)}, bf16[48,2560]{1,0:T(8,128)(2,1)S(1)}, u32[]{:S(2)}, u32[]{:S(2)}) collective-permute-start(bf16[48,2560]{1,0:T(8,128)(2,1)S(1)} %get-tuple-element.103), channel_id=1, source_target_pairs={{8,0},{9,1},{10,2},{11,3},{12,4},{13,5},{14,6},{15,7}} | collective-permute-start | bytes 737288 | tf_op jit(solution)/shard_map/ppermute | solution.py:314
  165.2 18.3 %collective-permute-start.40 = (bf16[48,2560]{1,0:T(8,128)(2,1)S(1)}, bf16[48,2560]{1,0:T(8,128)(2,1)S(1)}, u32[]{:S(2)}, u32[]{:S(2)}) collective-permute-start(bf16[48,2560]{1,0:T(8,128)(2,1)S(1)} %get-tuple-element.102), channel_id=1, source_target_pairs={{8,0},{9,1},{10,2},{11,3},{12,4},{13,5},{14,6},{15,7}} | collective-permute-start | bytes 737288 | tf_op jit(solution)/shard_map/ppermute | solution.py:314
  166.5 22.6 %collective-permute-start.39 = (bf16[48,2560]{1,0:T(8,128)(2,1)S(1)}, bf16[48,2560]{1,0:T(8,128)(2,1)S(1)}, u32[]{:S(2)}, u32[]{:S(2)}) collective-permute-start(bf16[48,2560]{1,0:T(8,128)(2,1)S(1)} %get-tuple-element.101), channel_id=1, source_target_pairs={{8,0},{9,1},{10,2},{11,3},{12,4},{13,5},{14,6},{15,7}} | collective-permute-start | bytes 737288 | tf_op jit(solution)/shard_map/ppermute | solution.py:314
  167.9 65.8 %collective-permute-start.37 = (bf16[64,2560]{1,0:T(8,128)(2,1)S(1)}, bf16[64,2560]{1,0:T(8,128)(2,1)S(1)}, u32[]{:S(2)}, u32[]{:S(2)}) collective-permute-start(bf16[64,2560]{1,0:T(8,128)(2,1)S(1)} %get-tuple-element.99), channel_id=1, source_target_pairs={{8,0},{9,1},{10,2},{11,3},{12,4},{13,5},{14,6},{15,7}} | collective-permute-start | bytes 983048 | tf_op jit(solution)/shard_map/ppermute | solution.py:314
  169.2 59.6 %collective-permute-start.38 = (bf16[48,2560]{1,0:T(8,128)(2,1)S(1)}, bf16[48,2560]{1,0:T(8,128)(2,1)S(1)}, u32[]{:S(2)}, u32[]{:S(2)}) collective-permute-start(bf16[48,2560]{1,0:T(8,128)(2,1)S(1)} %get-tuple-element.100), channel_id=1, source_target_pairs={{8,0},{9,1},{10,2},{11,3},{12,4},{13,5},{14,6},{15,7}} | collective-permute-start | bytes 737288 | tf_op jit(solution)/shard_map/ppermute | solution.py:314
  233.7 16.8 %slice-start = ((s8[6553600]{0:T(1024)(128)(4,1)}), s8[4194304]{0:T(1024)(128)(4,1)S(1)}, s32[]{:S(2)}) async-start(s8[6553600]{0:T(1024)(128)(4,1)} %bitcast.40), calls=%async_computation | async-start | bytes 8388608
  233.7 5.8 %copy-start.3 = (bf16[1,256,2560]{2,1,0:T(8,128)(2,1)S(1)}, bf16[1,256,2560]{2,1,0:T(8,128)(2,1)}, u32[]{:S(2)}) copy-start(bf16[1,256,2560]{2,1,0:T(8,128)(2,1)} %param.7) | copy-start | bytes 3932164
  233.7 16.8 %slice-start.1 = ((s8[6553600]{0:T(1024)(128)(4,1)}), s8[2359296]{0:T(1024)(128)(4,1)S(1)}, s32[]{:S(2)}) async-start(s8[6553600]{0:T(1024)(128)(4,1)} %bitcast.40), calls=%async_computation.1 | async-start | bytes 4718592
  240.1 1.2 collective-permute-start.42
  241.4 4.1 %collective-permute-start.43 = (f32[4,2560]{1,0:T(4,128)S(1)}, f32[4,2560]{1,0:T(4,128)S(1)}, u32[]{:S(2)}, u32[]{:S(2)}) collective-permute-start(f32[4,2560]{1,0:T(4,128)S(1)} %add.19), channel_id=1, source_target_pairs={{0,2},{1,3},{2,0},{3,1},{4,6},{5,7},{6,4},{7,5},{8,10},{9,11},{10,... | collective-permute-start | bytes 122888 | tf_op jit(solution)/shard_map/ppermute | solution.py:283
  245.5 5.0 %collective-permute-start.44 = (f32[4,2560]{1,0:T(4,128)S(1)}, f32[4,2560]{1,0:T(4,128)S(1)}, u32[]{:S(2)}, u32[]{:S(2)}) collective-permute-start(f32[4,2560]{1,0:T(4,128)S(1)} %add.20.left), channel_id=1, source_target_pairs={{0,4},{1,5},{2,6},{3,7},{4,0},{5,1},{6,2},{7,3},{8,12},{9,13},{10,... | collective-permute-start | bytes 122888 | tf_op jit(solution)/shard_map/ppermute | solution.py:283
  253.3 1.3 collective-permute-start.45
  254.6 3.8 %collective-permute-start.46 = (f32[4,1280]{1,0:T(4,128)S(1)}, f32[4,1280]{1,0:T(4,128)S(1)}, u32[]{:S(2)}, u32[]{:S(2)}) collective-permute-start(f32[4,1280]{1,0:T(4,128)S(1)} %add.21), channel_id=1, source_target_pairs={{0,2},{1,3},{2,0},{3,1},{4,6},{5,7},{6,4},{7,5},{8,10},{9,11},{10,... | collective-permute-start | bytes 61448 | tf_op jit(solution)/shard_map/ppermute | solution.py:283
  258.4 4.7 %collective-permute-start.47 = (f32[4,1280]{1,0:T(4,128)S(1)}, f32[4,1280]{1,0:T(4,128)S(1)}, u32[]{:S(2)}, u32[]{:S(2)}) collective-permute-start(f32[4,1280]{1,0:T(4,128)S(1)} %add.22), channel_id=1, source_target_pairs={{0,4},{1,5},{2,6},{3,7},{4,0},{5,1},{6,2},{7,3},{8,12},{9,13},{10,... | collective-permute-start | bytes 61448 | tf_op jit(solution)/shard_map/ppermute | solution.py:283

commit v3 on v2

--- a/solution.py
+++ b/solution.py
@@ -172,8 +172,13 @@
     at = pl.ds(first, block)
     read = at if arriving.shape[0] == row_count else pl.ds(0, block)
 
-    def body(w, arr, gate, *refs):
-        vg_ref, passed_ref, send = refs[-3:]
+    results = [(row_count, channels), (row_count, width)]
+    if section:
+        results.append((block, width))
+
+    def body(w, arr, gate, early, *refs):
+        del early
+        vg_ref, passed_ref, *send = refs[len(held) :]
 
         @pl.when(lax.axis_index("section") == section)
         def _():
@@ -196,7 +201,8 @@
                 )
                 passed = (arr[read, cols].astype(jnp.float32) + back).astype(jnp.bfloat16)
                 passed_ref[at, cols] = passed
-                send[:, cols] = passed
+                for ref in send:
+                    ref[:, cols] = passed
                 return carry
 
             lax.fori_loop(0, width // deep, backward, 0)
@@ -204,12 +210,8 @@
     return pl.pallas_call(
         body,
         in_specs=[VMEM] * 3 + [ANY] + [VMEM] * len(held),
-        out_specs=[VMEM] * 3,
-        out_shape=[
-            jax.ShapeDtypeStruct((row_count, channels), jnp.bfloat16),
-            jax.ShapeDtypeStruct((row_count, width), jnp.bfloat16),
-            jax.ShapeDtypeStruct((block, width), jnp.bfloat16),
-        ],
+        out_specs=[VMEM] * len(results),
+        out_shape=[jax.ShapeDtypeStruct(shape, jnp.bfloat16) for shape in results],
         input_output_aliases={4 + k: k for k in range(len(held))},
         compiler_params=pltpu.CompilerParams(vmem_limit_bytes=8 << 20),
         cost_estimate=pl.CostEstimate(
@@ -306,11 +308,12 @@
     held = []
     for section in reversed(range(sections)):
         for k, (first, block) in enumerate(zip(firsts, blocks)):
-            *held, send = stage(
+            held = stage(
                 whole, arriving[k], gate_rows, held, error_part,
                 section=section, first=first, block=block,
             )
             if section:
+                *held, send = held
                 arriving[k] = lax.ppermute(send, "section", [(section, section - 1)])
         if section == sections - 1:
             whole = finish(whole, held[:1])

time: 265 us -> 263 us (level)
  Pallas kernels: 31.4 us -> 27.9 us
    pallas_call x20, Pallas kernels: 25.3 us -> 21.8 us  [stage(): pl.pallas_call(body, in_specs=[VMEM] * 3 + [ANY] + [VMEM] * len(held), ou...]
  transfers between devices with their start and end apart: 48 -> 48, of which waited for: 20 -> 20; matrix products, arithmetic and copies ran while one was open for 4% -> 4% of each run, Pallas kernels for 9% -> 8%
where the time goes in v3:
time: 263 us; the launch traced here: 262 us
  waiting for transfers between devices  176 us (67%)
  starting transfers between devices  40.2 us (15%)
  Pallas kernels  27.9 us (11%)
  matrix products  9.31 us (4%)
  local copies, waits for them, and re-layouts  4.1 us (2%)
  other arithmetic  3.54 us (1%)
    ppermute x14, waiting for transfers between devices, permute(): return lax.ppermute(value, ('section', 'dp'), pairs)  111 us
    ppermute x15, waiting for transfers between devices, local(): arriving[k] = lax.ppermute(send, 'section', [(section, section - 1)])  45.6 us
    ppermute x14, starting transfers between devices, permute(): return lax.ppermute(value, ('section', 'dp'), pairs)  24.5 us
    pallas_call x20, Pallas kernels, stage(): pl.pallas_call(body, in_specs=[VMEM] * 3 + [ANY] + [VMEM] * len(held), ou...  21.8 us
    ppermute x6, waiting for transfers between devices, exchange(): return lax.ppermute(value, 'dp', [(i, i ^ by) for i in range(replicas)])  19.5 us
    ppermute x15, starting transfers between devices, local(): arriving[k] = lax.ppermute(send, 'section', [(section, section - 1)])  13.2 us
    dot_general x1, matrix products, local(): lax.dot_general(warm, error.astype(jnp.float32), (((1,), (1,)), ((), ()))...  8.01 us
  transfers between devices with their start and end apart: 48, of which 20 were waited for; matrix products, arithmetic and copies ran while one was open for 4% of the time, Pallas kernels for 8%

profile of v3, /device:TPU:0, one launch (start us, length us, event | category | flops | bytes accessed | tf_op | source)
XLA Modules:
  0.0 262.4 jit_solution(15774991723502494555)
XLA Ops:
  0.6 5.9 %collective-permute-start.2 = (bf16[320,1280]{1,0:T(8,128)(2,1)}, bf16[320,1280]{1,0:T(8,128)(2,1)}, u32[]{:S(2)}, u32[]{:S(2)}) collective-permute-start(bf16[320,1280]{1,0:T(8,128)(2,1)} %bitcast.44), channel_id=1, source_target_pairs={{0,2},{1,3},{2,4},{3,5},{4,6},{5,7},{8,10},{9,11},{10,12},{11,13},... | collective-permute-start | bytes 2457608 | tf_op jit(solution)/shard_map/ppermute | solution.py:74
  6.6 1.3 collective-permute-start
  7.8 5.4 %collective-permute-start.8 = (bf16[320,1280]{1,0:T(8,128)(2,1)}, bf16[320,1280]{1,0:T(8,128)(2,1)}, u32[]{:S(2)}, u32[]{:S(2)}) collective-permute-start(bf16[320,1280]{1,0:T(8,128)(2,1)} %bitcast.48), channel_id=1, source_target_pairs={{0,2},{1,3},{2,4},{3,5},{4,6},{5,7},{8,10},{9,11},{10,12},{11,13},... | collective-permute-start | bytes 2457608 | tf_op jit(solution)/shard_map/ppermute | solution.py:74
  13.3 1.3 collective-permute-start.6
  14.6 0.7 collective-permute-start.18
  15.3 9.3 %collective-permute-done.2.refs_7_ = bf16[320,1280]{1,0:T(8,128)(2,1)} collective-permute-done((bf16[320,1280]{1,0:T(8,128)(2,1)}, bf16[320,1280]{1,0:T(8,128)(2,1)}, u32[]{:S(2)}, u32[]{:S(2)}) %collective-permute-start.2) | collective-permute-done | bytes 819232 | tf_op jit(solution)/shard_map/ppermute | solution.py:74
  24.5 5.3 %collective-permute-done.refs_9_ = bf16[320,1280]{1,0:T(8,128)(2,1)} collective-permute-done((bf16[320,1280]{1,0:T(8,128)(2,1)}, bf16[320,1280]{1,0:T(8,128)(2,1)}, u32[]{:S(2)}, u32[]{:S(2)}) %collective-permute-start) | collective-permute-done | bytes 819232 | tf_op jit(solution)/shard_map/ppermute | solution.py:74
  29.9 11.1 %collective-permute-done.8.refs_3_ = bf16[320,1280]{1,0:T(8,128)(2,1)} collective-permute-done((bf16[320,1280]{1,0:T(8,128)(2,1)}, bf16[320,1280]{1,0:T(8,128)(2,1)}, u32[]{:S(2)}, u32[]{:S(2)}) %collective-permute-start.8) | collective-permute-done | bytes 819232 | tf_op jit(solution)/shard_map/ppermute | solution.py:74
  41.0 5.0 %collective-permute-done.6.refs_5_ = bf16[320,1280]{1,0:T(8,128)(2,1)} collective-permute-done((bf16[320,1280]{1,0:T(8,128)(2,1)}, bf16[320,1280]{1,0:T(8,128)(2,1)}, u32[]{:S(2)}, u32[]{:S(2)}) %collective-permute-start.6) | collective-permute-done | bytes 819232 | tf_op jit(solution)/shard_map/ppermute | solution.py:74
  46.0 0.7 collective-permute-start.3
  46.7 1.3 collective-permute-start.1
  48.1 1.0 copy-done.6
  49.1 0.7 collective-permute-start.9
  49.8 2.7 %pad_maximum_fusion = bf16[2,320,1280]{2,1,0:T(8,128)(2,1)} fusion(bf16[1,320,1280]{2,1,0:T(8,128)(2,1)} %param.9, bf16[1,320,1280]{2,1,0:T(8,128)(2,1)} %param.10), kind=kLoop, calls=%fused_computation.1 | loop fusion | flops 819200 | bytes 3276800 | tf_op jit(solution)/shard_map/stack | solution.py:126
  52.5 1.0 copy-done.8
  53.5 0.9 copy-done.10
  54.4 1.3 collective-permute-start.7
  56.2 15.2 %collective-permute-done.1.refs_6_ = bf16[320,1280]{1,0:T(8,128)(2,1)S(1)} collective-permute-done((bf16[320,1280]{1,0:T(8,128)(2,1)}, bf16[320,1280]{1,0:T(8,128)(2,1)S(1)}, u32[]{:S(2)}, u32[]{:S(2)}) %collective-permute-start.1) | collective-permute-done | bytes 819232 | tf_op jit(solution)/shard_map/ppermute | solution.py:74
  71.4 1.3 collective-permute-start.19
  72.9 16.1 %collective-permute-done.7.refs_2_ = bf16[320,1280]{1,0:T(8,128)(2,1)S(1)} collective-permute-done((bf16[320,1280]{1,0:T(8,128)(2,1)}, bf16[320,1280]{1,0:T(8,128)(2,1)S(1)}, u32[]{:S(2)}, u32[]{:S(2)}) %collective-permute-start.7) | collective-permute-done | bytes 819232 | tf_op jit(solution)/shard_map/ppermute | solution.py:74
  89.7 14.6 %collective-permute-done.19 = bf16[320,1280]{1,0:T(8,128)(2,1)S(1)} collective-permute-done((bf16[320,1280]{1,0:T(8,128)(2,1)}, bf16[320,1280]{1,0:T(8,128)(2,1)S(1)}, u32[]{:S(2)}, u32[]{:S(2)}) %collective-permute-start.19) | collective-permute-done | bytes 819232 | tf_op jit(solution)/shard_map/ppermute | solution.py:74
  104.3 1.3 collective-permute-start.20
  105.6 0.7 collective-permute-start.12
  106.3 1.3 collective-permute-start.10
  107.7 1.3 collective-permute-start.4
  109.0 12.3 %collective-permute-done.20.refs_8_ = bf16[320,1280]{1,0:T(8,128)(2,1)S(1)} collective-permute-done((bf16[320,1280]{1,0:T(8,128)(2,1)S(1)}, bf16[320,1280]{1,0:T(8,128)(2,1)S(1)}, u32[]{:S(2)}, u32[]{:S(2)}) %collective-permute-start.20) | collective-permute-done | bytes 819232 | tf_op jit(solution)/shard_map/ppermute | solution.py:74
  121.8 7.5 %collective-permute-done.10.refs_0_ = bf16[320,1280]{1,0:T(8,128)(2,1)S(1)} collective-permute-done((bf16[320,1280]{1,0:T(8,128)(2,1)S(1)}, bf16[320,1280]{1,0:T(8,128)(2,1)S(1)}, u32[]{:S(2)}, u32[]{:S(2)}) %collective-permute-start.10) | collective-permute-done | bytes 819232 | tf_op jit(solution)/shard_map/ppermute | solution.py:74
  129.4 14.4 %collective-permute-done.4.refs_0_ = bf16[320,1280]{1,0:T(8,128)(2,1)S(1)} collective-permute-done((bf16[320,1280]{1,0:T(8,128)(2,1)S(1)}, bf16[320,1280]{1,0:T(8,128)(2,1)S(1)}, u32[]{:S(2)}, u32[]{:S(2)}) %collective-permute-start.4) | collective-permute-done | bytes 819232 | tf_op jit(solution)/shard_map/ppermute | solution.py:74
  143.8 8.0 %fusion.2.early = f32[4,2560]{1,0:T(4,128)S(1)} fusion(f32[1,4,1280]{2,1,0:T(4,128)S(1)} %copy-done, bf16[1,2560,1280]{2,1,0:T(8,128)(2,1)} %param.11), kind=kOutput, calls=%fused_computation.6 | convolution fusion | flops 157286400 | bytes 6615040 | tf_op jit(solution)/shard_map/dot_general | solution.py:301
  151.9 2.2 put.4.refs_10_
  155.0 0.7 copy-done.1
  156.2 0.7 collective-permute-start.31
  156.9 0.7 collective-permute-start.30
  157.6 0.7 collective-permute-start.29
  158.3 0.7 collective-permute-start.27
  159.0 0.7 collective-permute-start.28
  160.0 0.7 collective-permute-start.36
  160.7 0.7 collective-permute-start.35
  161.5 0.7 collective-permute-start.34
  162.2 0.7 collective-permute-start.32
  162.9 0.7 collective-permute-start.33
  163.6 1.3 collective-permute-start.41
  165.2 1.3 collective-permute-start.40
  166.5 1.3 collective-permute-start.39
  167.9 1.3 collective-permute-start.37
  169.2 1.3 collective-permute-start.38
  170.5 7.3 %collective-permute-done.41.arr = bf16[48,2560]{1,0:T(8,128)(2,1)S(1)} collective-permute-done((bf16[48,2560]{1,0:T(8,128)(2,1)S(1)}, bf16[48,2560]{1,0:T(8,128)(2,1)S(1)}, u32[]{:S(2)}, u32[]{:S(2)}) %collective-permute-start.41) | collective-permute-done | bytes 245792 | tf_op jit(solution)/shard_map/ppermute | solution.py:317
  177.7 4.2 %shard_map.109 = (bf16[256,1280]{1,0:T(8,128)(2,1)S(1)}, bf16[256,2560]{1,0:T(8,128)(2,1)S(1)}) custom-call(bf16[2,2560,1280]{2,1,0:T(8,128)(2,1)S(1)} %put.7.w, bf16[48,2560]{1,0:T(8,128)(2,1)S(1)} %collective-permute-done.41.arr, bf16[256,1280]{1,0:T(8,128)(2,1)S(1)} %bitcast.35, ...), custom_call_target="tpu_custom_call", output_to_operand_aliasing={{0}: (4, {}), {1}: (5, {})} | custom-call | flops 629145600 | bytes 13107200 | tf_op jit(solution)/shard_map/pallas_call | solution.py:210
  182.0 1.5 collective-permute-done.40.arr
  183.5 4.2 %shard_map.110 = (bf16[256,1280]{1,0:T(8,128)(2,1)S(1)}, bf16[256,2560]{1,0:T(8,128)(2,1)S(1)}) custom-call(bf16[2,2560,1280]{2,1,0:T(8,128)(2,1)S(1)} %put.7.w, bf16[48,2560]{1,0:T(8,128)(2,1)S(1)} %collective-permute-done.40.arr, bf16[256,1280]{1,0:T(8,128)(2,1)S(1)} %bitcast.36, ...), custom_call_target="tpu_custom_call", output_to_operand_aliasing={{0}: (4, {}), {1}: (5, {})} | custom-call | flops 629145600 | bytes 13107200 | tf_op jit(solution)/shard_map/pallas_call | solution.py:210
  187.7 1.3 collective-permute-done.39.arr
  189.1 4.2 %shard_map.111 = (bf16[256,1280]{1,0:T(8,128)(2,1)S(1)}, bf16[256,2560]{1,0:T(8,128)(2,1)S(1)}) custom-call(bf16[2,2560,1280]{2,1,0:T(8,128)(2,1)S(1)} %put.7.w, bf16[48,2560]{1,0:T(8,128)(2,1)S(1)} %collective-permute-done.39.arr, bf16[256,1280]{1,0:T(8,128)(2,1)S(1)} %bitcast.37, ...), custom_call_target="tpu_custom_call", output_to_operand_aliasing={{0}: (4, {}), {1}: (5, {})} | custom-call | flops 629145600 | bytes 13107200 | tf_op jit(solution)/shard_map/pallas_call | solution.py:210
  193.3 35.4 %collective-permute-done.38.arr = bf16[48,2560]{1,0:T(8,128)(2,1)S(1)} collective-permute-done((bf16[48,2560]{1,0:T(8,128)(2,1)S(1)}, bf16[48,2560]{1,0:T(8,128)(2,1)S(1)}, u32[]{:S(2)}, u32[]{:S(2)}) %collective-permute-start.38) | collective-permute-done | bytes 245792 | tf_op jit(solution)/shard_map/ppermute | solution.py:317
  228.7 4.2 %shard_map.112 = (bf16[256,1280]{1,0:T(8,128)(2,1)S(1)}, bf16[256,2560]{1,0:T(8,128)(2,1)S(1)}) custom-call(bf16[2,2560,1280]{2,1,0:T(8,128)(2,1)S(1)} %put.7.w, bf16[48,2560]{1,0:T(8,128)(2,1)S(1)} %collective-permute-done.38.arr, bf16[256,1280]{1,0:T(8,128)(2,1)S(1)} %bitcast.38, ...), custom_call_target="tpu_custom_call", output_to_operand_aliasing={{0}: (4, {}), {1}: (5, {})} | custom-call | flops 629145600 | bytes 13107200 | tf_op jit(solution)/shard_map/pallas_call | solution.py:210
  233.0 4.4 %shard_map.113 = (bf16[256,1280]{1,0:T(8,128)(2,1)S(1)}, bf16[256,2560]{1,0:T(8,128)(2,1)S(1)}) custom-call(bf16[2,2560,1280]{2,1,0:T(8,128)(2,1)S(1)} %put.7.w, bf16[64,2560]{1,0:T(8,128)(2,1)S(1)} %collective-permute-done.37.arr, bf16[256,1280]{1,0:T(8,128)(2,1)S(1)} %bitcast.39, ...), custom_call_target="tpu_custom_call", output_to_operand_aliasing={{0}: (4, {}), {1}: (5, {})} | custom-call | flops 838860800 | bytes 13107200 | tf_op jit(solution)/shard_map/pallas_call | solution.py:210
  237.4 0.6 fusion
  238.1 0.7 convolution_add_fusion
  238.8 1.2 collective-permute-done.42
  240.2 3.8 %collective-permute-done.43 = f32[4,2560]{1,0:T(4,128)S(1)} collective-permute-done((f32[4,2560]{1,0:T(4,128)S(1)}, f32[4,2560]{1,0:T(4,128)S(1)}, u32[]{:S(2)}, u32[]{:S(2)}) %collective-permute-start.43) | collective-permute-done | bytes 40992 | tf_op jit(solution)/shard_map/ppermute | solution.py:285
  244.2 4.9 %collective-permute-done.44.right = f32[4,2560]{1,0:T(4,128)S(1)} collective-permute-done((f32[4,2560]{1,0:T(4,128)S(1)}, f32[4,2560]{1,0:T(4,128)S(1)}, u32[]{:S(2)}, u32[]{:S(2)}) %collective-permute-start.44) | collective-permute-done | bytes 40992 | tf_op jit(solution)/shard_map/ppermute | solution.py:285
  249.1 2.8 %second_half.1 = (f32[4,2560]{1,0:T(4,128)}, f32[4,1280]{1,0:T(4,128)S(1)}, bf16[256,2560]{1,0:T(8,128)(2,1)}) custom-call(f32[4,2560]{1,0:T(4,128)S(1)} %add.20.left, f32[4,2560]{1,0:T(4,128)S(1)} %collective-permute-done.44.right, bf16[256,2560]{1,0:T(8,128)(2,1)S(1)} %bitcast.43, bf16[256,1280]{1,0:T(8,128)(2,1)S(1)} %get-tuple-element.114.vg, ...), custom_call_target="tpu_custom_call" | custom-call | tf_op jit(solution)/shard_map/second_half/pallas_call | solution.py:268
  252.0 1.2 collective-permute-done.45
  253.4 3.7 %collective-permute-done.46 = f32[4,1280]{1,0:T(4,128)S(1)} collective-permute-done((f32[4,1280]{1,0:T(4,128)S(1)}, f32[4,1280]{1,0:T(4,128)S(1)}, u32[]{:S(2)}, u32[]{:S(2)}) %collective-permute-start.46) | collective-permute-done | bytes 20512 | tf_op jit(solution)/shard_map/ppermute | solution.py:285
  257.1 4.7 %collective-permute-done.47 = f32[4,1280]{1,0:T(4,128)S(1)} collective-permute-done((f32[4,1280]{1,0:T(4,128)S(1)}, f32[4,1280]{1,0:T(4,128)S(1)}, u32[]{:S(2)}, u32[]{:S(2)}) %collective-permute-start.47) | collective-permute-done | bytes 20512 | tf_op jit(solution)/shard_map/ppermute | solution.py:285
  (99 shorter events, 5.5 us)
Async XLA Ops:
  0.6 143.2 %copy-start = (f32[1,4,1280]{2,1,0:T(4,128)S(1)}, f32[1,4,1280]{2,1,0:T(4,128)}, u32[]{:S(2)}) copy-start(f32[1,4,1280]{2,1,0:T(4,128)} %param.13) | copy-start | bytes 61444
  0.6 23.9 %collective-permute-start.2 = (bf16[320,1280]{1,0:T(8,128)(2,1)}, bf16[320,1280]{1,0:T(8,128)(2,1)}, u32[]{:S(2)}, u32[]{:S(2)}) collective-permute-start(bf16[320,1280]{1,0:T(8,128)(2,1)} %bitcast.44), channel_id=1, source_target_pairs={{0,2},{1,3},{2,4},{3,5},{4,6},{5,7},{8,10},{9,11},{10,12},{11,13},... | collective-permute-start | bytes 2457608 | tf_op jit(solution)/shard_map/ppermute | solution.py:74
  6.6 23.3 %collective-permute-start = (bf16[320,1280]{1,0:T(8,128)(2,1)}, bf16[320,1280]{1,0:T(8,128)(2,1)}, u32[]{:S(2)}, u32[]{:S(2)}) collective-permute-start(bf16[320,1280]{1,0:T(8,128)(2,1)} %bitcast.45), channel_id=1, source_target_pairs={{2,0},{3,1},{4,2},{5,3},{6,4},{7,5},{10,8},{11,9},{12,10},{13,11},... | collective-permute-start | bytes 2457608 | tf_op jit(solution)/shard_map/ppermute | solution.py:74
  7.8 33.1 %collective-permute-start.8 = (bf16[320,1280]{1,0:T(8,128)(2,1)}, bf16[320,1280]{1,0:T(8,128)(2,1)}, u32[]{:S(2)}, u32[]{:S(2)}) collective-permute-start(bf16[320,1280]{1,0:T(8,128)(2,1)} %bitcast.48), channel_id=1, source_target_pairs={{0,2},{1,3},{2,4},{3,5},{4,6},{5,7},{8,10},{9,11},{10,12},{11,13},... | collective-permute-start | bytes 2457608 | tf_op jit(solution)/shard_map/ppermute | solution.py:74
  13.3 32.7 %collective-permute-start.6 = (bf16[320,1280]{1,0:T(8,128)(2,1)}, bf16[320,1280]{1,0:T(8,128)(2,1)}, u32[]{:S(2)}, u32[]{:S(2)}) collective-permute-start(bf16[320,1280]{1,0:T(8,128)(2,1)} %bitcast.49), channel_id=1, source_target_pairs={{2,0},{3,1},{4,2},{5,3},{6,4},{7,5},{10,8},{11,9},{12,10},{13,11},... | collective-permute-start | bytes 2457608 | tf_op jit(solution)/shard_map/ppermute | solution.py:74
  14.6 32.2 %collective-permute-start.18 = (bf16[320,1280]{1,0:T(8,128)(2,1)}, bf16[320,1280]{1,0:T(8,128)(2,1)S(1)}, u32[]{:S(2)}, u32[]{:S(2)}) collective-permute-start(bf16[320,1280]{1,0:T(8,128)(2,1)} %bitcast.46), channel_id=1, source_target_pairs={{26,2},{27,3},{28,4},{29,5}} | collective-permute-start | bytes 2457608 | tf_op jit(solution)/shard_map/ppermute | solution.py:74
  24.5 23.5 %collective-permute-start.25 = (bf16[320,1280]{1,0:T(8,128)(2,1)}, bf16[320,1280]{1,0:T(8,128)(2,1)S(1)}, u32[]{:S(2)}, u32[]{:S(2)}) collective-permute-start(bf16[320,1280]{1,0:T(8,128)(2,1)} %collective-permute-done.2.refs_7_), channel_id=1, source_target_pairs={{0,1},{1,0},{2,3},{3,2},{4,5},{5,4},{6,7},{7,6},{8,9},{9,8},{10,11... | collective-permute-start | bytes 2457608 | tf_op jit(solution)/shard_map/ppermute | solution.py:82
  29.9 22.6 %collective-permute-start.26 = (bf16[320,1280]{1,0:T(8,128)(2,1)}, bf16[320,1280]{1,0:T(8,128)(2,1)S(1)}, u32[]{:S(2)}, u32[]{:S(2)}) collective-permute-start(bf16[320,1280]{1,0:T(8,128)(2,1)} %collective-permute-done.refs_9_), channel_id=1, source_target_pairs={{0,1},{1,0},{2,3},{3,2},{4,5},{5,4},{6,7},{7,6},{8,9},{9,8},{10,11... | collective-permute-start | bytes 2457608 | tf_op jit(solution)/shard_map/ppermute | solution.py:82
  41.0 12.5 %collective-permute-start.23 = (bf16[320,1280]{1,0:T(8,128)(2,1)}, bf16[320,1280]{1,0:T(8,128)(2,1)S(1)}, u32[]{:S(2)}, u32[]{:S(2)}) collective-permute-start(bf16[320,1280]{1,0:T(8,128)(2,1)} %collective-permute-done.8.refs_3_), channel_id=1, source_target_pairs={{0,1},{1,0},{2,3},{3,2},{4,5},{5,4},{6,7},{7,6},{8,9},{9,8},{10,11... | collective-permute-start | bytes 2457608 | tf_op jit(solution)/shard_map/ppermute | solution.py:82
  46.0 9.6 %collective-permute-start.3 = (bf16[320,1280]{1,0:T(8,128)(2,1)}, bf16[320,1280]{1,0:T(8,128)(2,1)S(1)}, u32[]{:S(2)}, u32[]{:S(2)}) collective-permute-start(bf16[320,1280]{1,0:T(8,128)(2,1)} %collective-permute-done.2.refs_7_), channel_id=1, source_target_pairs={{2,4},{3,5},{4,6},{5,7},{10,12},{11,13},{12,14},{13,15},{18,20},{1... | collective-permute-start | bytes 2457608 | tf_op jit(solution)/shard_map/ppermute | solution.py:74
  46.7 1.3 copy-start.12
  46.7 24.7 %collective-permute-start.1 = (bf16[320,1280]{1,0:T(8,128)(2,1)}, bf16[320,1280]{1,0:T(8,128)(2,1)S(1)}, u32[]{:S(2)}, u32[]{:S(2)}) collective-permute-start(bf16[320,1280]{1,0:T(8,128)(2,1)} %collective-permute-done.refs_9_), channel_id=1, source_target_pairs={{2,0},{3,1},{4,2},{5,3},{10,8},{11,9},{12,10},{13,11},{18,16},{19,... | collective-permute-start | bytes 2457608 | tf_op jit(solution)/shard_map/ppermute | solution.py:74
  48.1 1.0 copy-start.6
  49.1 23.7 %collective-permute-start.9 = (bf16[320,1280]{1,0:T(8,128)(2,1)}, bf16[320,1280]{1,0:T(8,128)(2,1)S(1)}, u32[]{:S(2)}, u32[]{:S(2)}) collective-permute-start(bf16[320,1280]{1,0:T(8,128)(2,1)} %collective-permute-done.8.refs_3_), channel_id=1, source_target_pairs={{2,4},{3,5},{4,6},{5,7},{10,12},{11,13},{12,14},{13,15},{18,20},{1... | collective-permute-start | bytes 2457608 | tf_op jit(solution)/shard_map/ppermute | solution.py:74
  52.5 1.0 copy-start.8
  53.5 52.1 %collective-permute-start.22 = (bf16[2,320,1280]{2,1,0:T(8,128)(2,1)}, bf16[2,320,1280]{2,1,0:T(8,128)(2,1)}, u32[]{:S(2)}, u32[]{:S(2)}) collective-permute-start(bf16[2,320,1280]{2,1,0:T(8,128)(2,1)} %pad_maximum_fusion), channel_id=1, source_target_pairs={{0,1},{1,0},{2,3},{3,2},{4,5},{5,4},{6,7},{7,6},{8,9},{9,8},{10,11... | collective-permute-start | bytes 4915208 | tf_op jit(solution)/shard_map/ppermute | solution.py:82
  53.5 0.9 copy-start.10
  54.4 34.6 %collective-permute-start.7 = (bf16[320,1280]{1,0:T(8,128)(2,1)}, bf16[320,1280]{1,0:T(8,128)(2,1)S(1)}, u32[]{:S(2)}, u32[]{:S(2)}) collective-permute-start(bf16[320,1280]{1,0:T(8,128)(2,1)} %collective-permute-done.6.refs_5_), channel_id=1, source_target_pairs={{2,0},{3,1},{4,2},{5,3},{10,8},{11,9},{12,10},{13,11},{18,16},{19,... | collective-permute-start | bytes 2457608 | tf_op jit(solution)/shard_map/ppermute | solution.py:74
  55.7 33.5 %collective-permute-start.24 = (bf16[320,1280]{1,0:T(8,128)(2,1)}, bf16[320,1280]{1,0:T(8,128)(2,1)S(1)}, u32[]{:S(2)}, u32[]{:S(2)}) collective-permute-start(bf16[320,1280]{1,0:T(8,128)(2,1)} %collective-permute-done.6.refs_5_), channel_id=1, source_target_pairs={{0,1},{1,0},{2,3},{3,2},{4,5},{5,4},{6,7},{7,6},{8,9},{9,8},{10,11... | collective-permute-start | bytes 2457608 | tf_op jit(solution)/shard_map/ppermute | solution.py:82
  71.4 32.8 %collective-permute-start.19 = (bf16[320,1280]{1,0:T(8,128)(2,1)}, bf16[320,1280]{1,0:T(8,128)(2,1)S(1)}, u32[]{:S(2)}, u32[]{:S(2)}) collective-permute-start(bf16[320,1280]{1,0:T(8,128)(2,1)} %copy-done.12), channel_id=1, source_target_pairs={{2,0},{3,1},{4,6},{5,7}} | collective-permute-start | bytes 2457608 | tf_op jit(solution)/shard_map/ppermute | solution.py:74
  72.7 33.6 %collective-permute-start.16 = (bf16[320,1280]{1,0:T(8,128)(2,1)S(1)}, bf16[320,1280]{1,0:T(8,128)(2,1)S(1)}, u32[]{:S(2)}, u32[]{:S(2)}) collective-permute-start(bf16[320,1280]{1,0:T(8,128)(2,1)S(1)} %collective-permute-done.3.refs_4_), channel_id=1, source_target_pairs={{0,1},{1,0},{2,3},{3,2},{4,5},{5,4},{6,7},{7,6},{8,9},{9,8},{10,11... | collective-permute-start | bytes 2457608 | tf_op jit(solution)/shard_map/ppermute | solution.py:82
  89.0 18.7 %collective-permute-start.17 = (bf16[320,1280]{1,0:T(8,128)(2,1)S(1)}, bf16[320,1280]{1,0:T(8,128)(2,1)S(1)}, u32[]{:S(2)}, u32[]{:S(2)}) collective-permute-start(bf16[320,1280]{1,0:T(8,128)(2,1)S(1)} %collective-permute-done.1.refs_6_), channel_id=1, source_target_pairs={{0,1},{1,0},{2,3},{3,2},{4,5},{5,4},{6,7},{7,6},{8,9},{9,8},{10,11... | collective-permute-start | bytes 2457608 | tf_op jit(solution)/shard_map/ppermute | solution.py:82
  89.1 62.7 %copy-start.4 = (bf16[1,320,1280]{2,1,0:T(8,128)(2,1)S(1)}, bf16[1,320,1280]{2,1,0:T(8,128)(2,1)}, u32[]{:S(2)}) copy-start(bf16[1,320,1280]{2,1,0:T(8,128)(2,1)} %param.9) | copy-start | bytes 2457604
  89.1 62.7 %copy-start.5 = (bf16[1,320,1280]{2,1,0:T(8,128)(2,1)S(1)}, bf16[1,320,1280]{2,1,0:T(8,128)(2,1)}, u32[]{:S(2)}) copy-start(bf16[1,320,1280]{2,1,0:T(8,128)(2,1)} %param.10) | copy-start | bytes 2457604
  89.1 62.7 %copy-start.7 = (bf16[320,1280]{1,0:T(8,128)(2,1)S(1)}, bf16[320,1280]{1,0:T(8,128)(2,1)}, u32[]{:S(2)}) copy-start(bf16[320,1280]{1,0:T(8,128)(2,1)} %copy-done.6) | copy-start | bytes 2457604
  89.1 62.7 %copy-start.9 = (bf16[320,1280]{1,0:T(8,128)(2,1)S(1)}, bf16[320,1280]{1,0:T(8,128)(2,1)}, u32[]{:S(2)}) copy-start(bf16[320,1280]{1,0:T(8,128)(2,1)} %copy-done.8) | copy-start | bytes 2457604
  89.1 62.7 %copy-start.11 = (bf16[320,1280]{1,0:T(8,128)(2,1)S(1)}, bf16[320,1280]{1,0:T(8,128)(2,1)}, u32[]{:S(2)}) copy-start(bf16[320,1280]{1,0:T(8,128)(2,1)} %copy-done.10) | copy-start | bytes 2457604
  89.1 19.8 %collective-permute-start.14 = (bf16[320,1280]{1,0:T(8,128)(2,1)S(1)}, bf16[320,1280]{1,0:T(8,128)(2,1)S(1)}, u32[]{:S(2)}, u32[]{:S(2)}) collective-permute-start(bf16[320,1280]{1,0:T(8,128)(2,1)S(1)} %collective-permute-done.9.refs_0_), channel_id=1, source_target_pairs={{0,1},{1,0},{2,3},{3,2},{4,5},{5,4},{6,7},{7,6},{8,9},{9,8},{10,11... | collective-permute-start | bytes 2457608 | tf_op jit(solution)/shard_map/ppermute | solution.py:82
  104.3 17.1 %collective-permute-start.20 = (bf16[320,1280]{1,0:T(8,128)(2,1)S(1)}, bf16[320,1280]{1,0:T(8,128)(2,1)S(1)}, u32[]{:S(2)}, u32[]{:S(2)}) collective-permute-start(bf16[320,1280]{1,0:T(8,128)(2,1)S(1)} %collective-permute-done.19), channel_id=1, source_target_pairs={{0,24},{1,25},{6,30},{7,31}} | collective-permute-start | bytes 2457608 | tf_op jit(solution)/shard_map/ppermute | solution.py:74
  105.6 15.7 %collective-permute-start.12 = (bf16[320,1280]{1,0:T(8,128)(2,1)S(1)}, bf16[320,1280]{1,0:T(8,128)(2,1)S(1)}, u32[]{:S(2)}, u32[]{:S(2)}) collective-permute-start(bf16[320,1280]{1,0:T(8,128)(2,1)S(1)} %broadcast_select_fusion.1), channel_id=1, source_target_pairs={{26,24},{27,25},{28,30},{29,31}} | collective-permute-start | bytes 2457608 | tf_op jit(solution)/shard_map/ppermute | solution.py:74
  106.3 23.0 %collective-permute-start.10 = (bf16[320,1280]{1,0:T(8,128)(2,1)S(1)}, bf16[320,1280]{1,0:T(8,128)(2,1)S(1)}, u32[]{:S(2)}, u32[]{:S(2)}) collective-permute-start(bf16[320,1280]{1,0:T(8,128)(2,1)S(1)} %broadcast_select_fusion), channel_id=1, source_target_pairs={{2,0},{3,1},{4,6},{5,7},{10,8},{11,9},{12,14},{13,15},{18,16},{19,... | collective-permute-start | bytes 2457608 | tf_op jit(solution)/shard_map/ppermute | solution.py:74
  107.7 36.1 %collective-permute-start.4 = (bf16[320,1280]{1,0:T(8,128)(2,1)S(1)}, bf16[320,1280]{1,0:T(8,128)(2,1)S(1)}, u32[]{:S(2)}, u32[]{:S(2)}) collective-permute-start(bf16[320,1280]{1,0:T(8,128)(2,1)S(1)} %broadcast_select_fusion.1), channel_id=1, source_target_pairs={{2,0},{3,1},{4,6},{5,7},{10,8},{11,9},{12,14},{13,15},{18,16},{19,... | collective-permute-start | bytes 2457608 | tf_op jit(solution)/shard_map/ppermute | solution.py:74
  109.0 45.1 %collective-permute-start.15 = (bf16[320,1280]{1,0:T(8,128)(2,1)S(1)}, bf16[320,1280]{1,0:T(8,128)(2,1)S(1)}, u32[]{:S(2)}, u32[]{:S(2)}) collective-permute-start(bf16[320,1280]{1,0:T(8,128)(2,1)S(1)} %collective-permute-done.7.refs_2_), channel_id=1, source_target_pairs={{0,1},{1,0},{2,3},{3,2},{4,5},{5,4},{6,7},{7,6},{8,9},{9,8},{10,11... | collective-permute-start | bytes 2457608 | tf_op jit(solution)/shard_map/ppermute | solution.py:82
  121.3 32.8 %collective-permute-start.21 = (bf16[320,1280]{1,0:T(8,128)(2,1)S(1)}, bf16[320,1280]{1,0:T(8,128)(2,1)S(1)}, u32[]{:S(2)}, u32[]{:S(2)}) collective-permute-start(bf16[320,1280]{1,0:T(8,128)(2,1)S(1)} %collective-permute-done.20.refs_8_), channel_id=1, source_target_pairs={{0,1},{1,0},{2,3},{3,2},{4,5},{5,4},{6,7},{7,6},{8,9},{9,8},{10,11... | collective-permute-start | bytes 2457608 | tf_op jit(solution)/shard_map/ppermute | solution.py:82
  121.3 33.4 %collective-permute-start.13 = (bf16[320,1280]{1,0:T(8,128)(2,1)S(1)}, bf16[320,1280]{1,0:T(8,128)(2,1)S(1)}, u32[]{:S(2)}, u32[]{:S(2)}) collective-permute-start(bf16[320,1280]{1,0:T(8,128)(2,1)S(1)} %collective-permute-done.12.refs_2_), channel_id=1, source_target_pairs={{0,1},{1,0},{2,3},{3,2},{4,5},{5,4},{6,7},{7,6},{8,9},{9,8},{10,11... | collective-permute-start | bytes 2457608 | tf_op jit(solution)/shard_map/ppermute | solution.py:82
  129.4 25.3 %collective-permute-start.11 = (bf16[320,1280]{1,0:T(8,128)(2,1)S(1)}, bf16[320,1280]{1,0:T(8,128)(2,1)S(1)}, u32[]{:S(2)}, u32[]{:S(2)}) collective-permute-start(bf16[320,1280]{1,0:T(8,128)(2,1)S(1)} %collective-permute-done.10.refs_0_), channel_id=1, source_target_pairs={{0,1},{1,0},{2,3},{3,2},{4,5},{5,4},{6,7},{7,6},{8,9},{9,8},{10,11... | collective-permute-start | bytes 2457608 | tf_op jit(solution)/shard_map/ppermute | solution.py:82
  143.8 15.2 %collective-permute-start.5 = (bf16[320,1280]{1,0:T(8,128)(2,1)S(1)}, bf16[320,1280]{1,0:T(8,128)(2,1)S(1)}, u32[]{:S(2)}, u32[]{:S(2)}) collective-permute-start(bf16[320,1280]{1,0:T(8,128)(2,1)S(1)} %collective-permute-done.4.refs_0_), channel_id=1, source_target_pairs={{0,1},{1,0},{2,3},{3,2},{4,5},{5,4},{6,7},{7,6},{8,9},{9,8},{10,11... | collective-permute-start | bytes 2457608 | tf_op jit(solution)/shard_map/ppermute | solution.py:82
  154.7 1.1 copy-start.1
  154.7 1.5 copy-start.2
  156.2 3.8 %collective-permute-start.31 = (bf16[48,2560]{1,0:T(8,128)(2,1)S(1)}, bf16[48,2560]{1,0:T(8,128)(2,1)S(1)}, u32[]{:S(2)}, u32[]{:S(2)}) collective-permute-start(bf16[48,2560]{1,0:T(8,128)(2,1)S(1)} %get-tuple-element.74), channel_id=1, source_target_pairs={{24,16},{25,17},{26,18},{27,19},{28,20},{29,21},{30,22},{31,23}} | collective-permute-start | bytes 737288 | tf_op jit(solution)/shard_map/ppermute | solution.py:317
  156.9 3.8 %collective-permute-start.30 = (bf16[48,2560]{1,0:T(8,128)(2,1)S(1)}, bf16[48,2560]{1,0:T(8,128)(2,1)S(1)}, u32[]{:S(2)}, u32[]{:S(2)}) collective-permute-start(bf16[48,2560]{1,0:T(8,128)(2,1)S(1)} %get-tuple-element.73), channel_id=1, source_target_pairs={{24,16},{25,17},{26,18},{27,19},{28,20},{29,21},{30,22},{31,23}} | collective-permute-start | bytes 737288 | tf_op jit(solution)/shard_map/ppermute | solution.py:317
  157.6 3.8 %collective-permute-start.29 = (bf16[48,2560]{1,0:T(8,128)(2,1)S(1)}, bf16[48,2560]{1,0:T(8,128)(2,1)S(1)}, u32[]{:S(2)}, u32[]{:S(2)}) collective-permute-start(bf16[48,2560]{1,0:T(8,128)(2,1)S(1)} %get-tuple-element.72), channel_id=1, source_target_pairs={{24,16},{25,17},{26,18},{27,19},{28,20},{29,21},{30,22},{31,23}} | collective-permute-start | bytes 737288 | tf_op jit(solution)/shard_map/ppermute | solution.py:317
  158.3 3.9 %collective-permute-start.27 = (bf16[64,2560]{1,0:T(8,128)(2,1)S(1)}, bf16[64,2560]{1,0:T(8,128)(2,1)S(1)}, u32[]{:S(2)}, u32[]{:S(2)}) collective-permute-start(bf16[64,2560]{1,0:T(8,128)(2,1)S(1)} %get-tuple-element.70), channel_id=1, source_target_pairs={{24,16},{25,17},{26,18},{27,19},{28,20},{29,21},{30,22},{31,23}} | collective-permute-start | bytes 983048 | tf_op jit(solution)/shard_map/ppermute | solution.py:317
  159.0 3.1 %collective-permute-start.28 = (bf16[48,2560]{1,0:T(8,128)(2,1)S(1)}, bf16[48,2560]{1,0:T(8,128)(2,1)S(1)}, u32[]{:S(2)}, u32[]{:S(2)}) collective-permute-start(bf16[48,2560]{1,0:T(8,128)(2,1)S(1)} %get-tuple-element.71), channel_id=1, source_target_pairs={{24,16},{25,17},{26,18},{27,19},{28,20},{29,21},{30,22},{31,23}} | collective-permute-start | bytes 737288 | tf_op jit(solution)/shard_map/ppermute | solution.py:317
  160.0 3.6 %collective-permute-start.36 = (bf16[48,2560]{1,0:T(8,128)(2,1)S(1)}, bf16[48,2560]{1,0:T(8,128)(2,1)S(1)}, u32[]{:S(2)}, u32[]{:S(2)}) collective-permute-start(bf16[48,2560]{1,0:T(8,128)(2,1)S(1)} %get-tuple-element.88), channel_id=1, source_target_pairs={{16,8},{17,9},{18,10},{19,11},{20,12},{21,13},{22,14},{23,15}} | collective-permute-start | bytes 737288 | tf_op jit(solution)/shard_map/ppermute | solution.py:317
  160.7 4.2 %collective-permute-start.35 = (bf16[48,2560]{1,0:T(8,128)(2,1)S(1)}, bf16[48,2560]{1,0:T(8,128)(2,1)S(1)}, u32[]{:S(2)}, u32[]{:S(2)}) collective-permute-start(bf16[48,2560]{1,0:T(8,128)(2,1)S(1)} %get-tuple-element.87), channel_id=1, source_target_pairs={{16,8},{17,9},{18,10},{19,11},{20,12},{21,13},{22,14},{23,15}} | collective-permute-start | bytes 737288 | tf_op jit(solution)/shard_map/ppermute | solution.py:317
  161.5 5.0 %collective-permute-start.34 = (bf16[48,2560]{1,0:T(8,128)(2,1)S(1)}, bf16[48,2560]{1,0:T(8,128)(2,1)S(1)}, u32[]{:S(2)}, u32[]{:S(2)}) collective-permute-start(bf16[48,2560]{1,0:T(8,128)(2,1)S(1)} %get-tuple-element.86), channel_id=1, source_target_pairs={{16,8},{17,9},{18,10},{19,11},{20,12},{21,13},{22,14},{23,15}} | collective-permute-start | bytes 737288 | tf_op jit(solution)/shard_map/ppermute | solution.py:317
  162.2 5.6 %collective-permute-start.32 = (bf16[64,2560]{1,0:T(8,128)(2,1)S(1)}, bf16[64,2560]{1,0:T(8,128)(2,1)S(1)}, u32[]{:S(2)}, u32[]{:S(2)}) collective-permute-start(bf16[64,2560]{1,0:T(8,128)(2,1)S(1)} %get-tuple-element.84), channel_id=1, source_target_pairs={{16,8},{17,9},{18,10},{19,11},{20,12},{21,13},{22,14},{23,15}} | collective-permute-start | bytes 983048 | tf_op jit(solution)/shard_map/ppermute | solution.py:317
  162.9 4.9 %collective-permute-start.33 = (bf16[48,2560]{1,0:T(8,128)(2,1)S(1)}, bf16[48,2560]{1,0:T(8,128)(2,1)S(1)}, u32[]{:S(2)}, u32[]{:S(2)}) collective-permute-start(bf16[48,2560]{1,0:T(8,128)(2,1)S(1)} %get-tuple-element.85), channel_id=1, source_target_pairs={{16,8},{17,9},{18,10},{19,11},{20,12},{21,13},{22,14},{23,15}} | collective-permute-start | bytes 737288 | tf_op jit(solution)/shard_map/ppermute | solution.py:317
  163.6 14.1 %collective-permute-start.41 = (bf16[48,2560]{1,0:T(8,128)(2,1)S(1)}, bf16[48,2560]{1,0:T(8,128)(2,1)S(1)}, u32[]{:S(2)}, u32[]{:S(2)}) collective-permute-start(bf16[48,2560]{1,0:T(8,128)(2,1)S(1)} %get-tuple-element.103), channel_id=1, source_target_pairs={{8,0},{9,1},{10,2},{11,3},{12,4},{13,5},{14,6},{15,7}} | collective-permute-start | bytes 737288 | tf_op jit(solution)/shard_map/ppermute | solution.py:317
  165.2 18.3 %collective-permute-start.40 = (bf16[48,2560]{1,0:T(8,128)(2,1)S(1)}, bf16[48,2560]{1,0:T(8,128)(2,1)S(1)}, u32[]{:S(2)}, u32[]{:S(2)}) collective-permute-start(bf16[48,2560]{1,0:T(8,128)(2,1)S(1)} %get-tuple-element.102), channel_id=1, source_target_pairs={{8,0},{9,1},{10,2},{11,3},{12,4},{13,5},{14,6},{15,7}} | collective-permute-start | bytes 737288 | tf_op jit(solution)/shard_map/ppermute | solution.py:317
  166.5 22.6 %collective-permute-start.39 = (bf16[48,2560]{1,0:T(8,128)(2,1)S(1)}, bf16[48,2560]{1,0:T(8,128)(2,1)S(1)}, u32[]{:S(2)}, u32[]{:S(2)}) collective-permute-start(bf16[48,2560]{1,0:T(8,128)(2,1)S(1)} %get-tuple-element.101), channel_id=1, source_target_pairs={{8,0},{9,1},{10,2},{11,3},{12,4},{13,5},{14,6},{15,7}} | collective-permute-start | bytes 737288 | tf_op jit(solution)/shard_map/ppermute | solution.py:317
  167.9 65.1 %collective-permute-start.37 = (bf16[64,2560]{1,0:T(8,128)(2,1)S(1)}, bf16[64,2560]{1,0:T(8,128)(2,1)S(1)}, u32[]{:S(2)}, u32[]{:S(2)}) collective-permute-start(bf16[64,2560]{1,0:T(8,128)(2,1)S(1)} %get-tuple-element.99), channel_id=1, source_target_pairs={{8,0},{9,1},{10,2},{11,3},{12,4},{13,5},{14,6},{15,7}} | collective-permute-start | bytes 983048 | tf_op jit(solution)/shard_map/ppermute | solution.py:317
  169.2 59.6 %collective-permute-start.38 = (bf16[48,2560]{1,0:T(8,128)(2,1)S(1)}, bf16[48,2560]{1,0:T(8,128)(2,1)S(1)}, u32[]{:S(2)}, u32[]{:S(2)}) collective-permute-start(bf16[48,2560]{1,0:T(8,128)(2,1)S(1)} %get-tuple-element.100), channel_id=1, source_target_pairs={{8,0},{9,1},{10,2},{11,3},{12,4},{13,5},{14,6},{15,7}} | collective-permute-start | bytes 737288 | tf_op jit(solution)/shard_map/ppermute | solution.py:317
  233.0 16.1 %slice-start = ((s8[6553600]{0:T(1024)(128)(4,1)}), s8[4194304]{0:T(1024)(128)(4,1)S(1)}, s32[]{:S(2)}) async-start(s8[6553600]{0:T(1024)(128)(4,1)} %bitcast.40), calls=%async_computation | async-start | bytes 8388608
  233.0 5.1 %copy-start.3 = (bf16[1,256,2560]{2,1,0:T(8,128)(2,1)S(1)}, bf16[1,256,2560]{2,1,0:T(8,128)(2,1)}, u32[]{:S(2)}) copy-start(bf16[1,256,2560]{2,1,0:T(8,128)(2,1)} %param.7) | copy-start | bytes 3932164
  233.0 16.1 %slice-start.1 = ((s8[6553600]{0:T(1024)(128)(4,1)}), s8[2359296]{0:T(1024)(128)(4,1)S(1)}, s32[]{:S(2)}) async-start(s8[6553600]{0:T(1024)(128)(4,1)} %bitcast.40), calls=%async_computation.1 | async-start | bytes 4718592
  238.8 1.2 collective-permute-start.42
  240.0 4.1 %collective-permute-start.43 = (f32[4,2560]{1,0:T(4,128)S(1)}, f32[4,2560]{1,0:T(4,128)S(1)}, u32[]{:S(2)}, u32[]{:S(2)}) collective-permute-start(f32[4,2560]{1,0:T(4,128)S(1)} %add.19), channel_id=1, source_target_pairs={{0,2},{1,3},{2,0},{3,1},{4,6},{5,7},{6,4},{7,5},{8,10},{9,11},{10,... | collective-permute-start | bytes 122888 | tf_op jit(solution)/shard_map/ppermute | solution.py:285
  244.1 5.0 %collective-permute-start.44 = (f32[4,2560]{1,0:T(4,128)S(1)}, f32[4,2560]{1,0:T(4,128)S(1)}, u32[]{:S(2)}, u32[]{:S(2)}) collective-permute-start(f32[4,2560]{1,0:T(4,128)S(1)} %add.20.left), channel_id=1, source_target_pairs={{0,4},{1,5},{2,6},{3,7},{4,0},{5,1},{6,2},{7,3},{8,12},{9,13},{10,... | collective-permute-start | bytes 122888 | tf_op jit(solution)/shard_map/ppermute | solution.py:285
  251.9 1.3 collective-permute-start.45
  253.2 3.8 %collective-permute-start.46 = (f32[4,1280]{1,0:T(4,128)S(1)}, f32[4,1280]{1,0:T(4,128)S(1)}, u32[]{:S(2)}, u32[]{:S(2)}) collective-permute-start(f32[4,1280]{1,0:T(4,128)S(1)} %add.21), channel_id=1, source_target_pairs={{0,2},{1,3},{2,0},{3,1},{4,6},{5,7},{6,4},{7,5},{8,10},{9,11},{10,... | collective-permute-start | bytes 61448 | tf_op jit(solution)/shard_map/ppermute | solution.py:285
  257.0 4.7 %collective-permute-start.47 = (f32[4,1280]{1,0:T(4,128)S(1)}, f32[4,1280]{1,0:T(4,128)S(1)}, u32[]{:S(2)}, u32[]{:S(2)}) collective-permute-start(f32[4,1280]{1,0:T(4,128)S(1)} %add.22), channel_id=1, source_target_pairs={{0,4},{1,5},{2,6},{3,7},{4,0},{5,1},{6,2},{7,3},{8,12},{9,13},{10,... | collective-permute-start | bytes 61448 | tf_op jit(solution)/shard_map/ppermute | solution.py:285

commit v4 on v3

--- a/solution.py
+++ b/solution.py
@@ -8,7 +8,7 @@
 from jax.sharding import PartitionSpec as P
 
 
-SIXTEENTHS = (3, 3, 3, 3, 4)
+SIXTEENTHS = (4, 4, 4, 4)
 CORES = 2
 HIGHEST = lax.Precision.HIGHEST
 VMEM = pl.BlockSpec(memory_space=pltpu.VMEM)
@@ -101,6 +101,7 @@
     up, down = list(matrices), list(matrices)
     relay = None
     groups = [[], [], []]
+    late = {}
     for step in range(1, chips):
         for kind in range(len(matrices)):
             skip = dropped if step == 1 and kind == 1 else ()
@@ -113,11 +114,18 @@
                 low = lax.axis_index("dp") < replicas // 2
                 last = jnp.where(low, down[kind], up[kind])
                 moves = [(1, 0), (chips - 2, chips - 1)]
-                split = kind == 1 and top > 0
-                skip = [(s, c, s, d) for s in range(top) for c, d in moves] if split else ()
-                up[kind] = line(last, moves, skip)
-                if split:
-                    late = permute(last, skip)
+                if kind == 0 or not top:
+                    up[kind] = line(last, moves)
+                else:
+                    turns = {section: "late" for section in range(1, top)}
+                    turns |= {0: "last", top: f"{step}_{kind}"}
+                    late = {}
+                    for turn in dict.fromkeys(reversed(turns.values())):
+                        late[turn] = permute(
+                            last,
+                            [(s, c, s, d) for s in turns if turns[s] == turn for c, d in moves],
+                        )
+                    up[kind] = late[f"{step}_{kind}"]
         if step == 1:
             if relayed:
                 relay = permute(matrices[1], [(top, c, 0, c) for c in inner])
@@ -154,13 +162,23 @@
     for group in groups:
         whole = put(whole, group, shape, dtype)
 
-    def finish(whole, after):
-        if not top:
+    def finish(whole, turn, sections, after):
+        if turn not in late:
             return whole
-        other = swap(late)
-        pieces = shards(late, other, chips - 1, 0, 1, False)
-        pieces += shards(late, other, 1 - chips, chips - 1, chips, False)
-        return put(whole, [(1,) + piece for piece in pieces], shape, dtype, after)
+        other = swap(late[turn])
+
+        def here(piece):
+            kind, array, source, valid = piece
+
+            def both(rank):
+                section = lax.axis_index("section")
+                return valid(rank) & (section >= sections[0]) & (section < sections[1])
+
+            return kind, array, source, both
+
+        pieces = shards(late[turn], other, chips - 1, 0, 1)
+        pieces += shards(late[turn], other, 1 - chips, chips - 1, chips)
+        return put(whole, [here((1,) + piece) for piece in pieces], shape, dtype, after)
 
     return whole, finish
 
@@ -168,7 +186,7 @@
 def stage(whole, arriving, gates, held, early, *, section, first, block):
     width = arriving.shape[1]
     row_count, channels = gates.shape
-    lanes, deep = math.gcd(channels, 256), math.gcd(width, 512)
+    lanes, deep = channels, width // 2
     at = pl.ds(first, block)
     read = at if arriving.shape[0] == row_count else pl.ds(0, block)
 
@@ -316,7 +334,9 @@
                 *held, send = held
                 arriving[k] = lax.ppermute(send, "section", [(section, section - 1)])
         if section == sections - 1:
-            whole = finish(whole, held[:1])
+            whole = finish(whole, "late", (1, section), held[:1])
+        if section == min(1, sections - 1):
+            whole = finish(whole, "last", (0, 1), held[:1])
     value_grads, passed_rows = held
     projected = jnp.dot(value_grads.astype(jnp.float32), warm.T, precision=HIGHEST)
     factor = lax.dot_general(

time: 263 us -> 234 us (0.89)
  waiting for transfers between devices: 176 us -> 154 us
  Pallas kernels: 27.9 us -> 20.9 us
    ppermute x15 -> x12, waiting for transfers between devices: 45.6 us -> 31.4 us  [local(): arriving[k] = lax.ppermute(send, 'section', [(section, section - 1)])]
    ppermute x14 -> x15, waiting for transfers between devices: 111 us -> 103 us  [permute(): return lax.ppermute(value, ('section', 'dp'), pairs)]
    pallas_call x20 -> x16, Pallas kernels: 21.8 us -> 14.7 us  [stage(): pl.pallas_call(body, in_specs=[VMEM] * 3 + [ANY] + [VMEM] * len(held), ou...]
    ppermute x15 -> x12, starting transfers between devices: 13.2 us -> 10.6 us  [local(): arriving[k] = lax.ppermute(send, 'section', [(section, section - 1)])]
    ppermute x14 -> x15, starting transfers between devices: 24.5 us -> 26.1 us  [permute(): return lax.ppermute(value, ('section', 'dp'), pairs)]
  transfers between devices with their start and end apart: 48 -> 47, of which waited for: 20 -> 20; matrix products, arithmetic and copies ran while one was open for 4% -> 5% of each run, Pallas kernels for 8% -> 6%
where the time goes in v4:
time: 234 us; the launch traced here: 233 us
  waiting for transfers between devices  154 us (66%)
  starting transfers between devices  39.7 us (17%)
  Pallas kernels  20.9 us (9%)
  matrix products  9.32 us (4%)
  local copies, waits for them, and re-layouts  4.89 us (2%)
  other arithmetic  3.54 us (2%)
    ppermute x15, waiting for transfers between devices, permute(): return lax.ppermute(value, ('section', 'dp'), pairs)  103 us
    ppermute x12, waiting for transfers between devices, local(): arriving[k] = lax.ppermute(send, 'section', [(section, section - 1)])  31.4 us
    ppermute x15, starting transfers between devices, permute(): return lax.ppermute(value, ('section', 'dp'), pairs)  26.1 us
    ppermute x6, waiting for transfers between devices, exchange(): return lax.ppermute(value, 'dp', [(i, i ^ by) for i in range(replicas)])  19.5 us
    pallas_call x16, Pallas kernels, stage(): pl.pallas_call(body, in_specs=[VMEM] * 3 + [ANY] + [VMEM] * len(held), ou...  14.7 us
    ppermute x12, starting transfers between devices, local(): arriving[k] = lax.ppermute(send, 'section', [(section, section - 1)])  10.6 us
    dot_general x1, matrix products, local(): lax.dot_general(warm, error.astype(jnp.float32), (((1,), (1,)), ((), ()))...  8.01 us
    unnamed x32, local copies, waits for them, and re-layouts  4.89 us
  transfers between devices with their start and end apart: 47, of which 20 were waited for; matrix products, arithmetic and copies ran while one was open for 5% of the time, Pallas kernels for 6%

profile of v4, /device:TPU:0, one launch (start us, length us, event | category | flops | bytes accessed | tf_op | source)
XLA Modules:
  0.0 233.4 jit_solution(8482521564253545372)
XLA Ops:
  0.6 5.9 %collective-permute-start.2 = (bf16[320,1280]{1,0:T(8,128)(2,1)}, bf16[320,1280]{1,0:T(8,128)(2,1)}, u32[]{:S(2)}, u32[]{:S(2)}) collective-permute-start(bf16[320,1280]{1,0:T(8,128)(2,1)} %bitcast.40), channel_id=1, source_target_pairs={{0,2},{1,3},{2,4},{3,5},{4,6},{5,7},{8,10},{9,11},{10,12},{11,13},... | collective-permute-start | bytes 2457608 | tf_op jit(solution)/shard_map/ppermute | solution.py:74
  6.6 1.3 collective-permute-start
  7.8 5.4 %collective-permute-start.10 = (bf16[320,1280]{1,0:T(8,128)(2,1)}, bf16[320,1280]{1,0:T(8,128)(2,1)}, u32[]{:S(2)}, u32[]{:S(2)}) collective-permute-start(bf16[320,1280]{1,0:T(8,128)(2,1)} %bitcast.44), channel_id=1, source_target_pairs={{0,2},{1,3},{2,4},{3,5},{4,6},{5,7},{8,10},{9,11},{10,12},{11,13},... | collective-permute-start | bytes 2457608 | tf_op jit(solution)/shard_map/ppermute | solution.py:74
  13.3 1.3 collective-permute-start.8
  14.6 1.6 collective-permute-start.20
  16.2 8.3 %collective-permute-done.2.refs_7_ = bf16[320,1280]{1,0:T(8,128)(2,1)} collective-permute-done((bf16[320,1280]{1,0:T(8,128)(2,1)}, bf16[320,1280]{1,0:T(8,128)(2,1)}, u32[]{:S(2)}, u32[]{:S(2)}) %collective-permute-start.2) | collective-permute-done | bytes 819232 | tf_op jit(solution)/shard_map/ppermute | solution.py:74
  24.5 5.3 %collective-permute-done.refs_9_ = bf16[320,1280]{1,0:T(8,128)(2,1)} collective-permute-done((bf16[320,1280]{1,0:T(8,128)(2,1)}, bf16[320,1280]{1,0:T(8,128)(2,1)}, u32[]{:S(2)}, u32[]{:S(2)}) %collective-permute-start) | collective-permute-done | bytes 819232 | tf_op jit(solution)/shard_map/ppermute | solution.py:74
  29.9 11.1 %collective-permute-done.10.refs_3_ = bf16[320,1280]{1,0:T(8,128)(2,1)} collective-permute-done((bf16[320,1280]{1,0:T(8,128)(2,1)}, bf16[320,1280]{1,0:T(8,128)(2,1)}, u32[]{:S(2)}, u32[]{:S(2)}) %collective-permute-start.10) | collective-permute-done | bytes 819232 | tf_op jit(solution)/shard_map/ppermute | solution.py:74
  41.0 5.0 %collective-permute-done.8.refs_5_ = bf16[320,1280]{1,0:T(8,128)(2,1)} collective-permute-done((bf16[320,1280]{1,0:T(8,128)(2,1)}, bf16[320,1280]{1,0:T(8,128)(2,1)}, u32[]{:S(2)}, u32[]{:S(2)}) %collective-permute-start.8) | collective-permute-done | bytes 819232 | tf_op jit(solution)/shard_map/ppermute | solution.py:74
  46.0 0.7 collective-permute-start.3
  46.8 1.0 copy-done.6
  47.7 1.3 collective-permute-start.1
  49.0 2.7 %pad_maximum_fusion = bf16[2,320,1280]{2,1,0:T(8,128)(2,1)} fusion(bf16[1,320,1280]{2,1,0:T(8,128)(2,1)} %param.9, bf16[1,320,1280]{2,1,0:T(8,128)(2,1)} %param.10), kind=kLoop, calls=%fused_computation.1 | loop fusion | flops 819200 | bytes 3276800 | tf_op jit(solution)/shard_map/stack | solution.py:134
  51.7 0.9 copy-done.8
  53.1 0.9 copy-done.10
  54.0 0.7 collective-permute-start.11
  54.7 0.9 copy-done.12
  55.6 1.3 collective-permute-start.9
  56.9 1.3 collective-permute-start.21
  58.2 14.1 %collective-permute-done.1.refs_6_ = bf16[320,1280]{1,0:T(8,128)(2,1)S(1)} collective-permute-done((bf16[320,1280]{1,0:T(8,128)(2,1)}, bf16[320,1280]{1,0:T(8,128)(2,1)S(1)}, u32[]{:S(2)}, u32[]{:S(2)}) %collective-permute-start.1) | collective-permute-done | bytes 819232 | tf_op jit(solution)/shard_map/ppermute | solution.py:74
  72.5 0.6 collective-permute-start.19
  73.1 16.9 %collective-permute-done.9.refs_2_ = bf16[320,1280]{1,0:T(8,128)(2,1)S(1)} collective-permute-done((bf16[320,1280]{1,0:T(8,128)(2,1)}, bf16[320,1280]{1,0:T(8,128)(2,1)S(1)}, u32[]{:S(2)}, u32[]{:S(2)}) %collective-permute-start.9) | collective-permute-done | bytes 819232 | tf_op jit(solution)/shard_map/ppermute | solution.py:74
  90.1 16.9 %collective-permute-done.21 = bf16[320,1280]{1,0:T(8,128)(2,1)S(1)} collective-permute-done((bf16[320,1280]{1,0:T(8,128)(2,1)}, bf16[320,1280]{1,0:T(8,128)(2,1)S(1)}, u32[]{:S(2)}, u32[]{:S(2)}) %collective-permute-start.21) | collective-permute-done | bytes 819232 | tf_op jit(solution)/shard_map/ppermute | solution.py:74
  107.0 1.3 collective-permute-start.22
  108.4 0.7 collective-permute-start.14
  109.1 1.3 collective-permute-start.12
  110.5 0.7 collective-permute-start.6
  111.2 14.7 %collective-permute-done.22.refs_8_ = bf16[320,1280]{1,0:T(8,128)(2,1)S(1)} collective-permute-done((bf16[320,1280]{1,0:T(8,128)(2,1)S(1)}, bf16[320,1280]{1,0:T(8,128)(2,1)S(1)}, u32[]{:S(2)}, u32[]{:S(2)}) %collective-permute-start.22) | collective-permute-done | bytes 819232 | tf_op jit(solution)/shard_map/ppermute | solution.py:74
  126.4 4.4 %collective-permute-done.12.refs_0_ = bf16[320,1280]{1,0:T(8,128)(2,1)S(1)} collective-permute-done((bf16[320,1280]{1,0:T(8,128)(2,1)S(1)}, bf16[320,1280]{1,0:T(8,128)(2,1)S(1)}, u32[]{:S(2)}, u32[]{:S(2)}) %collective-permute-start.12) | collective-permute-done | bytes 819232 | tf_op jit(solution)/shard_map/ppermute | solution.py:74
  130.8 1.3 collective-permute-start.4
  132.7 8.0 %fusion.2.early = f32[4,2560]{1,0:T(4,128)S(1)} fusion(f32[1,4,1280]{2,1,0:T(4,128)S(1)} %copy-done, bf16[1,2560,1280]{2,1,0:T(8,128)(2,1)} %param.11), kind=kOutput, calls=%fused_computation.6 | convolution fusion | flops 157286400 | bytes 6615040 | tf_op jit(solution)/shard_map/dot_general | solution.py:319
  140.8 2.2 put.5.refs_10_
  143.9 0.7 copy-done.1
  145.1 0.7 collective-permute-start.32
  145.8 0.7 collective-permute-start.31
  146.5 0.7 collective-permute-start.30
  147.4 6.0 %collective-permute-done.4.refs_0_ = bf16[320,1280]{1,0:T(8,128)(2,1)S(1)} collective-permute-done((bf16[320,1280]{1,0:T(8,128)(2,1)S(1)}, bf16[320,1280]{1,0:T(8,128)(2,1)S(1)}, u32[]{:S(2)}, u32[]{:S(2)}) %collective-permute-start.4) | collective-permute-done | bytes 819232 | tf_op jit(solution)/shard_map/ppermute | solution.py:74
  153.3 0.7 collective-permute-start.29
  154.2 0.7 collective-permute-start.36
  154.9 0.7 collective-permute-start.35
  155.7 0.7 collective-permute-start.34
  156.4 0.7 collective-permute-start.33
  157.1 1.3 collective-permute-start.40
  158.5 1.3 collective-permute-start.39
  159.8 1.3 collective-permute-start.38
  161.4 1.3 collective-permute-start.37
  162.9 20.2 %collective-permute-done.40.arr = bf16[64,2560]{1,0:T(8,128)(2,1)S(1)} collective-permute-done((bf16[64,2560]{1,0:T(8,128)(2,1)S(1)}, bf16[64,2560]{1,0:T(8,128)(2,1)S(1)}, u32[]{:S(2)}, u32[]{:S(2)}) %collective-permute-start.40) | collective-permute-done | bytes 327712 | tf_op jit(solution)/shard_map/ppermute | solution.py:335
  183.2 3.5 %shard_map.106 = (bf16[256,1280]{1,0:T(8,128)(2,1)S(1)}, bf16[256,2560]{1,0:T(8,128)(2,1)S(1)}) custom-call(bf16[2,2560,1280]{2,1,0:T(8,128)(2,1)S(1)} %put.9.w, bf16[64,2560]{1,0:T(8,128)(2,1)S(1)} %collective-permute-done.40.arr, bf16[256,1280]{1,0:T(8,128)(2,1)S(1)} %bitcast.32, ...), custom_call_target="tpu_custom_call", output_to_operand_aliasing={{0}: (4, {}), {1}: (5, {})} | custom-call | flops 838860800 | bytes 13107200 | tf_op jit(solution)/shard_map/pallas_call | solution.py:228
  186.7 3.5 %collective-permute-done.39.arr = bf16[64,2560]{1,0:T(8,128)(2,1)S(1)} collective-permute-done((bf16[64,2560]{1,0:T(8,128)(2,1)S(1)}, bf16[64,2560]{1,0:T(8,128)(2,1)S(1)}, u32[]{:S(2)}, u32[]{:S(2)}) %collective-permute-start.39) | collective-permute-done | bytes 327712 | tf_op jit(solution)/shard_map/ppermute | solution.py:335
  190.2 3.5 %shard_map.107 = (bf16[256,1280]{1,0:T(8,128)(2,1)S(1)}, bf16[256,2560]{1,0:T(8,128)(2,1)S(1)}) custom-call(bf16[2,2560,1280]{2,1,0:T(8,128)(2,1)S(1)} %put.9.w, bf16[64,2560]{1,0:T(8,128)(2,1)S(1)} %collective-permute-done.39.arr, bf16[256,1280]{1,0:T(8,128)(2,1)S(1)} %bitcast.33, ...), custom_call_target="tpu_custom_call", output_to_operand_aliasing={{0}: (4, {}), {1}: (5, {})} | custom-call | flops 838860800 | bytes 13107200 | tf_op jit(solution)/shard_map/pallas_call | solution.py:228
  193.7 3.5 %collective-permute-done.38.arr = bf16[64,2560]{1,0:T(8,128)(2,1)S(1)} collective-permute-done((bf16[64,2560]{1,0:T(8,128)(2,1)S(1)}, bf16[64,2560]{1,0:T(8,128)(2,1)S(1)}, u32[]{:S(2)}, u32[]{:S(2)}) %collective-permute-start.38) | collective-permute-done | bytes 327712 | tf_op jit(solution)/shard_map/ppermute | solution.py:335
  197.2 3.5 %shard_map.108 = (bf16[256,1280]{1,0:T(8,128)(2,1)S(1)}, bf16[256,2560]{1,0:T(8,128)(2,1)S(1)}) custom-call(bf16[2,2560,1280]{2,1,0:T(8,128)(2,1)S(1)} %put.9.w, bf16[64,2560]{1,0:T(8,128)(2,1)S(1)} %collective-permute-done.38.arr, bf16[256,1280]{1,0:T(8,128)(2,1)S(1)} %bitcast.34, ...), custom_call_target="tpu_custom_call", output_to_operand_aliasing={{0}: (4, {}), {1}: (5, {})} | custom-call | flops 838860800 | bytes 13107200 | tf_op jit(solution)/shard_map/pallas_call | solution.py:228
  200.7 4.2 %collective-permute-done.37.arr = bf16[64,2560]{1,0:T(8,128)(2,1)S(1)} collective-permute-done((bf16[64,2560]{1,0:T(8,128)(2,1)S(1)}, bf16[64,2560]{1,0:T(8,128)(2,1)S(1)}, u32[]{:S(2)}, u32[]{:S(2)}) %collective-permute-start.37) | collective-permute-done | bytes 327712 | tf_op jit(solution)/shard_map/ppermute | solution.py:335
  204.9 3.5 %shard_map.109 = (bf16[256,1280]{1,0:T(8,128)(2,1)S(1)}, bf16[256,2560]{1,0:T(8,128)(2,1)S(1)}) custom-call(bf16[2,2560,1280]{2,1,0:T(8,128)(2,1)S(1)} %put.9.w, bf16[64,2560]{1,0:T(8,128)(2,1)S(1)} %collective-permute-done.37.arr, bf16[256,1280]{1,0:T(8,128)(2,1)S(1)} %bitcast.35, ...), custom_call_target="tpu_custom_call", output_to_operand_aliasing={{0}: (4, {}), {1}: (5, {})} | custom-call | flops 838860800 | bytes 13107200 | tf_op jit(solution)/shard_map/pallas_call | solution.py:228
  208.4 0.7 fusion
  209.1 0.7 convolution_add_fusion
  209.8 1.2 collective-permute-done.41
  211.2 3.8 %collective-permute-done.42 = f32[4,2560]{1,0:T(4,128)S(1)} collective-permute-done((f32[4,2560]{1,0:T(4,128)S(1)}, f32[4,2560]{1,0:T(4,128)S(1)}, u32[]{:S(2)}, u32[]{:S(2)}) %collective-permute-start.42) | collective-permute-done | bytes 40992 | tf_op jit(solution)/shard_map/ppermute | solution.py:303
  215.2 4.9 %collective-permute-done.43.right = f32[4,2560]{1,0:T(4,128)S(1)} collective-permute-done((f32[4,2560]{1,0:T(4,128)S(1)}, f32[4,2560]{1,0:T(4,128)S(1)}, u32[]{:S(2)}, u32[]{:S(2)}) %collective-permute-start.43) | collective-permute-done | bytes 40992 | tf_op jit(solution)/shard_map/ppermute | solution.py:303
  220.1 2.8 %second_half.1 = (f32[4,2560]{1,0:T(4,128)}, f32[4,1280]{1,0:T(4,128)S(1)}, bf16[256,2560]{1,0:T(8,128)(2,1)}) custom-call(f32[4,2560]{1,0:T(4,128)S(1)} %add.20.left, f32[4,2560]{1,0:T(4,128)S(1)} %collective-permute-done.43.right, bf16[256,2560]{1,0:T(8,128)(2,1)S(1)} %bitcast.39, bf16[256,1280]{1,0:T(8,128)(2,1)S(1)} %get-tuple-element.92.vg, ...), custom_call_target="tpu_custom_call" | custom-call | tf_op jit(solution)/shard_map/second_half/pallas_call | solution.py:286
  223.0 1.2 collective-permute-done.44
  224.4 3.7 %collective-permute-done.45 = f32[4,1280]{1,0:T(4,128)S(1)} collective-permute-done((f32[4,1280]{1,0:T(4,128)S(1)}, f32[4,1280]{1,0:T(4,128)S(1)}, u32[]{:S(2)}, u32[]{:S(2)}) %collective-permute-start.45) | collective-permute-done | bytes 20512 | tf_op jit(solution)/shard_map/ppermute | solution.py:303
  228.1 4.7 %collective-permute-done.46 = f32[4,1280]{1,0:T(4,128)S(1)} collective-permute-done((f32[4,1280]{1,0:T(4,128)S(1)}, f32[4,1280]{1,0:T(4,128)S(1)}, u32[]{:S(2)}, u32[]{:S(2)}) %collective-permute-start.46) | collective-permute-done | bytes 20512 | tf_op jit(solution)/shard_map/ppermute | solution.py:303
  232.8 0.6 multiply_bitcast_fusion
  (96 shorter events, 5.0 us)
Async XLA Ops:
  0.6 132.1 %copy-start = (f32[1,4,1280]{2,1,0:T(4,128)S(1)}, f32[1,4,1280]{2,1,0:T(4,128)}, u32[]{:S(2)}) copy-start(f32[1,4,1280]{2,1,0:T(4,128)} %param.13) | copy-start | bytes 61444
  0.6 23.9 %collective-permute-start.2 = (bf16[320,1280]{1,0:T(8,128)(2,1)}, bf16[320,1280]{1,0:T(8,128)(2,1)}, u32[]{:S(2)}, u32[]{:S(2)}) collective-permute-start(bf16[320,1280]{1,0:T(8,128)(2,1)} %bitcast.40), channel_id=1, source_target_pairs={{0,2},{1,3},{2,4},{3,5},{4,6},{5,7},{8,10},{9,11},{10,12},{11,13},... | collective-permute-start | bytes 2457608 | tf_op jit(solution)/shard_map/ppermute | solution.py:74
  6.6 23.3 %collective-permute-start = (bf16[320,1280]{1,0:T(8,128)(2,1)}, bf16[320,1280]{1,0:T(8,128)(2,1)}, u32[]{:S(2)}, u32[]{:S(2)}) collective-permute-start(bf16[320,1280]{1,0:T(8,128)(2,1)} %bitcast.41), channel_id=1, source_target_pairs={{2,0},{3,1},{4,2},{5,3},{6,4},{7,5},{10,8},{11,9},{12,10},{13,11},... | collective-permute-start | bytes 2457608 | tf_op jit(solution)/shard_map/ppermute | solution.py:74
  7.8 33.1 %collective-permute-start.10 = (bf16[320,1280]{1,0:T(8,128)(2,1)}, bf16[320,1280]{1,0:T(8,128)(2,1)}, u32[]{:S(2)}, u32[]{:S(2)}) collective-permute-start(bf16[320,1280]{1,0:T(8,128)(2,1)} %bitcast.44), channel_id=1, source_target_pairs={{0,2},{1,3},{2,4},{3,5},{4,6},{5,7},{8,10},{9,11},{10,12},{11,13},... | collective-permute-start | bytes 2457608 | tf_op jit(solution)/shard_map/ppermute | solution.py:74
  13.3 32.7 %collective-permute-start.8 = (bf16[320,1280]{1,0:T(8,128)(2,1)}, bf16[320,1280]{1,0:T(8,128)(2,1)}, u32[]{:S(2)}, u32[]{:S(2)}) collective-permute-start(bf16[320,1280]{1,0:T(8,128)(2,1)} %bitcast.45), channel_id=1, source_target_pairs={{2,0},{3,1},{4,2},{5,3},{6,4},{7,5},{10,8},{11,9},{12,10},{13,11},... | collective-permute-start | bytes 2457608 | tf_op jit(solution)/shard_map/ppermute | solution.py:74
  14.6 31.4 %collective-permute-start.20 = (bf16[320,1280]{1,0:T(8,128)(2,1)}, bf16[320,1280]{1,0:T(8,128)(2,1)}, u32[]{:S(2)}, u32[]{:S(2)}) collective-permute-start(bf16[320,1280]{1,0:T(8,128)(2,1)} %bitcast.42), channel_id=1, source_target_pairs={{26,2},{27,3},{28,4},{29,5}} | collective-permute-start | bytes 2457608 | tf_op jit(solution)/shard_map/ppermute | solution.py:74
  24.5 22.2 %collective-permute-start.27 = (bf16[320,1280]{1,0:T(8,128)(2,1)}, bf16[320,1280]{1,0:T(8,128)(2,1)S(1)}, u32[]{:S(2)}, u32[]{:S(2)}) collective-permute-start(bf16[320,1280]{1,0:T(8,128)(2,1)} %collective-permute-done.2.refs_7_), channel_id=1, source_target_pairs={{0,1},{1,0},{2,3},{3,2},{4,5},{5,4},{6,7},{7,6},{8,9},{9,8},{10,11... | collective-permute-start | bytes 2457608 | tf_op jit(solution)/shard_map/ppermute | solution.py:82
  29.9 21.8 %collective-permute-start.28 = (bf16[320,1280]{1,0:T(8,128)(2,1)}, bf16[320,1280]{1,0:T(8,128)(2,1)S(1)}, u32[]{:S(2)}, u32[]{:S(2)}) collective-permute-start(bf16[320,1280]{1,0:T(8,128)(2,1)} %collective-permute-done.refs_9_), channel_id=1, source_target_pairs={{0,1},{1,0},{2,3},{3,2},{4,5},{5,4},{6,7},{7,6},{8,9},{9,8},{10,11... | collective-permute-start | bytes 2457608 | tf_op jit(solution)/shard_map/ppermute | solution.py:82
  41.0 12.1 %collective-permute-start.25 = (bf16[320,1280]{1,0:T(8,128)(2,1)}, bf16[320,1280]{1,0:T(8,128)(2,1)S(1)}, u32[]{:S(2)}, u32[]{:S(2)}) collective-permute-start(bf16[320,1280]{1,0:T(8,128)(2,1)} %collective-permute-done.10.refs_3_), channel_id=1, source_target_pairs={{0,1},{1,0},{2,3},{3,2},{4,5},{5,4},{6,7},{7,6},{8,9},{9,8},{10,11... | collective-permute-start | bytes 2457608 | tf_op jit(solution)/shard_map/ppermute | solution.py:82
  46.0 8.7 %collective-permute-start.26 = (bf16[320,1280]{1,0:T(8,128)(2,1)}, bf16[320,1280]{1,0:T(8,128)(2,1)S(1)}, u32[]{:S(2)}, u32[]{:S(2)}) collective-permute-start(bf16[320,1280]{1,0:T(8,128)(2,1)} %collective-permute-done.8.refs_5_), channel_id=1, source_target_pairs={{0,1},{1,0},{2,3},{3,2},{4,5},{5,4},{6,7},{7,6},{8,9},{9,8},{10,11... | collective-permute-start | bytes 2457608 | tf_op jit(solution)/shard_map/ppermute | solution.py:82
  46.0 10.9 %collective-permute-start.3 = (bf16[320,1280]{1,0:T(8,128)(2,1)}, bf16[320,1280]{1,0:T(8,128)(2,1)S(1)}, u32[]{:S(2)}, u32[]{:S(2)}) collective-permute-start(bf16[320,1280]{1,0:T(8,128)(2,1)} %collective-permute-done.2.refs_7_), channel_id=1, source_target_pairs={{2,4},{3,5},{4,6},{5,7},{10,12},{11,13},{12,14},{13,15},{18,20},{1... | collective-permute-start | bytes 2457608 | tf_op jit(solution)/shard_map/ppermute | solution.py:74
  46.7 1.0 copy-start.6
  47.7 24.7 %collective-permute-start.1 = (bf16[320,1280]{1,0:T(8,128)(2,1)}, bf16[320,1280]{1,0:T(8,128)(2,1)S(1)}, u32[]{:S(2)}, u32[]{:S(2)}) collective-permute-start(bf16[320,1280]{1,0:T(8,128)(2,1)} %collective-permute-done.refs_9_), channel_id=1, source_target_pairs={{2,0},{3,1},{4,2},{5,3},{10,8},{11,9},{12,10},{13,11},{18,16},{19,... | collective-permute-start | bytes 2457608 | tf_op jit(solution)/shard_map/ppermute | solution.py:74
  51.7 0.9 copy-start.8
  52.6 55.8 %collective-permute-start.24 = (bf16[2,320,1280]{2,1,0:T(8,128)(2,1)}, bf16[2,320,1280]{2,1,0:T(8,128)(2,1)}, u32[]{:S(2)}, u32[]{:S(2)}) collective-permute-start(bf16[2,320,1280]{2,1,0:T(8,128)(2,1)} %pad_maximum_fusion), channel_id=1, source_target_pairs={{0,1},{1,0},{2,3},{3,2},{4,5},{5,4},{6,7},{7,6},{8,9},{9,8},{10,11... | collective-permute-start | bytes 4915208 | tf_op jit(solution)/shard_map/ppermute | solution.py:82
  53.1 0.9 copy-start.10
  54.0 18.5 %collective-permute-start.11 = (bf16[320,1280]{1,0:T(8,128)(2,1)}, bf16[320,1280]{1,0:T(8,128)(2,1)S(1)}, u32[]{:S(2)}, u32[]{:S(2)}) collective-permute-start(bf16[320,1280]{1,0:T(8,128)(2,1)} %collective-permute-done.10.refs_3_), channel_id=1, source_target_pairs={{2,4},{3,5},{4,6},{5,7},{10,12},{11,13},{12,14},{13,15},{18,20},{1... | collective-permute-start | bytes 2457608 | tf_op jit(solution)/shard_map/ppermute | solution.py:74
  54.7 0.9 copy-start.12
  55.6 34.3 %collective-permute-start.9 = (bf16[320,1280]{1,0:T(8,128)(2,1)}, bf16[320,1280]{1,0:T(8,128)(2,1)S(1)}, u32[]{:S(2)}, u32[]{:S(2)}) collective-permute-start(bf16[320,1280]{1,0:T(8,128)(2,1)} %collective-permute-done.8.refs_5_), channel_id=1, source_target_pairs={{2,0},{3,1},{4,2},{5,3},{10,8},{11,9},{12,10},{13,11},{18,16},{19,... | collective-permute-start | bytes 2457608 | tf_op jit(solution)/shard_map/ppermute | solution.py:74
  56.9 50.1 %collective-permute-start.21 = (bf16[320,1280]{1,0:T(8,128)(2,1)}, bf16[320,1280]{1,0:T(8,128)(2,1)S(1)}, u32[]{:S(2)}, u32[]{:S(2)}) collective-permute-start(bf16[320,1280]{1,0:T(8,128)(2,1)} %collective-permute-done.20), channel_id=1, source_target_pairs={{2,0},{3,1},{4,6},{5,7}} | collective-permute-start | bytes 2457608 | tf_op jit(solution)/shard_map/ppermute | solution.py:74
  72.4 36.7 %collective-permute-start.18 = (bf16[320,1280]{1,0:T(8,128)(2,1)S(1)}, bf16[320,1280]{1,0:T(8,128)(2,1)S(1)}, u32[]{:S(2)}, u32[]{:S(2)}) collective-permute-start(bf16[320,1280]{1,0:T(8,128)(2,1)S(1)} %collective-permute-done.3.refs_4_), channel_id=1, source_target_pairs={{0,1},{1,0},{2,3},{3,2},{4,5},{5,4},{6,7},{7,6},{8,9},{9,8},{10,11... | collective-permute-start | bytes 2457608 | tf_op jit(solution)/shard_map/ppermute | solution.py:82
  72.5 37.9 %collective-permute-start.19 = (bf16[320,1280]{1,0:T(8,128)(2,1)S(1)}, bf16[320,1280]{1,0:T(8,128)(2,1)S(1)}, u32[]{:S(2)}, u32[]{:S(2)}) collective-permute-start(bf16[320,1280]{1,0:T(8,128)(2,1)S(1)} %collective-permute-done.1.refs_6_), channel_id=1, source_target_pairs={{0,1},{1,0},{2,3},{3,2},{4,5},{5,4},{6,7},{7,6},{8,9},{9,8},{10,11... | collective-permute-start | bytes 2457608 | tf_op jit(solution)/shard_map/ppermute | solution.py:82
  89.9 20.6 %collective-permute-start.16 = (bf16[320,1280]{1,0:T(8,128)(2,1)S(1)}, bf16[320,1280]{1,0:T(8,128)(2,1)S(1)}, u32[]{:S(2)}, u32[]{:S(2)}) collective-permute-start(bf16[320,1280]{1,0:T(8,128)(2,1)S(1)} %collective-permute-done.11.refs_0_), channel_id=1, source_target_pairs={{0,1},{1,0},{2,3},{3,2},{4,5},{5,4},{6,7},{7,6},{8,9},{9,8},{10,11... | collective-permute-start | bytes 2457608 | tf_op jit(solution)/shard_map/ppermute | solution.py:82
  90.0 50.7 %copy-start.4 = (bf16[1,320,1280]{2,1,0:T(8,128)(2,1)S(1)}, bf16[1,320,1280]{2,1,0:T(8,128)(2,1)}, u32[]{:S(2)}) copy-start(bf16[1,320,1280]{2,1,0:T(8,128)(2,1)} %param.9) | copy-start | bytes 2457604
  90.0 50.7 %copy-start.5 = (bf16[1,320,1280]{2,1,0:T(8,128)(2,1)S(1)}, bf16[1,320,1280]{2,1,0:T(8,128)(2,1)}, u32[]{:S(2)}) copy-start(bf16[1,320,1280]{2,1,0:T(8,128)(2,1)} %param.10) | copy-start | bytes 2457604
  90.1 50.7 %copy-start.7 = (bf16[320,1280]{1,0:T(8,128)(2,1)S(1)}, bf16[320,1280]{1,0:T(8,128)(2,1)}, u32[]{:S(2)}) copy-start(bf16[320,1280]{1,0:T(8,128)(2,1)} %copy-done.6) | copy-start | bytes 2457604
  90.1 50.7 %copy-start.9 = (bf16[320,1280]{1,0:T(8,128)(2,1)S(1)}, bf16[320,1280]{1,0:T(8,128)(2,1)}, u32[]{:S(2)}) copy-start(bf16[320,1280]{1,0:T(8,128)(2,1)} %copy-done.8) | copy-start | bytes 2457604
  90.1 50.7 %copy-start.11 = (bf16[320,1280]{1,0:T(8,128)(2,1)S(1)}, bf16[320,1280]{1,0:T(8,128)(2,1)}, u32[]{:S(2)}) copy-start(bf16[320,1280]{1,0:T(8,128)(2,1)} %copy-done.10) | copy-start | bytes 2457604
  90.1 50.7 %copy-start.13 = (bf16[320,1280]{1,0:T(8,128)(2,1)S(1)}, bf16[320,1280]{1,0:T(8,128)(2,1)}, u32[]{:S(2)}) copy-start(bf16[320,1280]{1,0:T(8,128)(2,1)} %copy-done.12) | copy-start | bytes 2457604
  107.0 18.9 %collective-permute-start.22 = (bf16[320,1280]{1,0:T(8,128)(2,1)S(1)}, bf16[320,1280]{1,0:T(8,128)(2,1)S(1)}, u32[]{:S(2)}, u32[]{:S(2)}) collective-permute-start(bf16[320,1280]{1,0:T(8,128)(2,1)S(1)} %collective-permute-done.21), channel_id=1, source_target_pairs={{0,24},{1,25},{6,30},{7,31}} | collective-permute-start | bytes 2457608 | tf_op jit(solution)/shard_map/ppermute | solution.py:74
  108.4 17.5 %collective-permute-start.14 = (bf16[320,1280]{1,0:T(8,128)(2,1)S(1)}, bf16[320,1280]{1,0:T(8,128)(2,1)S(1)}, u32[]{:S(2)}, u32[]{:S(2)}) collective-permute-start(bf16[320,1280]{1,0:T(8,128)(2,1)S(1)} %broadcast_select_fusion.1), channel_id=1, source_target_pairs={{26,24},{27,25},{28,30},{29,31}} | collective-permute-start | bytes 2457608 | tf_op jit(solution)/shard_map/ppermute | solution.py:74
  109.1 21.7 %collective-permute-start.12 = (bf16[320,1280]{1,0:T(8,128)(2,1)S(1)}, bf16[320,1280]{1,0:T(8,128)(2,1)S(1)}, u32[]{:S(2)}, u32[]{:S(2)}) collective-permute-start(bf16[320,1280]{1,0:T(8,128)(2,1)S(1)} %broadcast_select_fusion), channel_id=1, source_target_pairs={{2,0},{3,1},{4,6},{5,7},{10,8},{11,9},{12,14},{13,15},{18,16},{19,... | collective-permute-start | bytes 2457608 | tf_op jit(solution)/shard_map/ppermute | solution.py:74
  110.4 20.4 %collective-permute-start.17 = (bf16[320,1280]{1,0:T(8,128)(2,1)S(1)}, bf16[320,1280]{1,0:T(8,128)(2,1)S(1)}, u32[]{:S(2)}, u32[]{:S(2)}) collective-permute-start(bf16[320,1280]{1,0:T(8,128)(2,1)S(1)} %collective-permute-done.9.refs_2_), channel_id=1, source_target_pairs={{0,1},{1,0},{2,3},{3,2},{4,5},{5,4},{6,7},{7,6},{8,9},{9,8},{10,11... | collective-permute-start | bytes 2457608 | tf_op jit(solution)/shard_map/ppermute | solution.py:82
  110.5 21.6 %collective-permute-start.6 = (bf16[320,1280]{1,0:T(8,128)(2,1)S(1)}, bf16[320,1280]{1,0:T(8,128)(2,1)S(1)}, u32[]{:S(2)}, u32[]{:S(2)}) collective-permute-start(bf16[320,1280]{1,0:T(8,128)(2,1)S(1)} %broadcast_select_fusion.1), channel_id=1, source_target_pairs={{10,8},{11,9},{12,14},{13,15},{18,16},{19,17},{20,22},{21,23}} | collective-permute-start | bytes 2457608 | tf_op jit(solution)/shard_map/ppermute | solution.py:74
  125.9 17.1 %collective-permute-start.23 = (bf16[320,1280]{1,0:T(8,128)(2,1)S(1)}, bf16[320,1280]{1,0:T(8,128)(2,1)S(1)}, u32[]{:S(2)}, u32[]{:S(2)}) collective-permute-start(bf16[320,1280]{1,0:T(8,128)(2,1)S(1)} %collective-permute-done.22.refs_8_), channel_id=1, source_target_pairs={{0,1},{1,0},{2,3},{3,2},{4,5},{5,4},{6,7},{7,6},{8,9},{9,8},{10,11... | collective-permute-start | bytes 2457608 | tf_op jit(solution)/shard_map/ppermute | solution.py:82
  125.9 17.7 %collective-permute-start.15 = (bf16[320,1280]{1,0:T(8,128)(2,1)S(1)}, bf16[320,1280]{1,0:T(8,128)(2,1)S(1)}, u32[]{:S(2)}, u32[]{:S(2)}) collective-permute-start(bf16[320,1280]{1,0:T(8,128)(2,1)S(1)} %collective-permute-done.14.refs_2_), channel_id=1, source_target_pairs={{0,1},{1,0},{2,3},{3,2},{4,5},{5,4},{6,7},{7,6},{8,9},{9,8},{10,11... | collective-permute-start | bytes 2457608 | tf_op jit(solution)/shard_map/ppermute | solution.py:82
  130.8 12.8 %collective-permute-start.13 = (bf16[320,1280]{1,0:T(8,128)(2,1)S(1)}, bf16[320,1280]{1,0:T(8,128)(2,1)S(1)}, u32[]{:S(2)}, u32[]{:S(2)}) collective-permute-start(bf16[320,1280]{1,0:T(8,128)(2,1)S(1)} %collective-permute-done.12.refs_0_), channel_id=1, source_target_pairs={{0,1},{1,0},{2,3},{3,2},{4,5},{5,4},{6,7},{7,6},{8,9},{9,8},{10,11... | collective-permute-start | bytes 2457608 | tf_op jit(solution)/shard_map/ppermute | solution.py:82
  130.8 22.5 %collective-permute-start.4 = (bf16[320,1280]{1,0:T(8,128)(2,1)S(1)}, bf16[320,1280]{1,0:T(8,128)(2,1)S(1)}, u32[]{:S(2)}, u32[]{:S(2)}) collective-permute-start(bf16[320,1280]{1,0:T(8,128)(2,1)S(1)} %broadcast_select_fusion.1), channel_id=1, source_target_pairs={{2,0},{3,1},{4,6},{5,7}} | collective-permute-start | bytes 2457608 | tf_op jit(solution)/shard_map/ppermute | solution.py:74
  132.1 21.9 %collective-permute-start.7 = (bf16[320,1280]{1,0:T(8,128)(2,1)S(1)}, bf16[320,1280]{1,0:T(8,128)(2,1)S(1)}, u32[]{:S(2)}, u32[]{:S(2)}) collective-permute-start(bf16[320,1280]{1,0:T(8,128)(2,1)S(1)} %collective-permute-done.6.refs_0_), channel_id=1, source_target_pairs={{0,1},{1,0},{2,3},{3,2},{4,5},{5,4},{6,7},{7,6},{8,9},{9,8},{10,11... | collective-permute-start | bytes 2457608 | tf_op jit(solution)/shard_map/ppermute | solution.py:82
  143.5 1.1 copy-start.1
  143.6 1.5 copy-start.2
  145.1 9.1 %collective-permute-start.32 = (bf16[64,2560]{1,0:T(8,128)(2,1)S(1)}, bf16[64,2560]{1,0:T(8,128)(2,1)S(1)}, u32[]{:S(2)}, u32[]{:S(2)}) collective-permute-start(bf16[64,2560]{1,0:T(8,128)(2,1)S(1)} %get-tuple-element.60), channel_id=1, source_target_pairs={{24,16},{25,17},{26,18},{27,19},{28,20},{29,21},{30,22},{31,23}} | collective-permute-start | bytes 983048 | tf_op jit(solution)/shard_map/ppermute | solution.py:335
  145.8 9.1 %collective-permute-start.31 = (bf16[64,2560]{1,0:T(8,128)(2,1)S(1)}, bf16[64,2560]{1,0:T(8,128)(2,1)S(1)}, u32[]{:S(2)}, u32[]{:S(2)}) collective-permute-start(bf16[64,2560]{1,0:T(8,128)(2,1)S(1)} %get-tuple-element.59), channel_id=1, source_target_pairs={{24,16},{25,17},{26,18},{27,19},{28,20},{29,21},{30,22},{31,23}} | collective-permute-start | bytes 983048 | tf_op jit(solution)/shard_map/ppermute | solution.py:335
  146.5 9.1 %collective-permute-start.30 = (bf16[64,2560]{1,0:T(8,128)(2,1)S(1)}, bf16[64,2560]{1,0:T(8,128)(2,1)S(1)}, u32[]{:S(2)}, u32[]{:S(2)}) collective-permute-start(bf16[64,2560]{1,0:T(8,128)(2,1)S(1)} %get-tuple-element.58), channel_id=1, source_target_pairs={{24,16},{25,17},{26,18},{27,19},{28,20},{29,21},{30,22},{31,23}} | collective-permute-start | bytes 983048 | tf_op jit(solution)/shard_map/ppermute | solution.py:335
  153.3 3.0 %collective-permute-start.29 = (bf16[64,2560]{1,0:T(8,128)(2,1)S(1)}, bf16[64,2560]{1,0:T(8,128)(2,1)S(1)}, u32[]{:S(2)}, u32[]{:S(2)}) collective-permute-start(bf16[64,2560]{1,0:T(8,128)(2,1)S(1)} %get-tuple-element.57), channel_id=1, source_target_pairs={{24,16},{25,17},{26,18},{27,19},{28,20},{29,21},{30,22},{31,23}} | collective-permute-start | bytes 983048 | tf_op jit(solution)/shard_map/ppermute | solution.py:335
  154.0 8.6 %collective-permute-start.5 = (bf16[320,1280]{1,0:T(8,128)(2,1)S(1)}, bf16[320,1280]{1,0:T(8,128)(2,1)S(1)}, u32[]{:S(2)}, u32[]{:S(2)}) collective-permute-start(bf16[320,1280]{1,0:T(8,128)(2,1)S(1)} %collective-permute-done.4.refs_0_), channel_id=1, source_target_pairs={{0,1},{1,0},{2,3},{3,2},{4,5},{5,4},{6,7},{7,6},{8,9},{9,8},{10,11... | collective-permute-start | bytes 2457608 | tf_op jit(solution)/shard_map/ppermute | solution.py:82
  154.2 2.9 %collective-permute-start.36 = (bf16[64,2560]{1,0:T(8,128)(2,1)S(1)}, bf16[64,2560]{1,0:T(8,128)(2,1)S(1)}, u32[]{:S(2)}, u32[]{:S(2)}) collective-permute-start(bf16[64,2560]{1,0:T(8,128)(2,1)S(1)} %get-tuple-element.71), channel_id=1, source_target_pairs={{16,8},{17,9},{18,10},{19,11},{20,12},{21,13},{22,14},{23,15}} | collective-permute-start | bytes 983048 | tf_op jit(solution)/shard_map/ppermute | solution.py:335
  154.9 3.5 %collective-permute-start.35 = (bf16[64,2560]{1,0:T(8,128)(2,1)S(1)}, bf16[64,2560]{1,0:T(8,128)(2,1)S(1)}, u32[]{:S(2)}, u32[]{:S(2)}) collective-permute-start(bf16[64,2560]{1,0:T(8,128)(2,1)S(1)} %get-tuple-element.70), channel_id=1, source_target_pairs={{16,8},{17,9},{18,10},{19,11},{20,12},{21,13},{22,14},{23,15}} | collective-permute-start | bytes 983048 | tf_op jit(solution)/shard_map/ppermute | solution.py:335
  155.7 4.1 %collective-permute-start.34 = (bf16[64,2560]{1,0:T(8,128)(2,1)S(1)}, bf16[64,2560]{1,0:T(8,128)(2,1)S(1)}, u32[]{:S(2)}, u32[]{:S(2)}) collective-permute-start(bf16[64,2560]{1,0:T(8,128)(2,1)S(1)} %get-tuple-element.69), channel_id=1, source_target_pairs={{16,8},{17,9},{18,10},{19,11},{20,12},{21,13},{22,14},{23,15}} | collective-permute-start | bytes 983048 | tf_op jit(solution)/shard_map/ppermute | solution.py:335
  156.4 4.7 %collective-permute-start.33 = (bf16[64,2560]{1,0:T(8,128)(2,1)S(1)}, bf16[64,2560]{1,0:T(8,128)(2,1)S(1)}, u32[]{:S(2)}, u32[]{:S(2)}) collective-permute-start(bf16[64,2560]{1,0:T(8,128)(2,1)S(1)} %get-tuple-element.68), channel_id=1, source_target_pairs={{16,8},{17,9},{18,10},{19,11},{20,12},{21,13},{22,14},{23,15}} | collective-permute-start | bytes 983048 | tf_op jit(solution)/shard_map/ppermute | solution.py:335
  157.1 26.0 %collective-permute-start.40 = (bf16[64,2560]{1,0:T(8,128)(2,1)S(1)}, bf16[64,2560]{1,0:T(8,128)(2,1)S(1)}, u32[]{:S(2)}, u32[]{:S(2)}) collective-permute-start(bf16[64,2560]{1,0:T(8,128)(2,1)S(1)} %get-tuple-element.84), channel_id=1, source_target_pairs={{8,0},{9,1},{10,2},{11,3},{12,4},{13,5},{14,6},{15,7}} | collective-permute-start | bytes 983048 | tf_op jit(solution)/shard_map/ppermute | solution.py:335
  158.5 31.7 %collective-permute-start.39 = (bf16[64,2560]{1,0:T(8,128)(2,1)S(1)}, bf16[64,2560]{1,0:T(8,128)(2,1)S(1)}, u32[]{:S(2)}, u32[]{:S(2)}) collective-permute-start(bf16[64,2560]{1,0:T(8,128)(2,1)S(1)} %get-tuple-element.83), channel_id=1, source_target_pairs={{8,0},{9,1},{10,2},{11,3},{12,4},{13,5},{14,6},{15,7}} | collective-permute-start | bytes 983048 | tf_op jit(solution)/shard_map/ppermute | solution.py:335
  159.8 37.4 %collective-permute-start.38 = (bf16[64,2560]{1,0:T(8,128)(2,1)S(1)}, bf16[64,2560]{1,0:T(8,128)(2,1)S(1)}, u32[]{:S(2)}, u32[]{:S(2)}) collective-permute-start(bf16[64,2560]{1,0:T(8,128)(2,1)S(1)} %get-tuple-element.82), channel_id=1, source_target_pairs={{8,0},{9,1},{10,2},{11,3},{12,4},{13,5},{14,6},{15,7}} | collective-permute-start | bytes 983048 | tf_op jit(solution)/shard_map/ppermute | solution.py:335
  161.4 43.5 %collective-permute-start.37 = (bf16[64,2560]{1,0:T(8,128)(2,1)S(1)}, bf16[64,2560]{1,0:T(8,128)(2,1)S(1)}, u32[]{:S(2)}, u32[]{:S(2)}) collective-permute-start(bf16[64,2560]{1,0:T(8,128)(2,1)S(1)} %get-tuple-element.81), channel_id=1, source_target_pairs={{8,0},{9,1},{10,2},{11,3},{12,4},{13,5},{14,6},{15,7}} | collective-permute-start | bytes 983048 | tf_op jit(solution)/shard_map/ppermute | solution.py:335
  204.9 15.2 %slice-start = ((s8[6553600]{0:T(1024)(128)(4,1)}), s8[4194304]{0:T(1024)(128)(4,1)S(1)}, s32[]{:S(2)}) async-start(s8[6553600]{0:T(1024)(128)(4,1)} %bitcast.36), calls=%async_computation | async-start | bytes 8388608
  204.9 4.2 %copy-start.3 = (bf16[1,256,2560]{2,1,0:T(8,128)(2,1)S(1)}, bf16[1,256,2560]{2,1,0:T(8,128)(2,1)}, u32[]{:S(2)}) copy-start(bf16[1,256,2560]{2,1,0:T(8,128)(2,1)} %param.7) | copy-start | bytes 3932164
  204.9 15.2 %slice-start.1 = ((s8[6553600]{0:T(1024)(128)(4,1)}), s8[2359296]{0:T(1024)(128)(4,1)S(1)}, s32[]{:S(2)}) async-start(s8[6553600]{0:T(1024)(128)(4,1)} %bitcast.36), calls=%async_computation.1 | async-start | bytes 4718592
  209.8 1.2 collective-permute-start.41
  211.0 4.1 %collective-permute-start.42 = (f32[4,2560]{1,0:T(4,128)S(1)}, f32[4,2560]{1,0:T(4,128)S(1)}, u32[]{:S(2)}, u32[]{:S(2)}) collective-permute-start(f32[4,2560]{1,0:T(4,128)S(1)} %add.19), channel_id=1, source_target_pairs={{0,2},{1,3},{2,0},{3,1},{4,6},{5,7},{6,4},{7,5},{8,10},{9,11},{10,... | collective-permute-start | bytes 122888 | tf_op jit(solution)/shard_map/ppermute | solution.py:303
  215.1 5.0 %collective-permute-start.43 = (f32[4,2560]{1,0:T(4,128)S(1)}, f32[4,2560]{1,0:T(4,128)S(1)}, u32[]{:S(2)}, u32[]{:S(2)}) collective-permute-start(f32[4,2560]{1,0:T(4,128)S(1)} %add.20.left), channel_id=1, source_target_pairs={{0,4},{1,5},{2,6},{3,7},{4,0},{5,1},{6,2},{7,3},{8,12},{9,13},{10,... | collective-permute-start | bytes 122888 | tf_op jit(solution)/shard_map/ppermute | solution.py:303
  222.9 1.3 collective-permute-start.44
  224.2 3.8 %collective-permute-start.45 = (f32[4,1280]{1,0:T(4,128)S(1)}, f32[4,1280]{1,0:T(4,128)S(1)}, u32[]{:S(2)}, u32[]{:S(2)}) collective-permute-start(f32[4,1280]{1,0:T(4,128)S(1)} %add.21), channel_id=1, source_target_pairs={{0,2},{1,3},{2,0},{3,1},{4,6},{5,7},{6,4},{7,5},{8,10},{9,11},{10,... | collective-permute-start | bytes 61448 | tf_op jit(solution)/shard_map/ppermute | solution.py:303
  228.0 4.7 %collective-permute-start.46 = (f32[4,1280]{1,0:T(4,128)S(1)}, f32[4,1280]{1,0:T(4,128)S(1)}, u32[]{:S(2)}, u32[]{:S(2)}) collective-permute-start(f32[4,1280]{1,0:T(4,128)S(1)} %add.22), channel_id=1, source_target_pairs={{0,4},{1,5},{2,6},{3,7},{4,0},{5,1},{6,2},{7,3},{8,12},{9,13},{10,... | collective-permute-start | bytes 61448 | tf_op jit(solution)/shard_map/ppermute | solution.py:303

commit v5 on v4

--- a/solution.py
+++ b/solution.py
@@ -264,28 +264,29 @@
     return jnp.concatenate(result, 0)
 
 
-def second_half(left, right, inputs, value_grads, error, passed_rows):
-    def body(left, right, acts, vg, err, passed, basis_ref, second_ref, out_ref, done):
+def second_half(parts, inputs, value_grads, error, passed_rows):
+    def body(*refs):
+        *parts, acts, vg, err, passed, basis_ref, second_ref, out_ref, done = refs
         copy = pltpu.make_async_copy(passed, out_ref, done)
         copy.start()
-        basis = orthonormal(left[...] + right[...])
+        basis = orthonormal(joined(*(part[...] for part in parts)))
         basis_ref[...] = basis
-        parts = split3(basis)
+        pieces = split3(basis)
         mapped = lax.dot_general(
-            parts, acts[...], (((1,), (1,)), ((), ())), preferred_element_type=jnp.float32
+            pieces, acts[...], (((1,), (1,)), ((), ())), preferred_element_type=jnp.float32
         )
-        second = jnp.dot(parts, err[...], preferred_element_type=jnp.float32)
+        second = jnp.dot(pieces, err[...], preferred_element_type=jnp.float32)
         second = second + jnp.dot(
             split3(join3(mapped)), vg[...], preferred_element_type=jnp.float32
         )
         second_ref[...] = join3(second)
         copy.wait()
 
-    rank, width = left.shape
+    rank, width = parts[0].shape
     channels = value_grads.shape[1]
     return pl.pallas_call(
         body,
-        in_specs=[VMEM] * 6,
+        in_specs=[VMEM] * (len(parts) + 4),
         out_specs=[VMEM, VMEM, ANY],
         out_shape=[
             jax.ShapeDtypeStruct((rank, width), jnp.float32),
@@ -295,7 +296,7 @@
         scratch_shapes=[pltpu.SemaphoreType.DMA],
         compiler_params=pltpu.CompilerParams(vmem_limit_bytes=8 << 20),
         name="second_half",
-    )(left, right, inputs, value_grads, error, passed_rows)
+    )(*parts, inputs, value_grads, error, passed_rows)
 
 
 def exchange(value, by):
@@ -303,12 +304,17 @@
     return lax.ppermute(value, "dp", [(i, i ^ by) for i in range(replicas)])
 
 
-def sum_but_last(value):
+def sum_parts(value):
+    replicas = lax.axis_size("dp")
     by = 1
-    while by * 2 < lax.axis_size("dp"):
+    while by * 4 < replicas:
         value = value + exchange(value, by)
         by *= 2
-    return value, exchange(value, by)
+    return value, exchange(value, by), exchange(value, 2 * by), exchange(value, 3 * by)
+
+
+def joined(first, second, third, fourth):
+    return (first + second) + (third + fourth)
 
 
 def local(acts, gates, w_value, w_out, residual_error, grad_top, warm_factor):
@@ -342,10 +348,9 @@
     factor = lax.dot_general(
         projected, inputs.astype(jnp.float32), (((0,), (0,)), ((), ())), precision=HIGHEST
     )
-    left, right = sum_but_last(factor + error_part)
-    basis, second, grad_in = second_half(left, right, inputs, value_grads, error, passed_rows)
-    left, right = sum_but_last(second)
-    right_out = (left + right) / math.sqrt(row_count * replicas * width)
+    parts = sum_parts(factor + error_part)
+    basis, second, grad_in = second_half(parts, inputs, value_grads, error, passed_rows)
+    right_out = joined(*sum_parts(second)) / math.sqrt(row_count * replicas * width)
     return grad_in[None], basis[None], right_out[None]
 
 

time: 234 us -> 233 us (level)
  waiting for transfers between devices: 154 us -> 145 us
  starting transfers between devices: 39.7 us -> 47.2 us
    ppermute x6 -> x8, waiting for transfers between devices: 19.5 us -> 9.92 us  [exchange(): return lax.ppermute(value, 'dp', [(i, i ^ by) for i in range(replicas)])]
    ppermute x6 -> x8, starting transfers between devices: 0.65 us -> 9 us  [exchange(): return lax.ppermute(value, 'dp', [(i, i ^ by) for i in range(replicas)])]
    unnamed x32 -> x34, local copies, waits for them, and re-layouts: 4.89 us -> 5.15 us
  transfers between devices with their start and end apart: 47 -> 49, of which waited for: 20 -> 20; matrix products, arithmetic and copies ran while one was open for 5% -> 5% of each run, Pallas kernels for 6% -> 6%
where the time goes in v5:
time: 233 us; the launch traced here: 232 us
  waiting for transfers between devices  145 us (62%)
  starting transfers between devices  47.2 us (20%)
  Pallas kernels  20.9 us (9%)
  matrix products  9.33 us (4%)
  local copies, waits for them, and re-layouts  5.15 us (2%)
  other arithmetic  3.53 us (2%)
    ppermute x15, waiting for transfers between devices, permute(): return lax.ppermute(value, ('section', 'dp'), pairs)  103 us
    ppermute x12, waiting for transfers between devices, local(): arriving[k] = lax.ppermute(send, 'section', [(section, section - 1)])  31.4 us
    ppermute x15, starting transfers between devices, permute(): return lax.ppermute(value, ('section', 'dp'), pairs)  25.2 us
    pallas_call x16, Pallas kernels, stage(): pl.pallas_call(body, in_specs=[VMEM] * 3 + [ANY] + [VMEM] * len(held), ou...  14.7 us
    ppermute x12, starting transfers between devices, local(): arriving[k] = lax.ppermute(send, 'section', [(section, section - 1)])  10.6 us
    ppermute x8, waiting for transfers between devices, exchange(): return lax.ppermute(value, 'dp', [(i, i ^ by) for i in range(replicas)])  9.92 us
    ppermute x8, starting transfers between devices, exchange(): return lax.ppermute(value, 'dp', [(i, i ^ by) for i in range(replicas)])  9 us
    dot_general x1, matrix products, local(): lax.dot_general(warm, error.astype(jnp.float32), (((1,), (1,)), ((), ()))...  8.01 us
  transfers between devices with their start and end apart: 49, of which 20 were waited for; matrix products, arithmetic and copies ran while one was open for 5% of the time, Pallas kernels for 6%

profile of v5, /device:TPU:0, one launch (start us, length us, event | category | flops | bytes accessed | tf_op | source)
XLA Modules:
  0.0 232.2 jit_solution(3536472480067178209)
XLA Ops:
  0.6 5.9 %collective-permute-start.2 = (bf16[320,1280]{1,0:T(8,128)(2,1)}, bf16[320,1280]{1,0:T(8,128)(2,1)}, u32[]{:S(2)}, u32[]{:S(2)}) collective-permute-start(bf16[320,1280]{1,0:T(8,128)(2,1)} %bitcast.40), channel_id=1, source_target_pairs={{0,2},{1,3},{2,4},{3,5},{4,6},{5,7},{8,10},{9,11},{10,12},{11,13},... | collective-permute-start | bytes 2457608 | tf_op jit(solution)/shard_map/ppermute | solution.py:74
  6.6 1.3 collective-permute-start
  7.8 5.5 %collective-permute-start.10 = (bf16[320,1280]{1,0:T(8,128)(2,1)}, bf16[320,1280]{1,0:T(8,128)(2,1)}, u32[]{:S(2)}, u32[]{:S(2)}) collective-permute-start(bf16[320,1280]{1,0:T(8,128)(2,1)} %bitcast.44), channel_id=1, source_target_pairs={{0,2},{1,3},{2,4},{3,5},{4,6},{5,7},{8,10},{9,11},{10,12},{11,13},... | collective-permute-start | bytes 2457608 | tf_op jit(solution)/shard_map/ppermute | solution.py:74
  13.3 1.3 collective-permute-start.8
  14.6 0.7 collective-permute-start.20
  15.3 9.2 %collective-permute-done.2.refs_7_ = bf16[320,1280]{1,0:T(8,128)(2,1)} collective-permute-done((bf16[320,1280]{1,0:T(8,128)(2,1)}, bf16[320,1280]{1,0:T(8,128)(2,1)}, u32[]{:S(2)}, u32[]{:S(2)}) %collective-permute-start.2) | collective-permute-done | bytes 819232 | tf_op jit(solution)/shard_map/ppermute | solution.py:74
  24.5 5.3 %collective-permute-done.refs_9_ = bf16[320,1280]{1,0:T(8,128)(2,1)} collective-permute-done((bf16[320,1280]{1,0:T(8,128)(2,1)}, bf16[320,1280]{1,0:T(8,128)(2,1)}, u32[]{:S(2)}, u32[]{:S(2)}) %collective-permute-start) | collective-permute-done | bytes 819232 | tf_op jit(solution)/shard_map/ppermute | solution.py:74
  29.9 11.1 %collective-permute-done.10.refs_3_ = bf16[320,1280]{1,0:T(8,128)(2,1)} collective-permute-done((bf16[320,1280]{1,0:T(8,128)(2,1)}, bf16[320,1280]{1,0:T(8,128)(2,1)}, u32[]{:S(2)}, u32[]{:S(2)}) %collective-permute-start.10) | collective-permute-done | bytes 819232 | tf_op jit(solution)/shard_map/ppermute | solution.py:74
  41.0 5.0 %collective-permute-done.8.refs_5_ = bf16[320,1280]{1,0:T(8,128)(2,1)} collective-permute-done((bf16[320,1280]{1,0:T(8,128)(2,1)}, bf16[320,1280]{1,0:T(8,128)(2,1)}, u32[]{:S(2)}, u32[]{:S(2)}) %collective-permute-start.8) | collective-permute-done | bytes 819232 | tf_op jit(solution)/shard_map/ppermute | solution.py:74
  46.0 0.7 collective-permute-start.3
  46.9 1.0 copy-done.6
  47.9 1.3 collective-permute-start.1
  49.2 2.7 %pad_maximum_fusion = bf16[2,320,1280]{2,1,0:T(8,128)(2,1)} fusion(bf16[1,320,1280]{2,1,0:T(8,128)(2,1)} %param.9, bf16[1,320,1280]{2,1,0:T(8,128)(2,1)} %param.10), kind=kLoop, calls=%fused_computation.1 | loop fusion | flops 819200 | bytes 3276800 | tf_op jit(solution)/shard_map/stack | solution.py:134
  51.9 1.0 copy-done.8
  53.4 0.9 copy-done.10
  54.3 0.7 collective-permute-start.11
  55.0 0.9 copy-done.12
  55.9 1.3 collective-permute-start.9
  57.2 1.3 collective-permute-start.21
  58.5 13.9 %collective-permute-done.1.refs_6_ = bf16[320,1280]{1,0:T(8,128)(2,1)S(1)} collective-permute-done((bf16[320,1280]{1,0:T(8,128)(2,1)}, bf16[320,1280]{1,0:T(8,128)(2,1)S(1)}, u32[]{:S(2)}, u32[]{:S(2)}) %collective-permute-start.1) | collective-permute-done | bytes 819232 | tf_op jit(solution)/shard_map/ppermute | solution.py:74
  73.1 16.9 %collective-permute-done.9.refs_2_ = bf16[320,1280]{1,0:T(8,128)(2,1)S(1)} collective-permute-done((bf16[320,1280]{1,0:T(8,128)(2,1)}, bf16[320,1280]{1,0:T(8,128)(2,1)S(1)}, u32[]{:S(2)}, u32[]{:S(2)}) %collective-permute-start.9) | collective-permute-done | bytes 819232 | tf_op jit(solution)/shard_map/ppermute | solution.py:74
  90.1 16.9 %collective-permute-done.21 = bf16[320,1280]{1,0:T(8,128)(2,1)S(1)} collective-permute-done((bf16[320,1280]{1,0:T(8,128)(2,1)}, bf16[320,1280]{1,0:T(8,128)(2,1)S(1)}, u32[]{:S(2)}, u32[]{:S(2)}) %collective-permute-start.21) | collective-permute-done | bytes 819232 | tf_op jit(solution)/shard_map/ppermute | solution.py:74
  107.0 1.3 collective-permute-start.22
  108.4 0.7 collective-permute-start.14
  109.1 1.3 collective-permute-start.12
  110.5 0.7 collective-permute-start.6
  111.2 14.7 %collective-permute-done.22.refs_8_ = bf16[320,1280]{1,0:T(8,128)(2,1)S(1)} collective-permute-done((bf16[320,1280]{1,0:T(8,128)(2,1)S(1)}, bf16[320,1280]{1,0:T(8,128)(2,1)S(1)}, u32[]{:S(2)}, u32[]{:S(2)}) %collective-permute-start.22) | collective-permute-done | bytes 819232 | tf_op jit(solution)/shard_map/ppermute | solution.py:74
  126.4 4.4 %collective-permute-done.12.refs_0_ = bf16[320,1280]{1,0:T(8,128)(2,1)S(1)} collective-permute-done((bf16[320,1280]{1,0:T(8,128)(2,1)S(1)}, bf16[320,1280]{1,0:T(8,128)(2,1)S(1)}, u32[]{:S(2)}, u32[]{:S(2)}) %collective-permute-start.12) | collective-permute-done | bytes 819232 | tf_op jit(solution)/shard_map/ppermute | solution.py:74
  130.8 1.3 collective-permute-start.4
  132.7 8.0 %fusion.2.early = f32[4,2560]{1,0:T(4,128)S(1)} fusion(f32[1,4,1280]{2,1,0:T(4,128)S(1)} %copy-done, bf16[1,2560,1280]{2,1,0:T(8,128)(2,1)} %param.11), kind=kOutput, calls=%fused_computation.6 | convolution fusion | flops 157286400 | bytes 6615040 | tf_op jit(solution)/shard_map/dot_general | solution.py:325
  140.8 2.2 put.5.refs_10_
  143.9 0.7 copy-done.1
  145.1 0.7 collective-permute-start.32
  145.8 0.7 collective-permute-start.31
  146.5 0.7 collective-permute-start.30
  147.4 6.0 %collective-permute-done.4.refs_0_ = bf16[320,1280]{1,0:T(8,128)(2,1)S(1)} collective-permute-done((bf16[320,1280]{1,0:T(8,128)(2,1)S(1)}, bf16[320,1280]{1,0:T(8,128)(2,1)S(1)}, u32[]{:S(2)}, u32[]{:S(2)}) %collective-permute-start.4) | collective-permute-done | bytes 819232 | tf_op jit(solution)/shard_map/ppermute | solution.py:74
  153.4 0.7 collective-permute-start.29
  154.2 0.7 collective-permute-start.36
  155.0 0.7 collective-permute-start.35
  155.7 0.7 collective-permute-start.34
  156.4 0.7 collective-permute-start.33
  157.1 1.3 collective-permute-start.40
  158.5 1.3 collective-permute-start.39
  159.8 1.3 collective-permute-start.38
  161.4 1.3 collective-permute-start.37
  162.9 20.2 %collective-permute-done.40.arr = bf16[64,2560]{1,0:T(8,128)(2,1)S(1)} collective-permute-done((bf16[64,2560]{1,0:T(8,128)(2,1)S(1)}, bf16[64,2560]{1,0:T(8,128)(2,1)S(1)}, u32[]{:S(2)}, u32[]{:S(2)}) %collective-permute-start.40) | collective-permute-done | bytes 327712 | tf_op jit(solution)/shard_map/ppermute | solution.py:341
  183.2 3.5 %shard_map.106 = (bf16[256,1280]{1,0:T(8,128)(2,1)S(1)}, bf16[256,2560]{1,0:T(8,128)(2,1)S(1)}) custom-call(bf16[2,2560,1280]{2,1,0:T(8,128)(2,1)S(1)} %put.9.w, bf16[64,2560]{1,0:T(8,128)(2,1)S(1)} %collective-permute-done.40.arr, bf16[256,1280]{1,0:T(8,128)(2,1)S(1)} %bitcast.32, ...), custom_call_target="tpu_custom_call", output_to_operand_aliasing={{0}: (4, {}), {1}: (5, {})} | custom-call | flops 838860800 | bytes 13107200 | tf_op jit(solution)/shard_map/pallas_call | solution.py:228
  186.7 3.5 %collective-permute-done.39.arr = bf16[64,2560]{1,0:T(8,128)(2,1)S(1)} collective-permute-done((bf16[64,2560]{1,0:T(8,128)(2,1)S(1)}, bf16[64,2560]{1,0:T(8,128)(2,1)S(1)}, u32[]{:S(2)}, u32[]{:S(2)}) %collective-permute-start.39) | collective-permute-done | bytes 327712 | tf_op jit(solution)/shard_map/ppermute | solution.py:341
  190.2 3.5 %shard_map.107 = (bf16[256,1280]{1,0:T(8,128)(2,1)S(1)}, bf16[256,2560]{1,0:T(8,128)(2,1)S(1)}) custom-call(bf16[2,2560,1280]{2,1,0:T(8,128)(2,1)S(1)} %put.9.w, bf16[64,2560]{1,0:T(8,128)(2,1)S(1)} %collective-permute-done.39.arr, bf16[256,1280]{1,0:T(8,128)(2,1)S(1)} %bitcast.33, ...), custom_call_target="tpu_custom_call", output_to_operand_aliasing={{0}: (4, {}), {1}: (5, {})} | custom-call | flops 838860800 | bytes 13107200 | tf_op jit(solution)/shard_map/pallas_call | solution.py:228
  193.7 3.5 %collective-permute-done.38.arr = bf16[64,2560]{1,0:T(8,128)(2,1)S(1)} collective-permute-done((bf16[64,2560]{1,0:T(8,128)(2,1)S(1)}, bf16[64,2560]{1,0:T(8,128)(2,1)S(1)}, u32[]{:S(2)}, u32[]{:S(2)}) %collective-permute-start.38) | collective-permute-done | bytes 327712 | tf_op jit(solution)/shard_map/ppermute | solution.py:341
  197.2 3.5 %shard_map.108 = (bf16[256,1280]{1,0:T(8,128)(2,1)S(1)}, bf16[256,2560]{1,0:T(8,128)(2,1)S(1)}) custom-call(bf16[2,2560,1280]{2,1,0:T(8,128)(2,1)S(1)} %put.9.w, bf16[64,2560]{1,0:T(8,128)(2,1)S(1)} %collective-permute-done.38.arr, bf16[256,1280]{1,0:T(8,128)(2,1)S(1)} %bitcast.34, ...), custom_call_target="tpu_custom_call", output_to_operand_aliasing={{0}: (4, {}), {1}: (5, {})} | custom-call | flops 838860800 | bytes 13107200 | tf_op jit(solution)/shard_map/pallas_call | solution.py:228
  200.8 4.2 %collective-permute-done.37.arr = bf16[64,2560]{1,0:T(8,128)(2,1)S(1)} collective-permute-done((bf16[64,2560]{1,0:T(8,128)(2,1)S(1)}, bf16[64,2560]{1,0:T(8,128)(2,1)S(1)}, u32[]{:S(2)}, u32[]{:S(2)}) %collective-permute-start.37) | collective-permute-done | bytes 327712 | tf_op jit(solution)/shard_map/ppermute | solution.py:341
  204.9 3.5 %shard_map.109 = (bf16[256,1280]{1,0:T(8,128)(2,1)S(1)}, bf16[256,2560]{1,0:T(8,128)(2,1)S(1)}) custom-call(bf16[2,2560,1280]{2,1,0:T(8,128)(2,1)S(1)} %put.9.w, bf16[64,2560]{1,0:T(8,128)(2,1)S(1)} %collective-permute-done.37.arr, bf16[256,1280]{1,0:T(8,128)(2,1)S(1)} %bitcast.35, ...), custom_call_target="tpu_custom_call", output_to_operand_aliasing={{0}: (4, {}), {1}: (5, {})} | custom-call | flops 838860800 | bytes 13107200 | tf_op jit(solution)/shard_map/pallas_call | solution.py:228
  208.4 0.7 fusion
  209.1 0.7 convolution_add_fusion
  209.8 1.2 collective-permute-done.41
  211.3 4.2 %collective-permute-start.44 = (f32[4,2560]{1,0:T(4,128)S(1)}, f32[4,2560]{1,0:T(4,128)S(1)}, u32[]{:S(2)}, u32[]{:S(2)}) collective-permute-start(f32[4,2560]{1,0:T(4,128)S(1)} %add.19.refs_0_), channel_id=1, source_target_pairs={{0,6},{1,7},{2,4},{3,5},{4,2},{5,3},{6,0},{7,1},{8,14},{9,15},{10,... | collective-permute-start | bytes 122888 | tf_op jit(solution)/shard_map/ppermute | solution.py:304
  215.6 2.4 %collective-permute-done.43.refs_2_ = f32[4,2560]{1,0:T(4,128)S(1)} collective-permute-done((f32[4,2560]{1,0:T(4,128)S(1)}, f32[4,2560]{1,0:T(4,128)S(1)}, u32[]{:S(2)}, u32[]{:S(2)}) %collective-permute-start.43) | collective-permute-done | bytes 40992 | tf_op jit(solution)/shard_map/ppermute | solution.py:304
  218.0 2.8 %second_half.1 = (f32[4,2560]{1,0:T(4,128)}, f32[4,1280]{1,0:T(4,128)S(1)}, bf16[256,2560]{1,0:T(8,128)(2,1)}) custom-call(f32[4,2560]{1,0:T(4,128)S(1)} %add.19.refs_0_, f32[4,2560]{1,0:T(4,128)S(1)} %collective-permute-done.42.refs_1_, f32[4,2560]{1,0:T(4,128)S(1)} %collective-permute-done.43.refs_2_, f32[4,2560]{1,0:T(4,128)S(1)} %collective-permute-done.44.refs_3_, ...), custom_call_target="tpu_custom_call" | custom-call | tf_op jit(solution)/shard_map/second_half/pallas_call | solution.py:287
  220.9 1.2 collective-permute-done.45
  222.0 1.0 collective-permute-start.46
  223.1 2.9 %collective-permute-start.47 = (f32[4,1280]{1,0:T(4,128)S(1)}, f32[4,1280]{1,0:T(4,128)S(1)}, u32[]{:S(2)}, u32[]{:S(2)}) collective-permute-start(f32[4,1280]{1,0:T(4,128)S(1)} %add.20), channel_id=1, source_target_pairs={{0,4},{1,5},{2,6},{3,7},{4,0},{5,1},{6,2},{7,3},{8,12},{9,13},{10,... | collective-permute-start | bytes 61448 | tf_op jit(solution)/shard_map/ppermute | solution.py:304
  226.5 1.3 collective-permute-done.47
  227.8 3.8 %collective-permute-done.48 = f32[4,1280]{1,0:T(4,128)S(1)} collective-permute-done((f32[4,1280]{1,0:T(4,128)S(1)}, f32[4,1280]{1,0:T(4,128)S(1)}, u32[]{:S(2)}, u32[]{:S(2)}) %collective-permute-start.48) | collective-permute-done | bytes 20512 | tf_op jit(solution)/shard_map/ppermute | solution.py:304
  (100 shorter events, 6.5 us)
Async XLA Ops:
  0.6 132.1 %copy-start = (f32[1,4,1280]{2,1,0:T(4,128)S(1)}, f32[1,4,1280]{2,1,0:T(4,128)}, u32[]{:S(2)}) copy-start(f32[1,4,1280]{2,1,0:T(4,128)} %param.13) | copy-start | bytes 61444
  0.6 23.9 %collective-permute-start.2 = (bf16[320,1280]{1,0:T(8,128)(2,1)}, bf16[320,1280]{1,0:T(8,128)(2,1)}, u32[]{:S(2)}, u32[]{:S(2)}) collective-permute-start(bf16[320,1280]{1,0:T(8,128)(2,1)} %bitcast.40), channel_id=1, source_target_pairs={{0,2},{1,3},{2,4},{3,5},{4,6},{5,7},{8,10},{9,11},{10,12},{11,13},... | collective-permute-start | bytes 2457608 | tf_op jit(solution)/shard_map/ppermute | solution.py:74
  6.6 23.3 %collective-permute-start = (bf16[320,1280]{1,0:T(8,128)(2,1)}, bf16[320,1280]{1,0:T(8,128)(2,1)}, u32[]{:S(2)}, u32[]{:S(2)}) collective-permute-start(bf16[320,1280]{1,0:T(8,128)(2,1)} %bitcast.41), channel_id=1, source_target_pairs={{2,0},{3,1},{4,2},{5,3},{6,4},{7,5},{10,8},{11,9},{12,10},{13,11},... | collective-permute-start | bytes 2457608 | tf_op jit(solution)/shard_map/ppermute | solution.py:74
  7.8 33.1 %collective-permute-start.10 = (bf16[320,1280]{1,0:T(8,128)(2,1)}, bf16[320,1280]{1,0:T(8,128)(2,1)}, u32[]{:S(2)}, u32[]{:S(2)}) collective-permute-start(bf16[320,1280]{1,0:T(8,128)(2,1)} %bitcast.44), channel_id=1, source_target_pairs={{0,2},{1,3},{2,4},{3,5},{4,6},{5,7},{8,10},{9,11},{10,12},{11,13},... | collective-permute-start | bytes 2457608 | tf_op jit(solution)/shard_map/ppermute | solution.py:74
  13.3 32.7 %collective-permute-start.8 = (bf16[320,1280]{1,0:T(8,128)(2,1)}, bf16[320,1280]{1,0:T(8,128)(2,1)}, u32[]{:S(2)}, u32[]{:S(2)}) collective-permute-start(bf16[320,1280]{1,0:T(8,128)(2,1)} %bitcast.45), channel_id=1, source_target_pairs={{2,0},{3,1},{4,2},{5,3},{6,4},{7,5},{10,8},{11,9},{12,10},{13,11},... | collective-permute-start | bytes 2457608 | tf_op jit(solution)/shard_map/ppermute | solution.py:74
  14.6 31.4 %collective-permute-start.20 = (bf16[320,1280]{1,0:T(8,128)(2,1)}, bf16[320,1280]{1,0:T(8,128)(2,1)S(1)}, u32[]{:S(2)}, u32[]{:S(2)}) collective-permute-start(bf16[320,1280]{1,0:T(8,128)(2,1)} %bitcast.42), channel_id=1, source_target_pairs={{26,2},{27,3},{28,4},{29,5}} | collective-permute-start | bytes 2457608 | tf_op jit(solution)/shard_map/ppermute | solution.py:74
  24.5 22.2 %collective-permute-start.27 = (bf16[320,1280]{1,0:T(8,128)(2,1)}, bf16[320,1280]{1,0:T(8,128)(2,1)S(1)}, u32[]{:S(2)}, u32[]{:S(2)}) collective-permute-start(bf16[320,1280]{1,0:T(8,128)(2,1)} %collective-permute-done.2.refs_7_), channel_id=1, source_target_pairs={{0,1},{1,0},{2,3},{3,2},{4,5},{5,4},{6,7},{7,6},{8,9},{9,8},{10,11... | collective-permute-start | bytes 2457608 | tf_op jit(solution)/shard_map/ppermute | solution.py:82
  29.9 22.0 %collective-permute-start.28 = (bf16[320,1280]{1,0:T(8,128)(2,1)}, bf16[320,1280]{1,0:T(8,128)(2,1)S(1)}, u32[]{:S(2)}, u32[]{:S(2)}) collective-permute-start(bf16[320,1280]{1,0:T(8,128)(2,1)} %collective-permute-done.refs_9_), channel_id=1, source_target_pairs={{0,1},{1,0},{2,3},{3,2},{4,5},{5,4},{6,7},{7,6},{8,9},{9,8},{10,11... | collective-permute-start | bytes 2457608 | tf_op jit(solution)/shard_map/ppermute | solution.py:82
  41.0 12.4 %collective-permute-start.25 = (bf16[320,1280]{1,0:T(8,128)(2,1)}, bf16[320,1280]{1,0:T(8,128)(2,1)S(1)}, u32[]{:S(2)}, u32[]{:S(2)}) collective-permute-start(bf16[320,1280]{1,0:T(8,128)(2,1)} %collective-permute-done.10.refs_3_), channel_id=1, source_target_pairs={{0,1},{1,0},{2,3},{3,2},{4,5},{5,4},{6,7},{7,6},{8,9},{9,8},{10,11... | collective-permute-start | bytes 2457608 | tf_op jit(solution)/shard_map/ppermute | solution.py:82
  46.0 9.0 %collective-permute-start.26 = (bf16[320,1280]{1,0:T(8,128)(2,1)}, bf16[320,1280]{1,0:T(8,128)(2,1)S(1)}, u32[]{:S(2)}, u32[]{:S(2)}) collective-permute-start(bf16[320,1280]{1,0:T(8,128)(2,1)} %collective-permute-done.8.refs_5_), channel_id=1, source_target_pairs={{0,1},{1,0},{2,3},{3,2},{4,5},{5,4},{6,7},{7,6},{8,9},{9,8},{10,11... | collective-permute-start | bytes 2457608 | tf_op jit(solution)/shard_map/ppermute | solution.py:82
  46.0 11.2 %collective-permute-start.3 = (bf16[320,1280]{1,0:T(8,128)(2,1)}, bf16[320,1280]{1,0:T(8,128)(2,1)S(1)}, u32[]{:S(2)}, u32[]{:S(2)}) collective-permute-start(bf16[320,1280]{1,0:T(8,128)(2,1)} %collective-permute-done.2.refs_7_), channel_id=1, source_target_pairs={{2,4},{3,5},{4,6},{5,7},{10,12},{11,13},{12,14},{13,15},{18,20},{1... | collective-permute-start | bytes 2457608 | tf_op jit(solution)/shard_map/ppermute | solution.py:74
  46.9 1.0 copy-start.6
  47.9 24.5 %collective-permute-start.1 = (bf16[320,1280]{1,0:T(8,128)(2,1)}, bf16[320,1280]{1,0:T(8,128)(2,1)S(1)}, u32[]{:S(2)}, u32[]{:S(2)}) collective-permute-start(bf16[320,1280]{1,0:T(8,128)(2,1)} %collective-permute-done.refs_9_), channel_id=1, source_target_pairs={{2,0},{3,1},{4,2},{5,3},{10,8},{11,9},{12,10},{13,11},{18,16},{19,... | collective-permute-start | bytes 2457608 | tf_op jit(solution)/shard_map/ppermute | solution.py:74
  51.9 1.0 copy-start.8
  52.9 55.5 %collective-permute-start.24 = (bf16[2,320,1280]{2,1,0:T(8,128)(2,1)}, bf16[2,320,1280]{2,1,0:T(8,128)(2,1)}, u32[]{:S(2)}, u32[]{:S(2)}) collective-permute-start(bf16[2,320,1280]{2,1,0:T(8,128)(2,1)} %pad_maximum_fusion), channel_id=1, source_target_pairs={{0,1},{1,0},{2,3},{3,2},{4,5},{5,4},{6,7},{7,6},{8,9},{9,8},{10,11... | collective-permute-start | bytes 4915208 | tf_op jit(solution)/shard_map/ppermute | solution.py:82
  54.3 18.2 %collective-permute-start.11 = (bf16[320,1280]{1,0:T(8,128)(2,1)}, bf16[320,1280]{1,0:T(8,128)(2,1)S(1)}, u32[]{:S(2)}, u32[]{:S(2)}) collective-permute-start(bf16[320,1280]{1,0:T(8,128)(2,1)} %collective-permute-done.10.refs_3_), channel_id=1, source_target_pairs={{2,4},{3,5},{4,6},{5,7},{10,12},{11,13},{12,14},{13,15},{18,20},{1... | collective-permute-start | bytes 2457608 | tf_op jit(solution)/shard_map/ppermute | solution.py:74
  55.0 0.9 copy-start.12
  55.9 34.0 %collective-permute-start.9 = (bf16[320,1280]{1,0:T(8,128)(2,1)}, bf16[320,1280]{1,0:T(8,128)(2,1)S(1)}, u32[]{:S(2)}, u32[]{:S(2)}) collective-permute-start(bf16[320,1280]{1,0:T(8,128)(2,1)} %collective-permute-done.8.refs_5_), channel_id=1, source_target_pairs={{2,0},{3,1},{4,2},{5,3},{10,8},{11,9},{12,10},{13,11},{18,16},{19,... | collective-permute-start | bytes 2457608 | tf_op jit(solution)/shard_map/ppermute | solution.py:74
  57.2 49.8 %collective-permute-start.21 = (bf16[320,1280]{1,0:T(8,128)(2,1)}, bf16[320,1280]{1,0:T(8,128)(2,1)S(1)}, u32[]{:S(2)}, u32[]{:S(2)}) collective-permute-start(bf16[320,1280]{1,0:T(8,128)(2,1)} %copy-done.14), channel_id=1, source_target_pairs={{2,0},{3,1},{4,6},{5,7}} | collective-permute-start | bytes 2457608 | tf_op jit(solution)/shard_map/ppermute | solution.py:74
  72.4 36.7 %collective-permute-start.18 = (bf16[320,1280]{1,0:T(8,128)(2,1)S(1)}, bf16[320,1280]{1,0:T(8,128)(2,1)S(1)}, u32[]{:S(2)}, u32[]{:S(2)}) collective-permute-start(bf16[320,1280]{1,0:T(8,128)(2,1)S(1)} %collective-permute-done.3.refs_4_), channel_id=1, source_target_pairs={{0,1},{1,0},{2,3},{3,2},{4,5},{5,4},{6,7},{7,6},{8,9},{9,8},{10,11... | collective-permute-start | bytes 2457608 | tf_op jit(solution)/shard_map/ppermute | solution.py:82
  72.5 37.9 %collective-permute-start.19 = (bf16[320,1280]{1,0:T(8,128)(2,1)S(1)}, bf16[320,1280]{1,0:T(8,128)(2,1)S(1)}, u32[]{:S(2)}, u32[]{:S(2)}) collective-permute-start(bf16[320,1280]{1,0:T(8,128)(2,1)S(1)} %collective-permute-done.1.refs_6_), channel_id=1, source_target_pairs={{0,1},{1,0},{2,3},{3,2},{4,5},{5,4},{6,7},{7,6},{8,9},{9,8},{10,11... | collective-permute-start | bytes 2457608 | tf_op jit(solution)/shard_map/ppermute | solution.py:82
  90.0 20.6 %collective-permute-start.16 = (bf16[320,1280]{1,0:T(8,128)(2,1)S(1)}, bf16[320,1280]{1,0:T(8,128)(2,1)S(1)}, u32[]{:S(2)}, u32[]{:S(2)}) collective-permute-start(bf16[320,1280]{1,0:T(8,128)(2,1)S(1)} %collective-permute-done.11.refs_0_), channel_id=1, source_target_pairs={{0,1},{1,0},{2,3},{3,2},{4,5},{5,4},{6,7},{7,6},{8,9},{9,8},{10,11... | collective-permute-start | bytes 2457608 | tf_op jit(solution)/shard_map/ppermute | solution.py:82
  90.1 50.6 %copy-start.4 = (bf16[1,320,1280]{2,1,0:T(8,128)(2,1)S(1)}, bf16[1,320,1280]{2,1,0:T(8,128)(2,1)}, u32[]{:S(2)}) copy-start(bf16[1,320,1280]{2,1,0:T(8,128)(2,1)} %param.9) | copy-start | bytes 2457604
  90.1 50.6 %copy-start.5 = (bf16[1,320,1280]{2,1,0:T(8,128)(2,1)S(1)}, bf16[1,320,1280]{2,1,0:T(8,128)(2,1)}, u32[]{:S(2)}) copy-start(bf16[1,320,1280]{2,1,0:T(8,128)(2,1)} %param.10) | copy-start | bytes 2457604
  90.1 50.6 %copy-start.7 = (bf16[320,1280]{1,0:T(8,128)(2,1)S(1)}, bf16[320,1280]{1,0:T(8,128)(2,1)}, u32[]{:S(2)}) copy-start(bf16[320,1280]{1,0:T(8,128)(2,1)} %copy-done.6) | copy-start | bytes 2457604
  90.1 50.6 %copy-start.9 = (bf16[320,1280]{1,0:T(8,128)(2,1)S(1)}, bf16[320,1280]{1,0:T(8,128)(2,1)}, u32[]{:S(2)}) copy-start(bf16[320,1280]{1,0:T(8,128)(2,1)} %copy-done.8) | copy-start | bytes 2457604
  90.1 50.6 %copy-start.11 = (bf16[320,1280]{1,0:T(8,128)(2,1)S(1)}, bf16[320,1280]{1,0:T(8,128)(2,1)}, u32[]{:S(2)}) copy-start(bf16[320,1280]{1,0:T(8,128)(2,1)} %copy-done.10) | copy-start | bytes 2457604
  90.1 50.6 %copy-start.13 = (bf16[320,1280]{1,0:T(8,128)(2,1)S(1)}, bf16[320,1280]{1,0:T(8,128)(2,1)}, u32[]{:S(2)}) copy-start(bf16[320,1280]{1,0:T(8,128)(2,1)} %copy-done.12) | copy-start | bytes 2457604
  107.0 18.9 %collective-permute-start.22 = (bf16[320,1280]{1,0:T(8,128)(2,1)S(1)}, bf16[320,1280]{1,0:T(8,128)(2,1)S(1)}, u32[]{:S(2)}, u32[]{:S(2)}) collective-permute-start(bf16[320,1280]{1,0:T(8,128)(2,1)S(1)} %collective-permute-done.21), channel_id=1, source_target_pairs={{0,24},{1,25},{6,30},{7,31}} | collective-permute-start | bytes 2457608 | tf_op jit(solution)/shard_map/ppermute | solution.py:74
  108.4 17.5 %collective-permute-start.14 = (bf16[320,1280]{1,0:T(8,128)(2,1)S(1)}, bf16[320,1280]{1,0:T(8,128)(2,1)S(1)}, u32[]{:S(2)}, u32[]{:S(2)}) collective-permute-start(bf16[320,1280]{1,0:T(8,128)(2,1)S(1)} %broadcast_select_fusion.1), channel_id=1, source_target_pairs={{26,24},{27,25},{28,30},{29,31}} | collective-permute-start | bytes 2457608 | tf_op jit(solution)/shard_map/ppermute | solution.py:74
  109.1 21.7 %collective-permute-start.12 = (bf16[320,1280]{1,0:T(8,128)(2,1)S(1)}, bf16[320,1280]{1,0:T(8,128)(2,1)S(1)}, u32[]{:S(2)}, u32[]{:S(2)}) collective-permute-start(bf16[320,1280]{1,0:T(8,128)(2,1)S(1)} %broadcast_select_fusion), channel_id=1, source_target_pairs={{2,0},{3,1},{4,6},{5,7},{10,8},{11,9},{12,14},{13,15},{18,16},{19,... | collective-permute-start | bytes 2457608 | tf_op jit(solution)/shard_map/ppermute | solution.py:74
  110.4 20.4 %collective-permute-start.17 = (bf16[320,1280]{1,0:T(8,128)(2,1)S(1)}, bf16[320,1280]{1,0:T(8,128)(2,1)S(1)}, u32[]{:S(2)}, u32[]{:S(2)}) collective-permute-start(bf16[320,1280]{1,0:T(8,128)(2,1)S(1)} %collective-permute-done.9.refs_2_), channel_id=1, source_target_pairs={{0,1},{1,0},{2,3},{3,2},{4,5},{5,4},{6,7},{7,6},{8,9},{9,8},{10,11... | collective-permute-start | bytes 2457608 | tf_op jit(solution)/shard_map/ppermute | solution.py:82
  110.5 21.6 %collective-permute-start.6 = (bf16[320,1280]{1,0:T(8,128)(2,1)S(1)}, bf16[320,1280]{1,0:T(8,128)(2,1)S(1)}, u32[]{:S(2)}, u32[]{:S(2)}) collective-permute-start(bf16[320,1280]{1,0:T(8,128)(2,1)S(1)} %broadcast_select_fusion.1), channel_id=1, source_target_pairs={{10,8},{11,9},{12,14},{13,15},{18,16},{19,17},{20,22},{21,23}} | collective-permute-start | bytes 2457608 | tf_op jit(solution)/shard_map/ppermute | solution.py:74
  125.9 17.1 %collective-permute-start.23 = (bf16[320,1280]{1,0:T(8,128)(2,1)S(1)}, bf16[320,1280]{1,0:T(8,128)(2,1)S(1)}, u32[]{:S(2)}, u32[]{:S(2)}) collective-permute-start(bf16[320,1280]{1,0:T(8,128)(2,1)S(1)} %collective-permute-done.22.refs_8_), channel_id=1, source_target_pairs={{0,1},{1,0},{2,3},{3,2},{4,5},{5,4},{6,7},{7,6},{8,9},{9,8},{10,11... | collective-permute-start | bytes 2457608 | tf_op jit(solution)/shard_map/ppermute | solution.py:82
  125.9 17.7 %collective-permute-start.15 = (bf16[320,1280]{1,0:T(8,128)(2,1)S(1)}, bf16[320,1280]{1,0:T(8,128)(2,1)S(1)}, u32[]{:S(2)}, u32[]{:S(2)}) collective-permute-start(bf16[320,1280]{1,0:T(8,128)(2,1)S(1)} %collective-permute-done.14.refs_2_), channel_id=1, source_target_pairs={{0,1},{1,0},{2,3},{3,2},{4,5},{5,4},{6,7},{7,6},{8,9},{9,8},{10,11... | collective-permute-start | bytes 2457608 | tf_op jit(solution)/shard_map/ppermute | solution.py:82
  130.8 12.8 %collective-permute-start.13 = (bf16[320,1280]{1,0:T(8,128)(2,1)S(1)}, bf16[320,1280]{1,0:T(8,128)(2,1)S(1)}, u32[]{:S(2)}, u32[]{:S(2)}) collective-permute-start(bf16[320,1280]{1,0:T(8,128)(2,1)S(1)} %collective-permute-done.12.refs_0_), channel_id=1, source_target_pairs={{0,1},{1,0},{2,3},{3,2},{4,5},{5,4},{6,7},{7,6},{8,9},{9,8},{10,11... | collective-permute-start | bytes 2457608 | tf_op jit(solution)/shard_map/ppermute | solution.py:82
  130.8 22.5 %collective-permute-start.4 = (bf16[320,1280]{1,0:T(8,128)(2,1)S(1)}, bf16[320,1280]{1,0:T(8,128)(2,1)S(1)}, u32[]{:S(2)}, u32[]{:S(2)}) collective-permute-start(bf16[320,1280]{1,0:T(8,128)(2,1)S(1)} %broadcast_select_fusion.1), channel_id=1, source_target_pairs={{2,0},{3,1},{4,6},{5,7}} | collective-permute-start | bytes 2457608 | tf_op jit(solution)/shard_map/ppermute | solution.py:74
  132.1 21.9 %collective-permute-start.7 = (bf16[320,1280]{1,0:T(8,128)(2,1)S(1)}, bf16[320,1280]{1,0:T(8,128)(2,1)S(1)}, u32[]{:S(2)}, u32[]{:S(2)}) collective-permute-start(bf16[320,1280]{1,0:T(8,128)(2,1)S(1)} %collective-permute-done.6.refs_0_), channel_id=1, source_target_pairs={{0,1},{1,0},{2,3},{3,2},{4,5},{5,4},{6,7},{7,6},{8,9},{9,8},{10,11... | collective-permute-start | bytes 2457608 | tf_op jit(solution)/shard_map/ppermute | solution.py:82
  143.6 1.1 copy-start.1
  143.6 1.5 copy-start.2
  145.1 9.1 %collective-permute-start.32 = (bf16[64,2560]{1,0:T(8,128)(2,1)S(1)}, bf16[64,2560]{1,0:T(8,128)(2,1)S(1)}, u32[]{:S(2)}, u32[]{:S(2)}) collective-permute-start(bf16[64,2560]{1,0:T(8,128)(2,1)S(1)} %get-tuple-element.60), channel_id=1, source_target_pairs={{24,16},{25,17},{26,18},{27,19},{28,20},{29,21},{30,22},{31,23}} | collective-permute-start | bytes 983048 | tf_op jit(solution)/shard_map/ppermute | solution.py:341
  145.8 9.1 %collective-permute-start.31 = (bf16[64,2560]{1,0:T(8,128)(2,1)S(1)}, bf16[64,2560]{1,0:T(8,128)(2,1)S(1)}, u32[]{:S(2)}, u32[]{:S(2)}) collective-permute-start(bf16[64,2560]{1,0:T(8,128)(2,1)S(1)} %get-tuple-element.59), channel_id=1, source_target_pairs={{24,16},{25,17},{26,18},{27,19},{28,20},{29,21},{30,22},{31,23}} | collective-permute-start | bytes 983048 | tf_op jit(solution)/shard_map/ppermute | solution.py:341
  146.5 9.1 %collective-permute-start.30 = (bf16[64,2560]{1,0:T(8,128)(2,1)S(1)}, bf16[64,2560]{1,0:T(8,128)(2,1)S(1)}, u32[]{:S(2)}, u32[]{:S(2)}) collective-permute-start(bf16[64,2560]{1,0:T(8,128)(2,1)S(1)} %get-tuple-element.58), channel_id=1, source_target_pairs={{24,16},{25,17},{26,18},{27,19},{28,20},{29,21},{30,22},{31,23}} | collective-permute-start | bytes 983048 | tf_op jit(solution)/shard_map/ppermute | solution.py:341
  153.4 3.0 %collective-permute-start.29 = (bf16[64,2560]{1,0:T(8,128)(2,1)S(1)}, bf16[64,2560]{1,0:T(8,128)(2,1)S(1)}, u32[]{:S(2)}, u32[]{:S(2)}) collective-permute-start(bf16[64,2560]{1,0:T(8,128)(2,1)S(1)} %get-tuple-element.57), channel_id=1, source_target_pairs={{24,16},{25,17},{26,18},{27,19},{28,20},{29,21},{30,22},{31,23}} | collective-permute-start | bytes 983048 | tf_op jit(solution)/shard_map/ppermute | solution.py:341
  154.0 8.6 %collective-permute-start.5 = (bf16[320,1280]{1,0:T(8,128)(2,1)S(1)}, bf16[320,1280]{1,0:T(8,128)(2,1)S(1)}, u32[]{:S(2)}, u32[]{:S(2)}) collective-permute-start(bf16[320,1280]{1,0:T(8,128)(2,1)S(1)} %collective-permute-done.4.refs_0_), channel_id=1, source_target_pairs={{0,1},{1,0},{2,3},{3,2},{4,5},{5,4},{6,7},{7,6},{8,9},{9,8},{10,11... | collective-permute-start | bytes 2457608 | tf_op jit(solution)/shard_map/ppermute | solution.py:82
  154.2 2.9 %collective-permute-start.36 = (bf16[64,2560]{1,0:T(8,128)(2,1)S(1)}, bf16[64,2560]{1,0:T(8,128)(2,1)S(1)}, u32[]{:S(2)}, u32[]{:S(2)}) collective-permute-start(bf16[64,2560]{1,0:T(8,128)(2,1)S(1)} %get-tuple-element.71), channel_id=1, source_target_pairs={{16,8},{17,9},{18,10},{19,11},{20,12},{21,13},{22,14},{23,15}} | collective-permute-start | bytes 983048 | tf_op jit(solution)/shard_map/ppermute | solution.py:341
  155.0 3.5 %collective-permute-start.35 = (bf16[64,2560]{1,0:T(8,128)(2,1)S(1)}, bf16[64,2560]{1,0:T(8,128)(2,1)S(1)}, u32[]{:S(2)}, u32[]{:S(2)}) collective-permute-start(bf16[64,2560]{1,0:T(8,128)(2,1)S(1)} %get-tuple-element.70), channel_id=1, source_target_pairs={{16,8},{17,9},{18,10},{19,11},{20,12},{21,13},{22,14},{23,15}} | collective-permute-start | bytes 983048 | tf_op jit(solution)/shard_map/ppermute | solution.py:341
  155.7 4.1 %collective-permute-start.34 = (bf16[64,2560]{1,0:T(8,128)(2,1)S(1)}, bf16[64,2560]{1,0:T(8,128)(2,1)S(1)}, u32[]{:S(2)}, u32[]{:S(2)}) collective-permute-start(bf16[64,2560]{1,0:T(8,128)(2,1)S(1)} %get-tuple-element.69), channel_id=1, source_target_pairs={{16,8},{17,9},{18,10},{19,11},{20,12},{21,13},{22,14},{23,15}} | collective-permute-start | bytes 983048 | tf_op jit(solution)/shard_map/ppermute | solution.py:341
  156.4 4.7 %collective-permute-start.33 = (bf16[64,2560]{1,0:T(8,128)(2,1)S(1)}, bf16[64,2560]{1,0:T(8,128)(2,1)S(1)}, u32[]{:S(2)}, u32[]{:S(2)}) collective-permute-start(bf16[64,2560]{1,0:T(8,128)(2,1)S(1)} %get-tuple-element.68), channel_id=1, source_target_pairs={{16,8},{17,9},{18,10},{19,11},{20,12},{21,13},{22,14},{23,15}} | collective-permute-start | bytes 983048 | tf_op jit(solution)/shard_map/ppermute | solution.py:341
  157.1 26.1 %collective-permute-start.40 = (bf16[64,2560]{1,0:T(8,128)(2,1)S(1)}, bf16[64,2560]{1,0:T(8,128)(2,1)S(1)}, u32[]{:S(2)}, u32[]{:S(2)}) collective-permute-start(bf16[64,2560]{1,0:T(8,128)(2,1)S(1)} %get-tuple-element.84), channel_id=1, source_target_pairs={{8,0},{9,1},{10,2},{11,3},{12,4},{13,5},{14,6},{15,7}} | collective-permute-start | bytes 983048 | tf_op jit(solution)/shard_map/ppermute | solution.py:341
  158.5 31.7 %collective-permute-start.39 = (bf16[64,2560]{1,0:T(8,128)(2,1)S(1)}, bf16[64,2560]{1,0:T(8,128)(2,1)S(1)}, u32[]{:S(2)}, u32[]{:S(2)}) collective-permute-start(bf16[64,2560]{1,0:T(8,128)(2,1)S(1)} %get-tuple-element.83), channel_id=1, source_target_pairs={{8,0},{9,1},{10,2},{11,3},{12,4},{13,5},{14,6},{15,7}} | collective-permute-start | bytes 983048 | tf_op jit(solution)/shard_map/ppermute | solution.py:341
  159.8 37.4 %collective-permute-start.38 = (bf16[64,2560]{1,0:T(8,128)(2,1)S(1)}, bf16[64,2560]{1,0:T(8,128)(2,1)S(1)}, u32[]{:S(2)}, u32[]{:S(2)}) collective-permute-start(bf16[64,2560]{1,0:T(8,128)(2,1)S(1)} %get-tuple-element.82), channel_id=1, source_target_pairs={{8,0},{9,1},{10,2},{11,3},{12,4},{13,5},{14,6},{15,7}} | collective-permute-start | bytes 983048 | tf_op jit(solution)/shard_map/ppermute | solution.py:341
  161.4 43.6 %collective-permute-start.37 = (bf16[64,2560]{1,0:T(8,128)(2,1)S(1)}, bf16[64,2560]{1,0:T(8,128)(2,1)S(1)}, u32[]{:S(2)}, u32[]{:S(2)}) collective-permute-start(bf16[64,2560]{1,0:T(8,128)(2,1)S(1)} %get-tuple-element.81), channel_id=1, source_target_pairs={{8,0},{9,1},{10,2},{11,3},{12,4},{13,5},{14,6},{15,7}} | collective-permute-start | bytes 983048 | tf_op jit(solution)/shard_map/ppermute | solution.py:341
  204.9 13.0 %slice-start = ((s8[6553600]{0:T(1024)(128)(4,1)}), s8[4194304]{0:T(1024)(128)(4,1)S(1)}, s32[]{:S(2)}) async-start(s8[6553600]{0:T(1024)(128)(4,1)} %bitcast.36), calls=%async_computation | async-start | bytes 8388608
  204.9 4.2 %copy-start.3 = (bf16[1,256,2560]{2,1,0:T(8,128)(2,1)S(1)}, bf16[1,256,2560]{2,1,0:T(8,128)(2,1)}, u32[]{:S(2)}) copy-start(bf16[1,256,2560]{2,1,0:T(8,128)(2,1)} %param.7) | copy-start | bytes 3932164
  204.9 13.0 %slice-start.1 = ((s8[6553600]{0:T(1024)(128)(4,1)}), s8[2359296]{0:T(1024)(128)(4,1)S(1)}, s32[]{:S(2)}) async-start(s8[6553600]{0:T(1024)(128)(4,1)} %bitcast.36), calls=%async_computation.1 | async-start | bytes 4718592
  209.8 1.2 collective-permute-start.41
  211.0 4.5 %collective-permute-start.42 = (f32[4,2560]{1,0:T(4,128)S(1)}, f32[4,2560]{1,0:T(4,128)S(1)}, u32[]{:S(2)}, u32[]{:S(2)}) collective-permute-start(f32[4,2560]{1,0:T(4,128)S(1)} %add.19.refs_0_), channel_id=1, source_target_pairs={{0,2},{1,3},{2,0},{3,1},{4,6},{5,7},{6,4},{7,5},{8,10},{9,11},{10,... | collective-permute-start | bytes 122888 | tf_op jit(solution)/shard_map/ppermute | solution.py:304
  211.3 6.7 %collective-permute-start.43 = (f32[4,2560]{1,0:T(4,128)S(1)}, f32[4,2560]{1,0:T(4,128)S(1)}, u32[]{:S(2)}, u32[]{:S(2)}) collective-permute-start(f32[4,2560]{1,0:T(4,128)S(1)} %add.19.refs_0_), channel_id=1, source_target_pairs={{0,4},{1,5},{2,6},{3,7},{4,0},{5,1},{6,2},{7,3},{8,12},{9,13},{10,... | collective-permute-start | bytes 122888 | tf_op jit(solution)/shard_map/ppermute | solution.py:304
  211.3 6.7 %collective-permute-start.44 = (f32[4,2560]{1,0:T(4,128)S(1)}, f32[4,2560]{1,0:T(4,128)S(1)}, u32[]{:S(2)}, u32[]{:S(2)}) collective-permute-start(f32[4,2560]{1,0:T(4,128)S(1)} %add.19.refs_0_), channel_id=1, source_target_pairs={{0,6},{1,7},{2,4},{3,5},{4,2},{5,3},{6,0},{7,1},{8,14},{9,15},{10,... | collective-permute-start | bytes 122888 | tf_op jit(solution)/shard_map/ppermute | solution.py:304
  220.8 1.3 collective-permute-start.45
  222.0 4.5 %collective-permute-start.46 = (f32[4,1280]{1,0:T(4,128)S(1)}, f32[4,1280]{1,0:T(4,128)S(1)}, u32[]{:S(2)}, u32[]{:S(2)}) collective-permute-start(f32[4,1280]{1,0:T(4,128)S(1)} %add.20), channel_id=1, source_target_pairs={{0,2},{1,3},{2,0},{3,1},{4,6},{5,7},{6,4},{7,5},{8,10},{9,11},{10,... | collective-permute-start | bytes 61448 | tf_op jit(solution)/shard_map/ppermute | solution.py:304
  223.1 4.7 %collective-permute-start.47 = (f32[4,1280]{1,0:T(4,128)S(1)}, f32[4,1280]{1,0:T(4,128)S(1)}, u32[]{:S(2)}, u32[]{:S(2)}) collective-permute-start(f32[4,1280]{1,0:T(4,128)S(1)} %add.20), channel_id=1, source_target_pairs={{0,4},{1,5},{2,6},{3,7},{4,0},{5,1},{6,2},{7,3},{8,12},{9,13},{10,... | collective-permute-start | bytes 61448 | tf_op jit(solution)/shard_map/ppermute | solution.py:304
  226.0 5.6 %collective-permute-start.48 = (f32[4,1280]{1,0:T(4,128)S(1)}, f32[4,1280]{1,0:T(4,128)S(1)}, u32[]{:S(2)}, u32[]{:S(2)}) collective-permute-start(f32[4,1280]{1,0:T(4,128)S(1)} %add.20), channel_id=1, source_target_pairs={{0,6},{1,7},{2,4},{3,5},{4,2},{5,3},{6,0},{7,1},{8,14},{9,15},{10,... | collective-permute-start | bytes 61448 | tf_op jit(solution)/shard_map/ppermute | solution.py:304
  (2 other events, 1.8 us)

commit v6 on v5

--- a/solution.py
+++ b/solution.py
@@ -56,7 +56,7 @@
     )(*arrays, *after, *held)
 
 
-def gather_weights(matrices):
+def gather_weights(matrices, meanwhile):
     sections = lax.axis_size("section")
     replicas = lax.axis_size("dp")
     chips = replicas // CORES
@@ -100,7 +100,7 @@
     dropped = [(top, c, top, d) for c, d in zip(inner, outer)] if relayed else []
     up, down = list(matrices), list(matrices)
     relay = None
-    groups = [[], [], []]
+    groups = [[], [], [], []]
     late = {}
     for step in range(1, chips):
         for kind in range(len(matrices)):
@@ -150,7 +150,7 @@
                 pieces = shards(up[kind], other, step, 0, 1, whose)
                 pieces += shards(up[kind], other, -step, step, chips, whose)
             behind = 2 * (chips - 1 - step) + len(matrices) - 1 - kind
-            groups[0 if behind > 3 else 1 if behind > 1 else 2] += [
+            groups[0 if behind > 3 else 1 if behind > 1 else 3 - behind] += [
                 (kind,) + piece for piece in pieces
             ]
         if relayed and step == chips - 2:
@@ -159,8 +159,10 @@
             pieces += shards(relay, other, -1, chips - 1, chips, True)
             groups[1] += [(1,) + piece for piece in pieces]
     whole = None
-    for group in groups:
-        whole = put(whole, group, shape, dtype)
+    for k, group in enumerate(groups):
+        if k == len(groups) - 1:
+            ready = meanwhile(whole)
+        whole = put(whole, group, shape, dtype, ready[:1] if k == len(groups) - 1 else ())
 
     def finish(whole, turn, sections, after):
         if turn not in late:
@@ -180,18 +182,17 @@
         pieces += shards(late[turn], other, 1 - chips, chips - 1, chips)
         return put(whole, [here((1,) + piece) for piece in pieces], shape, dtype, after)
 
-    return whole, finish
-
-
-def stage(whole, arriving, gates, held, early, *, section, first, block):
+    return whole, ready, finish
+
+
+def stage(whole, arriving, gates, held, early, *, section, first, block, forward, backward):
     width = arriving.shape[1]
     row_count, channels = gates.shape
-    lanes, deep = channels, width // 2
+    deep = width // 2
     at = pl.ds(first, block)
     read = at if arriving.shape[0] == row_count else pl.ds(0, block)
-
     results = [(row_count, channels), (row_count, width)]
-    if section:
+    if section and backward:
         results.append((block, width))
 
     def body(w, arr, gate, early, *refs):
@@ -200,19 +201,15 @@
 
         @pl.when(lax.axis_index("section") == section)
         def _():
-            def forward(step, carry):
-                cols = pl.ds(pl.multiple_of(step * lanes, lanes), lanes)
-                hidden = jnp.dot(
-                    arr[read], w[0, :width, cols], preferred_element_type=jnp.float32
-                )
-                hidden = hidden * gate[at, cols].astype(jnp.float32)
-                vg_ref[at, cols] = hidden.astype(jnp.bfloat16)
-                return carry
-
-            lax.fori_loop(0, channels // lanes, forward, 0)
-
-            def backward(step, carry):
-                cols = pl.ds(pl.multiple_of(step * deep, deep), deep)
+            if forward:
+                hidden = jnp.dot(arr[read], w[0], preferred_element_type=jnp.float32)
+                hidden = hidden * gate[at].astype(jnp.float32)
+                vg_ref[at] = hidden.astype(jnp.bfloat16)
+            if not backward:
+                return
+
+            def step(k, carry):
+                cols = pl.ds(pl.multiple_of(k * deep, deep), deep)
                 back = lax.dot_general(
                     vg_ref[at], w[1, cols], (((1,), (1,)), ((), ())),
                     preferred_element_type=jnp.float32,
@@ -223,7 +220,7 @@
                     ref[:, cols] = passed
                 return carry
 
-            lax.fori_loop(0, width // deep, backward, 0)
+            lax.fori_loop(0, width // deep, step, 0)
 
     return pl.pallas_call(
         body,
@@ -233,8 +230,8 @@
         input_output_aliases={4 + k: k for k in range(len(held))},
         compiler_params=pltpu.CompilerParams(vmem_limit_bytes=8 << 20),
         cost_estimate=pl.CostEstimate(
-            flops=4 * block * width * channels,
-            bytes_accessed=4 * width * channels,
+            flops=2 * (forward + backward) * block * width * channels,
+            bytes_accessed=2 * (forward + backward) * width * channels,
             transcendentals=0,
         ),
     )(whole, arriving, gates, early, *held)
@@ -304,17 +301,19 @@
     return lax.ppermute(value, "dp", [(i, i ^ by) for i in range(replicas)])
 
 
-def sum_parts(value):
+def sum_parts(value, turns):
     replicas = lax.axis_size("dp")
     by = 1
-    while by * 4 < replicas:
+    while by * (2 if turns else 4) < replicas:
         value = value + exchange(value, by)
         by *= 2
+    if turns:
+        return value, exchange(value, by)
     return value, exchange(value, by), exchange(value, 2 * by), exchange(value, 3 * by)
 
 
-def joined(first, second, third, fourth):
-    return (first + second) + (third + fourth)
+def joined(first, second, *others):
+    return (first + second) + joined(*others) if others else first + second
 
 
 def local(acts, gates, w_value, w_out, residual_error, grad_top, warm_factor):
@@ -325,32 +324,40 @@
     error_part = lax.dot_general(
         warm, error.astype(jnp.float32), (((1,), (1,)), ((), ())), precision=HIGHEST
     )
-    whole, finish = gather_weights((w_out[0], w_value[0]))
+    top = sections - 1
+
+    def forward_top(whole):
+        return stage(
+            whole, grad_top, gate_rows, (), error_part, section=top,
+            first=0, block=row_count, forward=True, backward=False,
+        )
+
+    whole, held, finish = gather_weights((w_out[0], w_value[0]), forward_top)
     blocks = [count * row_count // 16 for count in SIXTEENTHS]
     firsts = [sum(blocks[:k]) for k in range(len(blocks))]
     arriving = [grad_top] * len(blocks)
-    held = []
     for section in reversed(range(sections)):
         for k, (first, block) in enumerate(zip(firsts, blocks)):
             held = stage(
                 whole, arriving[k], gate_rows, held, error_part,
                 section=section, first=first, block=block,
+                forward=section < top, backward=True,
             )
             if section:
                 *held, send = held
                 arriving[k] = lax.ppermute(send, "section", [(section, section - 1)])
-        if section == sections - 1:
+        if section == top:
             whole = finish(whole, "late", (1, section), held[:1])
-        if section == min(1, sections - 1):
+        if section == min(1, top):
             whole = finish(whole, "last", (0, 1), held[:1])
     value_grads, passed_rows = held
     projected = jnp.dot(value_grads.astype(jnp.float32), warm.T, precision=HIGHEST)
     factor = lax.dot_general(
         projected, inputs.astype(jnp.float32), (((0,), (0,)), ((), ())), precision=HIGHEST
     )
-    parts = sum_parts(factor + error_part)
+    parts = sum_parts(factor + error_part, True)
     basis, second, grad_in = second_half(parts, inputs, value_grads, error, passed_rows)
-    right_out = joined(*sum_parts(second)) / math.sqrt(row_count * replicas * width)
+    right_out = joined(*sum_parts(second, False)) / math.sqrt(row_count * replicas * width)
     return grad_in[None], basis[None], right_out[None]
 
 

time: 233 us -> 235 us (level)
  waiting for transfers between devices: 145 us -> 151 us
  starting transfers between devices: 47.2 us -> 43.1 us
    ppermute x8 -> x7, starting transfers between devices: 9 us -> 4.68 us  [exchange(): return lax.ppermute(value, 'dp', [(i, i ^ by) for i in range(replicas)])]
    ppermute x12, waiting for transfers between devices: 31.4 us -> 35.2 us  [local(): arriving[k] = lax.ppermute(send, 'section', [(section, section - 1)])]
    ppermute x8 -> x7, waiting for transfers between devices: 9.92 us -> 13.2 us  [exchange(): return lax.ppermute(value, 'dp', [(i, i ^ by) for i in range(replicas)])]
    pallas_call x16 -> x17, Pallas kernels: 14.7 us -> 14.5 us  [stage(): pl.pallas_call(body, in_specs=[VMEM] * 3 + [ANY] + [VMEM] * len(held), ou...]
    unnamed x34 -> x36, local copies, waits for them, and re-layouts: 5.15 us -> 4.96 us
  transfers between devices with their start and end apart: 49 -> 48, of which waited for: 20 -> 19; matrix products, arithmetic and copies ran while one was open for 5% -> 5% of each run, Pallas kernels for 6% -> 6%
where the time goes in v6:
time: 235 us; the launch traced here: 234 us
  waiting for transfers between devices  151 us (64%)
  starting transfers between devices  43.1 us (18%)
  Pallas kernels  20.7 us (9%)
  matrix products  9.32 us (4%)
  local copies, waits for them, and re-layouts  4.96 us (2%)
  other arithmetic  3.53 us (2%)
    ppermute x15, waiting for transfers between devices, permute(): return lax.ppermute(value, ('section', 'dp'), pairs)  103 us
    ppermute x12, waiting for transfers between devices, local(): arriving[k] = lax.ppermute(send, 'section', [(section, section - 1)])  35.2 us
    ppermute x15, starting transfers between devices, permute(): return lax.ppermute(value, ('section', 'dp'), pairs)  25.5 us
    pallas_call x17, Pallas kernels, stage(): pl.pallas_call(body, in_specs=[VMEM] * 3 + [ANY] + [VMEM] * len(held), ou...  14.5 us
    ppermute x7, waiting for transfers between devices, exchange(): return lax.ppermute(value, 'dp', [(i, i ^ by) for i in range(replicas)])  13.2 us
    ppermute x12, starting transfers between devices, local(): arriving[k] = lax.ppermute(send, 'section', [(section, section - 1)])  10.6 us
    dot_general x1, matrix products, local(): lax.dot_general(warm, error.astype(jnp.float32), (((1,), (1,)), ((), ()))...  8.01 us
    unnamed x36, local copies, waits for them, and re-layouts  4.96 us
  transfers between devices with their start and end apart: 48, of which 19 were waited for; matrix products, arithmetic and copies ran while one was open for 5% of the time, Pallas kernels for 6%

profile of v6, /device:TPU:0, one launch (start us, length us, event | category | flops | bytes accessed | tf_op | source)
XLA Modules:
  0.0 234.0 jit_solution(2464299300466059764)
XLA Ops:
  0.6 5.0 %collective-permute-start.2 = (bf16[320,1280]{1,0:T(8,128)(2,1)}, bf16[320,1280]{1,0:T(8,128)(2,1)S(1)}, u32[]{:S(2)}, u32[]{:S(2)}) collective-permute-start(bf16[320,1280]{1,0:T(8,128)(2,1)} %bitcast.41), channel_id=1, source_target_pairs={{0,2},{1,3},{2,4},{3,5},{4,6},{5,7},{8,10},{9,11},{10,12},{11,13},... | collective-permute-start | bytes 2457608 | tf_op jit(solution)/shard_map/ppermute | solution.py:74
  5.7 1.3 collective-permute-start
  7.0 5.4 %collective-permute-start.12 = (bf16[320,1280]{1,0:T(8,128)(2,1)}, bf16[320,1280]{1,0:T(8,128)(2,1)}, u32[]{:S(2)}, u32[]{:S(2)}) collective-permute-start(bf16[320,1280]{1,0:T(8,128)(2,1)} %bitcast.45), channel_id=1, source_target_pairs={{0,2},{1,3},{2,4},{3,5},{4,6},{5,7},{8,10},{9,11},{10,12},{11,13},... | collective-permute-start | bytes 2457608 | tf_op jit(solution)/shard_map/ppermute | solution.py:74
  12.4 1.3 collective-permute-start.10
  13.7 1.7 collective-permute-start.20
  15.4 9.2 %collective-permute-done.2.refs_7_ = bf16[320,1280]{1,0:T(8,128)(2,1)S(1)} collective-permute-done((bf16[320,1280]{1,0:T(8,128)(2,1)}, bf16[320,1280]{1,0:T(8,128)(2,1)S(1)}, u32[]{:S(2)}, u32[]{:S(2)}) %collective-permute-start.2) | collective-permute-done | bytes 819232 | tf_op jit(solution)/shard_map/ppermute | solution.py:74
  24.5 4.4 %collective-permute-done.refs_9_ = bf16[320,1280]{1,0:T(8,128)(2,1)} collective-permute-done((bf16[320,1280]{1,0:T(8,128)(2,1)}, bf16[320,1280]{1,0:T(8,128)(2,1)}, u32[]{:S(2)}, u32[]{:S(2)}) %collective-permute-start) | collective-permute-done | bytes 819232 | tf_op jit(solution)/shard_map/ppermute | solution.py:74
  29.0 12.0 %collective-permute-done.12.refs_3_ = bf16[320,1280]{1,0:T(8,128)(2,1)} collective-permute-done((bf16[320,1280]{1,0:T(8,128)(2,1)}, bf16[320,1280]{1,0:T(8,128)(2,1)}, u32[]{:S(2)}, u32[]{:S(2)}) %collective-permute-start.12) | collective-permute-done | bytes 819232 | tf_op jit(solution)/shard_map/ppermute | solution.py:74
  41.0 4.2 %collective-permute-done.10.refs_5_ = bf16[320,1280]{1,0:T(8,128)(2,1)} collective-permute-done((bf16[320,1280]{1,0:T(8,128)(2,1)}, bf16[320,1280]{1,0:T(8,128)(2,1)}, u32[]{:S(2)}, u32[]{:S(2)}) %collective-permute-start.10) | collective-permute-done | bytes 819232 | tf_op jit(solution)/shard_map/ppermute | solution.py:74
  45.1 2.7 %pad_maximum_fusion = bf16[2,320,1280]{2,1,0:T(8,128)(2,1)} fusion(bf16[1,320,1280]{2,1,0:T(8,128)(2,1)} %param.9, bf16[1,320,1280]{2,1,0:T(8,128)(2,1)} %param.10), kind=kLoop, calls=%fused_computation.1 | loop fusion | flops 819200 | bytes 3276800 | tf_op jit(solution)/shard_map/stack | solution.py:134
  48.4 0.9 copy-done.8
  49.3 0.7 collective-permute-start.3
  50.0 0.9 copy-done.10
  50.9 1.3 collective-permute-start.1
  52.2 0.9 copy-done.12
  53.1 0.7 collective-permute-start.13
  53.8 1.0 copy-done.14
  54.8 1.3 collective-permute-start.11
  56.1 1.3 collective-permute-start.21
  57.4 19.0 %collective-permute-done.1.refs_6_ = bf16[320,1280]{1,0:T(8,128)(2,1)S(1)} collective-permute-done((bf16[320,1280]{1,0:T(8,128)(2,1)}, bf16[320,1280]{1,0:T(8,128)(2,1)S(1)}, u32[]{:S(2)}, u32[]{:S(2)}) %collective-permute-start.1) | collective-permute-done | bytes 819232 | tf_op jit(solution)/shard_map/ppermute | solution.py:74
  76.4 0.5 collective-permute-start.19
  76.9 17.0 %collective-permute-done.11.refs_2_ = bf16[320,1280]{1,0:T(8,128)(2,1)S(1)} collective-permute-done((bf16[320,1280]{1,0:T(8,128)(2,1)}, bf16[320,1280]{1,0:T(8,128)(2,1)S(1)}, u32[]{:S(2)}, u32[]{:S(2)}) %collective-permute-start.11) | collective-permute-done | bytes 819232 | tf_op jit(solution)/shard_map/ppermute | solution.py:74
  94.1 1.3 collective-permute-start.14
  95.4 16.3 %collective-permute-done.21 = bf16[320,1280]{1,0:T(8,128)(2,1)} collective-permute-done((bf16[320,1280]{1,0:T(8,128)(2,1)}, bf16[320,1280]{1,0:T(8,128)(2,1)}, u32[]{:S(2)}, u32[]{:S(2)}) %collective-permute-start.21) | collective-permute-done | bytes 819232 | tf_op jit(solution)/shard_map/ppermute | solution.py:74
  111.6 1.3 collective-permute-start.22
  113.2 0.8 collective-permute-start.8
  114.1 0.8 collective-permute-start.6
  115.0 14.4 %collective-permute-done.22.refs_8_ = bf16[320,1280]{1,0:T(8,128)(2,1)S(1)} collective-permute-done((bf16[320,1280]{1,0:T(8,128)(2,1)}, bf16[320,1280]{1,0:T(8,128)(2,1)S(1)}, u32[]{:S(2)}, u32[]{:S(2)}) %collective-permute-start.22) | collective-permute-done | bytes 819232 | tf_op jit(solution)/shard_map/ppermute | solution.py:74
  130.0 1.3 collective-permute-start.4
  131.8 8.0 %fusion.2.early = f32[4,2560]{1,0:T(4,128)S(1)} fusion(f32[1,4,1280]{2,1,0:T(4,128)S(1)} %copy-done, bf16[1,2560,1280]{2,1,0:T(8,128)(2,1)} %param.11), kind=kOutput, calls=%fused_computation.6 | convolution fusion | flops 157286400 | bytes 6615040 | tf_op jit(solution)/shard_map/dot_general | solution.py:324
  139.9 2.2 put.6.refs_10_
  142.1 0.6 put.7.refs_2_
  143.0 0.8 copy-done.1
  144.3 0.7 collective-permute-start.32
  145.0 0.7 collective-permute-start.31
  145.7 0.7 collective-permute-start.30
  146.4 6.0 %collective-permute-done.4.refs_0_ = bf16[320,1280]{1,0:T(8,128)(2,1)S(1)} collective-permute-done((bf16[320,1280]{1,0:T(8,128)(2,1)S(1)}, bf16[320,1280]{1,0:T(8,128)(2,1)S(1)}, u32[]{:S(2)}, u32[]{:S(2)}) %collective-permute-start.4) | collective-permute-done | bytes 819232 | tf_op jit(solution)/shard_map/ppermute | solution.py:74
  152.4 0.7 collective-permute-start.29
  153.3 0.7 collective-permute-start.36
  154.2 0.7 collective-permute-start.35
  154.9 0.7 collective-permute-start.34
  155.7 0.7 collective-permute-start.33
  156.4 1.3 collective-permute-start.40
  157.7 1.3 collective-permute-start.39
  159.1 1.3 collective-permute-start.38
  160.4 1.3 collective-permute-start.37
  162.0 24.0 %collective-permute-done.40.arr = bf16[64,2560]{1,0:T(8,128)(2,1)S(1)} collective-permute-done((bf16[64,2560]{1,0:T(8,128)(2,1)S(1)}, bf16[64,2560]{1,0:T(8,128)(2,1)S(1)}, u32[]{:S(2)}, u32[]{:S(2)}) %collective-permute-start.40) | collective-permute-done | bytes 327712 | tf_op jit(solution)/shard_map/ppermute | solution.py:348
  186.0 3.5 %shard_map.107 = (bf16[256,1280]{1,0:T(8,128)(2,1)S(1)}, bf16[256,2560]{1,0:T(8,128)(2,1)S(1)}) custom-call(bf16[2,2560,1280]{2,1,0:T(8,128)(2,1)S(1)} %put.11.w, bf16[64,2560]{1,0:T(8,128)(2,1)S(1)} %collective-permute-done.40.arr, bf16[256,1280]{1,0:T(8,128)(2,1)S(1)} %bitcast.33, ...), custom_call_target="tpu_custom_call", output_to_operand_aliasing={{0}: (4, {}), {1}: (5, {})} | custom-call | flops 838860800 | bytes 13107200 | tf_op jit(solution)/shard_map/pallas_call | solution.py:225
  189.5 3.5 %collective-permute-done.39.arr = bf16[64,2560]{1,0:T(8,128)(2,1)S(1)} collective-permute-done((bf16[64,2560]{1,0:T(8,128)(2,1)S(1)}, bf16[64,2560]{1,0:T(8,128)(2,1)S(1)}, u32[]{:S(2)}, u32[]{:S(2)}) %collective-permute-start.39) | collective-permute-done | bytes 327712 | tf_op jit(solution)/shard_map/ppermute | solution.py:348
  193.0 3.5 %shard_map.108 = (bf16[256,1280]{1,0:T(8,128)(2,1)S(1)}, bf16[256,2560]{1,0:T(8,128)(2,1)S(1)}) custom-call(bf16[2,2560,1280]{2,1,0:T(8,128)(2,1)S(1)} %put.11.w, bf16[64,2560]{1,0:T(8,128)(2,1)S(1)} %collective-permute-done.39.arr, bf16[256,1280]{1,0:T(8,128)(2,1)S(1)} %bitcast.34, ...), custom_call_target="tpu_custom_call", output_to_operand_aliasing={{0}: (4, {}), {1}: (5, {})} | custom-call | flops 838860800 | bytes 13107200 | tf_op jit(solution)/shard_map/pallas_call | solution.py:225
  196.5 3.5 %collective-permute-done.38.arr = bf16[64,2560]{1,0:T(8,128)(2,1)S(1)} collective-permute-done((bf16[64,2560]{1,0:T(8,128)(2,1)S(1)}, bf16[64,2560]{1,0:T(8,128)(2,1)S(1)}, u32[]{:S(2)}, u32[]{:S(2)}) %collective-permute-start.38) | collective-permute-done | bytes 327712 | tf_op jit(solution)/shard_map/ppermute | solution.py:348
  200.0 3.5 %shard_map.109 = (bf16[256,1280]{1,0:T(8,128)(2,1)S(1)}, bf16[256,2560]{1,0:T(8,128)(2,1)S(1)}) custom-call(bf16[2,2560,1280]{2,1,0:T(8,128)(2,1)S(1)} %put.11.w, bf16[64,2560]{1,0:T(8,128)(2,1)S(1)} %collective-permute-done.38.arr, bf16[256,1280]{1,0:T(8,128)(2,1)S(1)} %bitcast.35, ...), custom_call_target="tpu_custom_call", output_to_operand_aliasing={{0}: (4, {}), {1}: (5, {})} | custom-call | flops 838860800 | bytes 13107200 | tf_op jit(solution)/shard_map/pallas_call | solution.py:225
  203.6 4.2 %collective-permute-done.37.arr = bf16[64,2560]{1,0:T(8,128)(2,1)S(1)} collective-permute-done((bf16[64,2560]{1,0:T(8,128)(2,1)S(1)}, bf16[64,2560]{1,0:T(8,128)(2,1)S(1)}, u32[]{:S(2)}, u32[]{:S(2)}) %collective-permute-start.37) | collective-permute-done | bytes 327712 | tf_op jit(solution)/shard_map/ppermute | solution.py:348
  207.7 3.5 %shard_map.110 = (bf16[256,1280]{1,0:T(8,128)(2,1)S(1)}, bf16[256,2560]{1,0:T(8,128)(2,1)S(1)}) custom-call(bf16[2,2560,1280]{2,1,0:T(8,128)(2,1)S(1)} %put.11.w, bf16[64,2560]{1,0:T(8,128)(2,1)S(1)} %collective-permute-done.37.arr, bf16[256,1280]{1,0:T(8,128)(2,1)S(1)} %bitcast.36, ...), custom_call_target="tpu_custom_call", output_to_operand_aliasing={{0}: (4, {}), {1}: (5, {})} | custom-call | flops 838860800 | bytes 13107200 | tf_op jit(solution)/shard_map/pallas_call | solution.py:225
  211.3 0.7 fusion
  211.9 0.7 convolution_add_fusion
  212.6 1.2 collective-permute-done.41
  213.9 4.0 %collective-permute-done.42 = f32[4,2560]{1,0:T(4,128)S(1)} collective-permute-done((f32[4,2560]{1,0:T(4,128)S(1)}, f32[4,2560]{1,0:T(4,128)S(1)}, u32[]{:S(2)}, u32[]{:S(2)}) %collective-permute-start.42) | collective-permute-done | bytes 40992 | tf_op jit(solution)/shard_map/ppermute | solution.py:301
  218.0 4.9 %collective-permute-done.43.refs_1_ = f32[4,2560]{1,0:T(4,128)S(1)} collective-permute-done((f32[4,2560]{1,0:T(4,128)S(1)}, f32[4,2560]{1,0:T(4,128)S(1)}, u32[]{:S(2)}, u32[]{:S(2)}) %collective-permute-start.43) | collective-permute-done | bytes 40992 | tf_op jit(solution)/shard_map/ppermute | solution.py:301
  222.9 2.8 %second_half.1 = (f32[4,2560]{1,0:T(4,128)}, f32[4,1280]{1,0:T(4,128)S(1)}, bf16[256,2560]{1,0:T(8,128)(2,1)}) custom-call(f32[4,2560]{1,0:T(4,128)S(1)} %add.23.refs_0_, f32[4,2560]{1,0:T(4,128)S(1)} %collective-permute-done.43.refs_1_, bf16[256,2560]{1,0:T(8,128)(2,1)S(1)} %bitcast.40, bf16[256,1280]{1,0:T(8,128)(2,1)S(1)} %get-tuple-element.96.refs_3_, ...), custom_call_target="tpu_custom_call" | custom-call | tf_op jit(solution)/shard_map/second_half/pallas_call | solution.py:284
  225.8 1.2 collective-permute-done.44
  227.5 3.9 %collective-permute-start.47 = (f32[4,1280]{1,0:T(4,128)S(1)}, f32[4,1280]{1,0:T(4,128)S(1)}, u32[]{:S(2)}, u32[]{:S(2)}) collective-permute-start(f32[4,1280]{1,0:T(4,128)S(1)} %add.24), channel_id=1, source_target_pairs={{0,6},{1,7},{2,4},{3,5},{4,2},{5,3},{6,0},{7,1},{8,14},{9,15},{10,... | collective-permute-start | bytes 61448 | tf_op jit(solution)/shard_map/ppermute | solution.py:301
  231.8 1.6 collective-permute-done.47
  233.4 0.6 multiply_bitcast_fusion
  (103 shorter events, 4.8 us)
Async XLA Ops:
  0.6 131.1 %copy-start = (f32[1,4,1280]{2,1,0:T(4,128)S(1)}, f32[1,4,1280]{2,1,0:T(4,128)}, u32[]{:S(2)}) copy-start(f32[1,4,1280]{2,1,0:T(4,128)} %param.13) | copy-start | bytes 61444
  0.6 23.9 %collective-permute-start.2 = (bf16[320,1280]{1,0:T(8,128)(2,1)}, bf16[320,1280]{1,0:T(8,128)(2,1)S(1)}, u32[]{:S(2)}, u32[]{:S(2)}) collective-permute-start(bf16[320,1280]{1,0:T(8,128)(2,1)} %bitcast.41), channel_id=1, source_target_pairs={{0,2},{1,3},{2,4},{3,5},{4,6},{5,7},{8,10},{9,11},{10,12},{11,13},... | collective-permute-start | bytes 2457608 | tf_op jit(solution)/shard_map/ppermute | solution.py:74
  5.7 23.3 %collective-permute-start = (bf16[320,1280]{1,0:T(8,128)(2,1)}, bf16[320,1280]{1,0:T(8,128)(2,1)}, u32[]{:S(2)}, u32[]{:S(2)}) collective-permute-start(bf16[320,1280]{1,0:T(8,128)(2,1)} %bitcast.42), channel_id=1, source_target_pairs={{2,0},{3,1},{4,2},{5,3},{6,4},{7,5},{10,8},{11,9},{12,10},{13,11},... | collective-permute-start | bytes 2457608 | tf_op jit(solution)/shard_map/ppermute | solution.py:74
  7.0 34.0 %collective-permute-start.12 = (bf16[320,1280]{1,0:T(8,128)(2,1)}, bf16[320,1280]{1,0:T(8,128)(2,1)}, u32[]{:S(2)}, u32[]{:S(2)}) collective-permute-start(bf16[320,1280]{1,0:T(8,128)(2,1)} %bitcast.45), channel_id=1, source_target_pairs={{0,2},{1,3},{2,4},{3,5},{4,6},{5,7},{8,10},{9,11},{10,12},{11,13},... | collective-permute-start | bytes 2457608 | tf_op jit(solution)/shard_map/ppermute | solution.py:74
  12.4 32.7 %collective-permute-start.10 = (bf16[320,1280]{1,0:T(8,128)(2,1)}, bf16[320,1280]{1,0:T(8,128)(2,1)}, u32[]{:S(2)}, u32[]{:S(2)}) collective-permute-start(bf16[320,1280]{1,0:T(8,128)(2,1)} %bitcast.46), channel_id=1, source_target_pairs={{2,0},{3,1},{4,2},{5,3},{6,4},{7,5},{10,8},{11,9},{12,10},{13,11},... | collective-permute-start | bytes 2457608 | tf_op jit(solution)/shard_map/ppermute | solution.py:74
  13.7 34.2 %collective-permute-start.20 = (bf16[320,1280]{1,0:T(8,128)(2,1)}, bf16[320,1280]{1,0:T(8,128)(2,1)}, u32[]{:S(2)}, u32[]{:S(2)}) collective-permute-start(bf16[320,1280]{1,0:T(8,128)(2,1)} %bitcast.43), channel_id=1, source_target_pairs={{26,2},{27,3},{28,4},{29,5}} | collective-permute-start | bytes 2457608 | tf_op jit(solution)/shard_map/ppermute | solution.py:74
  24.5 23.8 %copy-start.6 = (bf16[320,1280]{1,0:T(8,128)(2,1)}, bf16[320,1280]{1,0:T(8,128)(2,1)S(1)}, u32[]{:S(2)}) copy-start(bf16[320,1280]{1,0:T(8,128)(2,1)S(1)} %collective-permute-done.2.refs_7_) | copy-start | bytes 2457604
  24.5 23.8 %collective-permute-start.27 = (bf16[320,1280]{1,0:T(8,128)(2,1)S(1)}, bf16[320,1280]{1,0:T(8,128)(2,1)S(1)}, u32[]{:S(2)}, u32[]{:S(2)}) collective-permute-start(bf16[320,1280]{1,0:T(8,128)(2,1)S(1)} %collective-permute-done.2.refs_7_), channel_id=1, source_target_pairs={{0,1},{1,0},{2,3},{3,2},{4,5},{5,4},{6,7},{7,6},{8,9},{9,8},{10,11... | collective-permute-start | bytes 2457608 | tf_op jit(solution)/shard_map/ppermute | solution.py:82
  29.0 21.0 %collective-permute-start.28 = (bf16[320,1280]{1,0:T(8,128)(2,1)}, bf16[320,1280]{1,0:T(8,128)(2,1)S(1)}, u32[]{:S(2)}, u32[]{:S(2)}) collective-permute-start(bf16[320,1280]{1,0:T(8,128)(2,1)} %collective-permute-done.refs_9_), channel_id=1, source_target_pairs={{0,1},{1,0},{2,3},{3,2},{4,5},{5,4},{6,7},{7,6},{8,9},{9,8},{10,11... | collective-permute-start | bytes 2457608 | tf_op jit(solution)/shard_map/ppermute | solution.py:82
  41.0 11.2 %collective-permute-start.25 = (bf16[320,1280]{1,0:T(8,128)(2,1)}, bf16[320,1280]{1,0:T(8,128)(2,1)S(1)}, u32[]{:S(2)}, u32[]{:S(2)}) collective-permute-start(bf16[320,1280]{1,0:T(8,128)(2,1)} %collective-permute-done.12.refs_3_), channel_id=1, source_target_pairs={{0,1},{1,0},{2,3},{3,2},{4,5},{5,4},{6,7},{7,6},{8,9},{9,8},{10,11... | collective-permute-start | bytes 2457608 | tf_op jit(solution)/shard_map/ppermute | solution.py:82
  45.1 8.7 %collective-permute-start.26 = (bf16[320,1280]{1,0:T(8,128)(2,1)}, bf16[320,1280]{1,0:T(8,128)(2,1)S(1)}, u32[]{:S(2)}, u32[]{:S(2)}) collective-permute-start(bf16[320,1280]{1,0:T(8,128)(2,1)} %collective-permute-done.10.refs_5_), channel_id=1, source_target_pairs={{0,1},{1,0},{2,3},{3,2},{4,5},{5,4},{6,7},{7,6},{8,9},{9,8},{10,11... | collective-permute-start | bytes 2457608 | tf_op jit(solution)/shard_map/ppermute | solution.py:82
  47.9 46.2 %collective-permute-start.24 = (bf16[2,320,1280]{2,1,0:T(8,128)(2,1)}, bf16[2,320,1280]{2,1,0:T(8,128)(2,1)}, u32[]{:S(2)}, u32[]{:S(2)}) collective-permute-start(bf16[2,320,1280]{2,1,0:T(8,128)(2,1)} %pad_maximum_fusion), channel_id=1, source_target_pairs={{0,1},{1,0},{2,3},{3,2},{4,5},{5,4},{6,7},{7,6},{8,9},{9,8},{10,11... | collective-permute-start | bytes 4915208 | tf_op jit(solution)/shard_map/ppermute | solution.py:82
  49.3 6.8 %collective-permute-start.3 = (bf16[320,1280]{1,0:T(8,128)(2,1)S(1)}, bf16[320,1280]{1,0:T(8,128)(2,1)S(1)}, u32[]{:S(2)}, u32[]{:S(2)}) collective-permute-start(bf16[320,1280]{1,0:T(8,128)(2,1)S(1)} %collective-permute-done.2.refs_7_), channel_id=1, source_target_pairs={{2,4},{3,5},{4,6},{5,7},{10,12},{11,13},{12,14},{13,15},{18,20},{1... | collective-permute-start | bytes 2457608 | tf_op jit(solution)/shard_map/ppermute | solution.py:74
  50.0 0.9 copy-start.10
  50.9 25.5 %collective-permute-start.1 = (bf16[320,1280]{1,0:T(8,128)(2,1)}, bf16[320,1280]{1,0:T(8,128)(2,1)S(1)}, u32[]{:S(2)}, u32[]{:S(2)}) collective-permute-start(bf16[320,1280]{1,0:T(8,128)(2,1)} %collective-permute-done.refs_9_), channel_id=1, source_target_pairs={{2,0},{3,1},{4,2},{5,3},{10,8},{11,9},{12,10},{13,11},{18,16},{19,... | collective-permute-start | bytes 2457608 | tf_op jit(solution)/shard_map/ppermute | solution.py:74
  53.1 23.4 %collective-permute-start.13 = (bf16[320,1280]{1,0:T(8,128)(2,1)}, bf16[320,1280]{1,0:T(8,128)(2,1)S(1)}, u32[]{:S(2)}, u32[]{:S(2)}) collective-permute-start(bf16[320,1280]{1,0:T(8,128)(2,1)} %collective-permute-done.12.refs_3_), channel_id=1, source_target_pairs={{2,4},{3,5},{4,6},{5,7},{10,12},{11,13},{12,14},{13,15},{18,20},{1... | collective-permute-start | bytes 2457608 | tf_op jit(solution)/shard_map/ppermute | solution.py:74
  53.8 1.0 copy-start.14
  54.8 39.2 %collective-permute-start.11 = (bf16[320,1280]{1,0:T(8,128)(2,1)}, bf16[320,1280]{1,0:T(8,128)(2,1)S(1)}, u32[]{:S(2)}, u32[]{:S(2)}) collective-permute-start(bf16[320,1280]{1,0:T(8,128)(2,1)} %collective-permute-done.10.refs_5_), channel_id=1, source_target_pairs={{2,0},{3,1},{4,2},{5,3},{10,8},{11,9},{12,10},{13,11},{18,16},{19,... | collective-permute-start | bytes 2457608 | tf_op jit(solution)/shard_map/ppermute | solution.py:74
  56.1 55.6 %collective-permute-start.21 = (bf16[320,1280]{1,0:T(8,128)(2,1)}, bf16[320,1280]{1,0:T(8,128)(2,1)}, u32[]{:S(2)}, u32[]{:S(2)}) collective-permute-start(bf16[320,1280]{1,0:T(8,128)(2,1)} %collective-permute-done.20), channel_id=1, source_target_pairs={{2,0},{3,1},{4,6},{5,7}} | collective-permute-start | bytes 2457608 | tf_op jit(solution)/shard_map/ppermute | solution.py:74
  76.4 36.7 %collective-permute-start.18 = (bf16[320,1280]{1,0:T(8,128)(2,1)S(1)}, bf16[320,1280]{1,0:T(8,128)(2,1)S(1)}, u32[]{:S(2)}, u32[]{:S(2)}) collective-permute-start(bf16[320,1280]{1,0:T(8,128)(2,1)S(1)} %collective-permute-done.3.refs_4_), channel_id=1, source_target_pairs={{0,1},{1,0},{2,3},{3,2},{4,5},{5,4},{6,7},{7,6},{8,9},{9,8},{10,11... | collective-permute-start | bytes 2457608 | tf_op jit(solution)/shard_map/ppermute | solution.py:82
  76.4 37.6 %collective-permute-start.19 = (bf16[320,1280]{1,0:T(8,128)(2,1)S(1)}, bf16[320,1280]{1,0:T(8,128)(2,1)S(1)}, u32[]{:S(2)}, u32[]{:S(2)}) collective-permute-start(bf16[320,1280]{1,0:T(8,128)(2,1)S(1)} %collective-permute-done.1.refs_6_), channel_id=1, source_target_pairs={{0,1},{1,0},{2,3},{3,2},{4,5},{5,4},{6,7},{7,6},{8,9},{9,8},{10,11... | collective-permute-start | bytes 2457608 | tf_op jit(solution)/shard_map/ppermute | solution.py:82
  94.0 20.1 %collective-permute-start.16 = (bf16[320,1280]{1,0:T(8,128)(2,1)S(1)}, bf16[320,1280]{1,0:T(8,128)(2,1)S(1)}, u32[]{:S(2)}, u32[]{:S(2)}) collective-permute-start(bf16[320,1280]{1,0:T(8,128)(2,1)S(1)} %collective-permute-done.13.refs_0_), channel_id=1, source_target_pairs={{0,1},{1,0},{2,3},{3,2},{4,5},{5,4},{6,7},{7,6},{8,9},{9,8},{10,11... | collective-permute-start | bytes 2457608 | tf_op jit(solution)/shard_map/ppermute | solution.py:82
  94.1 35.3 %collective-permute-start.14 = (bf16[320,1280]{1,0:T(8,128)(2,1)S(1)}, bf16[320,1280]{1,0:T(8,128)(2,1)S(1)}, u32[]{:S(2)}, u32[]{:S(2)}) collective-permute-start(bf16[320,1280]{1,0:T(8,128)(2,1)S(1)} %broadcast_select_fusion), channel_id=1, source_target_pairs={{2,0},{3,1},{4,6},{5,7},{10,8},{11,9},{12,14},{13,15},{18,16},{19,... | collective-permute-start | bytes 2457608 | tf_op jit(solution)/shard_map/ppermute | solution.py:74
  111.6 17.7 %collective-permute-start.22 = (bf16[320,1280]{1,0:T(8,128)(2,1)}, bf16[320,1280]{1,0:T(8,128)(2,1)S(1)}, u32[]{:S(2)}, u32[]{:S(2)}) collective-permute-start(bf16[320,1280]{1,0:T(8,128)(2,1)} %collective-permute-done.21), channel_id=1, source_target_pairs={{0,24},{1,25},{6,30},{7,31}} | collective-permute-start | bytes 2457608 | tf_op jit(solution)/shard_map/ppermute | solution.py:74
  113.1 26.7 %copy-start.4 = (bf16[1,320,1280]{2,1,0:T(8,128)(2,1)S(1)}, bf16[1,320,1280]{2,1,0:T(8,128)(2,1)}, u32[]{:S(2)}) copy-start(bf16[1,320,1280]{2,1,0:T(8,128)(2,1)} %param.9) | copy-start | bytes 2457604
  113.1 26.7 %copy-start.5 = (bf16[1,320,1280]{2,1,0:T(8,128)(2,1)S(1)}, bf16[1,320,1280]{2,1,0:T(8,128)(2,1)}, u32[]{:S(2)}) copy-start(bf16[1,320,1280]{2,1,0:T(8,128)(2,1)} %param.10) | copy-start | bytes 2457604
  113.1 26.7 %copy-start.7 = (bf16[320,1280]{1,0:T(8,128)(2,1)S(1)}, bf16[320,1280]{1,0:T(8,128)(2,1)}, u32[]{:S(2)}) copy-start(bf16[320,1280]{1,0:T(8,128)(2,1)} %copy-done.6) | copy-start | bytes 2457604
  113.1 26.7 %copy-start.9 = (bf16[320,1280]{1,0:T(8,128)(2,1)S(1)}, bf16[320,1280]{1,0:T(8,128)(2,1)}, u32[]{:S(2)}) copy-start(bf16[320,1280]{1,0:T(8,128)(2,1)} %copy-done.8) | copy-start | bytes 2457604
  113.1 26.7 %copy-start.11 = (bf16[320,1280]{1,0:T(8,128)(2,1)S(1)}, bf16[320,1280]{1,0:T(8,128)(2,1)}, u32[]{:S(2)}) copy-start(bf16[320,1280]{1,0:T(8,128)(2,1)} %copy-done.10) | copy-start | bytes 2457604
  113.1 26.7 %copy-start.13 = (bf16[320,1280]{1,0:T(8,128)(2,1)S(1)}, bf16[320,1280]{1,0:T(8,128)(2,1)}, u32[]{:S(2)}) copy-start(bf16[320,1280]{1,0:T(8,128)(2,1)} %copy-done.12) | copy-start | bytes 2457604
  113.1 26.7 %copy-start.15 = (bf16[320,1280]{1,0:T(8,128)(2,1)S(1)}, bf16[320,1280]{1,0:T(8,128)(2,1)}, u32[]{:S(2)}) copy-start(bf16[320,1280]{1,0:T(8,128)(2,1)} %copy-done.14) | copy-start | bytes 2457604
  113.2 16.7 %collective-permute-start.8 = (bf16[320,1280]{1,0:T(8,128)(2,1)S(1)}, bf16[320,1280]{1,0:T(8,128)(2,1)S(1)}, u32[]{:S(2)}, u32[]{:S(2)}) collective-permute-start(bf16[320,1280]{1,0:T(8,128)(2,1)S(1)} %broadcast_select_fusion.1), channel_id=1, source_target_pairs={{26,24},{27,25},{28,30},{29,31}} | collective-permute-start | bytes 2457608 | tf_op jit(solution)/shard_map/ppermute | solution.py:74
  114.0 15.9 %collective-permute-start.17 = (bf16[320,1280]{1,0:T(8,128)(2,1)S(1)}, bf16[320,1280]{1,0:T(8,128)(2,1)S(1)}, u32[]{:S(2)}, u32[]{:S(2)}) collective-permute-start(bf16[320,1280]{1,0:T(8,128)(2,1)S(1)} %collective-permute-done.11.refs_2_), channel_id=1, source_target_pairs={{0,1},{1,0},{2,3},{3,2},{4,5},{5,4},{6,7},{7,6},{8,9},{9,8},{10,11... | collective-permute-start | bytes 2457608 | tf_op jit(solution)/shard_map/ppermute | solution.py:82
  114.1 17.1 %collective-permute-start.6 = (bf16[320,1280]{1,0:T(8,128)(2,1)S(1)}, bf16[320,1280]{1,0:T(8,128)(2,1)S(1)}, u32[]{:S(2)}, u32[]{:S(2)}) collective-permute-start(bf16[320,1280]{1,0:T(8,128)(2,1)S(1)} %broadcast_select_fusion.1), channel_id=1, source_target_pairs={{10,8},{11,9},{12,14},{13,15},{18,16},{19,17},{20,22},{21,23}} | collective-permute-start | bytes 2457608 | tf_op jit(solution)/shard_map/ppermute | solution.py:74
  129.4 12.7 %collective-permute-start.23 = (bf16[320,1280]{1,0:T(8,128)(2,1)S(1)}, bf16[320,1280]{1,0:T(8,128)(2,1)S(1)}, u32[]{:S(2)}, u32[]{:S(2)}) collective-permute-start(bf16[320,1280]{1,0:T(8,128)(2,1)S(1)} %collective-permute-done.22.refs_8_), channel_id=1, source_target_pairs={{0,1},{1,0},{2,3},{3,2},{4,5},{5,4},{6,7},{7,6},{8,9},{9,8},{10,11... | collective-permute-start | bytes 2457608 | tf_op jit(solution)/shard_map/ppermute | solution.py:82
  129.4 13.3 %collective-permute-start.15 = (bf16[320,1280]{1,0:T(8,128)(2,1)S(1)}, bf16[320,1280]{1,0:T(8,128)(2,1)S(1)}, u32[]{:S(2)}, u32[]{:S(2)}) collective-permute-start(bf16[320,1280]{1,0:T(8,128)(2,1)S(1)} %collective-permute-done.14.refs_0_), channel_id=1, source_target_pairs={{0,1},{1,0},{2,3},{3,2},{4,5},{5,4},{6,7},{7,6},{8,9},{9,8},{10,11... | collective-permute-start | bytes 2457608 | tf_op jit(solution)/shard_map/ppermute | solution.py:82
  129.9 14.3 %collective-permute-start.9 = (bf16[320,1280]{1,0:T(8,128)(2,1)S(1)}, bf16[320,1280]{1,0:T(8,128)(2,1)S(1)}, u32[]{:S(2)}, u32[]{:S(2)}) collective-permute-start(bf16[320,1280]{1,0:T(8,128)(2,1)S(1)} %collective-permute-done.8.refs_0_), channel_id=1, source_target_pairs={{0,1},{1,0},{2,3},{3,2},{4,5},{5,4},{6,7},{7,6},{8,9},{9,8},{10,11... | collective-permute-start | bytes 2457608 | tf_op jit(solution)/shard_map/ppermute | solution.py:82
  130.0 22.5 %collective-permute-start.4 = (bf16[320,1280]{1,0:T(8,128)(2,1)S(1)}, bf16[320,1280]{1,0:T(8,128)(2,1)S(1)}, u32[]{:S(2)}, u32[]{:S(2)}) collective-permute-start(bf16[320,1280]{1,0:T(8,128)(2,1)S(1)} %broadcast_select_fusion.1), channel_id=1, source_target_pairs={{2,0},{3,1},{4,6},{5,7}} | collective-permute-start | bytes 2457608 | tf_op jit(solution)/shard_map/ppermute | solution.py:74
  131.3 21.9 %collective-permute-start.7 = (bf16[320,1280]{1,0:T(8,128)(2,1)S(1)}, bf16[320,1280]{1,0:T(8,128)(2,1)S(1)}, u32[]{:S(2)}, u32[]{:S(2)}) collective-permute-start(bf16[320,1280]{1,0:T(8,128)(2,1)S(1)} %collective-permute-done.6.refs_0_), channel_id=1, source_target_pairs={{0,1},{1,0},{2,3},{3,2},{4,5},{5,4},{6,7},{7,6},{8,9},{9,8},{10,11... | collective-permute-start | bytes 2457608 | tf_op jit(solution)/shard_map/ppermute | solution.py:82
  142.6 1.1 copy-start.1
  142.7 1.5 copy-start.2
  144.3 9.0 %collective-permute-start.32 = (bf16[64,2560]{1,0:T(8,128)(2,1)S(1)}, bf16[64,2560]{1,0:T(8,128)(2,1)S(1)}, u32[]{:S(2)}, u32[]{:S(2)}) collective-permute-start(bf16[64,2560]{1,0:T(8,128)(2,1)S(1)} %get-tuple-element.64), channel_id=1, source_target_pairs={{24,16},{25,17},{26,18},{27,19},{28,20},{29,21},{30,22},{31,23}} | collective-permute-start | bytes 983048 | tf_op jit(solution)/shard_map/ppermute | solution.py:348
  145.0 9.0 %collective-permute-start.31 = (bf16[64,2560]{1,0:T(8,128)(2,1)S(1)}, bf16[64,2560]{1,0:T(8,128)(2,1)S(1)}, u32[]{:S(2)}, u32[]{:S(2)}) collective-permute-start(bf16[64,2560]{1,0:T(8,128)(2,1)S(1)} %get-tuple-element.63), channel_id=1, source_target_pairs={{24,16},{25,17},{26,18},{27,19},{28,20},{29,21},{30,22},{31,23}} | collective-permute-start | bytes 983048 | tf_op jit(solution)/shard_map/ppermute | solution.py:348
  145.7 9.2 %collective-permute-start.30 = (bf16[64,2560]{1,0:T(8,128)(2,1)S(1)}, bf16[64,2560]{1,0:T(8,128)(2,1)S(1)}, u32[]{:S(2)}, u32[]{:S(2)}) collective-permute-start(bf16[64,2560]{1,0:T(8,128)(2,1)S(1)} %get-tuple-element.62), channel_id=1, source_target_pairs={{24,16},{25,17},{26,18},{27,19},{28,20},{29,21},{30,22},{31,23}} | collective-permute-start | bytes 983048 | tf_op jit(solution)/shard_map/ppermute | solution.py:348
  152.4 3.2 %collective-permute-start.29 = (bf16[64,2560]{1,0:T(8,128)(2,1)S(1)}, bf16[64,2560]{1,0:T(8,128)(2,1)S(1)}, u32[]{:S(2)}, u32[]{:S(2)}) collective-permute-start(bf16[64,2560]{1,0:T(8,128)(2,1)S(1)} %get-tuple-element.61), channel_id=1, source_target_pairs={{24,16},{25,17},{26,18},{27,19},{28,20},{29,21},{30,22},{31,23}} | collective-permute-start | bytes 983048 | tf_op jit(solution)/shard_map/ppermute | solution.py:348
  153.1 8.6 %collective-permute-start.5 = (bf16[320,1280]{1,0:T(8,128)(2,1)S(1)}, bf16[320,1280]{1,0:T(8,128)(2,1)S(1)}, u32[]{:S(2)}, u32[]{:S(2)}) collective-permute-start(bf16[320,1280]{1,0:T(8,128)(2,1)S(1)} %collective-permute-done.4.refs_0_), channel_id=1, source_target_pairs={{0,1},{1,0},{2,3},{3,2},{4,5},{5,4},{6,7},{7,6},{8,9},{9,8},{10,11... | collective-permute-start | bytes 2457608 | tf_op jit(solution)/shard_map/ppermute | solution.py:82
  153.3 3.0 %collective-permute-start.36 = (bf16[64,2560]{1,0:T(8,128)(2,1)S(1)}, bf16[64,2560]{1,0:T(8,128)(2,1)S(1)}, u32[]{:S(2)}, u32[]{:S(2)}) collective-permute-start(bf16[64,2560]{1,0:T(8,128)(2,1)S(1)} %get-tuple-element.75), channel_id=1, source_target_pairs={{16,8},{17,9},{18,10},{19,11},{20,12},{21,13},{22,14},{23,15}} | collective-permute-start | bytes 983048 | tf_op jit(solution)/shard_map/ppermute | solution.py:348
  154.2 3.5 %collective-permute-start.35 = (bf16[64,2560]{1,0:T(8,128)(2,1)S(1)}, bf16[64,2560]{1,0:T(8,128)(2,1)S(1)}, u32[]{:S(2)}, u32[]{:S(2)}) collective-permute-start(bf16[64,2560]{1,0:T(8,128)(2,1)S(1)} %get-tuple-element.74), channel_id=1, source_target_pairs={{16,8},{17,9},{18,10},{19,11},{20,12},{21,13},{22,14},{23,15}} | collective-permute-start | bytes 983048 | tf_op jit(solution)/shard_map/ppermute | solution.py:348
  154.9 4.1 %collective-permute-start.34 = (bf16[64,2560]{1,0:T(8,128)(2,1)S(1)}, bf16[64,2560]{1,0:T(8,128)(2,1)S(1)}, u32[]{:S(2)}, u32[]{:S(2)}) collective-permute-start(bf16[64,2560]{1,0:T(8,128)(2,1)S(1)} %get-tuple-element.73), channel_id=1, source_target_pairs={{16,8},{17,9},{18,10},{19,11},{20,12},{21,13},{22,14},{23,15}} | collective-permute-start | bytes 983048 | tf_op jit(solution)/shard_map/ppermute | solution.py:348
  155.7 4.7 %collective-permute-start.33 = (bf16[64,2560]{1,0:T(8,128)(2,1)S(1)}, bf16[64,2560]{1,0:T(8,128)(2,1)S(1)}, u32[]{:S(2)}, u32[]{:S(2)}) collective-permute-start(bf16[64,2560]{1,0:T(8,128)(2,1)S(1)} %get-tuple-element.72), channel_id=1, source_target_pairs={{16,8},{17,9},{18,10},{19,11},{20,12},{21,13},{22,14},{23,15}} | collective-permute-start | bytes 983048 | tf_op jit(solution)/shard_map/ppermute | solution.py:348
  156.4 29.6 %collective-permute-start.40 = (bf16[64,2560]{1,0:T(8,128)(2,1)S(1)}, bf16[64,2560]{1,0:T(8,128)(2,1)S(1)}, u32[]{:S(2)}, u32[]{:S(2)}) collective-permute-start(bf16[64,2560]{1,0:T(8,128)(2,1)S(1)} %get-tuple-element.88), channel_id=1, source_target_pairs={{8,0},{9,1},{10,2},{11,3},{12,4},{13,5},{14,6},{15,7}} | collective-permute-start | bytes 983048 | tf_op jit(solution)/shard_map/ppermute | solution.py:348
  157.7 35.3 %collective-permute-start.39 = (bf16[64,2560]{1,0:T(8,128)(2,1)S(1)}, bf16[64,2560]{1,0:T(8,128)(2,1)S(1)}, u32[]{:S(2)}, u32[]{:S(2)}) collective-permute-start(bf16[64,2560]{1,0:T(8,128)(2,1)S(1)} %get-tuple-element.87), channel_id=1, source_target_pairs={{8,0},{9,1},{10,2},{11,3},{12,4},{13,5},{14,6},{15,7}} | collective-permute-start | bytes 983048 | tf_op jit(solution)/shard_map/ppermute | solution.py:348
  159.1 41.0 %collective-permute-start.38 = (bf16[64,2560]{1,0:T(8,128)(2,1)S(1)}, bf16[64,2560]{1,0:T(8,128)(2,1)S(1)}, u32[]{:S(2)}, u32[]{:S(2)}) collective-permute-start(bf16[64,2560]{1,0:T(8,128)(2,1)S(1)} %get-tuple-element.86), channel_id=1, source_target_pairs={{8,0},{9,1},{10,2},{11,3},{12,4},{13,5},{14,6},{15,7}} | collective-permute-start | bytes 983048 | tf_op jit(solution)/shard_map/ppermute | solution.py:348
  160.4 47.3 %collective-permute-start.37 = (bf16[64,2560]{1,0:T(8,128)(2,1)S(1)}, bf16[64,2560]{1,0:T(8,128)(2,1)S(1)}, u32[]{:S(2)}, u32[]{:S(2)}) collective-permute-start(bf16[64,2560]{1,0:T(8,128)(2,1)S(1)} %get-tuple-element.85), channel_id=1, source_target_pairs={{8,0},{9,1},{10,2},{11,3},{12,4},{13,5},{14,6},{15,7}} | collective-permute-start | bytes 983048 | tf_op jit(solution)/shard_map/ppermute | solution.py:348
  207.7 15.2 %slice-start = ((s8[6553600]{0:T(1024)(128)(4,1)}), s8[4194304]{0:T(1024)(128)(4,1)S(1)}, s32[]{:S(2)}) async-start(s8[6553600]{0:T(1024)(128)(4,1)} %bitcast.37), calls=%async_computation | async-start | bytes 8388608
  207.7 4.2 %copy-start.3 = (bf16[1,256,2560]{2,1,0:T(8,128)(2,1)S(1)}, bf16[1,256,2560]{2,1,0:T(8,128)(2,1)}, u32[]{:S(2)}) copy-start(bf16[1,256,2560]{2,1,0:T(8,128)(2,1)} %param.7) | copy-start | bytes 3932164
  207.7 15.2 %slice-start.1 = ((s8[6553600]{0:T(1024)(128)(4,1)}), s8[2359296]{0:T(1024)(128)(4,1)S(1)}, s32[]{:S(2)}) async-start(s8[6553600]{0:T(1024)(128)(4,1)} %bitcast.37), calls=%async_computation.1 | async-start | bytes 4718592
  212.6 1.2 collective-permute-start.41
  213.8 4.1 %collective-permute-start.42 = (f32[4,2560]{1,0:T(4,128)S(1)}, f32[4,2560]{1,0:T(4,128)S(1)}, u32[]{:S(2)}, u32[]{:S(2)}) collective-permute-start(f32[4,2560]{1,0:T(4,128)S(1)} %add.22), channel_id=1, source_target_pairs={{0,2},{1,3},{2,0},{3,1},{4,6},{5,7},{6,4},{7,5},{8,10},{9,11},{10,... | collective-permute-start | bytes 122888 | tf_op jit(solution)/shard_map/ppermute | solution.py:301
  217.9 5.0 %collective-permute-start.43 = (f32[4,2560]{1,0:T(4,128)S(1)}, f32[4,2560]{1,0:T(4,128)S(1)}, u32[]{:S(2)}, u32[]{:S(2)}) collective-permute-start(f32[4,2560]{1,0:T(4,128)S(1)} %add.23.refs_0_), channel_id=1, source_target_pairs={{0,4},{1,5},{2,6},{3,7},{4,0},{5,1},{6,2},{7,3},{8,12},{9,13},{10,... | collective-permute-start | bytes 122888 | tf_op jit(solution)/shard_map/ppermute | solution.py:301
  225.7 1.3 collective-permute-start.44
  227.0 4.5 %collective-permute-start.45 = (f32[4,1280]{1,0:T(4,128)S(1)}, f32[4,1280]{1,0:T(4,128)S(1)}, u32[]{:S(2)}, u32[]{:S(2)}) collective-permute-start(f32[4,1280]{1,0:T(4,128)S(1)} %add.24), channel_id=1, source_target_pairs={{0,2},{1,3},{2,0},{3,1},{4,6},{5,7},{6,4},{7,5},{8,10},{9,11},{10,... | collective-permute-start | bytes 61448 | tf_op jit(solution)/shard_map/ppermute | solution.py:301
  227.1 4.7 %collective-permute-start.46 = (f32[4,1280]{1,0:T(4,128)S(1)}, f32[4,1280]{1,0:T(4,128)S(1)}, u32[]{:S(2)}, u32[]{:S(2)}) collective-permute-start(f32[4,1280]{1,0:T(4,128)S(1)} %add.24), channel_id=1, source_target_pairs={{0,4},{1,5},{2,6},{3,7},{4,0},{5,1},{6,2},{7,3},{8,12},{9,13},{10,... | collective-permute-start | bytes 61448 | tf_op jit(solution)/shard_map/ppermute | solution.py:301
  227.5 5.9 %collective-permute-start.47 = (f32[4,1280]{1,0:T(4,128)S(1)}, f32[4,1280]{1,0:T(4,128)S(1)}, u32[]{:S(2)}, u32[]{:S(2)}) collective-permute-start(f32[4,1280]{1,0:T(4,128)S(1)} %add.24), channel_id=1, source_target_pairs={{0,6},{1,7},{2,4},{3,5},{4,2},{5,3},{6,0},{7,1},{8,14},{9,15},{10,... | collective-permute-start | bytes 61448 | tf_op jit(solution)/shard_map/ppermute | solution.py:301
  (2 other events, 1.8 us)

commit v7 on v6

--- a/solution.py
+++ b/solution.py
@@ -261,12 +261,13 @@
     return jnp.concatenate(result, 0)
 
 
-def second_half(parts, inputs, value_grads, error, passed_rows):
+def second_half(parts, early, inputs, value_grads, error, passed_rows):
     def body(*refs):
         *parts, acts, vg, err, passed, basis_ref, second_ref, out_ref, done = refs
         copy = pltpu.make_async_copy(passed, out_ref, done)
         copy.start()
-        basis = orthonormal(joined(*(part[...] for part in parts)))
+        *parts, early = (part[...] for part in parts)
+        basis = orthonormal(joined(*parts) + early)
         basis_ref[...] = basis
         pieces = split3(basis)
         mapped = lax.dot_general(
@@ -283,7 +284,7 @@
     channels = value_grads.shape[1]
     return pl.pallas_call(
         body,
-        in_specs=[VMEM] * (len(parts) + 4),
+        in_specs=[VMEM] * (len(parts) + 5),
         out_specs=[VMEM, VMEM, ANY],
         out_shape=[
             jax.ShapeDtypeStruct((rank, width), jnp.float32),
@@ -293,7 +294,7 @@
         scratch_shapes=[pltpu.SemaphoreType.DMA],
         compiler_params=pltpu.CompilerParams(vmem_limit_bytes=8 << 20),
         name="second_half",
-    )(*parts, inputs, value_grads, error, passed_rows)
+    )(*parts, early, inputs, value_grads, error, passed_rows)
 
 
 def exchange(value, by):
@@ -301,15 +302,12 @@
     return lax.ppermute(value, "dp", [(i, i ^ by) for i in range(replicas)])
 
 
-def sum_parts(value, turns):
-    replicas = lax.axis_size("dp")
+def sum_parts(value):
     by = 1
-    while by * (2 if turns else 4) < replicas:
+    while by * 4 < lax.axis_size("dp"):
         value = value + exchange(value, by)
         by *= 2
-    if turns:
-        return value, exchange(value, by)
-    return value, exchange(value, by), exchange(value, 2 * by), exchange(value, 3 * by)
+    return (value,) + tuple(exchange(value, count * by) for count in (1, 2, 3))
 
 
 def joined(first, second, *others):
@@ -328,10 +326,12 @@
 
     def forward_top(whole):
         return stage(
-            whole, grad_top, gate_rows, (), error_part, section=top,
+            whole, grad_top, gate_rows, (), error_sum, section=top,
             first=0, block=row_count, forward=True, backward=False,
         )
 
+    error_parts = sum_parts(error_part)
+    error_sum = joined(*error_parts)
     whole, held, finish = gather_weights((w_out[0], w_value[0]), forward_top)
     blocks = [count * row_count // 16 for count in SIXTEENTHS]
     firsts = [sum(blocks[:k]) for k in range(len(blocks))]
@@ -339,7 +339,7 @@
     for section in reversed(range(sections)):
         for k, (first, block) in enumerate(zip(firsts, blocks)):
             held = stage(
-                whole, arriving[k], gate_rows, held, error_part,
+                whole, arriving[k], gate_rows, held, error_sum,
                 section=section, first=first, block=block,
                 forward=section < top, backward=True,
             )
@@ -355,9 +355,11 @@
     factor = lax.dot_general(
         projected, inputs.astype(jnp.float32), (((0,), (0,)), ((), ())), precision=HIGHEST
     )
-    parts = sum_parts(factor + error_part, True)
-    basis, second, grad_in = second_half(parts, inputs, value_grads, error, passed_rows)
-    right_out = joined(*sum_parts(second, False)) / math.sqrt(row_count * replicas * width)
+    parts = sum_parts(factor)
+    basis, second, grad_in = second_half(
+        parts, error_sum, inputs, value_grads, error, passed_rows
+    )
+    right_out = joined(*sum_parts(second)) / math.sqrt(row_count * replicas * width)
     return grad_in[None], basis[None], right_out[None]
 
 

time: 235 us -> 255 us (1.085)
  starting transfers between devices: 43.1 us -> 56.3 us
  waiting for transfers between devices: 151 us -> 158 us
    ppermute x7 -> x12, waiting for transfers between devices: 13.2 us -> 37.1 us  [exchange(): return lax.ppermute(value, 'dp', [(i, i ^ by) for i in range(replicas)])]
    ppermute x7 -> x12, starting transfers between devices: 4.68 us -> 16.6 us  [exchange(): return lax.ppermute(value, 'dp', [(i, i ^ by) for i in range(replicas)])]
    ppermute x15, waiting for transfers between devices: 103 us -> 93 us  [permute(): return lax.ppermute(value, ('section', 'dp'), pairs)]
    ppermute x12, waiting for transfers between devices: 35.2 us -> 27.8 us  [local(): arriving[k] = lax.ppermute(send, 'section', [(section, section - 1)])]
  transfers between devices with their start and end apart: 48 -> 53, of which waited for: 19 -> 20; matrix products, arithmetic and copies ran while one was open for 5% -> 4% of each run, Pallas kernels for 6% -> 6%
where the time goes in v7:
time: 255 us
  waiting for transfers between devices  158 us (62%)
  starting transfers between devices  56.3 us (22%)
  Pallas kernels  21.4 us (8%)
  matrix products  9.34 us (4%)
  local copies, waits for them, and re-layouts  4.85 us (2%)
  other arithmetic  3.45 us (1%)
    ppermute x15, waiting for transfers between devices, permute(): return lax.ppermute(value, ('section', 'dp'), pairs)  93 us
    ppermute x12, waiting for transfers between devices, exchange(): return lax.ppermute(value, 'dp', [(i, i ^ by) for i in range(replicas)])  37.1 us
    ppermute x12, waiting for transfers between devices, local(): arriving[k] = lax.ppermute(send, 'section', [(section, section - 1)])  27.8 us
    ppermute x15, starting transfers between devices, permute(): return lax.ppermute(value, ('section', 'dp'), pairs)  26.3 us
    ppermute x12, starting transfers between devices, exchange(): return lax.ppermute(value, 'dp', [(i, i ^ by) for i in range(replicas)])  16.6 us
    pallas_call x17, Pallas kernels, stage(): pl.pallas_call(body, in_specs=[VMEM] * 3 + [ANY] + [VMEM] * len(held), ou...  14.5 us
    ppermute x12, starting transfers between devices, local(): arriving[k] = lax.ppermute(send, 'section', [(section, section - 1)])  10.6 us
    dot_general x1, matrix products, local(): lax.dot_general(warm, error.astype(jnp.float32), (((1,), (1,)), ((), ()))...  8.01 us
  transfers between devices with their start and end apart: 53, of which 20 were waited for; matrix products, arithmetic and copies ran while one was open for 4% of the time, Pallas kernels for 6%

profile of v7, /device:TPU:0, one launch (start us, length us, event | category | flops | bytes accessed | tf_op | source)
XLA Modules:
  0.0 254.7 jit_solution(13600357111165524036)
XLA Ops:
  0.6 5.0 %collective-permute-start.2 = (bf16[320,1280]{1,0:T(8,128)(2,1)}, bf16[320,1280]{1,0:T(8,128)(2,1)S(1)}, u32[]{:S(2)}, u32[]{:S(2)}) collective-permute-start(bf16[320,1280]{1,0:T(8,128)(2,1)} %bitcast.41), channel_id=1, source_target_pairs={{0,2},{1,3},{2,4},{3,5},{4,6},{5,7},{8,10},{9,11},{10,12},{11,13},... | collective-permute-start | bytes 2457608 | tf_op jit(solution)/shard_map/ppermute | solution.py:74
  5.7 1.3 collective-permute-start
  7.0 5.6 %collective-permute-start.12 = (bf16[320,1280]{1,0:T(8,128)(2,1)}, bf16[320,1280]{1,0:T(8,128)(2,1)}, u32[]{:S(2)}, u32[]{:S(2)}) collective-permute-start(bf16[320,1280]{1,0:T(8,128)(2,1)} %bitcast.45), channel_id=1, source_target_pairs={{0,2},{1,3},{2,4},{3,5},{4,6},{5,7},{8,10},{9,11},{10,12},{11,13},... | collective-permute-start | bytes 2457608 | tf_op jit(solution)/shard_map/ppermute | solution.py:74
  12.6 1.3 collective-permute-start.10
  13.9 8.0 %fusion.2 = f32[4,2560]{1,0:T(4,128)S(1)} fusion(f32[1,4,1280]{2,1,0:T(4,128)S(1)} %copy-done, bf16[1,2560,1280]{2,1,0:T(8,128)(2,1)} %param.11), kind=kOutput, calls=%fused_computation.6 | convolution fusion | flops 157286400 | bytes 6615040 | tf_op jit(solution)/shard_map/dot_general | solution.py:322
  21.9 1.2 collective-permute-done.29
  23.1 2.7 %collective-permute-start.30 = (f32[4,2560]{1,0:T(4,128)S(1)}, f32[4,2560]{1,0:T(4,128)S(1)}, u32[]{:S(2)}, u32[]{:S(2)}) collective-permute-start(f32[4,2560]{1,0:T(4,128)S(1)} %add.27), channel_id=1, source_target_pairs={{0,2},{1,3},{2,0},{3,1},{4,6},{5,7},{6,4},{7,5},{8,10},{9,11},{10,... | collective-permute-start | bytes 122888 | tf_op jit(solution)/shard_map/ppermute | solution.py:302
  25.9 20.0 %collective-permute-done.30 = f32[4,2560]{1,0:T(4,128)S(1)} collective-permute-done((f32[4,2560]{1,0:T(4,128)S(1)}, f32[4,2560]{1,0:T(4,128)S(1)}, u32[]{:S(2)}, u32[]{:S(2)}) %collective-permute-start.30) | collective-permute-done | bytes 40992 | tf_op jit(solution)/shard_map/ppermute | solution.py:302
  45.9 3.0 %collective-permute-start.31 = (f32[4,2560]{1,0:T(4,128)S(1)}, f32[4,2560]{1,0:T(4,128)S(1)}, u32[]{:S(2)}, u32[]{:S(2)}) collective-permute-start(f32[4,2560]{1,0:T(4,128)S(1)} %add.27), channel_id=1, source_target_pairs={{0,4},{1,5},{2,6},{3,7},{4,0},{5,1},{6,2},{7,3},{8,12},{9,13},{10,... | collective-permute-start | bytes 122888 | tf_op jit(solution)/shard_map/ppermute | solution.py:302
  48.9 2.0 collective-permute-done.31
  50.9 1.9 collective-permute-start.32
  52.8 3.9 %collective-permute-done.32 = f32[4,2560]{1,0:T(4,128)S(1)} collective-permute-done((f32[4,2560]{1,0:T(4,128)S(1)}, f32[4,2560]{1,0:T(4,128)S(1)}, u32[]{:S(2)}, u32[]{:S(2)}) %collective-permute-start.32) | collective-permute-done | bytes 40992 | tf_op jit(solution)/shard_map/ppermute | solution.py:302
  56.7 1.6 collective-permute-start.20
  59.3 1.3 pad_maximum_fusion
  60.7 0.9 copy-done.8
  61.6 0.7 collective-permute-start.3
  62.3 0.9 copy-done.10
  63.2 1.3 collective-permute-start.1
  64.5 0.9 copy-done.12
  65.4 1.6 collective-permute-start.13
  67.0 0.9 copy-done.14
  67.9 1.3 collective-permute-start.11
  69.2 1.3 collective-permute-start.21
  70.5 32.6 %collective-permute-done.1.refs_6_ = bf16[320,1280]{1,0:T(8,128)(2,1)S(1)} collective-permute-done((bf16[320,1280]{1,0:T(8,128)(2,1)}, bf16[320,1280]{1,0:T(8,128)(2,1)S(1)}, u32[]{:S(2)}, u32[]{:S(2)}) %collective-permute-start.1) | collective-permute-done | bytes 819232 | tf_op jit(solution)/shard_map/ppermute | solution.py:74
  103.5 17.1 %collective-permute-done.11.refs_2_ = bf16[320,1280]{1,0:T(8,128)(2,1)} collective-permute-done((bf16[320,1280]{1,0:T(8,128)(2,1)}, bf16[320,1280]{1,0:T(8,128)(2,1)}, u32[]{:S(2)}, u32[]{:S(2)}) %collective-permute-start.11) | collective-permute-done | bytes 819232 | tf_op jit(solution)/shard_map/ppermute | solution.py:74
  120.7 1.4 broadcast_select_fusion
  122.1 1.4 collective-permute-start.14
  123.5 14.7 %collective-permute-done.21 = bf16[320,1280]{1,0:T(8,128)(2,1)} collective-permute-done((bf16[320,1280]{1,0:T(8,128)(2,1)}, bf16[320,1280]{1,0:T(8,128)(2,1)}, u32[]{:S(2)}, u32[]{:S(2)}) %collective-permute-start.21) | collective-permute-done | bytes 819232 | tf_op jit(solution)/shard_map/ppermute | solution.py:74
  138.2 1.3 collective-permute-start.22
  139.8 0.7 collective-permute-start.8
  140.5 0.7 collective-permute-start.6
  141.2 15.7 %collective-permute-done.22.refs_8_ = bf16[320,1280]{1,0:T(8,128)(2,1)S(1)} collective-permute-done((bf16[320,1280]{1,0:T(8,128)(2,1)}, bf16[320,1280]{1,0:T(8,128)(2,1)S(1)}, u32[]{:S(2)}, u32[]{:S(2)}) %collective-permute-start.22) | collective-permute-done | bytes 819232 | tf_op jit(solution)/shard_map/ppermute | solution.py:74
  157.5 1.3 collective-permute-start.4
  159.4 2.2 put.6.refs_10_
  161.7 1.3 put.7.refs_2_
  163.2 0.8 copy-done.1
  164.5 0.7 collective-permute-start.36
  165.3 0.7 collective-permute-start.35
  166.0 0.7 collective-permute-start.34
  166.7 12.8 %collective-permute-done.4.refs_0_ = bf16[320,1280]{1,0:T(8,128)(2,1)S(1)} collective-permute-done((bf16[320,1280]{1,0:T(8,128)(2,1)S(1)}, bf16[320,1280]{1,0:T(8,128)(2,1)S(1)}, u32[]{:S(2)}, u32[]{:S(2)}) %collective-permute-start.4) | collective-permute-done | bytes 819232 | tf_op jit(solution)/shard_map/ppermute | solution.py:74
  180.6 0.7 collective-permute-start.40
  181.3 0.7 collective-permute-start.39
  183.5 1.3 collective-permute-start.44
  184.8 1.3 collective-permute-start.43
  186.2 1.3 collective-permute-start.42
  187.5 1.3 collective-permute-start.41
  189.1 16.7 %collective-permute-done.44.arr = bf16[64,2560]{1,0:T(8,128)(2,1)S(1)} collective-permute-done((bf16[64,2560]{1,0:T(8,128)(2,1)S(1)}, bf16[64,2560]{1,0:T(8,128)(2,1)S(1)}, u32[]{:S(2)}, u32[]{:S(2)}) %collective-permute-start.44) | collective-permute-done | bytes 327712 | tf_op jit(solution)/shard_map/ppermute | solution.py:348
  205.8 3.5 %shard_map.107 = (bf16[256,1280]{1,0:T(8,128)(2,1)S(1)}, bf16[256,2560]{1,0:T(8,128)(2,1)S(1)}) custom-call(bf16[2,2560,1280]{2,1,0:T(8,128)(2,1)S(1)} %put.11.w, bf16[64,2560]{1,0:T(8,128)(2,1)S(1)} %collective-permute-done.44.arr, bf16[256,1280]{1,0:T(8,128)(2,1)S(1)} %bitcast.33, ...), custom_call_target="tpu_custom_call", output_to_operand_aliasing={{0}: (4, {}), {1}: (5, {})} | custom-call | flops 838860800 | bytes 13107200 | tf_op jit(solution)/shard_map/pallas_call | solution.py:225
  209.3 3.5 %collective-permute-done.43.arr = bf16[64,2560]{1,0:T(8,128)(2,1)S(1)} collective-permute-done((bf16[64,2560]{1,0:T(8,128)(2,1)S(1)}, bf16[64,2560]{1,0:T(8,128)(2,1)S(1)}, u32[]{:S(2)}, u32[]{:S(2)}) %collective-permute-start.43) | collective-permute-done | bytes 327712 | tf_op jit(solution)/shard_map/ppermute | solution.py:348
  212.8 3.5 %shard_map.108 = (bf16[256,1280]{1,0:T(8,128)(2,1)S(1)}, bf16[256,2560]{1,0:T(8,128)(2,1)S(1)}) custom-call(bf16[2,2560,1280]{2,1,0:T(8,128)(2,1)S(1)} %put.11.w, bf16[64,2560]{1,0:T(8,128)(2,1)S(1)} %collective-permute-done.43.arr, bf16[256,1280]{1,0:T(8,128)(2,1)S(1)} %bitcast.34, ...), custom_call_target="tpu_custom_call", output_to_operand_aliasing={{0}: (4, {}), {1}: (5, {})} | custom-call | flops 838860800 | bytes 13107200 | tf_op jit(solution)/shard_map/pallas_call | solution.py:225
  216.3 3.5 %collective-permute-done.42.arr = bf16[64,2560]{1,0:T(8,128)(2,1)S(1)} collective-permute-done((bf16[64,2560]{1,0:T(8,128)(2,1)S(1)}, bf16[64,2560]{1,0:T(8,128)(2,1)S(1)}, u32[]{:S(2)}, u32[]{:S(2)}) %collective-permute-start.42) | collective-permute-done | bytes 327712 | tf_op jit(solution)/shard_map/ppermute | solution.py:348
  219.8 3.5 %shard_map.109 = (bf16[256,1280]{1,0:T(8,128)(2,1)S(1)}, bf16[256,2560]{1,0:T(8,128)(2,1)S(1)}) custom-call(bf16[2,2560,1280]{2,1,0:T(8,128)(2,1)S(1)} %put.11.w, bf16[64,2560]{1,0:T(8,128)(2,1)S(1)} %collective-permute-done.42.arr, bf16[256,1280]{1,0:T(8,128)(2,1)S(1)} %bitcast.35, ...), custom_call_target="tpu_custom_call", output_to_operand_aliasing={{0}: (4, {}), {1}: (5, {})} | custom-call | flops 838860800 | bytes 13107200 | tf_op jit(solution)/shard_map/pallas_call | solution.py:225
  223.3 4.1 %collective-permute-done.41.arr = bf16[64,2560]{1,0:T(8,128)(2,1)S(1)} collective-permute-done((bf16[64,2560]{1,0:T(8,128)(2,1)S(1)}, bf16[64,2560]{1,0:T(8,128)(2,1)S(1)}, u32[]{:S(2)}, u32[]{:S(2)}) %collective-permute-start.41) | collective-permute-done | bytes 327712 | tf_op jit(solution)/shard_map/ppermute | solution.py:348
  227.4 3.5 %shard_map.110 = (bf16[256,1280]{1,0:T(8,128)(2,1)S(1)}, bf16[256,2560]{1,0:T(8,128)(2,1)S(1)}) custom-call(bf16[2,2560,1280]{2,1,0:T(8,128)(2,1)S(1)} %put.11.w, bf16[64,2560]{1,0:T(8,128)(2,1)S(1)} %collective-permute-done.41.arr, bf16[256,1280]{1,0:T(8,128)(2,1)S(1)} %bitcast.36, ...), custom_call_target="tpu_custom_call", output_to_operand_aliasing={{0}: (4, {}), {1}: (5, {})} | custom-call | flops 838860800 | bytes 13107200 | tf_op jit(solution)/shard_map/pallas_call | solution.py:225
  232.3 1.2 collective-permute-done.45
  233.7 4.3 %collective-permute-start.48 = (f32[4,2560]{1,0:T(4,128)S(1)}, f32[4,2560]{1,0:T(4,128)S(1)}, u32[]{:S(2)}, u32[]{:S(2)}) collective-permute-start(f32[4,2560]{1,0:T(4,128)S(1)} %add.31.refs_0_), channel_id=1, source_target_pairs={{0,6},{1,7},{2,4},{3,5},{4,2},{5,3},{6,0},{7,1},{8,14},{9,15},{10,... | collective-permute-start | bytes 122888 | tf_op jit(solution)/shard_map/ppermute | solution.py:302
  238.0 1.5 collective-permute-done.47.refs_2_
  239.5 0.9 collective-permute-done.48.refs_3_
  240.4 2.8 %second_half.1 = (f32[4,2560]{1,0:T(4,128)}, f32[4,1280]{1,0:T(4,128)S(1)}, bf16[256,2560]{1,0:T(8,128)(2,1)}) custom-call(f32[4,2560]{1,0:T(4,128)S(1)} %add.31.refs_0_, f32[4,2560]{1,0:T(4,128)S(1)} %collective-permute-done.46.refs_1_, f32[4,2560]{1,0:T(4,128)S(1)} %collective-permute-done.47.refs_2_, f32[4,2560]{1,0:T(4,128)S(1)} %collective-permute-done.48.refs_3_, ...), custom_call_target="tpu_custom_call" | custom-call | tf_op jit(solution)/shard_map/second_half/pallas_call | solution.py:285
  243.3 1.2 collective-permute-done.49
  244.5 1.1 collective-permute-start.50
  245.6 2.9 %collective-permute-start.51 = (f32[4,1280]{1,0:T(4,128)S(1)}, f32[4,1280]{1,0:T(4,128)S(1)}, u32[]{:S(2)}, u32[]{:S(2)}) collective-permute-start(f32[4,1280]{1,0:T(4,128)S(1)} %add.32), channel_id=1, source_target_pairs={{0,4},{1,5},{2,6},{3,7},{4,0},{5,1},{6,2},{7,3},{8,12},{9,13},{10,... | collective-permute-start | bytes 61448 | tf_op jit(solution)/shard_map/ppermute | solution.py:302
  248.9 1.3 collective-permute-done.51
  250.3 3.8 %collective-permute-done.52 = f32[4,1280]{1,0:T(4,128)S(1)} collective-permute-done((f32[4,1280]{1,0:T(4,128)S(1)}, f32[4,1280]{1,0:T(4,128)S(1)}, u32[]{:S(2)}, u32[]{:S(2)}) %collective-permute-start.52) | collective-permute-done | bytes 20512 | tf_op jit(solution)/shard_map/ppermute | solution.py:302
  (114 shorter events, 9.3 us)
Async XLA Ops:
  0.6 13.2 %copy-start = (f32[1,4,1280]{2,1,0:T(4,128)S(1)}, f32[1,4,1280]{2,1,0:T(4,128)}, u32[]{:S(2)}) copy-start(f32[1,4,1280]{2,1,0:T(4,128)} %param.13) | copy-start | bytes 61444
  0.6 57.6 %collective-permute-start.2 = (bf16[320,1280]{1,0:T(8,128)(2,1)}, bf16[320,1280]{1,0:T(8,128)(2,1)S(1)}, u32[]{:S(2)}, u32[]{:S(2)}) collective-permute-start(bf16[320,1280]{1,0:T(8,128)(2,1)} %bitcast.41), channel_id=1, source_target_pairs={{0,2},{1,3},{2,4},{3,5},{4,6},{5,7},{8,10},{9,11},{10,12},{11,13},... | collective-permute-start | bytes 2457608 | tf_op jit(solution)/shard_map/ppermute | solution.py:74
  5.7 52.6 %collective-permute-start = (bf16[320,1280]{1,0:T(8,128)(2,1)}, bf16[320,1280]{1,0:T(8,128)(2,1)}, u32[]{:S(2)}, u32[]{:S(2)}) collective-permute-start(bf16[320,1280]{1,0:T(8,128)(2,1)} %bitcast.42), channel_id=1, source_target_pairs={{2,0},{3,1},{4,2},{5,3},{6,4},{7,5},{10,8},{11,9},{12,10},{13,11},... | collective-permute-start | bytes 2457608 | tf_op jit(solution)/shard_map/ppermute | solution.py:74
  7.0 49.7 %copy-start.4 = (bf16[1,320,1280]{2,1,0:T(8,128)(2,1)S(1)}, bf16[1,320,1280]{2,1,0:T(8,128)(2,1)}, u32[]{:S(2)}) copy-start(bf16[1,320,1280]{2,1,0:T(8,128)(2,1)} %param.9) | copy-start | bytes 2457604
  7.0 52.3 %copy-start.5 = (bf16[1,320,1280]{2,1,0:T(8,128)(2,1)S(1)}, bf16[1,320,1280]{2,1,0:T(8,128)(2,1)}, u32[]{:S(2)}) copy-start(bf16[1,320,1280]{2,1,0:T(8,128)(2,1)} %param.10) | copy-start | bytes 2457604
  7.0 51.8 %collective-permute-start.12 = (bf16[320,1280]{1,0:T(8,128)(2,1)}, bf16[320,1280]{1,0:T(8,128)(2,1)}, u32[]{:S(2)}, u32[]{:S(2)}) collective-permute-start(bf16[320,1280]{1,0:T(8,128)(2,1)} %bitcast.45), channel_id=1, source_target_pairs={{0,2},{1,3},{2,4},{3,5},{4,6},{5,7},{8,10},{9,11},{10,12},{11,13},... | collective-permute-start | bytes 2457608 | tf_op jit(solution)/shard_map/ppermute | solution.py:74
  12.6 46.3 %collective-permute-start.10 = (bf16[320,1280]{1,0:T(8,128)(2,1)}, bf16[320,1280]{1,0:T(8,128)(2,1)}, u32[]{:S(2)}, u32[]{:S(2)}) collective-permute-start(bf16[320,1280]{1,0:T(8,128)(2,1)} %bitcast.46), channel_id=1, source_target_pairs={{2,0},{3,1},{4,2},{5,3},{6,4},{7,5},{10,8},{11,9},{12,10},{13,11},... | collective-permute-start | bytes 2457608 | tf_op jit(solution)/shard_map/ppermute | solution.py:74
  21.9 1.2 collective-permute-start.29
  23.1 22.8 %collective-permute-start.30 = (f32[4,2560]{1,0:T(4,128)S(1)}, f32[4,2560]{1,0:T(4,128)S(1)}, u32[]{:S(2)}, u32[]{:S(2)}) collective-permute-start(f32[4,2560]{1,0:T(4,128)S(1)} %add.27), channel_id=1, source_target_pairs={{0,2},{1,3},{2,0},{3,1},{4,6},{5,7},{6,4},{7,5},{8,10},{9,11},{10,... | collective-permute-start | bytes 122888 | tf_op jit(solution)/shard_map/ppermute | solution.py:302
  45.9 5.0 %collective-permute-start.31 = (f32[4,2560]{1,0:T(4,128)S(1)}, f32[4,2560]{1,0:T(4,128)S(1)}, u32[]{:S(2)}, u32[]{:S(2)}) collective-permute-start(f32[4,2560]{1,0:T(4,128)S(1)} %add.27), channel_id=1, source_target_pairs={{0,4},{1,5},{2,6},{3,7},{4,0},{5,1},{6,2},{7,3},{8,12},{9,13},{10,... | collective-permute-start | bytes 122888 | tf_op jit(solution)/shard_map/ppermute | solution.py:302
  50.9 5.8 %collective-permute-start.32 = (f32[4,2560]{1,0:T(4,128)S(1)}, f32[4,2560]{1,0:T(4,128)S(1)}, u32[]{:S(2)}, u32[]{:S(2)}) collective-permute-start(f32[4,2560]{1,0:T(4,128)S(1)} %add.27), channel_id=1, source_target_pairs={{0,6},{1,7},{2,4},{3,5},{4,2},{5,3},{6,0},{7,1},{8,14},{9,15},{10,... | collective-permute-start | bytes 122888 | tf_op jit(solution)/shard_map/ppermute | solution.py:302
  56.7 3.9 %collective-permute-start.20 = (bf16[320,1280]{1,0:T(8,128)(2,1)S(1)}, bf16[320,1280]{1,0:T(8,128)(2,1)}, u32[]{:S(2)}, u32[]{:S(2)}) collective-permute-start(bf16[320,1280]{1,0:T(8,128)(2,1)S(1)} %bitcast.43), channel_id=1, source_target_pairs={{26,2},{27,3},{28,4},{29,5}} | collective-permute-start | bytes 2457608 | tf_op jit(solution)/shard_map/ppermute | solution.py:74
  58.2 2.4 collective-permute-start.27
  58.3 4.1 %collective-permute-start.28 = (bf16[320,1280]{1,0:T(8,128)(2,1)}, bf16[320,1280]{1,0:T(8,128)(2,1)S(1)}, u32[]{:S(2)}, u32[]{:S(2)}) collective-permute-start(bf16[320,1280]{1,0:T(8,128)(2,1)} %collective-permute-done.refs_9_), channel_id=1, source_target_pairs={{0,1},{1,0},{2,3},{3,2},{4,5},{5,4},{6,7},{7,6},{8,9},{9,8},{10,11... | collective-permute-start | bytes 2457608 | tf_op jit(solution)/shard_map/ppermute | solution.py:82
  58.8 5.7 %collective-permute-start.25 = (bf16[320,1280]{1,0:T(8,128)(2,1)}, bf16[320,1280]{1,0:T(8,128)(2,1)S(1)}, u32[]{:S(2)}, u32[]{:S(2)}) collective-permute-start(bf16[320,1280]{1,0:T(8,128)(2,1)} %collective-permute-done.12.refs_3_), channel_id=1, source_target_pairs={{0,1},{1,0},{2,3},{3,2},{4,5},{5,4},{6,7},{7,6},{8,9},{9,8},{10,11... | collective-permute-start | bytes 2457608 | tf_op jit(solution)/shard_map/ppermute | solution.py:82
  58.8 8.1 %collective-permute-start.26 = (bf16[320,1280]{1,0:T(8,128)(2,1)}, bf16[320,1280]{1,0:T(8,128)(2,1)S(1)}, u32[]{:S(2)}, u32[]{:S(2)}) collective-permute-start(bf16[320,1280]{1,0:T(8,128)(2,1)} %collective-permute-done.10.refs_5_), channel_id=1, source_target_pairs={{0,1},{1,0},{2,3},{3,2},{4,5},{5,4},{6,7},{7,6},{8,9},{9,8},{10,11... | collective-permute-start | bytes 2457608 | tf_op jit(solution)/shard_map/ppermute | solution.py:82
  60.6 61.5 %collective-permute-start.24 = (bf16[2,320,1280]{2,1,0:T(8,128)(2,1)}, bf16[2,320,1280]{2,1,0:T(8,128)(2,1)}, u32[]{:S(2)}, u32[]{:S(2)}) collective-permute-start(bf16[2,320,1280]{2,1,0:T(8,128)(2,1)} %pad_maximum_fusion), channel_id=1, source_target_pairs={{0,1},{1,0},{2,3},{3,2},{4,5},{5,4},{6,7},{7,6},{8,9},{9,8},{10,11... | collective-permute-start | bytes 4915208 | tf_op jit(solution)/shard_map/ppermute | solution.py:82
  61.6 7.6 %collective-permute-start.3 = (bf16[320,1280]{1,0:T(8,128)(2,1)S(1)}, bf16[320,1280]{1,0:T(8,128)(2,1)S(1)}, u32[]{:S(2)}, u32[]{:S(2)}) collective-permute-start(bf16[320,1280]{1,0:T(8,128)(2,1)S(1)} %collective-permute-done.2.refs_7_), channel_id=1, source_target_pairs={{2,4},{3,5},{4,6},{5,7},{10,12},{11,13},{12,14},{13,15},{18,20},{1... | collective-permute-start | bytes 2457608 | tf_op jit(solution)/shard_map/ppermute | solution.py:74
  63.2 39.8 %collective-permute-start.1 = (bf16[320,1280]{1,0:T(8,128)(2,1)}, bf16[320,1280]{1,0:T(8,128)(2,1)S(1)}, u32[]{:S(2)}, u32[]{:S(2)}) collective-permute-start(bf16[320,1280]{1,0:T(8,128)(2,1)} %collective-permute-done.refs_9_), channel_id=1, source_target_pairs={{2,0},{3,1},{4,2},{5,3},{10,8},{11,9},{12,10},{13,11},{18,16},{19,... | collective-permute-start | bytes 2457608 | tf_op jit(solution)/shard_map/ppermute | solution.py:74
  65.4 37.7 %collective-permute-start.13 = (bf16[320,1280]{1,0:T(8,128)(2,1)}, bf16[320,1280]{1,0:T(8,128)(2,1)}, u32[]{:S(2)}, u32[]{:S(2)}) collective-permute-start(bf16[320,1280]{1,0:T(8,128)(2,1)} %collective-permute-done.12.refs_3_), channel_id=1, source_target_pairs={{2,4},{3,5},{4,6},{5,7},{10,12},{11,13},{12,14},{13,15},{18,20},{1... | collective-permute-start | bytes 2457608 | tf_op jit(solution)/shard_map/ppermute | solution.py:74
  67.9 52.8 %collective-permute-start.11 = (bf16[320,1280]{1,0:T(8,128)(2,1)}, bf16[320,1280]{1,0:T(8,128)(2,1)}, u32[]{:S(2)}, u32[]{:S(2)}) collective-permute-start(bf16[320,1280]{1,0:T(8,128)(2,1)} %collective-permute-done.10.refs_5_), channel_id=1, source_target_pairs={{2,0},{3,1},{4,2},{5,3},{10,8},{11,9},{12,10},{13,11},{18,16},{19,... | collective-permute-start | bytes 2457608 | tf_op jit(solution)/shard_map/ppermute | solution.py:74
  69.2 69.1 %collective-permute-start.21 = (bf16[320,1280]{1,0:T(8,128)(2,1)}, bf16[320,1280]{1,0:T(8,128)(2,1)}, u32[]{:S(2)}, u32[]{:S(2)}) collective-permute-start(bf16[320,1280]{1,0:T(8,128)(2,1)} %collective-permute-done.20), channel_id=1, source_target_pairs={{2,0},{3,1},{4,6},{5,7}} | collective-permute-start | bytes 2457608 | tf_op jit(solution)/shard_map/ppermute | solution.py:74
  103.0 36.7 %collective-permute-start.18 = (bf16[320,1280]{1,0:T(8,128)(2,1)S(1)}, bf16[320,1280]{1,0:T(8,128)(2,1)S(1)}, u32[]{:S(2)}, u32[]{:S(2)}) collective-permute-start(bf16[320,1280]{1,0:T(8,128)(2,1)S(1)} %collective-permute-done.3.refs_4_), channel_id=1, source_target_pairs={{0,1},{1,0},{2,3},{3,2},{4,5},{5,4},{6,7},{7,6},{8,9},{9,8},{10,11... | collective-permute-start | bytes 2457608 | tf_op jit(solution)/shard_map/ppermute | solution.py:82
  103.0 36.7 %collective-permute-start.19 = (bf16[320,1280]{1,0:T(8,128)(2,1)S(1)}, bf16[320,1280]{1,0:T(8,128)(2,1)S(1)}, u32[]{:S(2)}, u32[]{:S(2)}) collective-permute-start(bf16[320,1280]{1,0:T(8,128)(2,1)S(1)} %collective-permute-done.1.refs_6_), channel_id=1, source_target_pairs={{0,1},{1,0},{2,3},{3,2},{4,5},{5,4},{6,7},{7,6},{8,9},{9,8},{10,11... | collective-permute-start | bytes 2457608 | tf_op jit(solution)/shard_map/ppermute | solution.py:82
  120.7 19.8 %collective-permute-start.16 = (bf16[320,1280]{1,0:T(8,128)(2,1)}, bf16[320,1280]{1,0:T(8,128)(2,1)S(1)}, u32[]{:S(2)}, u32[]{:S(2)}) collective-permute-start(bf16[320,1280]{1,0:T(8,128)(2,1)} %collective-permute-done.13.refs_0_), channel_id=1, source_target_pairs={{0,1},{1,0},{2,3},{3,2},{4,5},{5,4},{6,7},{7,6},{8,9},{9,8},{10,11... | collective-permute-start | bytes 2457608 | tf_op jit(solution)/shard_map/ppermute | solution.py:82
  120.7 38.7 %copy-start.13 = (bf16[320,1280]{1,0:T(8,128)(2,1)S(1)}, bf16[320,1280]{1,0:T(8,128)(2,1)}, u32[]{:S(2)}) copy-start(bf16[320,1280]{1,0:T(8,128)(2,1)} %copy-done.12) | copy-start | bytes 2457604
  120.7 38.7 %copy-start.15 = (bf16[320,1280]{1,0:T(8,128)(2,1)S(1)}, bf16[320,1280]{1,0:T(8,128)(2,1)}, u32[]{:S(2)}) copy-start(bf16[320,1280]{1,0:T(8,128)(2,1)} %copy-done.14) | copy-start | bytes 2457604
  122.1 37.3 %copy-start.7 = (bf16[320,1280]{1,0:T(8,128)(2,1)S(1)}, bf16[320,1280]{1,0:T(8,128)(2,1)}, u32[]{:S(2)}) copy-start(bf16[320,1280]{1,0:T(8,128)(2,1)} %copy-done.6) | copy-start | bytes 2457604
  122.1 37.3 %copy-start.9 = (bf16[320,1280]{1,0:T(8,128)(2,1)S(1)}, bf16[320,1280]{1,0:T(8,128)(2,1)}, u32[]{:S(2)}) copy-start(bf16[320,1280]{1,0:T(8,128)(2,1)} %copy-done.8) | copy-start | bytes 2457604
  122.1 37.3 %copy-start.11 = (bf16[320,1280]{1,0:T(8,128)(2,1)S(1)}, bf16[320,1280]{1,0:T(8,128)(2,1)}, u32[]{:S(2)}) copy-start(bf16[320,1280]{1,0:T(8,128)(2,1)} %copy-done.10) | copy-start | bytes 2457604
  122.1 34.9 %collective-permute-start.14 = (bf16[320,1280]{1,0:T(8,128)(2,1)S(1)}, bf16[320,1280]{1,0:T(8,128)(2,1)S(1)}, u32[]{:S(2)}, u32[]{:S(2)}) collective-permute-start(bf16[320,1280]{1,0:T(8,128)(2,1)S(1)} %broadcast_select_fusion), channel_id=1, source_target_pairs={{2,0},{3,1},{4,6},{5,7},{10,8},{11,9},{12,14},{13,15},{18,16},{19,... | collective-permute-start | bytes 2457608 | tf_op jit(solution)/shard_map/ppermute | solution.py:74
  138.2 18.7 %collective-permute-start.22 = (bf16[320,1280]{1,0:T(8,128)(2,1)}, bf16[320,1280]{1,0:T(8,128)(2,1)S(1)}, u32[]{:S(2)}, u32[]{:S(2)}) collective-permute-start(bf16[320,1280]{1,0:T(8,128)(2,1)} %collective-permute-done.21), channel_id=1, source_target_pairs={{0,24},{1,25},{6,30},{7,31}} | collective-permute-start | bytes 2457608 | tf_op jit(solution)/shard_map/ppermute | solution.py:74
  139.7 17.8 %collective-permute-start.17 = (bf16[320,1280]{1,0:T(8,128)(2,1)}, bf16[320,1280]{1,0:T(8,128)(2,1)S(1)}, u32[]{:S(2)}, u32[]{:S(2)}) collective-permute-start(bf16[320,1280]{1,0:T(8,128)(2,1)} %collective-permute-done.11.refs_2_), channel_id=1, source_target_pairs={{0,1},{1,0},{2,3},{3,2},{4,5},{5,4},{6,7},{7,6},{8,9},{9,8},{10,11... | collective-permute-start | bytes 2457608 | tf_op jit(solution)/shard_map/ppermute | solution.py:82
  139.8 19.0 %collective-permute-start.8 = (bf16[320,1280]{1,0:T(8,128)(2,1)S(1)}, bf16[320,1280]{1,0:T(8,128)(2,1)S(1)}, u32[]{:S(2)}, u32[]{:S(2)}) collective-permute-start(bf16[320,1280]{1,0:T(8,128)(2,1)S(1)} %broadcast_select_fusion.1), channel_id=1, source_target_pairs={{26,24},{27,25},{28,30},{29,31}} | collective-permute-start | bytes 2457608 | tf_op jit(solution)/shard_map/ppermute | solution.py:74
  140.5 18.4 %collective-permute-start.6 = (bf16[320,1280]{1,0:T(8,128)(2,1)S(1)}, bf16[320,1280]{1,0:T(8,128)(2,1)S(1)}, u32[]{:S(2)}, u32[]{:S(2)}) collective-permute-start(bf16[320,1280]{1,0:T(8,128)(2,1)S(1)} %broadcast_select_fusion.1), channel_id=1, source_target_pairs={{10,8},{11,9},{12,14},{13,15},{18,16},{19,17},{20,22},{21,23}} | collective-permute-start | bytes 2457608 | tf_op jit(solution)/shard_map/ppermute | solution.py:74
  157.0 4.7 %collective-permute-start.23 = (bf16[320,1280]{1,0:T(8,128)(2,1)S(1)}, bf16[320,1280]{1,0:T(8,128)(2,1)S(1)}, u32[]{:S(2)}, u32[]{:S(2)}) collective-permute-start(bf16[320,1280]{1,0:T(8,128)(2,1)S(1)} %collective-permute-done.22.refs_8_), channel_id=1, source_target_pairs={{0,1},{1,0},{2,3},{3,2},{4,5},{5,4},{6,7},{7,6},{8,9},{9,8},{10,11... | collective-permute-start | bytes 2457608 | tf_op jit(solution)/shard_map/ppermute | solution.py:82
  157.0 6.0 %collective-permute-start.15 = (bf16[320,1280]{1,0:T(8,128)(2,1)S(1)}, bf16[320,1280]{1,0:T(8,128)(2,1)S(1)}, u32[]{:S(2)}, u32[]{:S(2)}) collective-permute-start(bf16[320,1280]{1,0:T(8,128)(2,1)S(1)} %collective-permute-done.14.refs_0_), channel_id=1, source_target_pairs={{0,1},{1,0},{2,3},{3,2},{4,5},{5,4},{6,7},{7,6},{8,9},{9,8},{10,11... | collective-permute-start | bytes 2457608 | tf_op jit(solution)/shard_map/ppermute | solution.py:82
  157.5 22.0 %collective-permute-start.4 = (bf16[320,1280]{1,0:T(8,128)(2,1)S(1)}, bf16[320,1280]{1,0:T(8,128)(2,1)S(1)}, u32[]{:S(2)}, u32[]{:S(2)}) collective-permute-start(bf16[320,1280]{1,0:T(8,128)(2,1)S(1)} %broadcast_select_fusion.1), channel_id=1, source_target_pairs={{2,0},{3,1},{4,6},{5,7}} | collective-permute-start | bytes 2457608 | tf_op jit(solution)/shard_map/ppermute | solution.py:74
  158.8 5.7 %collective-permute-start.9 = (bf16[320,1280]{1,0:T(8,128)(2,1)S(1)}, bf16[320,1280]{1,0:T(8,128)(2,1)S(1)}, u32[]{:S(2)}, u32[]{:S(2)}) collective-permute-start(bf16[320,1280]{1,0:T(8,128)(2,1)S(1)} %collective-permute-done.8.refs_0_), channel_id=1, source_target_pairs={{0,1},{1,0},{2,3},{3,2},{4,5},{5,4},{6,7},{7,6},{8,9},{9,8},{10,11... | collective-permute-start | bytes 2457608 | tf_op jit(solution)/shard_map/ppermute | solution.py:82
  158.9 21.3 %collective-permute-start.7 = (bf16[320,1280]{1,0:T(8,128)(2,1)S(1)}, bf16[320,1280]{1,0:T(8,128)(2,1)S(1)}, u32[]{:S(2)}, u32[]{:S(2)}) collective-permute-start(bf16[320,1280]{1,0:T(8,128)(2,1)S(1)} %collective-permute-done.6.refs_0_), channel_id=1, source_target_pairs={{0,1},{1,0},{2,3},{3,2},{4,5},{5,4},{6,7},{7,6},{8,9},{9,8},{10,11... | collective-permute-start | bytes 2457608 | tf_op jit(solution)/shard_map/ppermute | solution.py:82
  164.5 15.8 %collective-permute-start.36 = (bf16[64,2560]{1,0:T(8,128)(2,1)S(1)}, bf16[64,2560]{1,0:T(8,128)(2,1)S(1)}, u32[]{:S(2)}, u32[]{:S(2)}) collective-permute-start(bf16[64,2560]{1,0:T(8,128)(2,1)S(1)} %get-tuple-element.64), channel_id=1, source_target_pairs={{24,16},{25,17},{26,18},{27,19},{28,20},{29,21},{30,22},{31,23}} | collective-permute-start | bytes 983048 | tf_op jit(solution)/shard_map/ppermute | solution.py:348
  165.3 16.0 %collective-permute-start.35 = (bf16[64,2560]{1,0:T(8,128)(2,1)S(1)}, bf16[64,2560]{1,0:T(8,128)(2,1)S(1)}, u32[]{:S(2)}, u32[]{:S(2)}) collective-permute-start(bf16[64,2560]{1,0:T(8,128)(2,1)S(1)} %get-tuple-element.63), channel_id=1, source_target_pairs={{24,16},{25,17},{26,18},{27,19},{28,20},{29,21},{30,22},{31,23}} | collective-permute-start | bytes 983048 | tf_op jit(solution)/shard_map/ppermute | solution.py:348
  166.0 16.0 %collective-permute-start.34 = (bf16[64,2560]{1,0:T(8,128)(2,1)S(1)}, bf16[64,2560]{1,0:T(8,128)(2,1)S(1)}, u32[]{:S(2)}, u32[]{:S(2)}) collective-permute-start(bf16[64,2560]{1,0:T(8,128)(2,1)S(1)} %get-tuple-element.62), channel_id=1, source_target_pairs={{24,16},{25,17},{26,18},{27,19},{28,20},{29,21},{30,22},{31,23}} | collective-permute-start | bytes 983048 | tf_op jit(solution)/shard_map/ppermute | solution.py:348
  179.5 3.2 %collective-permute-start.33 = (bf16[64,2560]{1,0:T(8,128)(2,1)S(1)}, bf16[64,2560]{1,0:T(8,128)(2,1)S(1)}, u32[]{:S(2)}, u32[]{:S(2)}) collective-permute-start(bf16[64,2560]{1,0:T(8,128)(2,1)S(1)} %get-tuple-element.61), channel_id=1, source_target_pairs={{24,16},{25,17},{26,18},{27,19},{28,20},{29,21},{30,22},{31,23}} | collective-permute-start | bytes 983048 | tf_op jit(solution)/shard_map/ppermute | solution.py:348
  180.2 8.6 %collective-permute-start.5 = (bf16[320,1280]{1,0:T(8,128)(2,1)S(1)}, bf16[320,1280]{1,0:T(8,128)(2,1)S(1)}, u32[]{:S(2)}, u32[]{:S(2)}) collective-permute-start(bf16[320,1280]{1,0:T(8,128)(2,1)S(1)} %collective-permute-done.4.refs_0_), channel_id=1, source_target_pairs={{0,1},{1,0},{2,3},{3,2},{4,5},{5,4},{6,7},{7,6},{8,9},{9,8},{10,11... | collective-permute-start | bytes 2457608 | tf_op jit(solution)/shard_map/ppermute | solution.py:82
  180.6 2.9 %collective-permute-start.40 = (bf16[64,2560]{1,0:T(8,128)(2,1)S(1)}, bf16[64,2560]{1,0:T(8,128)(2,1)S(1)}, u32[]{:S(2)}, u32[]{:S(2)}) collective-permute-start(bf16[64,2560]{1,0:T(8,128)(2,1)S(1)} %get-tuple-element.75), channel_id=1, source_target_pairs={{16,8},{17,9},{18,10},{19,11},{20,12},{21,13},{22,14},{23,15}} | collective-permute-start | bytes 983048 | tf_op jit(solution)/shard_map/ppermute | solution.py:348
  181.3 3.5 %collective-permute-start.39 = (bf16[64,2560]{1,0:T(8,128)(2,1)S(1)}, bf16[64,2560]{1,0:T(8,128)(2,1)S(1)}, u32[]{:S(2)}, u32[]{:S(2)}) collective-permute-start(bf16[64,2560]{1,0:T(8,128)(2,1)S(1)} %get-tuple-element.74), channel_id=1, source_target_pairs={{16,8},{17,9},{18,10},{19,11},{20,12},{21,13},{22,14},{23,15}} | collective-permute-start | bytes 983048 | tf_op jit(solution)/shard_map/ppermute | solution.py:348
  182.0 4.1 %collective-permute-start.38 = (bf16[64,2560]{1,0:T(8,128)(2,1)S(1)}, bf16[64,2560]{1,0:T(8,128)(2,1)S(1)}, u32[]{:S(2)}, u32[]{:S(2)}) collective-permute-start(bf16[64,2560]{1,0:T(8,128)(2,1)S(1)} %get-tuple-element.73), channel_id=1, source_target_pairs={{16,8},{17,9},{18,10},{19,11},{20,12},{21,13},{22,14},{23,15}} | collective-permute-start | bytes 983048 | tf_op jit(solution)/shard_map/ppermute | solution.py:348
  182.8 4.7 %collective-permute-start.37 = (bf16[64,2560]{1,0:T(8,128)(2,1)S(1)}, bf16[64,2560]{1,0:T(8,128)(2,1)S(1)}, u32[]{:S(2)}, u32[]{:S(2)}) collective-permute-start(bf16[64,2560]{1,0:T(8,128)(2,1)S(1)} %get-tuple-element.72), channel_id=1, source_target_pairs={{16,8},{17,9},{18,10},{19,11},{20,12},{21,13},{22,14},{23,15}} | collective-permute-start | bytes 983048 | tf_op jit(solution)/shard_map/ppermute | solution.py:348
  183.5 22.3 %collective-permute-start.44 = (bf16[64,2560]{1,0:T(8,128)(2,1)S(1)}, bf16[64,2560]{1,0:T(8,128)(2,1)S(1)}, u32[]{:S(2)}, u32[]{:S(2)}) collective-permute-start(bf16[64,2560]{1,0:T(8,128)(2,1)S(1)} %get-tuple-element.88), channel_id=1, source_target_pairs={{8,0},{9,1},{10,2},{11,3},{12,4},{13,5},{14,6},{15,7}} | collective-permute-start | bytes 983048 | tf_op jit(solution)/shard_map/ppermute | solution.py:348
  184.8 27.9 %collective-permute-start.43 = (bf16[64,2560]{1,0:T(8,128)(2,1)S(1)}, bf16[64,2560]{1,0:T(8,128)(2,1)S(1)}, u32[]{:S(2)}, u32[]{:S(2)}) collective-permute-start(bf16[64,2560]{1,0:T(8,128)(2,1)S(1)} %get-tuple-element.87), channel_id=1, source_target_pairs={{8,0},{9,1},{10,2},{11,3},{12,4},{13,5},{14,6},{15,7}} | collective-permute-start | bytes 983048 | tf_op jit(solution)/shard_map/ppermute | solution.py:348
  186.2 33.6 %collective-permute-start.42 = (bf16[64,2560]{1,0:T(8,128)(2,1)S(1)}, bf16[64,2560]{1,0:T(8,128)(2,1)S(1)}, u32[]{:S(2)}, u32[]{:S(2)}) collective-permute-start(bf16[64,2560]{1,0:T(8,128)(2,1)S(1)} %get-tuple-element.86), channel_id=1, source_target_pairs={{8,0},{9,1},{10,2},{11,3},{12,4},{13,5},{14,6},{15,7}} | collective-permute-start | bytes 983048 | tf_op jit(solution)/shard_map/ppermute | solution.py:348
  187.5 39.9 %collective-permute-start.41 = (bf16[64,2560]{1,0:T(8,128)(2,1)S(1)}, bf16[64,2560]{1,0:T(8,128)(2,1)S(1)}, u32[]{:S(2)}, u32[]{:S(2)}) collective-permute-start(bf16[64,2560]{1,0:T(8,128)(2,1)S(1)} %get-tuple-element.85), channel_id=1, source_target_pairs={{8,0},{9,1},{10,2},{11,3},{12,4},{13,5},{14,6},{15,7}} | collective-permute-start | bytes 983048 | tf_op jit(solution)/shard_map/ppermute | solution.py:348
  227.4 13.0 %slice-start = ((s8[6553600]{0:T(1024)(128)(4,1)}), s8[4194304]{0:T(1024)(128)(4,1)S(1)}, s32[]{:S(2)}) async-start(s8[6553600]{0:T(1024)(128)(4,1)} %bitcast.37), calls=%async_computation | async-start | bytes 8388608
  227.4 4.2 %copy-start.3 = (bf16[1,256,2560]{2,1,0:T(8,128)(2,1)S(1)}, bf16[1,256,2560]{2,1,0:T(8,128)(2,1)}, u32[]{:S(2)}) copy-start(bf16[1,256,2560]{2,1,0:T(8,128)(2,1)} %param.7) | copy-start | bytes 3932164
  227.4 13.0 %slice-start.1 = ((s8[6553600]{0:T(1024)(128)(4,1)}), s8[2359296]{0:T(1024)(128)(4,1)S(1)}, s32[]{:S(2)}) async-start(s8[6553600]{0:T(1024)(128)(4,1)} %bitcast.37), calls=%async_computation.1 | async-start | bytes 4718592
  232.3 1.2 collective-permute-start.45
  233.5 4.5 %collective-permute-start.46 = (f32[4,2560]{1,0:T(4,128)S(1)}, f32[4,2560]{1,0:T(4,128)S(1)}, u32[]{:S(2)}, u32[]{:S(2)}) collective-permute-start(f32[4,2560]{1,0:T(4,128)S(1)} %add.31.refs_0_), channel_id=1, source_target_pairs={{0,2},{1,3},{2,0},{3,1},{4,6},{5,7},{6,4},{7,5},{8,10},{9,11},{10,... | collective-permute-start | bytes 122888 | tf_op jit(solution)/shard_map/ppermute | solution.py:302
  233.6 5.9 %collective-permute-start.47 = (f32[4,2560]{1,0:T(4,128)S(1)}, f32[4,2560]{1,0:T(4,128)S(1)}, u32[]{:S(2)}, u32[]{:S(2)}) collective-permute-start(f32[4,2560]{1,0:T(4,128)S(1)} %add.31.refs_0_), channel_id=1, source_target_pairs={{0,4},{1,5},{2,6},{3,7},{4,0},{5,1},{6,2},{7,3},{8,12},{9,13},{10,... | collective-permute-start | bytes 122888 | tf_op jit(solution)/shard_map/ppermute | solution.py:302
  233.7 6.7 %collective-permute-start.48 = (f32[4,2560]{1,0:T(4,128)S(1)}, f32[4,2560]{1,0:T(4,128)S(1)}, u32[]{:S(2)}, u32[]{:S(2)}) collective-permute-start(f32[4,2560]{1,0:T(4,128)S(1)} %add.31.refs_0_), channel_id=1, source_target_pairs={{0,6},{1,7},{2,4},{3,5},{4,2},{5,3},{6,0},{7,1},{8,14},{9,15},{10,... | collective-permute-start | bytes 122888 | tf_op jit(solution)/shard_map/ppermute | solution.py:302
  243.2 1.3 collective-permute-start.49
  244.5 4.5 %collective-permute-start.50 = (f32[4,1280]{1,0:T(4,128)S(1)}, f32[4,1280]{1,0:T(4,128)S(1)}, u32[]{:S(2)}, u32[]{:S(2)}) collective-permute-start(f32[4,1280]{1,0:T(4,128)S(1)} %add.32), channel_id=1, source_target_pairs={{0,2},{1,3},{2,0},{3,1},{4,6},{5,7},{6,4},{7,5},{8,10},{9,11},{10,... | collective-permute-start | bytes 61448 | tf_op jit(solution)/shard_map/ppermute | solution.py:302
  245.6 4.7 %collective-permute-start.51 = (f32[4,1280]{1,0:T(4,128)S(1)}, f32[4,1280]{1,0:T(4,128)S(1)}, u32[]{:S(2)}, u32[]{:S(2)}) collective-permute-start(f32[4,1280]{1,0:T(4,128)S(1)} %add.32), channel_id=1, source_target_pairs={{0,4},{1,5},{2,6},{3,7},{4,0},{5,1},{6,2},{7,3},{8,12},{9,13},{10,... | collective-permute-start | bytes 61448 | tf_op jit(solution)/shard_map/ppermute | solution.py:302
  248.5 5.6 %collective-permute-start.52 = (f32[4,1280]{1,0:T(4,128)S(1)}, f32[4,1280]{1,0:T(4,128)S(1)}, u32[]{:S(2)}, u32[]{:S(2)}) collective-permute-start(f32[4,1280]{1,0:T(4,128)S(1)} %add.32), channel_id=1, source_target_pairs={{0,6},{1,7},{2,4},{3,5},{4,2},{5,3},{6,0},{7,1},{8,14},{9,15},{10,... | collective-permute-start | bytes 61448 | tf_op jit(solution)/shard_map/ppermute | solution.py:302
  (7 other events, 8.6 us)

commit v8 on v6

--- a/solution.py
+++ b/solution.py
@@ -188,7 +188,7 @@
 def stage(whole, arriving, gates, held, early, *, section, first, block, forward, backward):
     width = arriving.shape[1]
     row_count, channels = gates.shape
-    deep = width // 2
+    deep = width // 2 if forward else width
     at = pl.ds(first, block)
     read = at if arriving.shape[0] == row_count else pl.ds(0, block)
     results = [(row_count, channels), (row_count, width)]
@@ -266,7 +266,7 @@
         *parts, acts, vg, err, passed, basis_ref, second_ref, out_ref, done = refs
         copy = pltpu.make_async_copy(passed, out_ref, done)
         copy.start()
-        basis = orthonormal(joined(*(part[...] for part in parts)))
+        basis = orthonormal(parts[0][...] + parts[1][...])
         basis_ref[...] = basis
         pieces = split3(basis)
         mapped = lax.dot_general(
@@ -301,19 +301,33 @@
     return lax.ppermute(value, "dp", [(i, i ^ by) for i in range(replicas)])
 
 
-def sum_parts(value, turns):
-    replicas = lax.axis_size("dp")
+def sum_parts(value):
     by = 1
-    while by * (2 if turns else 4) < replicas:
+    while by * 2 < lax.axis_size("dp"):
         value = value + exchange(value, by)
         by *= 2
-    if turns:
-        return value, exchange(value, by)
-    return value, exchange(value, by), exchange(value, 2 * by), exchange(value, 3 * by)
-
-
-def joined(first, second, *others):
-    return (first + second) + joined(*others) if others else first + second
+    return value, exchange(value, by)
+
+
+def first_half(value_grads, inputs, warm, error_part):
+    def body(vg, acts, warm, error, out):
+        projected = lax.dot_general(
+            split3(warm[...]), vg[...], (((1,), (1,)), ((), ())),
+            preferred_element_type=jnp.float32,
+        )
+        factor = jnp.dot(
+            split3(join3(projected)), acts[...], preferred_element_type=jnp.float32
+        )
+        out[...] = join3(factor) + error[...]
+
+    return pl.pallas_call(
+        body,
+        in_specs=[VMEM] * 4,
+        out_specs=VMEM,
+        out_shape=jax.ShapeDtypeStruct(error_part.shape, jnp.float32),
+        compiler_params=pltpu.CompilerParams(vmem_limit_bytes=8 << 20),
+        name="first_half",
+    )(value_grads, inputs, warm, error_part)
 
 
 def local(acts, gates, w_value, w_out, residual_error, grad_top, warm_factor):
@@ -351,13 +365,9 @@
         if section == min(1, top):
             whole = finish(whole, "last", (0, 1), held[:1])
     value_grads, passed_rows = held
-    projected = jnp.dot(value_grads.astype(jnp.float32), warm.T, precision=HIGHEST)
-    factor = lax.dot_general(
-        projected, inputs.astype(jnp.float32), (((0,), (0,)), ((), ())), precision=HIGHEST
-    )
-    parts = sum_parts(factor + error_part, True)
+    parts = sum_parts(first_half(value_grads, inputs, warm, error_part))
     basis, second, grad_in = second_half(parts, inputs, value_grads, error, passed_rows)
-    right_out = joined(*sum_parts(second, False)) / math.sqrt(row_count * replicas * width)
+    right_out = sum(sum_parts(second)) / math.sqrt(row_count * replicas * width)
     return grad_in[None], basis[None], right_out[None]
 
 

time: 235 us -> 236 us (level)
  waiting for transfers between devices: 151 us -> 157 us
  starting transfers between devices: 43.1 us -> 38.8 us
    ppermute x7 -> x6, waiting for transfers between devices: 13.2 us -> 19.7 us  [exchange(): return lax.ppermute(value, 'dp', [(i, i ^ by) for i in range(replicas)])]
    ppermute x7 -> x6, starting transfers between devices: 4.68 us -> 0.42 us  [exchange(): return lax.ppermute(value, 'dp', [(i, i ^ by) for i in range(replicas)])]
  transfers between devices with their start and end apart: 48 -> 47, of which waited for: 19 -> 19; matrix products, arithmetic and copies ran while one was open for 5% -> 5% of each run, Pallas kernels for 6% -> 6%
where the time goes in v8:
time: 236 us
  waiting for transfers between devices  157 us (67%)
  starting transfers between devices  38.8 us (16%)
  Pallas kernels  21.8 us (9%)
  matrix products  8.01 us (3%)
  local copies, waits for them, and re-layouts  4.97 us (2%)
  other arithmetic  3.54 us (2%)
    ppermute x15, waiting for transfers between devices, permute(): return lax.ppermute(value, ('section', 'dp'), pairs)  102 us
    ppermute x12, waiting for transfers between devices, local(): arriving[k] = lax.ppermute(send, 'section', [(section, section - 1)])  35 us
    ppermute x15, starting transfers between devices, permute(): return lax.ppermute(value, ('section', 'dp'), pairs)  25.5 us
    ppermute x6, waiting for transfers between devices, exchange(): return lax.ppermute(value, 'dp', [(i, i ^ by) for i in range(replicas)])  19.7 us
    pallas_call x17, Pallas kernels, stage(): pl.pallas_call(body, in_specs=[VMEM] * 3 + [ANY] + [VMEM] * len(held), ou...  14.7 us
    ppermute x12, starting transfers between devices, local(): arriving[k] = lax.ppermute(send, 'section', [(section, section - 1)])  10.6 us
    dot_general x1, matrix products, local(): lax.dot_general(warm, error.astype(jnp.float32), (((1,), (1,)), ((), ()))...  8.01 us
    unnamed x36, local copies, waits for them, and re-layouts  4.97 us
  transfers between devices with their start and end apart: 47, of which 19 were waited for; matrix products, arithmetic and copies ran while one was open for 5% of the time, Pallas kernels for 6%

profile of v8, /device:TPU:0, one launch (start us, length us, event | category | flops | bytes accessed | tf_op | source)
XLA Modules:
  0.0 235.6 jit_solution(8858511466408443831)
XLA Ops:
  0.6 5.0 %collective-permute-start.2 = (bf16[320,1280]{1,0:T(8,128)(2,1)}, bf16[320,1280]{1,0:T(8,128)(2,1)S(1)}, u32[]{:S(2)}, u32[]{:S(2)}) collective-permute-start(bf16[320,1280]{1,0:T(8,128)(2,1)} %bitcast.36), channel_id=1, source_target_pairs={{0,2},{1,3},{2,4},{3,5},{4,6},{5,7},{8,10},{9,11},{10,12},{11,13},... | collective-permute-start | bytes 2457608 | tf_op jit(solution)/shard_map/ppermute | solution.py:74
  5.6 1.3 collective-permute-start
  6.9 5.5 %collective-permute-start.12 = (bf16[320,1280]{1,0:T(8,128)(2,1)}, bf16[320,1280]{1,0:T(8,128)(2,1)}, u32[]{:S(2)}, u32[]{:S(2)}) collective-permute-start(bf16[320,1280]{1,0:T(8,128)(2,1)} %bitcast.40), channel_id=1, source_target_pairs={{0,2},{1,3},{2,4},{3,5},{4,6},{5,7},{8,10},{9,11},{10,12},{11,13},... | collective-permute-start | bytes 2457608 | tf_op jit(solution)/shard_map/ppermute | solution.py:74
  12.4 1.3 collective-permute-start.10
  13.7 1.6 collective-permute-start.20
  15.3 9.2 %collective-permute-done.2.refs_7_ = bf16[320,1280]{1,0:T(8,128)(2,1)S(1)} collective-permute-done((bf16[320,1280]{1,0:T(8,128)(2,1)}, bf16[320,1280]{1,0:T(8,128)(2,1)S(1)}, u32[]{:S(2)}, u32[]{:S(2)}) %collective-permute-start.2) | collective-permute-done | bytes 819232 | tf_op jit(solution)/shard_map/ppermute | solution.py:74
  24.5 4.4 %collective-permute-done.refs_9_ = bf16[320,1280]{1,0:T(8,128)(2,1)} collective-permute-done((bf16[320,1280]{1,0:T(8,128)(2,1)}, bf16[320,1280]{1,0:T(8,128)(2,1)}, u32[]{:S(2)}, u32[]{:S(2)}) %collective-permute-start) | collective-permute-done | bytes 819232 | tf_op jit(solution)/shard_map/ppermute | solution.py:74
  29.0 12.0 %collective-permute-done.12.refs_3_ = bf16[320,1280]{1,0:T(8,128)(2,1)} collective-permute-done((bf16[320,1280]{1,0:T(8,128)(2,1)}, bf16[320,1280]{1,0:T(8,128)(2,1)}, u32[]{:S(2)}, u32[]{:S(2)}) %collective-permute-start.12) | collective-permute-done | bytes 819232 | tf_op jit(solution)/shard_map/ppermute | solution.py:74
  41.0 4.2 %collective-permute-done.10.refs_5_ = bf16[320,1280]{1,0:T(8,128)(2,1)} collective-permute-done((bf16[320,1280]{1,0:T(8,128)(2,1)}, bf16[320,1280]{1,0:T(8,128)(2,1)}, u32[]{:S(2)}, u32[]{:S(2)}) %collective-permute-start.10) | collective-permute-done | bytes 819232 | tf_op jit(solution)/shard_map/ppermute | solution.py:74
  45.1 2.7 %pad_maximum_fusion = bf16[2,320,1280]{2,1,0:T(8,128)(2,1)} fusion(bf16[1,320,1280]{2,1,0:T(8,128)(2,1)} %param.9, bf16[1,320,1280]{2,1,0:T(8,128)(2,1)} %param.10), kind=kLoop, calls=%fused_computation | loop fusion | flops 819200 | bytes 3276800 | tf_op jit(solution)/shard_map/stack | solution.py:134
  48.4 0.9 copy-done.7
  49.3 0.7 collective-permute-start.3
  50.0 0.9 copy-done.9
  50.9 1.3 collective-permute-start.1
  52.2 0.9 copy-done.11
  53.1 0.7 collective-permute-start.13
  53.8 1.0 copy-done.13
  54.8 1.3 collective-permute-start.11
  56.1 1.3 collective-permute-start.21
  57.4 19.0 %collective-permute-done.1.refs_6_ = bf16[320,1280]{1,0:T(8,128)(2,1)S(1)} collective-permute-done((bf16[320,1280]{1,0:T(8,128)(2,1)}, bf16[320,1280]{1,0:T(8,128)(2,1)S(1)}, u32[]{:S(2)}, u32[]{:S(2)}) %collective-permute-start.1) | collective-permute-done | bytes 819232 | tf_op jit(solution)/shard_map/ppermute | solution.py:74
  76.4 0.5 collective-permute-start.19
  76.9 17.0 %collective-permute-done.11.refs_2_ = bf16[320,1280]{1,0:T(8,128)(2,1)S(1)} collective-permute-done((bf16[320,1280]{1,0:T(8,128)(2,1)}, bf16[320,1280]{1,0:T(8,128)(2,1)S(1)}, u32[]{:S(2)}, u32[]{:S(2)}) %collective-permute-start.11) | collective-permute-done | bytes 819232 | tf_op jit(solution)/shard_map/ppermute | solution.py:74
  94.1 1.3 collective-permute-start.14
  95.4 16.2 %collective-permute-done.21 = bf16[320,1280]{1,0:T(8,128)(2,1)} collective-permute-done((bf16[320,1280]{1,0:T(8,128)(2,1)}, bf16[320,1280]{1,0:T(8,128)(2,1)}, u32[]{:S(2)}, u32[]{:S(2)}) %collective-permute-start.21) | collective-permute-done | bytes 819232 | tf_op jit(solution)/shard_map/ppermute | solution.py:74
  111.6 1.3 collective-permute-start.22
  113.2 0.8 collective-permute-start.8
  114.1 0.8 collective-permute-start.6
  115.0 14.4 %collective-permute-done.22.refs_8_ = bf16[320,1280]{1,0:T(8,128)(2,1)S(1)} collective-permute-done((bf16[320,1280]{1,0:T(8,128)(2,1)}, bf16[320,1280]{1,0:T(8,128)(2,1)S(1)}, u32[]{:S(2)}, u32[]{:S(2)}) %collective-permute-start.22) | collective-permute-done | bytes 819232 | tf_op jit(solution)/shard_map/ppermute | solution.py:74
  129.4 0.5 collective-permute-start.15
  130.0 1.3 collective-permute-start.4
  131.8 8.0 %fusion.early.error = f32[4,2560]{1,0:T(4,128)S(1)} fusion(bf16[1,2560,1280]{2,1,0:T(8,128)(2,1)} %param.11, f32[1,4,1280]{2,1,0:T(4,128)S(1)} %copy-done.15), kind=kOutput, calls=%fused_computation.4 | convolution fusion | flops 157286400 | bytes 6615040 | tf_op jit(solution)/shard_map/dot_general | solution.py:338
  139.9 2.2 put.6.refs_10_
  142.1 0.6 put.7.refs_2_
  143.0 0.8 copy-done
  144.3 0.7 collective-permute-start.32
  145.0 0.7 collective-permute-start.31
  145.7 0.7 collective-permute-start.30
  146.6 5.9 %collective-permute-done.4.refs_0_ = bf16[320,1280]{1,0:T(8,128)(2,1)S(1)} collective-permute-done((bf16[320,1280]{1,0:T(8,128)(2,1)S(1)}, bf16[320,1280]{1,0:T(8,128)(2,1)S(1)}, u32[]{:S(2)}, u32[]{:S(2)}) %collective-permute-start.4) | collective-permute-done | bytes 819232 | tf_op jit(solution)/shard_map/ppermute | solution.py:74
  152.4 0.7 collective-permute-start.29
  153.3 0.7 collective-permute-start.36
  154.0 0.7 collective-permute-start.35
  154.8 0.7 collective-permute-start.34
  155.5 0.7 collective-permute-start.33
  156.2 1.3 collective-permute-start.40
  157.6 1.3 collective-permute-start.39
  158.9 1.3 collective-permute-start.38
  160.4 1.3 collective-permute-start.37
  162.0 23.8 %collective-permute-done.40.arr = bf16[64,2560]{1,0:T(8,128)(2,1)S(1)} collective-permute-done((bf16[64,2560]{1,0:T(8,128)(2,1)S(1)}, bf16[64,2560]{1,0:T(8,128)(2,1)S(1)}, u32[]{:S(2)}, u32[]{:S(2)}) %collective-permute-start.40) | collective-permute-done | bytes 327712 | tf_op jit(solution)/shard_map/ppermute | solution.py:362
  185.8 3.5 %shard_map.107 = (bf16[256,1280]{1,0:T(8,128)(2,1)S(1)}, bf16[256,2560]{1,0:T(8,128)(2,1)S(1)}) custom-call(bf16[2,2560,1280]{2,1,0:T(8,128)(2,1)S(1)} %put.11.w, bf16[64,2560]{1,0:T(8,128)(2,1)S(1)} %collective-permute-done.40.arr, bf16[256,1280]{1,0:T(8,128)(2,1)S(1)} %bitcast.27, ...), custom_call_target="tpu_custom_call", output_to_operand_aliasing={{0}: (4, {}), {1}: (5, {})} | custom-call | flops 838860800 | bytes 13107200 | tf_op jit(solution)/shard_map/pallas_call | solution.py:225
  189.3 3.5 %collective-permute-done.39.arr = bf16[64,2560]{1,0:T(8,128)(2,1)S(1)} collective-permute-done((bf16[64,2560]{1,0:T(8,128)(2,1)S(1)}, bf16[64,2560]{1,0:T(8,128)(2,1)S(1)}, u32[]{:S(2)}, u32[]{:S(2)}) %collective-permute-start.39) | collective-permute-done | bytes 327712 | tf_op jit(solution)/shard_map/ppermute | solution.py:362
  192.9 3.5 %shard_map.108 = (bf16[256,1280]{1,0:T(8,128)(2,1)S(1)}, bf16[256,2560]{1,0:T(8,128)(2,1)S(1)}) custom-call(bf16[2,2560,1280]{2,1,0:T(8,128)(2,1)S(1)} %put.11.w, bf16[64,2560]{1,0:T(8,128)(2,1)S(1)} %collective-permute-done.39.arr, bf16[256,1280]{1,0:T(8,128)(2,1)S(1)} %bitcast.28, ...), custom_call_target="tpu_custom_call", output_to_operand_aliasing={{0}: (4, {}), {1}: (5, {})} | custom-call | flops 838860800 | bytes 13107200 | tf_op jit(solution)/shard_map/pallas_call | solution.py:225
  196.4 3.5 %collective-permute-done.38.arr = bf16[64,2560]{1,0:T(8,128)(2,1)S(1)} collective-permute-done((bf16[64,2560]{1,0:T(8,128)(2,1)S(1)}, bf16[64,2560]{1,0:T(8,128)(2,1)S(1)}, u32[]{:S(2)}, u32[]{:S(2)}) %collective-permute-start.38) | collective-permute-done | bytes 327712 | tf_op jit(solution)/shard_map/ppermute | solution.py:362
  199.9 3.5 %shard_map.109 = (bf16[256,1280]{1,0:T(8,128)(2,1)S(1)}, bf16[256,2560]{1,0:T(8,128)(2,1)S(1)}) custom-call(bf16[2,2560,1280]{2,1,0:T(8,128)(2,1)S(1)} %put.11.w, bf16[64,2560]{1,0:T(8,128)(2,1)S(1)} %collective-permute-done.38.arr, bf16[256,1280]{1,0:T(8,128)(2,1)S(1)} %bitcast.29, ...), custom_call_target="tpu_custom_call", output_to_operand_aliasing={{0}: (4, {}), {1}: (5, {})} | custom-call | flops 838860800 | bytes 13107200 | tf_op jit(solution)/shard_map/pallas_call | solution.py:225
  203.4 4.2 %collective-permute-done.37.arr = bf16[64,2560]{1,0:T(8,128)(2,1)S(1)} collective-permute-done((bf16[64,2560]{1,0:T(8,128)(2,1)S(1)}, bf16[64,2560]{1,0:T(8,128)(2,1)S(1)}, u32[]{:S(2)}, u32[]{:S(2)}) %collective-permute-start.37) | collective-permute-done | bytes 327712 | tf_op jit(solution)/shard_map/ppermute | solution.py:362
  207.6 3.5 %shard_map.110 = (bf16[256,1280]{1,0:T(8,128)(2,1)S(1)}, bf16[256,2560]{1,0:T(8,128)(2,1)S(1)}) custom-call(bf16[2,2560,1280]{2,1,0:T(8,128)(2,1)S(1)} %put.11.w, bf16[64,2560]{1,0:T(8,128)(2,1)S(1)} %collective-permute-done.37.arr, bf16[256,1280]{1,0:T(8,128)(2,1)S(1)} %bitcast.30, ...), custom_call_target="tpu_custom_call", output_to_operand_aliasing={{0}: (4, {}), {1}: (5, {})} | custom-call | flops 838860800 | bytes 13107200 | tf_op jit(solution)/shard_map/pallas_call | solution.py:225
  211.1 0.9 first_half.1
  212.1 1.2 collective-permute-done.41
  213.4 4.0 %collective-permute-done.42 = f32[4,2560]{1,0:T(4,128)S(1)} collective-permute-done((f32[4,2560]{1,0:T(4,128)S(1)}, f32[4,2560]{1,0:T(4,128)S(1)}, u32[]{:S(2)}, u32[]{:S(2)}) %collective-permute-start.42) | collective-permute-done | bytes 40992 | tf_op jit(solution)/shard_map/ppermute | solution.py:301
  217.4 4.9 %collective-permute-done.43.refs_1_ = f32[4,2560]{1,0:T(4,128)S(1)} collective-permute-done((f32[4,2560]{1,0:T(4,128)S(1)}, f32[4,2560]{1,0:T(4,128)S(1)}, u32[]{:S(2)}, u32[]{:S(2)}) %collective-permute-start.43) | collective-permute-done | bytes 40992 | tf_op jit(solution)/shard_map/ppermute | solution.py:301
  222.3 2.8 %second_half.1 = (f32[4,2560]{1,0:T(4,128)}, f32[4,1280]{1,0:T(4,128)S(1)}, bf16[256,2560]{1,0:T(8,128)(2,1)}) custom-call(f32[4,2560]{1,0:T(4,128)S(1)} %add.16.refs_0_, f32[4,2560]{1,0:T(4,128)S(1)} %collective-permute-done.43.refs_1_, bf16[256,2560]{1,0:T(8,128)(2,1)S(1)} %bitcast.35, bf16[256,1280]{1,0:T(8,128)(2,1)S(1)} %get-tuple-element.96.vg.refs_3_, ...), custom_call_target="tpu_custom_call" | custom-call | tf_op jit(solution)/shard_map/second_half/pallas_call | solution.py:284
  225.2 1.2 collective-permute-done.44
  226.5 3.8 %collective-permute-done.45 = f32[4,1280]{1,0:T(4,128)S(1)} collective-permute-done((f32[4,1280]{1,0:T(4,128)S(1)}, f32[4,1280]{1,0:T(4,128)S(1)}, u32[]{:S(2)}, u32[]{:S(2)}) %collective-permute-start.45) | collective-permute-done | bytes 20512 | tf_op jit(solution)/shard_map/ppermute | solution.py:301
  230.3 4.7 %collective-permute-done.46 = f32[4,1280]{1,0:T(4,128)S(1)} collective-permute-done((f32[4,1280]{1,0:T(4,128)S(1)}, f32[4,1280]{1,0:T(4,128)S(1)}, u32[]{:S(2)}, u32[]{:S(2)}) %collective-permute-start.46) | collective-permute-done | bytes 20512 | tf_op jit(solution)/shard_map/ppermute | solution.py:301
  235.0 0.6 multiply_bitcast_fusion
  (101 shorter events, 3.7 us)
Async XLA Ops:
  0.6 23.9 %collective-permute-start.2 = (bf16[320,1280]{1,0:T(8,128)(2,1)}, bf16[320,1280]{1,0:T(8,128)(2,1)S(1)}, u32[]{:S(2)}, u32[]{:S(2)}) collective-permute-start(bf16[320,1280]{1,0:T(8,128)(2,1)} %bitcast.36), channel_id=1, source_target_pairs={{0,2},{1,3},{2,4},{3,5},{4,6},{5,7},{8,10},{9,11},{10,12},{11,13},... | collective-permute-start | bytes 2457608 | tf_op jit(solution)/shard_map/ppermute | solution.py:74
  5.6 23.3 %collective-permute-start = (bf16[320,1280]{1,0:T(8,128)(2,1)}, bf16[320,1280]{1,0:T(8,128)(2,1)}, u32[]{:S(2)}, u32[]{:S(2)}) collective-permute-start(bf16[320,1280]{1,0:T(8,128)(2,1)} %bitcast.37), channel_id=1, source_target_pairs={{2,0},{3,1},{4,2},{5,3},{6,4},{7,5},{10,8},{11,9},{12,10},{13,11},... | collective-permute-start | bytes 2457608 | tf_op jit(solution)/shard_map/ppermute | solution.py:74
  6.9 34.0 %collective-permute-start.12 = (bf16[320,1280]{1,0:T(8,128)(2,1)}, bf16[320,1280]{1,0:T(8,128)(2,1)}, u32[]{:S(2)}, u32[]{:S(2)}) collective-permute-start(bf16[320,1280]{1,0:T(8,128)(2,1)} %bitcast.40), channel_id=1, source_target_pairs={{0,2},{1,3},{2,4},{3,5},{4,6},{5,7},{8,10},{9,11},{10,12},{11,13},... | collective-permute-start | bytes 2457608 | tf_op jit(solution)/shard_map/ppermute | solution.py:74
  12.4 32.7 %collective-permute-start.10 = (bf16[320,1280]{1,0:T(8,128)(2,1)}, bf16[320,1280]{1,0:T(8,128)(2,1)}, u32[]{:S(2)}, u32[]{:S(2)}) collective-permute-start(bf16[320,1280]{1,0:T(8,128)(2,1)} %bitcast.41), channel_id=1, source_target_pairs={{2,0},{3,1},{4,2},{5,3},{6,4},{7,5},{10,8},{11,9},{12,10},{13,11},... | collective-permute-start | bytes 2457608 | tf_op jit(solution)/shard_map/ppermute | solution.py:74
  13.7 34.2 %collective-permute-start.20 = (bf16[320,1280]{1,0:T(8,128)(2,1)}, bf16[320,1280]{1,0:T(8,128)(2,1)}, u32[]{:S(2)}, u32[]{:S(2)}) collective-permute-start(bf16[320,1280]{1,0:T(8,128)(2,1)} %bitcast.38), channel_id=1, source_target_pairs={{26,2},{27,3},{28,4},{29,5}} | collective-permute-start | bytes 2457608 | tf_op jit(solution)/shard_map/ppermute | solution.py:74
  24.5 23.8 %copy-start.5 = (bf16[320,1280]{1,0:T(8,128)(2,1)}, bf16[320,1280]{1,0:T(8,128)(2,1)S(1)}, u32[]{:S(2)}) copy-start(bf16[320,1280]{1,0:T(8,128)(2,1)S(1)} %collective-permute-done.2.refs_7_) | copy-start | bytes 2457604
  24.5 23.8 %collective-permute-start.27 = (bf16[320,1280]{1,0:T(8,128)(2,1)S(1)}, bf16[320,1280]{1,0:T(8,128)(2,1)S(1)}, u32[]{:S(2)}, u32[]{:S(2)}) collective-permute-start(bf16[320,1280]{1,0:T(8,128)(2,1)S(1)} %collective-permute-done.2.refs_7_), channel_id=1, source_target_pairs={{0,1},{1,0},{2,3},{3,2},{4,5},{5,4},{6,7},{7,6},{8,9},{9,8},{10,11... | collective-permute-start | bytes 2457608 | tf_op jit(solution)/shard_map/ppermute | solution.py:82
  29.0 21.0 %collective-permute-start.28 = (bf16[320,1280]{1,0:T(8,128)(2,1)}, bf16[320,1280]{1,0:T(8,128)(2,1)S(1)}, u32[]{:S(2)}, u32[]{:S(2)}) collective-permute-start(bf16[320,1280]{1,0:T(8,128)(2,1)} %collective-permute-done.refs_9_), channel_id=1, source_target_pairs={{0,1},{1,0},{2,3},{3,2},{4,5},{5,4},{6,7},{7,6},{8,9},{9,8},{10,11... | collective-permute-start | bytes 2457608 | tf_op jit(solution)/shard_map/ppermute | solution.py:82
  41.0 11.2 %collective-permute-start.25 = (bf16[320,1280]{1,0:T(8,128)(2,1)}, bf16[320,1280]{1,0:T(8,128)(2,1)S(1)}, u32[]{:S(2)}, u32[]{:S(2)}) collective-permute-start(bf16[320,1280]{1,0:T(8,128)(2,1)} %collective-permute-done.12.refs_3_), channel_id=1, source_target_pairs={{0,1},{1,0},{2,3},{3,2},{4,5},{5,4},{6,7},{7,6},{8,9},{9,8},{10,11... | collective-permute-start | bytes 2457608 | tf_op jit(solution)/shard_map/ppermute | solution.py:82
  45.1 8.7 %collective-permute-start.26 = (bf16[320,1280]{1,0:T(8,128)(2,1)}, bf16[320,1280]{1,0:T(8,128)(2,1)S(1)}, u32[]{:S(2)}, u32[]{:S(2)}) collective-permute-start(bf16[320,1280]{1,0:T(8,128)(2,1)} %collective-permute-done.10.refs_5_), channel_id=1, source_target_pairs={{0,1},{1,0},{2,3},{3,2},{4,5},{5,4},{6,7},{7,6},{8,9},{9,8},{10,11... | collective-permute-start | bytes 2457608 | tf_op jit(solution)/shard_map/ppermute | solution.py:82
  47.8 46.2 %collective-permute-start.24 = (bf16[2,320,1280]{2,1,0:T(8,128)(2,1)}, bf16[2,320,1280]{2,1,0:T(8,128)(2,1)}, u32[]{:S(2)}, u32[]{:S(2)}) collective-permute-start(bf16[2,320,1280]{2,1,0:T(8,128)(2,1)} %pad_maximum_fusion), channel_id=1, source_target_pairs={{0,1},{1,0},{2,3},{3,2},{4,5},{5,4},{6,7},{7,6},{8,9},{9,8},{10,11... | collective-permute-start | bytes 4915208 | tf_op jit(solution)/shard_map/ppermute | solution.py:82
  48.4 0.9 copy-start.7
  49.3 6.8 %collective-permute-start.3 = (bf16[320,1280]{1,0:T(8,128)(2,1)S(1)}, bf16[320,1280]{1,0:T(8,128)(2,1)S(1)}, u32[]{:S(2)}, u32[]{:S(2)}) collective-permute-start(bf16[320,1280]{1,0:T(8,128)(2,1)S(1)} %collective-permute-done.2.refs_7_), channel_id=1, source_target_pairs={{2,4},{3,5},{4,6},{5,7},{10,12},{11,13},{12,14},{13,15},{18,20},{1... | collective-permute-start | bytes 2457608 | tf_op jit(solution)/shard_map/ppermute | solution.py:74
  50.0 0.9 copy-start.9
  50.9 25.5 %collective-permute-start.1 = (bf16[320,1280]{1,0:T(8,128)(2,1)}, bf16[320,1280]{1,0:T(8,128)(2,1)S(1)}, u32[]{:S(2)}, u32[]{:S(2)}) collective-permute-start(bf16[320,1280]{1,0:T(8,128)(2,1)} %collective-permute-done.refs_9_), channel_id=1, source_target_pairs={{2,0},{3,1},{4,2},{5,3},{10,8},{11,9},{12,10},{13,11},{18,16},{19,... | collective-permute-start | bytes 2457608 | tf_op jit(solution)/shard_map/ppermute | solution.py:74
  53.1 23.4 %collective-permute-start.13 = (bf16[320,1280]{1,0:T(8,128)(2,1)}, bf16[320,1280]{1,0:T(8,128)(2,1)S(1)}, u32[]{:S(2)}, u32[]{:S(2)}) collective-permute-start(bf16[320,1280]{1,0:T(8,128)(2,1)} %collective-permute-done.12.refs_3_), channel_id=1, source_target_pairs={{2,4},{3,5},{4,6},{5,7},{10,12},{11,13},{12,14},{13,15},{18,20},{1... | collective-permute-start | bytes 2457608 | tf_op jit(solution)/shard_map/ppermute | solution.py:74
  53.8 1.0 copy-start.13
  54.8 39.2 %collective-permute-start.11 = (bf16[320,1280]{1,0:T(8,128)(2,1)}, bf16[320,1280]{1,0:T(8,128)(2,1)S(1)}, u32[]{:S(2)}, u32[]{:S(2)}) collective-permute-start(bf16[320,1280]{1,0:T(8,128)(2,1)} %collective-permute-done.10.refs_5_), channel_id=1, source_target_pairs={{2,0},{3,1},{4,2},{5,3},{10,8},{11,9},{12,10},{13,11},{18,16},{19,... | collective-permute-start | bytes 2457608 | tf_op jit(solution)/shard_map/ppermute | solution.py:74
  56.1 55.6 %collective-permute-start.21 = (bf16[320,1280]{1,0:T(8,128)(2,1)}, bf16[320,1280]{1,0:T(8,128)(2,1)}, u32[]{:S(2)}, u32[]{:S(2)}) collective-permute-start(bf16[320,1280]{1,0:T(8,128)(2,1)} %collective-permute-done.20), channel_id=1, source_target_pairs={{2,0},{3,1},{4,6},{5,7}} | collective-permute-start | bytes 2457608 | tf_op jit(solution)/shard_map/ppermute | solution.py:74
  76.4 36.7 %collective-permute-start.18 = (bf16[320,1280]{1,0:T(8,128)(2,1)S(1)}, bf16[320,1280]{1,0:T(8,128)(2,1)S(1)}, u32[]{:S(2)}, u32[]{:S(2)}) collective-permute-start(bf16[320,1280]{1,0:T(8,128)(2,1)S(1)} %collective-permute-done.3.refs_4_), channel_id=1, source_target_pairs={{0,1},{1,0},{2,3},{3,2},{4,5},{5,4},{6,7},{7,6},{8,9},{9,8},{10,11... | collective-permute-start | bytes 2457608 | tf_op jit(solution)/shard_map/ppermute | solution.py:82
  76.4 37.6 %collective-permute-start.19 = (bf16[320,1280]{1,0:T(8,128)(2,1)S(1)}, bf16[320,1280]{1,0:T(8,128)(2,1)S(1)}, u32[]{:S(2)}, u32[]{:S(2)}) collective-permute-start(bf16[320,1280]{1,0:T(8,128)(2,1)S(1)} %collective-permute-done.1.refs_6_), channel_id=1, source_target_pairs={{0,1},{1,0},{2,3},{3,2},{4,5},{5,4},{6,7},{7,6},{8,9},{9,8},{10,11... | collective-permute-start | bytes 2457608 | tf_op jit(solution)/shard_map/ppermute | solution.py:82
  94.0 20.1 %collective-permute-start.16 = (bf16[320,1280]{1,0:T(8,128)(2,1)S(1)}, bf16[320,1280]{1,0:T(8,128)(2,1)S(1)}, u32[]{:S(2)}, u32[]{:S(2)}) collective-permute-start(bf16[320,1280]{1,0:T(8,128)(2,1)S(1)} %collective-permute-done.13.refs_0_), channel_id=1, source_target_pairs={{0,1},{1,0},{2,3},{3,2},{4,5},{5,4},{6,7},{7,6},{8,9},{9,8},{10,11... | collective-permute-start | bytes 2457608 | tf_op jit(solution)/shard_map/ppermute | solution.py:82
  94.1 37.7 %copy-start.15 = (f32[1,4,1280]{2,1,0:T(4,128)S(1)}, f32[1,4,1280]{2,1,0:T(4,128)}, u32[]{:S(2)}) copy-start(f32[1,4,1280]{2,1,0:T(4,128)} %param.13) | copy-start | bytes 61444
  94.1 35.3 %collective-permute-start.14 = (bf16[320,1280]{1,0:T(8,128)(2,1)S(1)}, bf16[320,1280]{1,0:T(8,128)(2,1)S(1)}, u32[]{:S(2)}, u32[]{:S(2)}) collective-permute-start(bf16[320,1280]{1,0:T(8,128)(2,1)S(1)} %broadcast_select_fusion), channel_id=1, source_target_pairs={{2,0},{3,1},{4,6},{5,7},{10,8},{11,9},{12,14},{13,15},{18,16},{19,... | collective-permute-start | bytes 2457608 | tf_op jit(solution)/shard_map/ppermute | solution.py:74
  111.6 17.7 %collective-permute-start.22 = (bf16[320,1280]{1,0:T(8,128)(2,1)}, bf16[320,1280]{1,0:T(8,128)(2,1)S(1)}, u32[]{:S(2)}, u32[]{:S(2)}) collective-permute-start(bf16[320,1280]{1,0:T(8,128)(2,1)} %collective-permute-done.21), channel_id=1, source_target_pairs={{0,24},{1,25},{6,30},{7,31}} | collective-permute-start | bytes 2457608 | tf_op jit(solution)/shard_map/ppermute | solution.py:74
  113.1 26.7 %copy-start.3 = (bf16[1,320,1280]{2,1,0:T(8,128)(2,1)S(1)}, bf16[1,320,1280]{2,1,0:T(8,128)(2,1)}, u32[]{:S(2)}) copy-start(bf16[1,320,1280]{2,1,0:T(8,128)(2,1)} %param.9) | copy-start | bytes 2457604
  113.1 26.7 %copy-start.4 = (bf16[1,320,1280]{2,1,0:T(8,128)(2,1)S(1)}, bf16[1,320,1280]{2,1,0:T(8,128)(2,1)}, u32[]{:S(2)}) copy-start(bf16[1,320,1280]{2,1,0:T(8,128)(2,1)} %param.10) | copy-start | bytes 2457604
  113.1 26.7 %copy-start.6 = (bf16[320,1280]{1,0:T(8,128)(2,1)S(1)}, bf16[320,1280]{1,0:T(8,128)(2,1)}, u32[]{:S(2)}) copy-start(bf16[320,1280]{1,0:T(8,128)(2,1)} %copy-done.5) | copy-start | bytes 2457604
  113.1 26.7 %copy-start.8 = (bf16[320,1280]{1,0:T(8,128)(2,1)S(1)}, bf16[320,1280]{1,0:T(8,128)(2,1)}, u32[]{:S(2)}) copy-start(bf16[320,1280]{1,0:T(8,128)(2,1)} %copy-done.7) | copy-start | bytes 2457604
  113.1 26.7 %copy-start.10 = (bf16[320,1280]{1,0:T(8,128)(2,1)S(1)}, bf16[320,1280]{1,0:T(8,128)(2,1)}, u32[]{:S(2)}) copy-start(bf16[320,1280]{1,0:T(8,128)(2,1)} %copy-done.9) | copy-start | bytes 2457604
  113.1 26.7 %copy-start.12 = (bf16[320,1280]{1,0:T(8,128)(2,1)S(1)}, bf16[320,1280]{1,0:T(8,128)(2,1)}, u32[]{:S(2)}) copy-start(bf16[320,1280]{1,0:T(8,128)(2,1)} %copy-done.11) | copy-start | bytes 2457604
  113.1 26.7 %copy-start.14 = (bf16[320,1280]{1,0:T(8,128)(2,1)S(1)}, bf16[320,1280]{1,0:T(8,128)(2,1)}, u32[]{:S(2)}) copy-start(bf16[320,1280]{1,0:T(8,128)(2,1)} %copy-done.13) | copy-start | bytes 2457604
  113.2 16.7 %collective-permute-start.8 = (bf16[320,1280]{1,0:T(8,128)(2,1)S(1)}, bf16[320,1280]{1,0:T(8,128)(2,1)S(1)}, u32[]{:S(2)}, u32[]{:S(2)}) collective-permute-start(bf16[320,1280]{1,0:T(8,128)(2,1)S(1)} %broadcast_select_fusion.1), channel_id=1, source_target_pairs={{26,24},{27,25},{28,30},{29,31}} | collective-permute-start | bytes 2457608 | tf_op jit(solution)/shard_map/ppermute | solution.py:74
  114.0 15.9 %collective-permute-start.17 = (bf16[320,1280]{1,0:T(8,128)(2,1)S(1)}, bf16[320,1280]{1,0:T(8,128)(2,1)S(1)}, u32[]{:S(2)}, u32[]{:S(2)}) collective-permute-start(bf16[320,1280]{1,0:T(8,128)(2,1)S(1)} %collective-permute-done.11.refs_2_), channel_id=1, source_target_pairs={{0,1},{1,0},{2,3},{3,2},{4,5},{5,4},{6,7},{7,6},{8,9},{9,8},{10,11... | collective-permute-start | bytes 2457608 | tf_op jit(solution)/shard_map/ppermute | solution.py:82
  114.1 17.1 %collective-permute-start.6 = (bf16[320,1280]{1,0:T(8,128)(2,1)S(1)}, bf16[320,1280]{1,0:T(8,128)(2,1)S(1)}, u32[]{:S(2)}, u32[]{:S(2)}) collective-permute-start(bf16[320,1280]{1,0:T(8,128)(2,1)S(1)} %broadcast_select_fusion.1), channel_id=1, source_target_pairs={{10,8},{11,9},{12,14},{13,15},{18,16},{19,17},{20,22},{21,23}} | collective-permute-start | bytes 2457608 | tf_op jit(solution)/shard_map/ppermute | solution.py:74
  129.4 12.7 %collective-permute-start.23 = (bf16[320,1280]{1,0:T(8,128)(2,1)S(1)}, bf16[320,1280]{1,0:T(8,128)(2,1)S(1)}, u32[]{:S(2)}, u32[]{:S(2)}) collective-permute-start(bf16[320,1280]{1,0:T(8,128)(2,1)S(1)} %collective-permute-done.22.refs_8_), channel_id=1, source_target_pairs={{0,1},{1,0},{2,3},{3,2},{4,5},{5,4},{6,7},{7,6},{8,9},{9,8},{10,11... | collective-permute-start | bytes 2457608 | tf_op jit(solution)/shard_map/ppermute | solution.py:82
  129.4 13.3 %collective-permute-start.15 = (bf16[320,1280]{1,0:T(8,128)(2,1)S(1)}, bf16[320,1280]{1,0:T(8,128)(2,1)S(1)}, u32[]{:S(2)}, u32[]{:S(2)}) collective-permute-start(bf16[320,1280]{1,0:T(8,128)(2,1)S(1)} %collective-permute-done.14.refs_0_), channel_id=1, source_target_pairs={{0,1},{1,0},{2,3},{3,2},{4,5},{5,4},{6,7},{7,6},{8,9},{9,8},{10,11... | collective-permute-start | bytes 2457608 | tf_op jit(solution)/shard_map/ppermute | solution.py:82
  129.9 14.3 %collective-permute-start.9 = (bf16[320,1280]{1,0:T(8,128)(2,1)S(1)}, bf16[320,1280]{1,0:T(8,128)(2,1)S(1)}, u32[]{:S(2)}, u32[]{:S(2)}) collective-permute-start(bf16[320,1280]{1,0:T(8,128)(2,1)S(1)} %collective-permute-done.8.refs_0_), channel_id=1, source_target_pairs={{0,1},{1,0},{2,3},{3,2},{4,5},{5,4},{6,7},{7,6},{8,9},{9,8},{10,11... | collective-permute-start | bytes 2457608 | tf_op jit(solution)/shard_map/ppermute | solution.py:82
  130.0 22.5 %collective-permute-start.4 = (bf16[320,1280]{1,0:T(8,128)(2,1)S(1)}, bf16[320,1280]{1,0:T(8,128)(2,1)S(1)}, u32[]{:S(2)}, u32[]{:S(2)}) collective-permute-start(bf16[320,1280]{1,0:T(8,128)(2,1)S(1)} %broadcast_select_fusion.1), channel_id=1, source_target_pairs={{2,0},{3,1},{4,6},{5,7}} | collective-permute-start | bytes 2457608 | tf_op jit(solution)/shard_map/ppermute | solution.py:74
  131.3 21.9 %collective-permute-start.7 = (bf16[320,1280]{1,0:T(8,128)(2,1)S(1)}, bf16[320,1280]{1,0:T(8,128)(2,1)S(1)}, u32[]{:S(2)}, u32[]{:S(2)}) collective-permute-start(bf16[320,1280]{1,0:T(8,128)(2,1)S(1)} %collective-permute-done.6.refs_0_), channel_id=1, source_target_pairs={{0,1},{1,0},{2,3},{3,2},{4,5},{5,4},{6,7},{7,6},{8,9},{9,8},{10,11... | collective-permute-start | bytes 2457608 | tf_op jit(solution)/shard_map/ppermute | solution.py:82
  142.6 1.1 copy-start
  142.7 1.5 copy-start.1
  144.3 9.0 %collective-permute-start.32 = (bf16[64,2560]{1,0:T(8,128)(2,1)S(1)}, bf16[64,2560]{1,0:T(8,128)(2,1)S(1)}, u32[]{:S(2)}, u32[]{:S(2)}) collective-permute-start(bf16[64,2560]{1,0:T(8,128)(2,1)S(1)} %get-tuple-element.64), channel_id=1, source_target_pairs={{24,16},{25,17},{26,18},{27,19},{28,20},{29,21},{30,22},{31,23}} | collective-permute-start | bytes 983048 | tf_op jit(solution)/shard_map/ppermute | solution.py:362
  145.0 9.0 %collective-permute-start.31 = (bf16[64,2560]{1,0:T(8,128)(2,1)S(1)}, bf16[64,2560]{1,0:T(8,128)(2,1)S(1)}, u32[]{:S(2)}, u32[]{:S(2)}) collective-permute-start(bf16[64,2560]{1,0:T(8,128)(2,1)S(1)} %get-tuple-element.63), channel_id=1, source_target_pairs={{24,16},{25,17},{26,18},{27,19},{28,20},{29,21},{30,22},{31,23}} | collective-permute-start | bytes 983048 | tf_op jit(solution)/shard_map/ppermute | solution.py:362
  145.7 9.1 %collective-permute-start.30 = (bf16[64,2560]{1,0:T(8,128)(2,1)S(1)}, bf16[64,2560]{1,0:T(8,128)(2,1)S(1)}, u32[]{:S(2)}, u32[]{:S(2)}) collective-permute-start(bf16[64,2560]{1,0:T(8,128)(2,1)S(1)} %get-tuple-element.62), channel_id=1, source_target_pairs={{24,16},{25,17},{26,18},{27,19},{28,20},{29,21},{30,22},{31,23}} | collective-permute-start | bytes 983048 | tf_op jit(solution)/shard_map/ppermute | solution.py:362
  152.4 3.0 %collective-permute-start.29 = (bf16[64,2560]{1,0:T(8,128)(2,1)S(1)}, bf16[64,2560]{1,0:T(8,128)(2,1)S(1)}, u32[]{:S(2)}, u32[]{:S(2)}) collective-permute-start(bf16[64,2560]{1,0:T(8,128)(2,1)S(1)} %get-tuple-element.61), channel_id=1, source_target_pairs={{24,16},{25,17},{26,18},{27,19},{28,20},{29,21},{30,22},{31,23}} | collective-permute-start | bytes 983048 | tf_op jit(solution)/shard_map/ppermute | solution.py:362
  153.1 8.6 %collective-permute-start.5 = (bf16[320,1280]{1,0:T(8,128)(2,1)S(1)}, bf16[320,1280]{1,0:T(8,128)(2,1)S(1)}, u32[]{:S(2)}, u32[]{:S(2)}) collective-permute-start(bf16[320,1280]{1,0:T(8,128)(2,1)S(1)} %collective-permute-done.4.refs_0_), channel_id=1, source_target_pairs={{0,1},{1,0},{2,3},{3,2},{4,5},{5,4},{6,7},{7,6},{8,9},{9,8},{10,11... | collective-permute-start | bytes 2457608 | tf_op jit(solution)/shard_map/ppermute | solution.py:82
  153.3 2.9 %collective-permute-start.36 = (bf16[64,2560]{1,0:T(8,128)(2,1)S(1)}, bf16[64,2560]{1,0:T(8,128)(2,1)S(1)}, u32[]{:S(2)}, u32[]{:S(2)}) collective-permute-start(bf16[64,2560]{1,0:T(8,128)(2,1)S(1)} %get-tuple-element.75), channel_id=1, source_target_pairs={{16,8},{17,9},{18,10},{19,11},{20,12},{21,13},{22,14},{23,15}} | collective-permute-start | bytes 983048 | tf_op jit(solution)/shard_map/ppermute | solution.py:362
  154.0 3.5 %collective-permute-start.35 = (bf16[64,2560]{1,0:T(8,128)(2,1)S(1)}, bf16[64,2560]{1,0:T(8,128)(2,1)S(1)}, u32[]{:S(2)}, u32[]{:S(2)}) collective-permute-start(bf16[64,2560]{1,0:T(8,128)(2,1)S(1)} %get-tuple-element.74), channel_id=1, source_target_pairs={{16,8},{17,9},{18,10},{19,11},{20,12},{21,13},{22,14},{23,15}} | collective-permute-start | bytes 983048 | tf_op jit(solution)/shard_map/ppermute | solution.py:362
  154.8 4.1 %collective-permute-start.34 = (bf16[64,2560]{1,0:T(8,128)(2,1)S(1)}, bf16[64,2560]{1,0:T(8,128)(2,1)S(1)}, u32[]{:S(2)}, u32[]{:S(2)}) collective-permute-start(bf16[64,2560]{1,0:T(8,128)(2,1)S(1)} %get-tuple-element.73), channel_id=1, source_target_pairs={{16,8},{17,9},{18,10},{19,11},{20,12},{21,13},{22,14},{23,15}} | collective-permute-start | bytes 983048 | tf_op jit(solution)/shard_map/ppermute | solution.py:362
  155.5 4.7 %collective-permute-start.33 = (bf16[64,2560]{1,0:T(8,128)(2,1)S(1)}, bf16[64,2560]{1,0:T(8,128)(2,1)S(1)}, u32[]{:S(2)}, u32[]{:S(2)}) collective-permute-start(bf16[64,2560]{1,0:T(8,128)(2,1)S(1)} %get-tuple-element.72), channel_id=1, source_target_pairs={{16,8},{17,9},{18,10},{19,11},{20,12},{21,13},{22,14},{23,15}} | collective-permute-start | bytes 983048 | tf_op jit(solution)/shard_map/ppermute | solution.py:362
  156.2 29.6 %collective-permute-start.40 = (bf16[64,2560]{1,0:T(8,128)(2,1)S(1)}, bf16[64,2560]{1,0:T(8,128)(2,1)S(1)}, u32[]{:S(2)}, u32[]{:S(2)}) collective-permute-start(bf16[64,2560]{1,0:T(8,128)(2,1)S(1)} %get-tuple-element.88), channel_id=1, source_target_pairs={{8,0},{9,1},{10,2},{11,3},{12,4},{13,5},{14,6},{15,7}} | collective-permute-start | bytes 983048 | tf_op jit(solution)/shard_map/ppermute | solution.py:362
  157.6 35.3 %collective-permute-start.39 = (bf16[64,2560]{1,0:T(8,128)(2,1)S(1)}, bf16[64,2560]{1,0:T(8,128)(2,1)S(1)}, u32[]{:S(2)}, u32[]{:S(2)}) collective-permute-start(bf16[64,2560]{1,0:T(8,128)(2,1)S(1)} %get-tuple-element.87), channel_id=1, source_target_pairs={{8,0},{9,1},{10,2},{11,3},{12,4},{13,5},{14,6},{15,7}} | collective-permute-start | bytes 983048 | tf_op jit(solution)/shard_map/ppermute | solution.py:362
  158.9 41.0 %collective-permute-start.38 = (bf16[64,2560]{1,0:T(8,128)(2,1)S(1)}, bf16[64,2560]{1,0:T(8,128)(2,1)S(1)}, u32[]{:S(2)}, u32[]{:S(2)}) collective-permute-start(bf16[64,2560]{1,0:T(8,128)(2,1)S(1)} %get-tuple-element.86), channel_id=1, source_target_pairs={{8,0},{9,1},{10,2},{11,3},{12,4},{13,5},{14,6},{15,7}} | collective-permute-start | bytes 983048 | tf_op jit(solution)/shard_map/ppermute | solution.py:362
  160.4 47.1 %collective-permute-start.37 = (bf16[64,2560]{1,0:T(8,128)(2,1)S(1)}, bf16[64,2560]{1,0:T(8,128)(2,1)S(1)}, u32[]{:S(2)}, u32[]{:S(2)}) collective-permute-start(bf16[64,2560]{1,0:T(8,128)(2,1)S(1)} %get-tuple-element.85), channel_id=1, source_target_pairs={{8,0},{9,1},{10,2},{11,3},{12,4},{13,5},{14,6},{15,7}} | collective-permute-start | bytes 983048 | tf_op jit(solution)/shard_map/ppermute | solution.py:362
  207.6 14.8 %slice-start = ((s8[6553600]{0:T(1024)(128)(4,1)}), s8[4194304]{0:T(1024)(128)(4,1)S(1)}, s32[]{:S(2)}) async-start(s8[6553600]{0:T(1024)(128)(4,1)} %bitcast.31), calls=%async_computation | async-start | bytes 8388608
  207.6 3.5 %copy-start.2 = (bf16[1,256,2560]{2,1,0:T(8,128)(2,1)S(1)}, bf16[1,256,2560]{2,1,0:T(8,128)(2,1)}, u32[]{:S(2)}) copy-start(bf16[1,256,2560]{2,1,0:T(8,128)(2,1)} %param.7) | copy-start | bytes 3932164
  207.6 14.8 %slice-start.1 = ((s8[6553600]{0:T(1024)(128)(4,1)}), s8[2359296]{0:T(1024)(128)(4,1)S(1)}, s32[]{:S(2)}) async-start(s8[6553600]{0:T(1024)(128)(4,1)} %bitcast.31), calls=%async_computation.1 | async-start | bytes 4718592
  212.0 1.3 collective-permute-start.41
  213.3 4.1 %collective-permute-start.42 = (f32[4,2560]{1,0:T(4,128)S(1)}, f32[4,2560]{1,0:T(4,128)S(1)}, u32[]{:S(2)}, u32[]{:S(2)}) collective-permute-start(f32[4,2560]{1,0:T(4,128)S(1)} %add.15), channel_id=1, source_target_pairs={{0,2},{1,3},{2,0},{3,1},{4,6},{5,7},{6,4},{7,5},{8,10},{9,11},{10,... | collective-permute-start | bytes 122888 | tf_op jit(solution)/shard_map/ppermute | solution.py:301
  217.4 5.0 %collective-permute-start.43 = (f32[4,2560]{1,0:T(4,128)S(1)}, f32[4,2560]{1,0:T(4,128)S(1)}, u32[]{:S(2)}, u32[]{:S(2)}) collective-permute-start(f32[4,2560]{1,0:T(4,128)S(1)} %add.16.refs_0_), channel_id=1, source_target_pairs={{0,4},{1,5},{2,6},{3,7},{4,0},{5,1},{6,2},{7,3},{8,12},{9,13},{10,... | collective-permute-start | bytes 122888 | tf_op jit(solution)/shard_map/ppermute | solution.py:301
  225.2 1.3 collective-permute-start.44
  226.4 3.8 %collective-permute-start.45 = (f32[4,1280]{1,0:T(4,128)S(1)}, f32[4,1280]{1,0:T(4,128)S(1)}, u32[]{:S(2)}, u32[]{:S(2)}) collective-permute-start(f32[4,1280]{1,0:T(4,128)S(1)} %add.17), channel_id=1, source_target_pairs={{0,2},{1,3},{2,0},{3,1},{4,6},{5,7},{6,4},{7,5},{8,10},{9,11},{10,... | collective-permute-start | bytes 61448 | tf_op jit(solution)/shard_map/ppermute | solution.py:301
  230.3 4.7 %collective-permute-start.46 = (f32[4,1280]{1,0:T(4,128)S(1)}, f32[4,1280]{1,0:T(4,128)S(1)}, u32[]{:S(2)}, u32[]{:S(2)}) collective-permute-start(f32[4,1280]{1,0:T(4,128)S(1)} %add.18), channel_id=1, source_target_pairs={{0,4},{1,5},{2,6},{3,7},{4,0},{5,1},{6,2},{7,3},{8,12},{9,13},{10,... | collective-permute-start | bytes 61448 | tf_op jit(solution)/shard_map/ppermute | solution.py:301
  (1 other events, 0.9 us)
